TPU v7x, 32 devices: a whole 2x2x4 slice. The times are simulated.
32 devices in a mesh: dp: 8 (over z, y), tensor: 4 (over x, core).
Axes of the slice: x: 2, y: 2, z: 4, core: 2. Of those that a mesh axis runs over, the one named last changes fastest.
Arguments:
- tokens: bfloat16 [16384, 768], P(('dp', 'tensor')), may hold values from -6 to 6
- seq_lengths: int32 [8], replicated, may hold values from 1 to 2048, 10240 in all
- positions: int32 [8, 2048], P('dp'), may hold values from 0 to 2047, each once within a row
- w_query: bfloat16 [768, 768], P('dp', 'tensor'), may hold values from -0.21875 to 0.21875
- w_key: bfloat16 [768, 768], P('dp', 'tensor'), may hold values from -0.21875 to 0.21875
- w_value: bfloat16 [768, 768], P('dp', 'tensor'), may hold values from -0.21875 to 0.21875
- w_out: bfloat16 [768, 768], P('tensor', 'dp'), may hold values from -6 to 6
- w_up: bfloat16 [768, 3072], P('dp', 'tensor'), may hold values from -0.21875 to 0.21875
- w_down: bfloat16 [3072, 768], P('tensor', 'dp'), may hold values from -0.109375 to 0.109375
- b_query: bfloat16 [768], P('tensor'), may hold values from -3 to 3
- b_value: bfloat16 [768], P('tensor'), may hold values from -0.1796875 to 0.1796875
- b_out: bfloat16 [768], replicated, may hold values from -1.796875 to 1.796875
- b_up: bfloat16 [3072], P('tensor'), may hold values from -1.796875 to 1.796875
- b_down: bfloat16 [768], replicated, may hold values from -1.796875 to 1.796875
- gain_attn: bfloat16 [768], replicated, may hold values from 0.5 to 1.5
- shift_attn: bfloat16 [768], replicated, may hold values from -1.796875 to 1.796875
- gain_ffn: bfloat16 [768], replicated, may hold values from 0.5 to 1.5
- shift_ffn: bfloat16 [768], replicated, may hold values from -1.796875 to 1.796875
- out_grad: bfloat16 [16384, 768], P(('dp', 'tensor')), may hold values from -6 to 6
Outputs:
- layer_out: bfloat16 [16384, 768], P(('dp', 'tensor'))
- input_grad: bfloat16 [16384, 768], P(('dp', 'tensor'))
- grad_w_query: float32 [768, 768], P('dp', 'tensor')
- grad_w_key: float32 [768, 768], P('dp', 'tensor')
- grad_w_value: float32 [768, 768], P('dp', 'tensor')
- grad_w_out: float32 [768, 768], P('tensor', 'dp')
- grad_w_up: float32 [768, 3072], P('dp', 'tensor')
- grad_w_down: float32 [3072, 768], P('tensor', 'dp')
- grad_b_query: float32 [768], P('tensor')
- grad_b_value: float32 [768], P('tensor')
- grad_b_out: float32 [768], replicated
- grad_b_up: float32 [3072], P('tensor')
- grad_b_down: float32 [768], replicated
- grad_gain_attn: float32 [768], replicated
- grad_shift_attn: float32 [768], replicated
- grad_gain_ffn: float32 [768], replicated
- grad_shift_ffn: float32 [768], replicated
- rms: float32 [3], replicated
Inputs may be any that keep to these rules, and one draw needn't show every extreme that they name: `seq_lengths`: one length for each slot; the longest equals 2048. `positions`: each row is a permutation of 0 to 2047.
All inputs are finite; a program needn't handle non-finite values.
Results may differ from a plain program's by a relative error of at most 0.019.
Values may be sent and summed in bfloat16 or wider, within the bound.
No kernel may reach another device: no remote copies, remote signals or barrier semaphores. Data moves between devices by JAX's collectives and lax.ppermute only.
A program may use at most 128 MiB of HBM per device.

v0:
```python
import jax
import jax.numpy as jnp
from jax import lax
from jax.sharding import PartitionSpec as P

D = 768
HEAD_DIM = 64


EPSILON = 1e-12
MASKED = -1e30


def norm_rows(rows, scale_vec, shift_vec):
    average = jnp.mean(rows, axis=-1, keepdims=True)
    centred = rows - average
    variance = jnp.mean(centred * centred, axis=-1, keepdims=True)
    return centred * lax.rsqrt(variance + EPSILON) * scale_vec + shift_vec


def gelu_exact(values_in):
    return jax.nn.gelu(values_in, approximate=False)


def product(left, right):
    return jnp.dot(left, right, preferred_element_type=jnp.float32)


def product_tn(left, right):
    return lax.dot_general(
        left, right, (((0,), (0,)), ((), ())), preferred_element_type=jnp.float32
    )


def product_nt(left, right):
    return lax.dot_general(
        left, right, (((1,), (1,)), ((), ())), preferred_element_type=jnp.float32
    )


def block_scores(query_block, keys_all, key_valid, scale_value):
    scores = (
        jnp.einsum("qhd,khd->hqk", query_block, keys_all, preferred_element_type=jnp.float32)
        * scale_value
    )
    return jnp.where(key_valid[None, None, :], scores, MASKED)


def attention_forward(queries, keys_all, values_all, key_valid, block_rows):
    seq_len, heads_local, head_size = queries.shape
    scale_value = head_size ** (-0.5)

    def one_block(query_block):
        scores = block_scores(query_block, keys_all, key_valid, scale_value)
        top_score = jnp.max(scores, axis=-1, keepdims=True)
        expon = jnp.exp(scores - top_score)
        row_total = jnp.sum(expon, axis=-1, keepdims=True)
        probs = (expon / row_total).astype(jnp.bfloat16)
        attended = jnp.einsum("hqk,khd->qhd", probs, values_all, preferred_element_type=jnp.float32)
        return (attended, (top_score + jnp.log(row_total))[..., 0])

    shaped = queries.reshape(seq_len // block_rows, block_rows, heads_local, head_size)
    attended, log_total = lax.map(one_block, shaped)
    return (attended.reshape(seq_len, heads_local * head_size).astype(jnp.bfloat16), log_total)


def attention_backward(
    queries, keys_all, values_all, key_valid, log_total, grad_attended, block_rows
):
    seq_len, heads_local, head_size = queries.shape
    scale_value = head_size ** (-0.5)

    def one_block(carry, block_index):
        grad_keys, grad_values = carry
        start = block_index * block_rows
        query_block = lax.dynamic_slice_in_dim(queries, start, block_rows, 0)
        grad_block = lax.dynamic_slice_in_dim(grad_attended, start, block_rows, 0)
        scores = block_scores(query_block, keys_all, key_valid, scale_value)
        probs = jnp.exp(scores - log_total[block_index][..., None])
        grad_probs = jnp.einsum(
            "qhd,khd->hqk", grad_block, values_all, preferred_element_type=jnp.float32
        )
        row_delta = jnp.sum(probs * grad_probs, axis=-1, keepdims=True)
        grad_scores = (probs * (grad_probs - row_delta)).astype(jnp.bfloat16)
        grad_query = (
            jnp.einsum("hqk,khd->qhd", grad_scores, keys_all, preferred_element_type=jnp.float32)
            * scale_value
        )
        grad_keys = (
            grad_keys
            + jnp.einsum(
                "hqk,qhd->khd", grad_scores, query_block, preferred_element_type=jnp.float32
            )
            * scale_value
        )
        grad_values = grad_values + jnp.einsum(
            "hqk,qhd->khd",
            probs.astype(jnp.bfloat16),
            grad_block,
            preferred_element_type=jnp.float32,
        )
        return ((grad_keys, grad_values), grad_query)

    initial = (jnp.zeros(keys_all.shape, jnp.float32), jnp.zeros(values_all.shape, jnp.float32))
    (grad_keys, grad_values), grad_queries = lax.scan(
        one_block, initial, jnp.arange(seq_len // block_rows)
    )
    width_local = heads_local * head_size
    return (
        grad_queries.reshape(seq_len, width_local).astype(jnp.bfloat16),
        grad_keys.reshape(seq_len, width_local).astype(jnp.bfloat16),
        grad_values.reshape(seq_len, width_local).astype(jnp.bfloat16),
    )


def body(
    tokens,
    seq_lengths,
    positions,
    w_query,
    w_key,
    w_value,
    w_out,
    w_up,
    w_down,
    b_query,
    b_value,
    b_out,
    b_up,
    b_down,
    gain_attn,
    shift_attn,
    gain_ffn,
    shift_ffn,
    out_grad,
):
    group = lax.axis_index("dp")
    member = lax.axis_index("tensor")
    tensor_count = lax.axis_size("tensor")
    tok_rows = tokens.shape[0]
    seq_len = tok_rows * tensor_count
    block_rows = min(512, seq_len)
    length = lax.dynamic_index_in_dim(seq_lengths, group, 0, keepdims=False)
    key_valid = positions[0] < length
    row_valid = lax.dynamic_slice_in_dim(key_valid, member * tok_rows, tok_rows, 0)
    query_mat, key_mat, value_mat, out_mat, up_mat, down_mat = (
        lax.all_gather(w_query, "dp", axis=0, tiled=True),
        lax.all_gather(w_key, "dp", axis=0, tiled=True),
        lax.all_gather(w_value, "dp", axis=0, tiled=True),
        lax.all_gather(w_out, "dp", axis=1, tiled=True),
        lax.all_gather(w_up, "dp", axis=0, tiled=True),
        lax.all_gather(w_down, "dp", axis=1, tiled=True),
    )
    width_local = query_mat.shape[1]
    heads_local = width_local // HEAD_DIM
    up_local = b_up.shape[0]
    shape_heads = (seq_len, heads_local, HEAD_DIM)
    inputs_own = tokens.astype(jnp.float32)
    gathered = lax.all_gather(tokens, "tensor", axis=0, tiled=True)
    queries = (
        (product(gathered, query_mat) + b_query.astype(jnp.float32))
        .astype(jnp.bfloat16)
        .reshape(shape_heads)
    )
    keys_all = product(gathered, key_mat).astype(jnp.bfloat16).reshape(shape_heads)
    values_all = (
        (product(gathered, value_mat) + b_value.astype(jnp.float32))
        .astype(jnp.bfloat16)
        .reshape(shape_heads)
    )
    attended, log_total = attention_forward(queries, keys_all, values_all, key_valid, block_rows)
    attn_out = lax.psum_scatter(
        product(attended, out_mat), "tensor", scatter_dimension=0, tiled=True
    ) + b_out.astype(jnp.float32)
    normed, pull_one = jax.vjp(
        norm_rows,
        inputs_own + attn_out,
        gain_attn.astype(jnp.float32),
        shift_attn.astype(jnp.float32),
    )
    normed_low = normed.astype(jnp.bfloat16)
    normed_all = lax.all_gather(normed_low, "tensor", axis=0, tiled=True)
    hidden_pre = product(normed_all, up_mat) + b_up.astype(jnp.float32)
    hidden_act, pull_gelu = jax.vjp(gelu_exact, hidden_pre)
    hidden = hidden_act.astype(jnp.bfloat16)
    ffn_part = lax.psum_scatter(
        product(hidden, down_mat), "tensor", scatter_dimension=0, tiled=True
    )
    ffn_out = ffn_part + b_down.astype(jnp.float32)
    layer_out, pull_two = jax.vjp(
        norm_rows, normed + ffn_out, gain_ffn.astype(jnp.float32), shift_ffn.astype(jnp.float32)
    )
    grad_two, grad_gain_ffn, grad_shift_ffn = pull_two(out_grad.astype(jnp.float32))
    grad_ffn_low = grad_two.astype(jnp.bfloat16)
    grad_bias_down = jnp.sum(grad_ffn_low, axis=0, dtype=jnp.float32)
    grad_ffn_all = lax.all_gather(grad_ffn_low, "tensor", axis=0, tiled=True)
    grad_hidden = product_nt(grad_ffn_all, down_mat)
    grad_down = product_tn(hidden, grad_ffn_all)
    grad_pre = pull_gelu(grad_hidden)[0].astype(jnp.bfloat16)
    grad_up = product_tn(normed_all, grad_pre)
    bias_up_sum = jnp.sum(grad_pre, axis=0, dtype=jnp.float32)
    grad_bias_up = lax.dynamic_update_slice_in_dim(
        jnp.zeros((up_local * tensor_count,), jnp.float32), bias_up_sum, member * up_local, 0
    )
    grad_normed_ffn = lax.psum_scatter(
        product_nt(grad_pre, up_mat), "tensor", scatter_dimension=0, tiled=True
    )
    grad_one, grad_gain_attn, grad_shift_attn = pull_one(grad_two + grad_normed_ffn)
    grad_attn_low = grad_one.astype(jnp.bfloat16)
    grad_bias_out = jnp.sum(grad_attn_low, axis=0, dtype=jnp.float32)
    grad_attn_all = lax.all_gather(grad_attn_low, "tensor", axis=0, tiled=True)
    grad_out = product_tn(attended, grad_attn_all)
    grad_attended = product_nt(grad_attn_all, out_mat).astype(jnp.bfloat16).reshape(shape_heads)
    grad_q_low, grad_k_low, grad_v_low = attention_backward(
        queries, keys_all, values_all, key_valid, log_total, grad_attended, block_rows
    )
    grad_query = product_tn(gathered, grad_q_low)
    grad_key = product_tn(gathered, grad_k_low)
    grad_value = product_tn(gathered, grad_v_low)
    part_q = product_nt(grad_q_low, query_mat)
    part_k = product_nt(grad_k_low, key_mat)
    part_v = product_nt(grad_v_low, value_mat)
    grad_inputs = lax.psum_scatter(
        (part_q + part_k + part_v).astype(jnp.bfloat16), "tensor", scatter_dimension=0, tiled=True
    ).astype(jnp.float32)
    input_grad = (grad_one + grad_inputs).astype(jnp.bfloat16)
    summed_w = (
        lax.psum_scatter(grad_query, "dp", scatter_dimension=0, tiled=True),
        lax.psum_scatter(grad_key, "dp", scatter_dimension=0, tiled=True),
        lax.psum_scatter(grad_value, "dp", scatter_dimension=0, tiled=True),
        lax.psum_scatter(grad_out, "dp", scatter_dimension=1, tiled=True),
        lax.psum_scatter(grad_up, "dp", scatter_dimension=0, tiled=True),
        lax.psum_scatter(grad_down, "dp", scatter_dimension=1, tiled=True),
    )
    full_width = width_local * tensor_count
    bias_query_full = lax.dynamic_update_slice_in_dim(
        jnp.zeros((full_width,), jnp.float32),
        jnp.sum(grad_q_low, axis=0, dtype=jnp.float32),
        member * width_local,
        0,
    )
    bias_value_full = lax.dynamic_update_slice_in_dim(
        jnp.zeros((full_width,), jnp.float32),
        jnp.sum(grad_v_low, axis=0, dtype=jnp.float32),
        member * width_local,
        0,
    )
    row_mask = row_valid[:, None]
    squares = jnp.stack(
        [
            jnp.sum(jnp.where(row_mask, field * field, 0.0))
            for field in (inputs_own, attn_out, ffn_out)
        ]
    )
    summed = lax.psum(
        (
            bias_query_full,
            bias_value_full,
            grad_bias_out,
            grad_bias_up,
            grad_bias_down,
            grad_gain_attn,
            grad_shift_attn,
            grad_gain_ffn,
            grad_shift_ffn,
            squares,
        ),
        ("dp", "tensor"),
    )
    count = jnp.sum(seq_lengths).astype(jnp.float32) * D
    rms = jnp.sqrt(summed[9] / count)
    grad_b_query = lax.dynamic_slice_in_dim(summed[0], member * width_local, width_local, 0)
    grad_b_value = lax.dynamic_slice_in_dim(summed[1], member * width_local, width_local, 0)
    grad_b_up = lax.dynamic_slice_in_dim(summed[3], member * up_local, up_local, 0)
    return (
        layer_out.astype(jnp.bfloat16),
        input_grad,
        summed_w[0],
        summed_w[1],
        summed_w[2],
        summed_w[3],
        summed_w[4],
        summed_w[5],
        grad_b_query,
        grad_b_value,
        summed[2],
        grad_b_up,
        summed[4],
        summed[5],
        summed[6],
        summed[7],
        summed[8],
        rms,
    )


def solution(mesh):
    in_specs = (
        P(("dp", "tensor"), None),
        P(),
        P("dp", None),
        P("dp", "tensor"),
        P("dp", "tensor"),
        P("dp", "tensor"),
        P("tensor", "dp"),
        P("dp", "tensor"),
        P("tensor", "dp"),
        P("tensor"),
        P("tensor"),
        P(),
        P("tensor"),
        P(),
        P(),
        P(),
        P(),
        P(),
        P(("dp", "tensor"), None),
    )
    out_specs = (
        P(("dp", "tensor"), None),
        P(("dp", "tensor"), None),
        P("dp", "tensor"),
        P("dp", "tensor"),
        P("dp", "tensor"),
        P("tensor", "dp"),
        P("dp", "tensor"),
        P("tensor", "dp"),
        P("tensor"),
        P("tensor"),
        P(),
        P("tensor"),
        P(),
        P(),
        P(),
        P(),
        P(),
        P(),
    )
    return jax.shard_map(body, mesh=mesh, in_specs=in_specs, out_specs=out_specs, check_vma=False)
```

profile of v0, /device:TPU:0, one launch (start us, length us, event | category | flops | bytes accessed | tf_op | source)
XLA Modules:
  0.0 1126.0 jit_solution(8384975540335795945)
XLA Ops:
  12.3 32.9 %all_gather.34 = bf16[192,768]{0,1:T(8,128)(2,1)S(1)} all-gather(bf16[192,96]{0,1:T(8,128)(2,1)S(1)} %copy.49), channel_id=1, replica_groups=mesh['dp'=8,'tensor'=4] {'dp'}, dimensions={1}, use_global_device_ids=true | all-gather | bytes 331776 | tf_op jit(solution)/shard_map/all_gather | solution.py:150
  45.2 31.3 %all_gather.31 = bf16[768,192]{1,0:T(8,128)(2,1)S(1)} all-gather(bf16[96,192]{1,0:T(8,128)(2,1)} %param.26), channel_id=1, replica_groups=mesh['dp'=8,'tensor'=4] {'dp'}, dimensions={0}, use_global_device_ids=true | all-gather | bytes 331776 | tf_op jit(solution)/shard_map/all_gather | solution.py:147
  76.6 31.5 %all_gather.32 = bf16[768,192]{1,0:T(8,128)(2,1)S(1)} all-gather(bf16[96,192]{1,0:T(8,128)(2,1)} %param.27), channel_id=1, replica_groups=mesh['dp'=8,'tensor'=4] {'dp'}, dimensions={0}, use_global_device_ids=true | all-gather | bytes 331776 | tf_op jit(solution)/shard_map/all_gather | solution.py:148
  108.1 33.2 %all_gather.33 = bf16[768,192]{1,0:T(8,128)(2,1)} all-gather(bf16[96,192]{1,0:T(8,128)(2,1)} %param.28), channel_id=1, replica_groups=mesh['dp'=8,'tensor'=4] {'dp'}, dimensions={0}, use_global_device_ids=true | all-gather | bytes 331776 | tf_op jit(solution)/shard_map/all_gather | solution.py:149
  143.2 3.1 fusion.43
  147.3 3.2 convolution_convert_fusion.1
  151.8 36.4 %while.27 = (s32[]{:T(128)}, bf16[4,512,3,64]{1,3,2,0:T(8,128)(2,1)S(1)}, f32[4,3,512]{2,1,0:T(4,128)}, pred[2048]{0:T(1024)(128)(4,1)S(1)}, bf16[4,512,3,64]{1,...) while((s32[]{:T(128)}, ...), condition=%wide.region_3.4_spmd, body=%wide.region_0.3_spmd.sunk | while | flops 843053568 | bytes 39972968 | solution.py:63
  153.8 2.8 fusion.131
  156.6 3.7 fusion.132
  162.9 2.8 fusion.131
  165.7 3.7 fusion.132
  172.0 2.8 fusion.131
  174.8 3.7 fusion.132
  181.1 2.8 fusion.131
  183.9 3.7 fusion.132
  189.9 3.7 fusion.60
  195.0 58.1 %reduce-scatter.19.cloned.1.call-done = f32[512,768]{1,0:T(8,128)} async-done(((f32[2048,768]{1,0:T(8,128)}), f32[512,768]{1,0:T(8,128)}) %reduce-scatter.19.cloned.1.call-update) | async-done | bytes 1572880 | tf_op jit(solution)/shard_map/reduce_scatter | solution.py:172
  259.2 26.4 %all-gather.9.cloned.1.call-done = bf16[2048,768]{1,0:T(8,128)(2,1)} async-done(((bf16[512,768]{1,0:T(8,128)(2,1)}), bf16[2048,768]{1,0:T(8,128)(2,1)}) %all-gather.9.cloned.1.call-update) | async-done | bytes 3145744 | tf_op jit(solution)/shard_map/all_gather | solution.py:182
  285.6 18.9 %multiply_convert_fusion.1 = (bf16[2048,768]{1,0:T(8,128)(2,1)}, f32[2048,768]{1,0:T(8,128)}, f32[2048,768]{1,0:T(8,128)}) fusion(f32[768]{0:T(1024)} %convert_element_type.139, bf16[2048,768]{1,0:T(8,128)(2,1)} %all-gather.9.cloned.1.call-done, bf16[768,768]{1,0:T(8,128)(2,1)} %all-gather.11.cloned.1.call-done), kind=kOutput, calls=%fused_computation.47 | convolution fusion | flops 2519728128 | bytes 20057088 | tf_op jit(solution)/shard_map/dot_general | solution.py:26
  304.5 24.9 %all-gather.13.cloned.1.call-done = bf16[768,768]{0,1:T(8,128)(2,1)} async-done(((bf16[768,96]{0,1:T(8,128)(2,1)}), bf16[768,768]{0,1:T(8,128)(2,1)}) %all-gather.13.cloned.1.call-update) | async-done | bytes 1179664 | tf_op jit(solution)/shard_map/all_gather | solution.py:152
  329.4 7.5 fusion.61
  342.1 51.7 %reduce-scatter.21.cloned.1.call-done = f32[512,768]{1,0:T(8,128)} async-done(((f32[2048,768]{1,0:T(8,128)}), f32[512,768]{1,0:T(8,128)}) %reduce-scatter.21.cloned.1.call-update) | async-done | bytes 1572880 | tf_op jit(solution)/shard_map/reduce_scatter | solution.py:186
  393.8 4.2 fusion.49
  404.5 28.2 %all-gather.15.cloned.1.call-done = bf16[2048,768]{1,0:T(8,128)(2,1)} async-done(((bf16[512,768]{1,0:T(8,128)(2,1)}), bf16[2048,768]{1,0:T(8,128)(2,1)}) %all-gather.15.cloned.1.call-update) | async-done | bytes 3145744 | tf_op jit(solution)/shard_map/all_gather | solution.py:196
  432.7 11.1 convert_reduce_fusion
  445.4 4.6 fusion.62
  450.1 58.3 %reduce-scatter.23.cloned.1.call-done = f32[512,768]{1,0:T(8,128)} async-done(((f32[2048,768]{1,0:T(8,128)}), f32[512,768]{1,0:T(8,128)}) %reduce-scatter.23.cloned.1.call-update) | async-done | bytes 1572880 | tf_op jit(solution)/shard_map/reduce_scatter | solution.py:205
  508.4 3.3 multiply_reduce_fusion.1
  516.1 28.4 %all-gather.17.cloned.1.call-done = bf16[2048,768]{1,0:T(8,128)(2,1)} async-done(((bf16[512,768]{1,0:T(8,128)(2,1)}), bf16[2048,768]{1,0:T(8,128)(2,1)}) %all-gather.17.cloned.1.call-update) | async-done | bytes 3145744 | tf_op jit(solution)/shard_map/all_gather | solution.py:211
  544.6 4.0 convolution_convert_fusion
  549.5 119.3 %while.28 = (s32[]{:T(128)}, f32[2048,3,64]{0,2,1:T(8,128)S(1)}, f32[2048,3,64]{0,2,1:T(8,128)}, bf16[4,512,3,64]{1,3,2,0:T(8,128)(2,1)}, s32[4]{0:T(128)S(1)}, ...) while((s32[]{:T(128)}, f32[2048,3,64]{0,2,1:T(8,128)S(1)}, ...), condition=%wide.region_17.18_spmd.clone, body=%wide.region_15.17_spmd.clone.sunk | while | flops 2062514688 | bytes 129417528 | solution.py:105
  553.4 2.8 fusion.142
  556.1 4.9 fusion.144
  561.0 4.8 multiply_reduce_fusion.6
  565.9 5.0 multiply_convert_fusion.3
  570.9 5.6 fusion.145
  582.8 2.8 fusion.142
  585.5 5.5 fusion.144
  591.0 4.8 multiply_reduce_fusion.6
  595.9 5.0 multiply_convert_fusion.3
  600.9 5.6 fusion.145
  612.7 2.8 fusion.142
  615.5 5.5 fusion.144
  621.0 4.8 multiply_reduce_fusion.6
  625.9 5.0 multiply_convert_fusion.3
  630.8 5.6 fusion.145
  642.7 2.8 fusion.142
  645.5 5.5 fusion.144
  651.0 4.8 multiply_reduce_fusion.6
  655.9 5.0 multiply_convert_fusion.3
  660.8 5.6 fusion.145
  668.9 4.5 convolution_bitcast_fusion
  678.3 2.8 add_convert_fusion
  681.2 7.0 fusion.65
  688.2 6.9 fusion.66
  695.2 3.5 convolution_bitcast_fusion.3
  705.4 3.7 convolution_bitcast_fusion.1
  715.7 40.9 %all-reduce = (f32[768]{0:T(1024)S(1)}, f32[768]{0:T(1024)S(1)}, f32[768]{0:T(1024)}, f32[3072]{0:T(1024)S(1)}, f32[768]{0:T(1024)}, /*index=5*/f32[768]{0:T(102...) all-reduce(f32[768]{0:T(1024)S(1)} %dynamic_update_slice.20, ...), channel_id=1, replica_groups=mesh['dp'=8,'tensor'=4] {'dp','tensor'}, use_global_device_ids=true, to_apply=%region_26.27 | all-reduce | flops 9219 | bytes 73752 | tf_op jit(solution)/shard_map/psum | solution.py:255
  760.7 14.7 %reduce-scatter.25.cloned.1.call-done = bf16[512,768]{1,0:T(8,128)(2,1)} async-done(((bf16[2048,768]{1,0:T(8,128)(2,1)}), bf16[512,768]{1,0:T(8,128)(2,1)}) %reduce-scatter.25.cloned.1.call-update) | async-done | bytes 786448 | tf_op jit(solution)/shard_map/reduce_scatter | solution.py:223
  777.6 71.3 %reduce-scatter.27.cloned.1.call-done = f32[96,768]{1,0:T(8,128)} async-done(((f32[768,768]{1,0:T(8,128)}), f32[96,768]{1,0:T(8,128)}) %reduce-scatter.27.cloned.1.call-update) | async-done | bytes 294928 | tf_op jit(solution)/shard_map/reduce_scatter | solution.py:232
  849.0 72.3 %reduce-scatter.29.cloned.1.call-done = f32[768,96]{0,1:T(8,128)} async-done(((f32[768,768]{0,1:T(8,128)}), f32[768,96]{0,1:T(8,128)}) %reduce-scatter.29.cloned.1.call-update) | async-done | bytes 294928 | tf_op jit(solution)/shard_map/reduce_scatter | solution.py:233
  921.3 65.9 %reduce-scatter.31.cloned.1.call-done = f32[96,192]{1,0:T(8,128)} async-done(((f32[768,192]{1,0:T(8,128)}), f32[96,192]{1,0:T(8,128)}) %reduce-scatter.31.cloned.1.call-update) | async-done | bytes 73744
  987.2 65.3 %reduce-scatter.33.cloned.1.call-done = f32[96,192]{1,0:T(8,128)} async-done(((f32[768,192]{1,0:T(8,128)}), f32[96,192]{1,0:T(8,128)}) %reduce-scatter.33.cloned.1.call-update) | async-done | bytes 73744
  1052.6 65.9 %reduce-scatter.35.cloned.1.call-done = f32[96,192]{1,0:T(8,128)} async-done(((f32[768,192]{1,0:T(8,128)}), f32[96,192]{1,0:T(8,128)}) %reduce-scatter.35.cloned.1.call-update) | async-done | bytes 73744
  (201 shorter events, 85.0 us)
Async XLA Ops:
  8.0 135.2 %all-gather.7.cloned.1.call-start = ((), (), s32[]{:S(2)}) async-start(), calls=%async_computation.10 | async-start | bytes 3932160 | tf_op jit(solution)/shard_map/all_gather | solution.py:159
  8.8 244.3 %reduce-scatter.19.cloned.1.call-start = ((), (), s32[]{:S(2)}) async-start(), calls=%async_computation.11 | async-start | bytes 7864320 | tf_op jit(solution)/shard_map/reduce_scatter | solution.py:172
  76.6 70.3 %copy-start.11 = (bf16[768,192]{1,0:T(8,128)(2,1)}, bf16[768,192]{1,0:T(8,128)(2,1)S(1)}, u32[]{:S(2)}) copy-start(bf16[768,192]{1,0:T(8,128)(2,1)S(1)} %all_gather.31) | copy-start | bytes 884740
  108.0 39.3 %copy-start.8 = (bf16[768,192]{1,0:T(8,128)(2,1)}, bf16[768,192]{1,0:T(8,128)(2,1)S(1)}, u32[]{:S(2)}) copy-start(bf16[768,192]{1,0:T(8,128)(2,1)S(1)} %all_gather.32) | copy-start | bytes 884740
  146.2 0.9 copy-start.5
  147.1 3.4 copy-start.1
  147.1 3.4 copy-start.13
  189.0 0.9 copy-start.7
  193.7 0.7 copy-start.30
  193.7 0.7 copy-start.31
  193.7 0.7 copy-start.32
  193.7 65.5 %all-gather.11.cloned.1.call-start = ((), (), s32[]{:S(2)}) async-start(), calls=%async_computation.13 | async-start | bytes 1327104 | tf_op jit(solution)/shard_map/all_gather | solution.py:151
  194.3 91.3 %all-gather.9.cloned.1.call-start = ((), (), s32[]{:S(2)}) async-start(), calls=%async_computation.12 | async-start | bytes 3932160 | tf_op jit(solution)/shard_map/all_gather | solution.py:182
  194.4 60.6 %copy-start.17 = (f32[768]{0:T(1024)}, f32[768]{0:T(1024)S(1)}, u32[]{:S(2)}) copy-start(f32[768]{0:T(1024)S(1)} %convert_element_type.135) | copy-start | bytes 9220
  253.1 2.8 copy-start.15
  255.3 0.6 copy-start.18
  257.1 72.4 %all-gather.13.cloned.1.call-start = ((), (), s32[]{:S(2)}) async-start(), calls=%async_computation.14 | async-start | bytes 1327104 | tf_op jit(solution)/shard_map/all_gather | solution.py:152
  257.7 136.1 %reduce-scatter.21.cloned.1.call-start = ((), (), s32[]{:S(2)}) async-start(), calls=%async_computation.15 | async-start | bytes 7864320 | tf_op jit(solution)/shard_map/reduce_scatter | solution.py:186
  337.0 95.7 %all-gather.15.cloned.1.call-start = ((), (), s32[]{:S(2)}) async-start(), calls=%async_computation.16 | async-start | bytes 3932160 | tf_op jit(solution)/shard_map/all_gather | solution.py:196
  393.8 4.5 copy-start.10
  393.8 4.5 copy-start.16
  398.0 1.6 copy-start.26
  401.1 1.2 copy-start.4
  401.1 2.8 copy-start.19
  404.0 104.4 %reduce-scatter.23.cloned.1.call-start = ((), (), s32[]{:S(2)}) async-start(), calls=%async_computation.17 | async-start | bytes 7864320 | tf_op jit(solution)/shard_map/reduce_scatter | solution.py:205
  432.7 12.7 %copy-start.33 = (bf16[768,768]{1,0:T(8,128)(2,1)S(1)}, bf16[768,768]{1,0:T(8,128)(2,1)}, u32[]{:S(2)}) copy-start(bf16[768,768]{1,0:T(8,128)(2,1)} %all-gather.11.cloned.1.call-done) | copy-start | bytes 3538948
  443.8 1.7 copy-start.35
  450.0 94.5 %all-gather.17.cloned.1.call-start = ((), (), s32[]{:S(2)}) async-start(), calls=%async_computation.18 | async-start | bytes 3932160 | tf_op jit(solution)/shard_map/all_gather | solution.py:211
  513.0 1.2 copy-start.2
  513.0 2.8 copy-start.20
  515.9 243.2 %reduce-scatter.37.cloned.1.call-start = ((), (), s32[]{:S(2)}) async-start(), calls=%async_computation.25 | async-start | bytes 884736
  570.9 5.6 copy-start
  600.8 5.6 copy-start
  630.8 5.6 copy-start
  660.8 5.6 copy-start
  668.9 4.8 copy-start.9
  673.4 102.0 %reduce-scatter.25.cloned.1.call-start = ((), (), s32[]{:S(2)}) async-start(), calls=%async_computation.19 | async-start | bytes 3932160 | tf_op jit(solution)/shard_map/reduce_scatter | solution.py:223
  673.7 2.7 copy-start.6
  674.8 2.5 copy-start.12
  677.2 1.1 copy-start.14
  681.1 167.8 %reduce-scatter.27.cloned.1.call-start = ((), (), s32[]{:S(2)}) async-start(), calls=%async_computation.20 | async-start | bytes 2654208 | tf_op jit(solution)/shard_map/reduce_scatter | solution.py:232
  688.2 233.1 %reduce-scatter.29.cloned.1.call-start = ((), (), s32[]{:S(2)}) async-start(), calls=%async_computation.21 | async-start | bytes 2654208 | tf_op jit(solution)/shard_map/reduce_scatter | solution.py:233
  695.2 292.1 %reduce-scatter.31.cloned.1.call-start = ((), (), s32[]{:S(2)}) async-start(), calls=%async_computation.22 | async-start | bytes 884736
  701.0 351.5 %reduce-scatter.33.cloned.1.call-start = ((), (), s32[]{:S(2)}) async-start(), calls=%async_computation.23 | async-start | bytes 884736
  705.0 6.3 copy-start.34
  705.0 9.6 copy-start.29
  705.0 10.7 copy-start.22
  705.0 10.6 copy-start.23
  705.0 10.6 copy-start.24
  705.0 10.6 copy-start.25
  705.0 10.6 copy-start.27
  705.0 10.6 copy-start.28
  705.1 70.3 %copy-start.3 = (f32[512,768]{1,0:T(8,128)S(1)}, f32[512,768]{1,0:T(8,128)}, u32[]{:S(2)}) copy-start(f32[512,768]{1,0:T(8,128)} %copy-done.2) | copy-start | bytes 4718596
  705.1 70.3 %copy-start.21 = (f32[512]{0:T(512)S(1)}, f32[512]{0:T(512)}, u32[]{:S(2)}) copy-start(f32[512]{0:T(512)} %copy-done.20) | copy-start | bytes 6148
  705.1 413.3 %reduce-scatter.35.cloned.1.call-start = ((), (), s32[]{:S(2)}) async-start(), calls=%async_computation.24 | async-start | bytes 884736
Sparse Core Ops, SparseCore 0:
  10.4 31.2 all-gather.6
  193.8 59.2 reduce-scatter.18
  404.1 28.5 all-gather.14
  516.0 28.5 all-gather.16
Sparse Core Ops, SparseCore 1:
  196.6 42.3 all-gather.10
  257.2 28.4 all-gather.8
  287.9 41.5 all-gather.12
  337.0 56.7 reduce-scatter.20
  450.1 58.2 reduce-scatter.22
  673.5 62.5 reduce-scatter.36
  738.5 36.8 reduce-scatter.24
  779.7 69.2 reduce-scatter.26
  853.3 67.9 reduce-scatter.28
  925.5 61.6 reduce-scatter.30
  991.0 61.5 reduce-scatter.32
  1056.8 61.5 reduce-scatter.34
where the time goes:
time: 1140 us; the launch traced here: 1130 us
  waiting for transfers between devices  634 us (56%)
  matrix products  197 us (17%)
  blocking collectives  170 us (15%)
  other arithmetic  68.6 us (6%)
  local copies, waits for them, and re-layouts  27.8 us (2%)
  between operations  17 us (1%)
    unnamed x20, waiting for transfers between devices  199 us
    reduce_scatter x1, waiting for transfers between devices, body(): lax.psum_scatter(grad_down, 'dp', scatter_dimension=1, tiled=True)  72.3 us
    reduce_scatter x1, waiting for transfers between devices, body(): lax.psum_scatter(grad_up, 'dp', scatter_dimension=0, tiled=True)  71.3 us
    reduce_scatter x1, waiting for transfers between devices, body(): lax.psum_scatter(product_nt(grad_pre, up_mat), 'tensor', scatter_dimensio...  58.3 us
    reduce_scatter x1, waiting for transfers between devices, body(): lax.psum_scatter(product(attended, out_mat), 'tensor', scatter_dimension=...  58.1 us
    reduce_scatter x1, waiting for transfers between devices, body(): lax.psum_scatter(product(hidden, down_mat), 'tensor', scatter_dimension=0...  51.7 us
    psum x1, blocking collectives, body(): lax.psum((bias_query_full, bias_value_full, grad_bias_out, grad_bias_up,...  40.9 us
    dot_general x6, matrix products, product(): return jnp.dot(left, right, preferred_element_type=jnp.float32)  37.6 us
  transfers between devices with their start and end apart: 16, of which 13 were waited for; matrix products, arithmetic and copies ran while one was open for 7% of the time, Pallas kernels for 0%

commit v1 on v0

v1 whole, which is shorter than its diff:
```python
import functools

import jax
import jax.numpy as jnp
from jax import lax
from jax.experimental import pallas as pl
from jax.experimental.pallas import tpu as pltpu
from jax.sharding import PartitionSpec as P

HEAD_DIM = 64
LANES = 128
EPSILON = 1e-12
MASKED = -1e30
BF16 = jnp.bfloat16
F32 = jnp.float32
NT = (((1,), (1,)), ((), ()))
TN = (((0,), (0,)), ((), ()))
VMEM_LIMIT = 64 << 20


def dot(left, right):
    return jnp.dot(left, right, preferred_element_type=F32)


def dot_nt(left, right):
    return lax.dot_general(left, right, NT, preferred_element_type=F32)


def dot_tn(left, right):
    return lax.dot_general(left, right, TN, preferred_element_type=F32)


def in_three(column):
    first = column.astype(BF16)
    rest = column - first.astype(F32)
    second = rest.astype(BF16)
    third = (rest - second.astype(F32)).astype(BF16)
    return first, second, third


def swap(value, axis, bits):
    size = lax.axis_size(axis)
    return lax.ppermute(value, axis, [(i, i ^ bits) for i in range(size)])


def bit_of(axis, bit):
    return (lax.axis_index(axis) >> bit) & 1


def gather_bits(block, axis, order, at):
    done = []
    for bit in order:
        place = at + sum(other > bit for other in done)
        got = swap(block, axis, 1 << bit)
        upper = bit_of(axis, bit) == 1
        low = jnp.where(upper, got, block)
        high = jnp.where(upper, block, got)
        block = jnp.stack([low, high], axis=place)
        done.append(bit)
    return block


def scatter_bits(partial, axis, order, at):
    left = sorted(order, reverse=True)
    for bit in order:
        place = at + left.index(bit)
        mine = bit_of(axis, bit)
        away = lax.dynamic_index_in_dim(partial, 1 - mine, place, keepdims=False)
        keep = lax.dynamic_index_in_dim(partial, mine, place, keepdims=False)
        got = swap(away.astype(BF16), axis, 1 << bit)
        partial = keep.astype(F32) + got.astype(F32)
        left.remove(bit)
    return partial


def forward_kernel(*refs, rows, heads):
    x_refs, (w_ref, b_ref, mask_ref), rest = refs[:4], refs[4:7], refs[7:]
    q_out, k_out, v_out, o_out = rest[:4]
    packed = rest[4:8]
    q_s, k_s, v_s = rest[8:]
    seq = 4 * rows
    block = rows // 2
    lane = lax.broadcasted_iota(jnp.int32, (1, LANES), 1)
    head_lane = lane < HEAD_DIM
    one_q = jnp.where(lane == HEAD_DIM, 1.0, 0.0)
    one_k = jnp.where((lane > HEAD_DIM) & (lane <= HEAD_DIM + 3), 1.0, 0.0)
    one_v = jnp.where((lane >= HEAD_DIM) & (lane < HEAD_DIM + 3), 1.0, 0.0)
    for j in range(4):
        part = pl.ds(j * rows, rows)
        both = dot(x_refs[j][...], w_ref[0]) + b_ref[0]
        first = both[:, :LANES]
        second = jnp.concatenate([both[:, LANES:], both[:, LANES:]], axis=1)
        query = first.astype(BF16).astype(F32) * (HEAD_DIM**-0.5)
        q_s[part, :] = jnp.where(head_lane, query, one_q).astype(BF16)
        key = jnp.where(head_lane, pltpu.roll(first, HEAD_DIM, 1), one_k)
        k_s[part, :] = jnp.where(lane == HEAD_DIM, mask_ref[part, :], key).astype(BF16)
        v_s[part, :] = jnp.where(head_lane, second, one_v).astype(BF16)
    k_out[0] = k_s[...]
    v_out[0] = v_s[...]

    def scores_of(i):
        query = q_s[pl.ds(i * block, block), :]
        scores = dot_nt(query, k_s[...])
        return query, scores, jnp.max(scores, axis=-1, keepdims=True)

    def attend(i, query, scores, top):
        expon = jnp.exp(scores - top).astype(BF16)
        total = dot(expon, v_s[...])
        row_sum = total[:, HEAD_DIM : HEAD_DIM + 1]
        out = total * (1.0 / row_sum)
        place = pl.ds(i * block, block)
        o_out[0, place, :] = out
        one, two, three = in_three(-(top + jnp.log(row_sum)))
        q_out[0, place, :] = jnp.where(
            lane == HEAD_DIM + 1,
            one,
            jnp.where(lane == HEAD_DIM + 2, two, jnp.where(lane == HEAD_DIM + 3, three, query)),
        )
        return out

    blocks = seq // block
    held = scores_of(0)
    even = None
    for i in range(blocks):
        following = scores_of(i + 1) if i + 1 < blocks else None
        out = attend(i, *held)
        if i % 2 == 0:
            even = out
        else:
            pair = jnp.where(head_lane, even, pltpu.roll(out, HEAD_DIM, 1))
            packed[i // 2][0] = pair.astype(BF16)
        held = following


def attention_forward(parts, weight, bias, mask):
    rows, width = parts[0].shape
    heads = weight.shape[0]
    seq = 4 * rows
    block = rows // 2
    per_head = pl.BlockSpec((1, seq, LANES), lambda h: (h, 0, 0))
    whole = pl.BlockSpec((rows, width), lambda h: (0, 0))
    piece = pl.BlockSpec((1, block, LANES), lambda h: (h, 0, 0))
    kept = jax.ShapeDtypeStruct((heads, seq, LANES), BF16)
    return pl.pallas_call(
        functools.partial(forward_kernel, rows=rows, heads=heads),
        grid=(heads,),
        in_specs=[whole] * 4
        + [
            pl.BlockSpec((1,) + weight.shape[1:], lambda h: (h, 0, 0)),
            pl.BlockSpec((1,) + bias.shape[1:], lambda h: (h, 0, 0)),
            pl.BlockSpec((seq, LANES), lambda h: (0, 0)),
        ],
        out_specs=[per_head] * 4 + [piece] * 4,
        out_shape=[kept, kept, kept, jax.ShapeDtypeStruct((heads, seq, LANES), F32)]
        + [jax.ShapeDtypeStruct((heads, block, LANES), BF16)] * 4,
        scratch_shapes=[pltpu.VMEM((seq, LANES), BF16)] * 3,
        compiler_params=pltpu.CompilerParams(vmem_limit_bytes=VMEM_LIMIT - (1 << 20)),
        cost_estimate=pl.CostEstimate(
            flops=heads * (4 * seq * seq * 256 + 2 * seq * width * 256),
            bytes_accessed=8 << 20,
            transcendentals=heads * seq * seq,
        ),
        name="attention_forward",
    )(*parts, weight, bias, mask)


def backward_kernel(*refs, rows, heads):
    q_ref, k_ref, v_ref, o_ref = refs[:4]
    d_refs, x_refs, w_ref = refs[4:8], refs[8:12], refs[12]
    gw_ref, gb_ref = refs[13:15]
    dx_refs = refs[15:19]
    x_t, dx_s, dk_s, dv_s, g_s = refs[19:]
    seq = 4 * rows
    block = rows // 2
    head = pl.program_id(0)
    lane = lax.broadcasted_iota(jnp.int32, (1, LANES), 1)
    head_lane = lane < HEAD_DIM
    scale = HEAD_DIM**-0.5

    @pl.when(head == 0)
    def _():
        for j in range(4):
            x_t[:, j * rows : (j + 1) * rows] = x_refs[j][...].T

    for i in range(seq // block):
        place = pl.ds(i * block, block)
        query = q_ref[0, place, :]
        grad = d_refs[i // 2][0].astype(F32)
        if i % 2 == 1:
            grad = pltpu.roll(grad, HEAD_DIM, 1)
        grad = jnp.where(head_lane, grad, 0.0)
        delta = jnp.sum(grad * o_ref[0, place, :], axis=-1, keepdims=True)
        one, two, three = in_three(-delta)
        grad = grad.astype(BF16)
        grad_and = jnp.where(
            lane == HEAD_DIM,
            one,
            jnp.where(lane == HEAD_DIM + 1, two, jnp.where(lane == HEAD_DIM + 2, three, grad)),
        )
        probs = jnp.exp(dot_nt(k_ref[0], query))
        lifted = dot_nt(v_ref[0], grad_and)
        grad_scores = (probs * lifted).astype(BF16)
        values_part = dot(probs.astype(BF16), grad)
        keys_part = dot(grad_scores, query)
        if i == 0:
            dv_s[...] = values_part
            dk_s[...] = keys_part
        else:
            dv_s[...] += values_part
            dk_s[...] += keys_part
        grad_query = dot_tn(grad_scores, k_ref[0]) * scale
        g_s[place, :LANES] = jnp.where(head_lane, grad_query, 0.0).astype(BF16)
    both = jnp.where(head_lane, g_s[:, :LANES].astype(F32), pltpu.roll(dk_s[...], HEAD_DIM, 1))
    g_s[:, :LANES] = both.astype(BF16)
    g_s[:, LANES:] = dv_s[:, :HEAD_DIM].astype(BF16)
    grads = g_s[...]
    gb_ref[0] = jnp.sum(grads.astype(F32), axis=0, keepdims=True)
    gw_ref[0] = dot(x_t[...], grads).astype(BF16)
    for j in range(4):
        part = pl.ds(j * rows, rows)
        passed = dot_nt(g_s[part, :], w_ref[0])

        @pl.when(head == 0)
        def _():
            dx_s[part, :] = passed

        @pl.when((head > 0) & (head < heads - 1))
        def _():
            dx_s[part, :] += passed

        @pl.when(head == heads - 1)
        def _():
            dx_refs[j][...] = (dx_s[part, :] + passed).astype(BF16)


def attention_backward(kept, grads, parts, weight):
    rows, width = parts[0].shape
    heads = weight.shape[0]
    seq = 4 * rows
    block = rows // 2
    per_head = pl.BlockSpec((1, seq, LANES), lambda h: (h, 0, 0))
    whole = pl.BlockSpec((rows, width), lambda h: (0, 0))
    piece = pl.BlockSpec((1, block, LANES), lambda h: (h, 0, 0))
    three = 3 * HEAD_DIM
    w_spec = pl.BlockSpec((1, width, three), lambda h: (h, 0, 0))
    return pl.pallas_call(
        functools.partial(backward_kernel, rows=rows, heads=heads),
        grid=(heads,),
        in_specs=[per_head] * 4 + [piece] * 4 + [whole] * 4 + [w_spec],
        out_specs=[w_spec, pl.BlockSpec((1, 1, three), lambda h: (h, 0, 0))] + [whole] * 4,
        out_shape=[
            jax.ShapeDtypeStruct((heads, width, three), BF16),
            jax.ShapeDtypeStruct((heads, 1, three), F32),
        ]
        + [jax.ShapeDtypeStruct((rows, width), BF16)] * 4,
        scratch_shapes=[
            pltpu.VMEM((width, seq), BF16),
            pltpu.VMEM((seq, width), F32),
            pltpu.VMEM((seq, LANES), F32),
            pltpu.VMEM((seq, LANES), F32),
            pltpu.VMEM((seq, three), BF16),
        ],
        compiler_params=pltpu.CompilerParams(vmem_limit_bytes=VMEM_LIMIT - (1 << 20)),
        cost_estimate=pl.CostEstimate(
            flops=heads * (10 * seq * seq * 256 + 4 * seq * width * 256),
            bytes_accessed=16 << 20,
            transcendentals=heads * seq * seq,
        ),
        name="attention_backward",
    )(*kept, *grads, *parts, weight)


def middle_kernel(*refs, rows, width, pieces):
    att = refs[:4]
    x_ref, og_ref, mask_ref, wo_ref, up_ref, down_ref, bup_ref, vec_ref = refs[4:12]
    lo_ref, done_ref, sums_ref, gbup_ref, gup_ref, gdown_ref, gout_ref = refs[12:19]
    ga = refs[19:23]
    att_s, wo_s, hid_s, slope_s, nrm_s, nb_s, n1_s, rs_s, ffn_s, gf_s, gft_s, nbt_s, acc_s, pre_s = (
        refs[23:]
    )
    step = pl.program_id(0)
    chunk = 128
    cols = width // pieces
    lane = lax.broadcasted_iota(jnp.int32, (1, LANES), 1)
    head_lane = lane < HEAD_DIM
    half = rows // 2
    b_out, b_down, gain_a, shift_a, gain_f, shift_f = (vec_ref[i : i + 1, :] for i in range(6))

    def row_loop(work):
        @pl.loop(0, rows // chunk)
        def _(i):
            work(pl.ds(pl.multiple_of(i * chunk, chunk), chunk))

    def add_sum(index, value):
        sums_ref[index : index + 1, :] += jnp.sum(value, axis=0, keepdims=True)

    def mean(value):
        return jnp.mean(value, axis=-1, keepdims=True)

    def normal(value):
        centred = value - mean(value)
        inverse = lax.rsqrt(mean(centred * centred) + EPSILON)
        return centred * inverse, inverse

    def norm_back(grad, unit, inverse, gain):
        scaled = grad * gain
        return (scaled - mean(scaled) - unit * mean(scaled * unit)) * inverse

    @pl.when(step == 0)
    def _():
        sums_ref[...] = jnp.zeros_like(sums_ref)
        for j in range(pieces):
            for h in range(cols // HEAD_DIM):
                at = j * cols + h * HEAD_DIM
                att_s[:half, at : at + HEAD_DIM] = att[j][h][:, :HEAD_DIM]
                att_s[half:, at : at + HEAD_DIM] = att[j][h][:, HEAD_DIM:]
            wo_s[:, j * cols : (j + 1) * cols] = wo_ref[j]
        ffn_s[...] = dot_nt(att_s[...], wo_s[...])

        def first_norm(r):
            value = x_ref[r, :].astype(F32)
            attn = ffn_s[r, :] + b_out
            valid = mask_ref[r, :1] > 0.0
            add_sum(6, jnp.where(valid, value * value, 0.0))
            add_sum(7, jnp.where(valid, attn * attn, 0.0))
            unit, inverse = normal(value + attn)
            normed = unit * gain_a + shift_a
            n1_s[r, :] = unit
            rs_s[r, :] = jnp.broadcast_to(inverse, (chunk, LANES))
            nrm_s[r, :] = normed
            nb_s[r, :] = normed.astype(BF16)

        row_loop(first_norm)

    @pl.when(step < pieces)
    def _():
        pre_s[...] = dot(nb_s[...], up_ref[0]) + bup_ref[0]

        def gelu(r):
            pre = pre_s[r, :]
            cdf = 0.5 * (1.0 + lax.erf(pre * (0.5**0.5)))
            pdf = jnp.exp(pre * pre * -0.5) * (2.0 * jnp.pi) ** -0.5
            hid_s[step, r, :] = (pre * cdf).astype(BF16)
            slope_s[step, r, :] = cdf + pre * pdf

        row_loop(gelu)
        part = dot_nt(hid_s[step], down_ref[0])

        @pl.when(step == 0)
        def _():
            ffn_s[...] = part

        @pl.when(step > 0)
        def _():
            ffn_s[...] += part

    @pl.when(step == pieces - 1)
    def _():
        def second_norm(r):
            ffn = ffn_s[r, :] + b_down
            valid = mask_ref[r, :1] > 0.0
            add_sum(8, jnp.where(valid, ffn * ffn, 0.0))
            unit, inverse = normal(nrm_s[r, :] + ffn)
            lo_ref[r, :] = (unit * gain_f + shift_f).astype(BF16)
            grad = og_ref[r, :].astype(F32)
            add_sum(4, grad * unit)
            add_sum(5, grad)
            d_two = norm_back(grad, unit, inverse, gain_f)
            low = d_two.astype(BF16)
            add_sum(1, low.astype(F32))
            acc_s[r, :] = d_two
            gf_s[r, :] = low

        row_loop(second_norm)
        gft_s[...] = gf_s[...].T
        nbt_s[...] = nb_s[...].T

    @pl.when(step >= pieces)
    def _():
        j = 2 * pieces - 1 - step
        grad_hidden = dot(gf_s[...], down_ref[0])
        pre_s[...] = grad_hidden * slope_s[j]
        low = pre_s[...].astype(BF16)
        gbup_ref[0] = jnp.sum(low.astype(F32), axis=0, keepdims=True)
        gdown_ref[0] = dot(gft_s[...], hid_s[j]).astype(BF16)
        gup_ref[0] = dot(nbt_s[...], low).astype(BF16)
        acc_s[...] += dot_nt(low, up_ref[0])

    @pl.when(step == 2 * pieces - 1)
    def _():
        def first_back(r):
            grad = acc_s[r, :]
            unit = n1_s[r, :]
            add_sum(2, grad * unit)
            add_sum(3, grad)
            d_one = norm_back(grad, unit, rs_s[r, :1], gain_a)
            low = d_one.astype(BF16)
            add_sum(0, low.astype(F32))
            done_ref[r, :] = d_one
            gf_s[r, :] = low

        row_loop(first_back)
        low = gf_s[...]
        gout = dot_tn(low, att_s[...])
        for j in range(pieces):
            gout_ref[j] = gout[:, j * cols : (j + 1) * cols].astype(BF16)
        back = dot(low, wo_s[...]).astype(BF16)
        for j in range(pieces):
            for h in range(cols // HEAD_DIM):
                at = j * cols + h * HEAD_DIM
                ga[j][h, :, :HEAD_DIM] = back[:half, at : at + HEAD_DIM]
                ga[j][h, :, HEAD_DIM:] = back[half:, at : at + HEAD_DIM]


def middle(att, tokens, out_grad, row_mask, w_out, w_up, w_down, b_up, vectors):
    rows, width = tokens.shape
    pieces = w_up.shape[0]
    hidden = w_up.shape[2]
    heads, half, _ = att[0].shape
    cols = width // pieces

    def fixed(shape):
        return pl.BlockSpec(shape, lambda s: (0,) * len(shape))

    def chunked(shape):
        return pl.BlockSpec((1,) + shape, lambda s: (jnp.minimum(s, 2 * pieces - 1 - s), 0, 0))

    def late(shape):
        return pl.BlockSpec((1,) + shape, lambda s: (jnp.minimum(pieces - 1, 2 * pieces - 1 - s), 0, 0))

    shape = jax.ShapeDtypeStruct
    return pl.pallas_call(
        functools.partial(middle_kernel, rows=rows, width=width, pieces=pieces),
        grid=(2 * pieces,),
        in_specs=[fixed(att[0].shape)] * 4
        + [fixed((rows, width))] * 2
        + [
            fixed(row_mask.shape),
            fixed(w_out.shape),
            chunked((width, hidden)),
            chunked((width, hidden)),
            chunked((1, hidden)),
            fixed(vectors.shape),
        ],
        out_specs=[
            fixed((rows, width)),
            fixed((rows, width)),
            fixed((16, width)),
            late((1, hidden)),
            late((width, hidden)),
            late((width, hidden)),
            fixed((pieces, width, cols)),
        ]
        + [fixed(att[0].shape)] * 4,
        out_shape=[
            shape((rows, width), BF16),
            shape((rows, width), F32),
            shape((16, width), F32),
            shape((pieces, 1, hidden), F32),
            shape((pieces, width, hidden), BF16),
            shape((pieces, width, hidden), BF16),
            shape((pieces, width, cols), BF16),
        ]
        + [shape(att[0].shape, BF16)] * 4,
        scratch_shapes=[
            pltpu.VMEM((rows, width), BF16),
            pltpu.VMEM((width, width), BF16),
            pltpu.VMEM((pieces, rows, hidden), BF16),
            pltpu.VMEM((pieces, rows, hidden), F32),
            pltpu.VMEM((rows, width), F32),
            pltpu.VMEM((rows, width), BF16),
            pltpu.VMEM((rows, width), F32),
            pltpu.VMEM((rows, LANES), F32),
            pltpu.VMEM((rows, width), F32),
            pltpu.VMEM((rows, width), BF16),
            pltpu.VMEM((width, rows), BF16),
            pltpu.VMEM((width, rows), BF16),
            pltpu.VMEM((rows, width), F32),
            pltpu.VMEM((rows, hidden), F32),
        ],
        compiler_params=pltpu.CompilerParams(vmem_limit_bytes=VMEM_LIMIT - (1 << 20)),
        cost_estimate=pl.CostEstimate(
            flops=6 * rows * width * (width + 2 * pieces * hidden),
            bytes_accessed=48 << 20,
            transcendentals=rows * pieces * hidden,
        ),
        name="middle",
    )(*att, tokens, out_grad, row_mask, w_out, w_up, w_down, b_up, vectors)


def body(
    tokens,
    seq_lengths,
    positions,
    w_query,
    w_key,
    w_value,
    w_out,
    w_up,
    w_down,
    b_query,
    b_value,
    b_out,
    b_up,
    b_down,
    gain_attn,
    shift_attn,
    gain_ffn,
    shift_ffn,
    out_grad,
):
    group = lax.axis_index("dp")
    member = lax.axis_index("tensor")
    dp_count = lax.axis_size("dp")
    bits = dp_count.bit_length() - 1
    down_order = list(range(bits))[::-1]
    rows, width = tokens.shape
    own_cols = w_query.shape[1]
    heads = own_cols // HEAD_DIM
    share = w_query.shape[0]
    hidden = w_up.shape[1]

    across = swap(tokens, "tensor", 2)
    parts = [tokens, swap(tokens, "tensor", 1), across, swap(across, "tensor", 1)]

    by_head = [w.reshape(share, heads, HEAD_DIM) for w in (w_query, w_key, w_value)]
    own_qkv = jnp.stack(by_head, axis=2).reshape(share, heads, 3 * HEAD_DIM).transpose(1, 0, 2)
    w_qkv = gather_bits(own_qkv, "dp", down_order, 1).reshape(heads, width, 3 * HEAD_DIM)

    bias_q = b_query.astype(F32).reshape(heads, HEAD_DIM)
    bias_v = b_value.astype(F32).reshape(heads, HEAD_DIM)
    bias = jnp.stack([bias_q, jnp.zeros_like(bias_q), bias_v], axis=1).reshape(heads, 1, 3 * HEAD_DIM)

    length = lax.dynamic_index_in_dim(seq_lengths, group, 0, keepdims=False)
    valid = (positions[0] < length).reshape(4, rows)
    valid = jnp.stack([lax.dynamic_index_in_dim(valid, member ^ j, 0, keepdims=False) for j in range(4)])
    key_bias = jnp.where(valid.reshape(4 * rows, 1), 0.0, MASKED).astype(F32)
    key_mask = jnp.broadcast_to(key_bias, (4 * rows, LANES))
    row_mask = jnp.broadcast_to(valid[0][:, None].astype(F32), (rows, LANES))

    q, k, v, attended_f, *pieces = attention_forward(parts, w_qkv, bias, key_mask)

    rest = jnp.concatenate([w_up, w_down.T, w_out.T], axis=1)
    rest = gather_bits(rest, "dp", down_order, 0).reshape(width, -1)
    beyond = swap(rest, "tensor", 2)
    packs = [rest, swap(rest, "tensor", 1), beyond, swap(beyond, "tensor", 1)]
    up_all = jnp.stack([pack[:, :hidden] for pack in packs])
    down_all = jnp.stack([pack[:, hidden : 2 * hidden] for pack in packs])
    out_all = jnp.stack([pack[:, 2 * hidden :] for pack in packs])
    own_b_up = b_up.astype(F32).reshape(1, hidden)
    b_up_all = jnp.stack([own_b_up] + [swap(own_b_up, "tensor", j) for j in (1, 2, 3)])
    vectors = jnp.stack(
        [vec.astype(F32) for vec in (b_out, b_down, gain_attn, shift_attn, gain_ffn, shift_ffn)] + [jnp.zeros((width,), F32)] * 2
    )
    att = [pieces[0]] + [swap(pieces[j], "tensor", j) for j in (1, 2, 3)]
    layer_out, d_one, sums, g_b_up, g_up, g_down, g_out, *back = middle(
        att, tokens, out_grad, row_mask, out_all, up_all, down_all, b_up_all, vectors
    )
    grads = [back[0]] + [swap(back[j], "tensor", j) for j in (1, 2, 3)]

    g_qkv, g_bias, *dx = attention_backward((q, k, v, attended_f), grads, parts, w_qkv)

    near = [dx[0].astype(F32) + swap(dx[1], "tensor", 1).astype(F32)]
    far = (dx[2].astype(F32) + swap(dx[3], "tensor", 1).astype(F32)).astype(BF16)
    input_grad = (d_one + near[0] + swap(far, "tensor", 2).astype(F32)).astype(BF16)

    packs = jnp.concatenate([g_up, g_down, g_out], axis=2)
    got = swap(packs[1::2], "tensor", 1)
    packs = packs[0::2].astype(F32) + got.astype(F32)
    pack = packs[0] + swap(packs[1].astype(BF16), "tensor", 2).astype(F32)
    two = (2,) * bits
    pack = scatter_bits(pack.reshape(two + (share, -1)), "dp", list(range(bits)), 0)
    g_qkv = scatter_bits(g_qkv.reshape((heads,) + two + (share, -1)), "dp", list(range(bits)), 1)
    g_qkv = g_qkv.reshape(heads, share, 3, HEAD_DIM)
    g_q, g_k, g_v = (g_qkv[:, :, i].transpose(1, 0, 2).reshape(share, own_cols) for i in range(3))

    small = jnp.concatenate([sums[:9], jnp.zeros((1, width), F32)])
    ups = g_b_up[:, 0]
    sent = jnp.concatenate([small, ups[1:2], ups[3:4]])
    got = swap(sent, "tensor", 1)
    small, ups = small + got[:10], ups[0::2] + got[10:]
    got = swap(jnp.concatenate([small, ups[1:2]]), "tensor", 2)
    small = jnp.concatenate([small + got[:10], ups[:1] + got[10:]])
    bias_rows = g_bias.reshape(heads, 3, HEAD_DIM)
    for bit in range(bits):
        small = small + swap(small, "dp", 1 << bit)
        bias_rows = bias_rows + swap(bias_rows, "dp", 1 << bit)
    count = jnp.sum(seq_lengths).astype(F32) * width
    rms = jnp.sqrt(jnp.sum(small[6:9], axis=-1) / count)
    return (
        layer_out,
        input_grad,
        g_q,
        g_k,
        g_v,
        pack[:, 2 * hidden :].T,
        pack[:, :hidden],
        pack[:, hidden : 2 * hidden].T,
        bias_rows[:, 0].reshape(own_cols),
        bias_rows[:, 2].reshape(own_cols),
        small[0],
        small[10],
        small[1],
        small[2],
        small[3],
        small[4],
        small[5],
        rms,
    )


def solution(mesh):
    in_specs = (
        P(("dp", "tensor"), None),
        P(),
        P("dp", None),
        P("dp", "tensor"),
        P("dp", "tensor"),
        P("dp", "tensor"),
        P("tensor", "dp"),
        P("dp", "tensor"),
        P("tensor", "dp"),
        P("tensor"),
        P("tensor"),
        P(),
        P("tensor"),
        P(),
        P(),
        P(),
        P(),
        P(),
        P(("dp", "tensor"), None),
    )
    out_specs = (
        P(("dp", "tensor"), None),
        P(("dp", "tensor"), None),
        P("dp", "tensor"),
        P("dp", "tensor"),
        P("dp", "tensor"),
        P("tensor", "dp"),
        P("dp", "tensor"),
        P("tensor", "dp"),
        P("tensor"),
        P("tensor"),
        P(),
        P("tensor"),
        P(),
        P(),
        P(),
        P(),
        P(),
        P(),
    )
    return jax.shard_map(body, mesh=mesh, in_specs=in_specs, out_specs=out_specs, check_vma=False)
```

time: 1140 us -> 504 us (0.44)
  waiting for transfers between devices: 634 us -> 191 us
  matrix products: 197 us -> 0 us
  blocking collectives: 170 us -> 0 us
  Pallas kernels: 0 us -> 123 us
  local copies, waits for them, and re-layouts: 27.8 us -> 103 us
  starting transfers between devices: 1.93 us -> 44.3 us
  other arithmetic: 68.6 us -> 36.3 us
  between operations: 17 us -> 2.39 us
    reduce_scatter x6 -> x0, waiting for transfers between devices: 326 us -> none  [the longest x1 72.3 us: body(): lax.psum_scatter(grad_down, 'dp', scatter_dimension=1, tiled=True)]
    unnamed x20 -> x0, waiting for transfers between devices: 199 us -> none
    dot_general x45 -> x0, matrix products: 192 us -> none  [the longest x6 37.6 us: product(): return jnp.dot(left, right, preferred_element_type=jnp.float32)]
    ppermute x0 -> x40, waiting for transfers between devices: none -> 191 us  [swap(): return lax.ppermute(value, axis, [(i, i ^ bits) for i in range(size)])]
    all_gather x4 -> x0, blocking collectives: 129 us -> none  [the longest x1 33.2 us: body(): lax.all_gather(w_value, 'dp', axis=0, tiled=True)]
    pallas_call x0 -> x3, Pallas kernels: none -> 123 us  [the longest x1 62.9 us: attention_backward(): pl.pallas_call(functools.partial(backward_kernel, rows=rows, heads=heads)...]
    all_gather x6 -> x0, waiting for transfers between devices: 108 us -> none  [the longest x1 28.4 us: body(): grad_attn_all = lax.all_gather(grad_attn_low, 'tensor', axis=0, tiled=True)]
    ppermute x0 -> x40, starting transfers between devices: none -> 44.3 us  [swap(): return lax.ppermute(value, axis, [(i, i ^ bits) for i in range(size)])]
  transfers between devices with their start and end apart: 16 -> 40, of which waited for: 13 -> 17; matrix products, arithmetic and copies ran while one was open for 7% -> 20% of each run, Pallas kernels for 0% -> 17%
where the time goes in v1:
time: 504 us; the launch traced here: 499 us
  waiting for transfers between devices  191 us (38%)
  Pallas kernels  123 us (24%)
  local copies, waits for them, and re-layouts  103 us (20%)
  starting transfers between devices  44.3 us (9%)
  other arithmetic  36.3 us (7%)
    ppermute x40, waiting for transfers between devices, swap(): return lax.ppermute(value, axis, [(i, i ^ bits) for i in range(size)])  191 us
    pallas_call x1, Pallas kernels, attention_backward(): pl.pallas_call(functools.partial(backward_kernel, rows=rows, heads=heads)...  62.9 us
    ppermute x40, starting transfers between devices, swap(): return lax.ppermute(value, axis, [(i, i ^ bits) for i in range(size)])  44.3 us
    unnamed x88, local copies, waits for them, and re-layouts  38.1 us
    pallas_call x1, Pallas kernels, middle(): pl.pallas_call(functools.partial(middle_kernel, rows=rows, width=width, p...  36.1 us
    pallas_call x1, Pallas kernels, attention_forward(): pl.pallas_call(functools.partial(forward_kernel, rows=rows, heads=heads),...  23.6 us
    ppermute x2, local copies, waits for them, and re-layouts, swap(): return lax.ppermute(value, axis, [(i, i ^ bits) for i in range(size)])  11.2 us
    slice x2, local copies, waits for them, and re-layouts, body(): got = swap(packs[1::2], 'tensor', 1)  11 us
  transfers between devices with their start and end apart: 40, of which 17 were waited for; matrix products, arithmetic and copies ran while one was open for 20% of the time, Pallas kernels for 17%

profile of v1, /device:TPU:0, one launch (start us, length us, event | category | flops | bytes accessed | tf_op | source)
XLA Modules:
  0.0 499.1 jit_solution(14452345118679821016)
XLA Ops:
  2.6 4.1 collective-permute-start.9
  6.7 15.4 %collective-permute-done.9 = bf16[96,1728]{1,0:T(8,128)(2,1)S(1)} collective-permute-done((bf16[96,1728]{1,0:T(8,128)(2,1)S(1)}, bf16[96,1728]{1,0:T(8,128)(2,1)S(1)}, u32[]{:S(2)}, u32[]{:S(2)}) %collective-permute-start.9) | collective-permute-done | bytes 331808 | tf_op jit(solution)/shard_map/ppermute | solution.py:43
  24.1 15.9 %collective-permute-done.10 = bf16[2,96,1728]{2,1,0:T(8,128)(2,1)S(1)} collective-permute-done((bf16[2,96,1728]{2,1,0:T(8,128)(2,1)S(1)}, bf16[2,96,1728]{2,1,0:T(8,128)(2,1)S(1)}, u32[]{:S(2)}, u32[]{:S(2)}) %collective-permute-start.10) | collective-permute-done | bytes 663584 | tf_op jit(solution)/shard_map/ppermute | solution.py:43
  42.6 29.4 %collective-permute-done.11 = bf16[2,2,96,1728]{3,2,0,1:T(8,128)(2,1)S(1)} collective-permute-done((bf16[2,2,96,1728]{3,2,0,1:T(8,128)(2,1)}, bf16[2,2,96,1728]{3,2,0,1:T(8,128)(2,1)S(1)}, u32[]{:S(2)}, u32[]{:S(2)}) %collective-permute-start.11) | collective-permute-done | bytes 1327136 | tf_op jit(solution)/shard_map/ppermute | solution.py:43
  72.7 3.1 copy.71
  77.5 4.5 collective-permute-start.3
  83.7 3.8 collective-permute-done.3
  88.9 7.0 %collective-permute-done.4 = bf16[3,2,96,192]{2,3,0,1:T(8,128)(2,1)S(1)} collective-permute-done((bf16[3,2,96,192]{2,3,0,1:T(8,128)(2,1)S(1)}, bf16[3,2,96,192]{2,3,0,1:T(8,128)(2,1)S(1)}, u32[]{:S(2)}, u32[]{:S(2)}) %collective-permute-start.4) | collective-permute-done | bytes 221216 | tf_op jit(solution)/shard_map/ppermute | solution.py:43
  96.8 53.1 %collective-permute-done.16 = f32[1,768]{1,0:T(1,128)S(1)} collective-permute-done((f32[1,768]{1,0:T(1,128)S(1)}, f32[1,768]{1,0:T(1,128)S(1)}, u32[]{:S(2)}, u32[]{:S(2)}) %collective-permute-start.16) | collective-permute-done | bytes 3104 | tf_op jit(solution)/shard_map/ppermute | solution.py:43
  154.2 7.4 %collective-permute-done.5 = bf16[3,2,2,96,192]{3,4,0,1,2:T(8,128)(2,1)S(1)} collective-permute-done((bf16[3,2,2,96,192]{3,4,0,1,2:T(8,128)(2,1)S(1)}, bf16[3,2,2,96,192]{3,4,0,1,2:T(8,128)(2,1)S(1)}, u32[]{:S(2)}, u32[]{:S(2)}) %collective-permute-start.5) | collective-permute-done | bytes 442400 | tf_op jit(solution)/shard_map/ppermute | solution.py:43
  165.0 23.6 %attention_forward.1 = (bf16[3,2048,128]{2,1,0:T(8,128)(2,1)}, bf16[3,2048,128]{2,1,0:T(8,128)(2,1)}, bf16[3,2048,128]{2,1,0:T(8,128)(2,1)}, f32[3,2048,128]{2,1...) custom-call(bf16[512,768]{1,0:T(8,128)(2,1)} %refs_8_.1, ...), custom_call_target="tpu_custom_call" | custom-call | flops 15300820992 | bytes 8388608 | tf_op jit(solution)/shard_map/attention_forward/pallas_call | solution.py:144
  190.6 1.8 slice_bitcast_fusion.3
  192.3 3.2 slice_bitcast_fusion.1
  195.6 2.8 fusion.8
  199.1 2.8 fusion.9
  202.5 1.6 copy.101
  204.1 2.6 copy.102
  206.7 1.7 slice.182
  208.4 1.9 copy.95
  210.3 1.7 slice.183
  212.0 1.9 copy.96
  213.9 3.2 fusion.10
  217.1 2.4 copy.100
  219.4 2.4 copy.103
  221.8 7.0 %pad_maximum_fusion = (bf16[4,768,768]{2,1,0:T(8,128)(2,1)}, bf16[4,768,768]{2,1,0:T(8,128)(2,1)}) fusion(bf16[1,768,768]{2,1,0:T(8,128)(2,1)} %bitcast.130, bf16[1,768,768]{2,1,0:T(8,128)(2,1)S(1)} %bitcast.127, bf16[1,768,768]{2,1,0:T(8,128)(2,1)S(1)} %bitcast.126, bf16[1,768,768]{2,1,0:T(8,128)(2,1)} %get-tuple-element.134, ...), kind=kLoop, calls=%fused_computation.4 | loop fusion | flops 14155776 | bytes 18874368 | tf_op jit(solution)/shard_map/stack | solution.py:547
  229.9 2.8 pad_maximum_fusion.3.refs_7_
  233.6 36.1 %middle.1 = (bf16[512,768]{1,0:T(8,128)(2,1)}, f32[512,768]{1,0:T(8,128)}, f32[16,768]{1,0:T(8,128)}, f32[4,1,768]{2,1,0:T(1,128)}, bf16[4,768,768]{2,1,0:T(8,12...) custom-call(bf16[3,256,128]{2,1,0:T(8,128)(2,1)} %get-tuple-element., ...), custom_call_target="tpu_custom_call" | custom-call | flops 16307453952 | bytes 50331648 | tf_op jit(solution)/shard_map/middle/pallas_call | solution.py:432
  269.7 2.8 constant_dynamic-update-slice_fusion.2
  275.0 4.2 copy-done.2
  279.1 2.7 slice.152
  281.9 8.3 %copy.84 = bf16[2,768,1728]{1,2,0:T(8,128)(2,1)} copy(bf16[2,768,1728]{2,1,0:T(8,128)(2,1)} %slice.152) | data formatting | bytes 10616832 | tf_op jit(solution)/shard_map/slice | solution.py:568
  291.1 7.3 %collective-permute-done.35 = f32[12,768]{1,0:T(8,128)S(1)} collective-permute-done((f32[12,768]{1,0:T(8,128)S(1)}, f32[12,768]{1,0:T(8,128)S(1)}, u32[]{:S(2)}, u32[]{:S(2)}) %collective-permute-start.35) | collective-permute-done | bytes 36896 | tf_op jit(solution)/shard_map/ppermute | solution.py:43
  300.0 2.7 collective-permute-done.36
  304.2 2.7 collective-permute-done.37
  307.0 4.0 collective-permute-start.38
  310.9 2.1 collective-permute-done.38
  313.0 4.7 collective-permute-start.39
  319.1 1.6 collective-permute-start.19
  320.9 7.9 %copy.85 = bf16[2,768,1728]{2,1,0:T(8,128)(2,1)} copy(bf16[2,768,1728]{1,2,0:T(8,128)(2,1)} %collective-permute-done.27) | data formatting | bytes 10616832 | tf_op jit(solution)/shard_map/ppermute | solution.py:43
  328.9 5.4 %convert_add_fusion = f32[2,768,1728]{2,1,0:T(8,128)S(1)} fusion(bf16[2,768,1728]{2,1,0:T(8,128)(2,1)} %copy.85, bf16[4,768,1728]{2,1,0:T(8,128)(2,1)} %copy-done.2), kind=kLoop, calls=%fused_computation | loop fusion | flops 7962624 | bytes 21233664 | tf_op jit(solution)/shard_map/add | solution.py:569
  334.3 4.2 copy-done
  338.4 1.9 fusion.1
  340.3 4.5 copy.86
  344.8 1.5 collective-permute-start.28
  347.2 62.9 %attention_backward.1 = (bf16[3,768,192]{2,1,0:T(8,128)(2,1)}, f32[3,1,192]{2,1,0:T(1,128)}, bf16[512,768]{1,0:T(8,128)(2,1)}, bf16[512,768]{1,0:T(8,128)(2,1)},...) custom-call(bf16[3,2048,128]{2,1,0:T(8,128)(2,1)} %get-tuple-element.49.refs_0_, ...), custom_call_target="tpu_custom_call" | custom-call | flops 37044092928 | bytes 16777216 | tf_op jit(solution)/shard_map/attention_backward/pallas_call | solution.py:246
  410.9 1.5 collective-permute-start.32
  415.3 3.3 copy.87
  418.6 3.1 fusion
  421.7 2.4 copy-done.3
  425.4 1.5 collective-permute-start.29
  428.8 2.0 collective-permute-done.33
  430.8 1.7 collective-permute-start.34
  437.1 3.5 collective-permute-done.25
  440.7 1.8 collective-permute-start.26
  442.5 17.1 %collective-permute-done.29 = bf16[2,2,96,1728]{3,2,0,1:T(8,128)(2,1)} collective-permute-done((bf16[2,2,96,1728]{3,2,0,1:T(8,128)(2,1)}, bf16[2,2,96,1728]{3,2,0,1:T(8,128)(2,1)}, u32[]{:S(2)}, u32[]{:S(2)}) %collective-permute-start.29) | collective-permute-done | bytes 1327136 | tf_op jit(solution)/shard_map/ppermute | solution.py:43
  459.6 2.5 bitcast_add_fusion
  463.9 2.2 add_convert_fusion.1
  467.3 1.6 copy.90
  469.0 1.6 copy.91
  470.6 1.6 copy.92
  472.2 7.4 %collective-permute-done.30 = bf16[2,96,1728]{2,1,0:T(8,128)(2,1)} collective-permute-done((bf16[2,96,1728]{2,1,0:T(8,128)(2,1)}, bf16[2,96,1728]{2,1,0:T(8,128)(2,1)}, u32[]{:S(2)}, u32[]{:S(2)}) %collective-permute-start.30) | collective-permute-done | bytes 663584 | tf_op jit(solution)/shard_map/ppermute | solution.py:43
  481.0 3.5 collective-permute-done.23
  484.5 2.5 add_convert_fusion
  487.0 10.2 %collective-permute-done.31 = bf16[96,1728]{1,0:T(8,128)(2,1)S(1)} collective-permute-done((bf16[96,1728]{1,0:T(8,128)(2,1)S(1)}, bf16[96,1728]{1,0:T(8,128)(2,1)S(1)}, u32[]{:S(2)}, u32[]{:S(2)}) %collective-permute-start.31) | collective-permute-done | bytes 331808 | tf_op jit(solution)/shard_map/ppermute | solution.py:43
  (211 shorter events, 51.0 us)
Async XLA Ops:
  2.6 19.5 %collective-permute-start.9 = (bf16[96,1728]{1,0:T(8,128)(2,1)S(1)}, bf16[96,1728]{1,0:T(8,128)(2,1)S(1)}, u32[]{:S(2)}, u32[]{:S(2)}) collective-permute-start(bf16[96,1728]{1,0:T(8,128)(2,1)S(1)} %pad_maximum_fusion.8), channel_id=1, source_target_pairs={{0,16},{4,20},{8,24},{12,28},{16,0},{20,4},{24,8},{28,12},{1,17},{... | collective-permute-start | bytes 995336 | tf_op jit(solution)/shard_map/ppermute | solution.py:43
  23.3 16.7 %collective-permute-start.10 = (bf16[2,96,1728]{2,1,0:T(8,128)(2,1)S(1)}, bf16[2,96,1728]{2,1,0:T(8,128)(2,1)S(1)}, u32[]{:S(2)}, u32[]{:S(2)}) collective-permute-start(bf16[2,96,1728]{2,1,0:T(8,128)(2,1)S(1)} %pad_maximum_fusion.6), channel_id=1, source_target_pairs={{0,8},{4,12},{8,0},{12,4},{16,24},{20,28},{24,16},{28,20},{1,9},{5... | collective-permute-start | bytes 1990664 | tf_op jit(solution)/shard_map/ppermute | solution.py:43
  41.3 30.7 %collective-permute-start.11 = (bf16[2,2,96,1728]{3,2,0,1:T(8,128)(2,1)}, bf16[2,2,96,1728]{3,2,0,1:T(8,128)(2,1)S(1)}, u32[]{:S(2)}, u32[]{:S(2)}) collective-permute-start(bf16[2,2,96,1728]{3,2,0,1:T(8,128)(2,1)} %pad_maximum_fusion.4), channel_id=1, source_target_pairs={{0,4},{4,0},{8,12},{12,8},{16,20},{20,16},{24,28},{28,24},{1,5},{5... | collective-permute-start | bytes 3981320 | tf_op jit(solution)/shard_map/ppermute | solution.py:43
  72.6 4.5 copy-start.10
  72.6 4.6 copy-start.11
  72.6 4.7 copy-start.12
  72.7 9.9 %copy-start.15 = (bf16[768]{0:T(1024)(128)(2,1)S(1)}, bf16[768]{0:T(1024)(128)(2,1)}, u32[]{:S(2)}) copy-start(bf16[768]{0:T(1024)(128)(2,1)} %param.31) | copy-start | bytes 4612
  72.7 10.4 %copy-start.32 = (s32[8]{0:T(128)S(1)}, s32[8]{0:T(128)}, u32[]{:S(2)}) copy-start(s32[8]{0:T(128)} %param.20) | copy-start | bytes 100
  75.8 12.3 %copy-start.14 = (s32[1,2048]{1,0:T(1,128)S(1)}, s32[1,2048]{1,0:T(1,128)}, u32[]{:S(2)}) copy-start(s32[1,2048]{1,0:T(1,128)} %param.21) | copy-start | bytes 24580
  75.8 86.0 %collective-permute-start.13 = (bf16[768,1728]{0,1:T(8,128)(2,1)}, bf16[768,1728]{0,1:T(8,128)(2,1)}, u32[]{:S(2)}, u32[]{:S(2)}) collective-permute-start(bf16[768,1728]{0,1:T(8,128)(2,1)} %copy.71), channel_id=1, source_target_pairs={{0,2},{1,3},{2,0},{3,1},{4,6},{5,7},{6,4},{7,5},{8,10},{9,11},{10,... | collective-permute-start | bytes 7962632 | tf_op jit(solution)/shard_map/ppermute | solution.py:43
  77.5 10.0 %collective-permute-start.3 = (bf16[3,96,192]{1,2,0:T(8,128)(2,1)S(1)}, bf16[3,96,192]{1,2,0:T(8,128)(2,1)S(1)}, u32[]{:S(2)}, u32[]{:S(2)}) collective-permute-start(bf16[3,96,192]{1,2,0:T(8,128)(2,1)S(1)} %bitcast.141), channel_id=1, source_target_pairs={{0,16},{4,20},{8,24},{12,28},{16,0},{20,4},{24,8},{28,12},{1,17},{... | collective-permute-start | bytes 331784 | tf_op jit(solution)/shard_map/ppermute | solution.py:43
  82.0 69.2 %collective-permute-start.1 = (bf16[512,768]{1,0:T(8,128)(2,1)}, bf16[512,768]{1,0:T(8,128)(2,1)S(1)}, u32[]{:S(2)}, u32[]{:S(2)}) collective-permute-start(bf16[512,768]{1,0:T(8,128)(2,1)} %refs_8_.1), channel_id=1, source_target_pairs={{0,2},{1,3},{2,0},{3,1},{4,6},{5,7},{6,4},{7,5},{8,10},{9,11},{10,... | collective-permute-start | bytes 2359304 | tf_op jit(solution)/shard_map/ppermute | solution.py:43
  82.6 81.0 %collective-permute-start = (bf16[512,768]{1,0:T(8,128)(2,1)}, bf16[512,768]{1,0:T(8,128)(2,1)}, u32[]{:S(2)}, u32[]{:S(2)}) collective-permute-start(bf16[512,768]{1,0:T(8,128)(2,1)} %refs_8_.1), channel_id=1, source_target_pairs={{0,1},{1,0},{2,3},{3,2},{4,5},{5,4},{6,7},{7,6},{8,9},{9,8},{10,11... | collective-permute-start | bytes 2359304 | tf_op jit(solution)/shard_map/ppermute | solution.py:43
  82.6 14.1 %collective-permute-start.15 = (f32[1,768]{1,0:T(1,128)S(1)}, f32[1,768]{1,0:T(1,128)S(1)}, u32[]{:S(2)}, u32[]{:S(2)}) collective-permute-start(f32[1,768]{1,0:T(1,128)S(1)} %reshape.111), channel_id=1, source_target_pairs={{0,1},{1,0},{2,3},{3,2},{4,5},{5,4},{6,7},{7,6},{8,9},{9,8},{10,11... | collective-permute-start | bytes 9224 | tf_op jit(solution)/shard_map/ppermute | solution.py:43
  87.5 63.8 %copy-start.23 = (bf16[192]{0:T(256)(128)(2,1)S(1)}, bf16[192]{0:T(256)(128)(2,1)}, u32[]{:S(2)}) copy-start(bf16[192]{0:T(256)(128)(2,1)} %param.28) | copy-start | bytes 1156
  87.5 63.9 %copy-start.24 = (bf16[192]{0:T(256)(128)(2,1)S(1)}, bf16[192]{0:T(256)(128)(2,1)}, u32[]{:S(2)}) copy-start(bf16[192]{0:T(256)(128)(2,1)} %param.29) | copy-start | bytes 1156
  87.6 65.2 %copy-start.16 = (bf16[768]{0:T(1024)(128)(2,1)S(1)}, bf16[768]{0:T(1024)(128)(2,1)}, u32[]{:S(2)}) copy-start(bf16[768]{0:T(1024)(128)(2,1)} %param.30) | copy-start | bytes 4612
  87.6 65.2 %copy-start.17 = (bf16[768]{0:T(1024)(128)(2,1)S(1)}, bf16[768]{0:T(1024)(128)(2,1)}, u32[]{:S(2)}) copy-start(bf16[768]{0:T(1024)(128)(2,1)} %param.32) | copy-start | bytes 4612
  87.6 65.2 %copy-start.18 = (bf16[768]{0:T(1024)(128)(2,1)S(1)}, bf16[768]{0:T(1024)(128)(2,1)}, u32[]{:S(2)}) copy-start(bf16[768]{0:T(1024)(128)(2,1)} %param.33) | copy-start | bytes 4612
  87.6 65.2 %copy-start.19 = (bf16[768]{0:T(1024)(128)(2,1)S(1)}, bf16[768]{0:T(1024)(128)(2,1)}, u32[]{:S(2)}) copy-start(bf16[768]{0:T(1024)(128)(2,1)} %param.34) | copy-start | bytes 4612
  87.6 65.3 %copy-start.20 = (bf16[768]{0:T(1024)(128)(2,1)S(1)}, bf16[768]{0:T(1024)(128)(2,1)}, u32[]{:S(2)}) copy-start(bf16[768]{0:T(1024)(128)(2,1)} %param.35) | copy-start | bytes 4612
  87.6 65.3 %copy-start.21 = (bf16[768]{0:T(1024)(128)(2,1)S(1)}, bf16[768]{0:T(1024)(128)(2,1)}, u32[]{:S(2)}) copy-start(bf16[768]{0:T(1024)(128)(2,1)} %param.36) | copy-start | bytes 4612
  87.7 8.2 %collective-permute-start.4 = (bf16[3,2,96,192]{2,3,0,1:T(8,128)(2,1)S(1)}, bf16[3,2,96,192]{2,3,0,1:T(8,128)(2,1)S(1)}, u32[]{:S(2)}, u32[]{:S(2)}) collective-permute-start(bf16[3,2,96,192]{2,3,0,1:T(8,128)(2,1)S(1)} %pad_maximum_fusion.9), channel_id=1, source_target_pairs={{0,8},{4,12},{8,0},{12,4},{16,24},{20,28},{24,16},{28,20},{1,9},{5... | collective-permute-start | bytes 663560 | tf_op jit(solution)/shard_map/ppermute | solution.py:43
  95.9 54.0 %collective-permute-start.16 = (f32[1,768]{1,0:T(1,128)S(1)}, f32[1,768]{1,0:T(1,128)S(1)}, u32[]{:S(2)}, u32[]{:S(2)}) collective-permute-start(f32[1,768]{1,0:T(1,128)S(1)} %reshape.111), channel_id=1, source_target_pairs={{0,2},{1,3},{2,0},{3,1},{4,6},{5,7},{6,4},{7,5},{8,10},{9,11},{10,... | collective-permute-start | bytes 9224 | tf_op jit(solution)/shard_map/ppermute | solution.py:43
  96.7 54.9 %collective-permute-start.17 = (f32[1,768]{1,0:T(1,128)S(1)}, f32[1,768]{1,0:T(1,128)S(1)}, u32[]{:S(2)}, u32[]{:S(2)}) collective-permute-start(f32[1,768]{1,0:T(1,128)S(1)} %reshape.111), channel_id=1, source_target_pairs={{0,3},{1,2},{2,1},{3,0},{4,7},{5,6},{6,5},{7,4},{8,11},{9,10},{10,... | collective-permute-start | bytes 9224 | tf_op jit(solution)/shard_map/ppermute | solution.py:43
  149.9 11.7 %collective-permute-start.5 = (bf16[3,2,2,96,192]{3,4,0,1,2:T(8,128)(2,1)S(1)}, bf16[3,2,2,96,192]{3,4,0,1,2:T(8,128)(2,1)S(1)}, u32[]{:S(2)}, u32[]{:S(2)}) collective-permute-start(bf16[3,2,2,96,192]{3,4,0,1,2:T(8,128)(2,1)S(1)} %pad_maximum_fusion.7), channel_id=1, source_target_pairs={{0,4},{4,0},{8,12},{12,8},{16,20},{20,16},{24,28},{28,24},{1,5},{5... | collective-permute-start | bytes 1327112 | tf_op jit(solution)/shard_map/ppermute | solution.py:43
  151.2 10.9 %copy-start.25 = (bf16[512,768]{1,0:T(8,128)(2,1)}, bf16[512,768]{1,0:T(8,128)(2,1)S(1)}, u32[]{:S(2)}) copy-start(bf16[512,768]{1,0:T(8,128)(2,1)S(1)} %collective-permute-done.1.refs_2_.refs_10_) | copy-start | bytes 2359300
  151.2 12.4 %collective-permute-start.2 = (bf16[512,768]{1,0:T(8,128)(2,1)S(1)}, bf16[512,768]{1,0:T(8,128)(2,1)}, u32[]{:S(2)}, u32[]{:S(2)}) collective-permute-start(bf16[512,768]{1,0:T(8,128)(2,1)S(1)} %collective-permute-done.1.refs_2_.refs_10_), channel_id=1, source_target_pairs={{0,1},{1,0},{2,3},{3,2},{4,5},{5,4},{6,7},{7,6},{8,9},{9,8},{10,11... | collective-permute-start | bytes 2359304 | tf_op jit(solution)/shard_map/ppermute | solution.py:43
  151.6 44.0 %collective-permute-start.12 = (bf16[768,1728]{0,1:T(8,128)(2,1)}, bf16[768,1728]{0,1:T(8,128)(2,1)}, u32[]{:S(2)}, u32[]{:S(2)}) collective-permute-start(bf16[768,1728]{0,1:T(8,128)(2,1)} %copy.71), channel_id=1, source_target_pairs={{0,1},{1,0},{2,3},{3,2},{4,5},{5,4},{6,7},{7,6},{8,9},{9,8},{10,11... | collective-permute-start | bytes 7962632 | tf_op jit(solution)/shard_map/ppermute | solution.py:43
  161.8 52.1 %collective-permute-start.14 = (bf16[768,1728]{0,1:T(8,128)(2,1)}, bf16[768,1728]{0,1:T(8,128)(2,1)}, u32[]{:S(2)}, u32[]{:S(2)}) collective-permute-start(bf16[768,1728]{0,1:T(8,128)(2,1)} %collective-permute-done.13), channel_id=1, source_target_pairs={{0,1},{1,0},{2,3},{3,2},{4,5},{5,4},{6,7},{7,6},{8,9},{9,8},{10,11... | collective-permute-start | bytes 7962632 | tf_op jit(solution)/shard_map/ppermute | solution.py:43
  188.6 44.1 %collective-permute-start.6 = (bf16[3,256,128]{2,1,0:T(8,128)(2,1)}, bf16[3,256,128]{2,1,0:T(8,128)(2,1)}, u32[]{:S(2)}, u32[]{:S(2)}) collective-permute-start(bf16[3,256,128]{2,1,0:T(8,128)(2,1)} %get-tuple-element.44), channel_id=1, source_target_pairs={{0,1},{1,0},{2,3},{3,2},{4,5},{5,4},{6,7},{7,6},{8,9},{9,8},{10,11... | collective-permute-start | bytes 589832 | tf_op jit(solution)/shard_map/ppermute | solution.py:43
  189.1 43.6 %collective-permute-start.7 = (bf16[3,256,128]{2,1,0:T(8,128)(2,1)}, bf16[3,256,128]{2,1,0:T(8,128)(2,1)}, u32[]{:S(2)}, u32[]{:S(2)}) collective-permute-start(bf16[3,256,128]{2,1,0:T(8,128)(2,1)} %get-tuple-element.45), channel_id=1, source_target_pairs={{0,2},{1,3},{2,0},{3,1},{4,6},{5,7},{6,4},{7,5},{8,10},{9,11},{10,... | collective-permute-start | bytes 589832 | tf_op jit(solution)/shard_map/ppermute | solution.py:43
  190.5 42.2 %collective-permute-start.8 = (bf16[3,256,128]{2,1,0:T(8,128)(2,1)}, bf16[3,256,128]{2,1,0:T(8,128)(2,1)}, u32[]{:S(2)}, u32[]{:S(2)}) collective-permute-start(bf16[3,256,128]{2,1,0:T(8,128)(2,1)} %get-tuple-element.46), channel_id=1, source_target_pairs={{0,3},{1,2},{2,1},{3,0},{4,7},{5,6},{6,5},{7,4},{8,11},{9,10},{10,... | collective-permute-start | bytes 589832 | tf_op jit(solution)/shard_map/ppermute | solution.py:43
  281.9 9.1 %copy-start.13 = (f32[4,1,768]{2,1,0:T(1,128)S(1)}, f32[4,1,768]{2,1,0:T(1,128)}, u32[]{:S(2)}) copy-start(f32[4,1,768]{2,1,0:T(1,128)} %get-tuple-element.67) | copy-start | bytes 36868
  281.9 9.1 %copy-start.9 = (f32[16,768]{1,0:T(8,128)S(1)}, f32[16,768]{1,0:T(8,128)}, u32[]{:S(2)}) copy-start(f32[16,768]{1,0:T(8,128)} %get-tuple-element.66) | copy-start | bytes 147460
  281.9 16.6 %copy-start.22 = (pred[10]{0:T(512)(128)(4,1)S(1)}, pred[10]{0:T(512)(128)(4,1)}, u32[]{:S(2)}) copy-start(pred[10]{0:T(512)(128)(4,1)} %constant.81.clone.1) | copy-start | bytes 34
  281.9 37.1 %copy-start.28 = (bf16[3,256,128]{2,1,0:T(8,128)(2,1)S(1)}, bf16[3,256,128]{2,1,0:T(8,128)(2,1)}, u32[]{:S(2)}) copy-start(bf16[3,256,128]{2,1,0:T(8,128)(2,1)} %get-tuple-element.54) | copy-start | bytes 589828
  281.9 37.2 %copy-start.27 = (bf16[3,256,128]{2,1,0:T(8,128)(2,1)S(1)}, bf16[3,256,128]{2,1,0:T(8,128)(2,1)}, u32[]{:S(2)}) copy-start(bf16[3,256,128]{2,1,0:T(8,128)(2,1)} %get-tuple-element.55) | copy-start | bytes 589828
  281.9 38.7 %copy-start.26 = (bf16[3,256,128]{2,1,0:T(8,128)(2,1)S(1)}, bf16[3,256,128]{2,1,0:T(8,128)(2,1)}, u32[]{:S(2)}) copy-start(bf16[3,256,128]{2,1,0:T(8,128)(2,1)} %get-tuple-element.56) | copy-start | bytes 589828
  290.2 30.7 %collective-permute-start.27 = (bf16[2,768,1728]{1,2,0:T(8,128)(2,1)}, bf16[2,768,1728]{1,2,0:T(8,128)(2,1)}, u32[]{:S(2)}, u32[]{:S(2)}) collective-permute-start(bf16[2,768,1728]{1,2,0:T(8,128)(2,1)} %copy.84), channel_id=1, source_target_pairs={{0,1},{1,0},{2,3},{3,2},{4,5},{5,4},{6,7},{7,6},{8,9},{9,8},{10,11... | collective-permute-start | bytes 15925256 | tf_op jit(solution)/shard_map/ppermute | solution.py:43
  291.1 7.4 %collective-permute-start.35 = (f32[12,768]{1,0:T(8,128)S(1)}, f32[12,768]{1,0:T(8,128)S(1)}, u32[]{:S(2)}, u32[]{:S(2)}) collective-permute-start(f32[12,768]{1,0:T(8,128)S(1)} %pad_maximum_fusion.11), channel_id=1, source_target_pairs={{0,1},{1,0},{2,3},{3,2},{4,5},{5,4},{6,7},{7,6},{8,9},{9,8},{10,11... | collective-permute-start | bytes 110600 | tf_op jit(solution)/shard_map/ppermute | solution.py:43
  298.6 4.2 collective-permute-start.36
  302.8 4.2 collective-permute-start.37
  307.0 6.0 %collective-permute-start.38 = (f32[11,768]{1,0:T(8,128)S(1)}, f32[11,768]{1,0:T(8,128)S(1)}, u32[]{:S(2)}, u32[]{:S(2)}) collective-permute-start(f32[11,768]{1,0:T(8,128)S(1)} %fusion.12), channel_id=1, source_target_pairs={{0,8},{4,12},{8,0},{12,4},{16,24},{20,28},{24,16},{28,20},{1,9},{5... | collective-permute-start | bytes 101384 | tf_op jit(solution)/shard_map/ppermute | solution.py:43
  313.0 7.9 %collective-permute-start.39 = (f32[11,768]{1,0:T(8,128)S(1)}, f32[11,768]{1,0:T(8,128)S(1)}, u32[]{:S(2)}, u32[]{:S(2)}) collective-permute-start(f32[11,768]{1,0:T(8,128)S(1)} %add.147), channel_id=1, source_target_pairs={{0,16},{4,20},{8,24},{12,28},{16,0},{20,4},{24,8},{28,12},{1,17},{... | collective-permute-start | bytes 101384 | tf_op jit(solution)/shard_map/ppermute | solution.py:43
  319.0 27.4 %collective-permute-start.18 = (bf16[3,256,128]{2,1,0:T(8,128)(2,1)S(1)}, bf16[3,256,128]{2,1,0:T(8,128)(2,1)S(1)}, u32[]{:S(2)}, u32[]{:S(2)}) collective-permute-start(bf16[3,256,128]{2,1,0:T(8,128)(2,1)S(1)} %copy-done.28), channel_id=1, source_target_pairs={{0,1},{1,0},{2,3},{3,2},{4,5},{5,4},{6,7},{7,6},{8,9},{9,8},{10,11... | collective-permute-start | bytes 589832 | tf_op jit(solution)/shard_map/ppermute | solution.py:43
  319.1 27.3 %collective-permute-start.19 = (bf16[3,256,128]{2,1,0:T(8,128)(2,1)S(1)}, bf16[3,256,128]{2,1,0:T(8,128)(2,1)S(1)}, u32[]{:S(2)}, u32[]{:S(2)}) collective-permute-start(bf16[3,256,128]{2,1,0:T(8,128)(2,1)S(1)} %copy-done.27), channel_id=1, source_target_pairs={{0,2},{1,3},{2,0},{3,1},{4,6},{5,7},{6,4},{7,5},{8,10},{9,11},{10,... | collective-permute-start | bytes 589832 | tf_op jit(solution)/shard_map/ppermute | solution.py:43
  320.6 25.8 %collective-permute-start.20 = (bf16[3,256,128]{2,1,0:T(8,128)(2,1)S(1)}, bf16[3,256,128]{2,1,0:T(8,128)(2,1)S(1)}, u32[]{:S(2)}, u32[]{:S(2)}) collective-permute-start(bf16[3,256,128]{2,1,0:T(8,128)(2,1)S(1)} %copy-done.26), channel_id=1, source_target_pairs={{0,3},{1,2},{2,1},{3,0},{4,7},{5,6},{6,5},{7,4},{8,11},{9,10},{10,... | collective-permute-start | bytes 589832 | tf_op jit(solution)/shard_map/ppermute | solution.py:43
  334.3 4.2 copy-start
  344.8 70.5 %collective-permute-start.28 = (bf16[768,1728]{0,1:T(8,128)(2,1)}, bf16[768,1728]{0,1:T(8,128)(2,1)}, u32[]{:S(2)}, u32[]{:S(2)}) collective-permute-start(bf16[768,1728]{0,1:T(8,128)(2,1)} %copy.86), channel_id=1, source_target_pairs={{0,2},{1,3},{2,0},{3,1},{4,6},{5,7},{6,4},{7,5},{8,10},{9,11},{10,... | collective-permute-start | bytes 7962632 | tf_op jit(solution)/shard_map/ppermute | solution.py:43
  410.9 16.2 %collective-permute-start.32 = (f32[3,3,64]{2,1,0:T(4,128)S(1)}, f32[3,3,64]{2,1,0:T(4,128)S(1)}, u32[]{:S(2)}, u32[]{:S(2)}) collective-permute-start(f32[3,3,64]{2,1,0:T(4,128)S(1)} %reshape.118), channel_id=1, source_target_pairs={{0,4},{4,0},{8,12},{12,8},{16,20},{20,16},{24,28},{28,24},{1,5},{5... | collective-permute-start | bytes 6920 | tf_op jit(solution)/shard_map/ppermute | solution.py:43
  414.8 17.7 %collective-permute-start.24 = (bf16[3,2,2,96,192]{3,4,0,1,2:T(8,128)(2,1)}, bf16[3,2,2,96,192]{3,4,0,1,2:T(8,128)(2,1)}, u32[]{:S(2)}, u32[]{:S(2)}) collective-permute-start(bf16[3,2,2,96,192]{3,4,0,1,2:T(8,128)(2,1)} %bitcast.41), channel_id=1, source_target_pairs={{0,4},{4,0},{8,12},{12,8},{16,20},{20,16},{24,28},{28,24},{1,5},{5... | collective-permute-start | bytes 1327112 | tf_op jit(solution)/shard_map/ppermute | solution.py:43
  425.4 34.2 %collective-permute-start.29 = (bf16[2,2,96,1728]{3,2,0,1:T(8,128)(2,1)}, bf16[2,2,96,1728]{3,2,0,1:T(8,128)(2,1)}, u32[]{:S(2)}, u32[]{:S(2)}) collective-permute-start(bf16[2,2,96,1728]{3,2,0,1:T(8,128)(2,1)} %fusion.2), channel_id=1, source_target_pairs={{0,4},{4,0},{8,12},{12,8},{16,20},{20,16},{24,28},{28,24},{1,5},{5... | collective-permute-start | bytes 3981320 | tf_op jit(solution)/shard_map/ppermute | solution.py:43
  427.1 3.7 collective-permute-start.33
  430.8 5.0 %collective-permute-start.34 = (f32[3,3,64]{2,1,0:T(4,128)S(1)}, f32[3,3,64]{2,1,0:T(4,128)S(1)}, u32[]{:S(2)}, u32[]{:S(2)}) collective-permute-start(f32[3,3,64]{2,1,0:T(4,128)S(1)} %add.140), channel_id=1, source_target_pairs={{0,16},{4,20},{8,24},{12,28},{16,0},{20,4},{24,8},{28,12},{1,17},{... | collective-permute-start | bytes 6920 | tf_op jit(solution)/shard_map/ppermute | solution.py:43
  433.8 6.8 %collective-permute-start.25 = (bf16[3,2,96,192]{2,3,0,1:T(8,128)(2,1)S(1)}, bf16[3,2,96,192]{2,3,0,1:T(8,128)(2,1)S(1)}, u32[]{:S(2)}, u32[]{:S(2)}) collective-permute-start(bf16[3,2,96,192]{2,3,0,1:T(8,128)(2,1)S(1)} %fusion.5), channel_id=1, source_target_pairs={{0,8},{4,12},{8,0},{12,4},{16,24},{20,28},{24,16},{28,20},{1,9},{5... | collective-permute-start | bytes 663560 | tf_op jit(solution)/shard_map/ppermute | solution.py:43
  435.3 28.6 %collective-permute-start.22 = (bf16[512,768]{1,0:T(8,128)(2,1)}, bf16[512,768]{1,0:T(8,128)(2,1)}, u32[]{:S(2)}, u32[]{:S(2)}) collective-permute-start(bf16[512,768]{1,0:T(8,128)(2,1)} %get-tuple-element.60), channel_id=1, source_target_pairs={{0,1},{1,0},{2,3},{3,2},{4,5},{5,4},{6,7},{7,6},{8,9},{9,8},{10,11... | collective-permute-start | bytes 2359304 | tf_op jit(solution)/shard_map/ppermute | solution.py:43
  435.3 45.7 %collective-permute-start.21 = (bf16[512,768]{1,0:T(8,128)(2,1)}, bf16[512,768]{1,0:T(8,128)(2,1)S(1)}, u32[]{:S(2)}, u32[]{:S(2)}) collective-permute-start(bf16[512,768]{1,0:T(8,128)(2,1)} %get-tuple-element.58), channel_id=1, source_target_pairs={{0,1},{1,0},{2,3},{3,2},{4,5},{5,4},{6,7},{7,6},{8,9},{9,8},{10,11... | collective-permute-start | bytes 2359304 | tf_op jit(solution)/shard_map/ppermute | solution.py:43
  440.7 23.2 %collective-permute-start.26 = (bf16[3,96,192]{1,2,0:T(8,128)(2,1)S(1)}, bf16[3,96,192]{1,2,0:T(8,128)(2,1)S(1)}, u32[]{:S(2)}, u32[]{:S(2)}) collective-permute-start(bf16[3,96,192]{1,2,0:T(8,128)(2,1)S(1)} %fusion.6), channel_id=1, source_target_pairs={{0,16},{4,20},{8,24},{12,28},{16,0},{20,4},{24,8},{28,12},{1,17},{... | collective-permute-start | bytes 331784 | tf_op jit(solution)/shard_map/ppermute | solution.py:43
  463.1 16.6 %collective-permute-start.30 = (bf16[2,96,1728]{2,1,0:T(8,128)(2,1)}, bf16[2,96,1728]{2,1,0:T(8,128)(2,1)}, u32[]{:S(2)}, u32[]{:S(2)}) collective-permute-start(bf16[2,96,1728]{2,1,0:T(8,128)(2,1)} %fusion.3), channel_id=1, source_target_pairs={{0,8},{4,12},{8,0},{12,4},{16,24},{20,28},{24,16},{28,20},{1,9},{5... | collective-permute-start | bytes 1990664 | tf_op jit(solution)/shard_map/ppermute | solution.py:43
  466.1 18.4 %collective-permute-start.23 = (bf16[512,768]{1,0:T(8,128)(2,1)}, bf16[512,768]{1,0:T(8,128)(2,1)}, u32[]{:S(2)}, u32[]{:S(2)}) collective-permute-start(bf16[512,768]{1,0:T(8,128)(2,1)} %add_convert_fusion.1), channel_id=1, source_target_pairs={{0,2},{1,3},{2,0},{3,1},{4,6},{5,7},{6,4},{7,5},{8,10},{9,11},{10,... | collective-permute-start | bytes 2359304 | tf_op jit(solution)/shard_map/ppermute | solution.py:43
  472.2 12.3 %copy-start.6 = (f32[512,768]{1,0:T(8,128)S(1)}, f32[512,768]{1,0:T(8,128)}, u32[]{:S(2)}) copy-start(f32[512,768]{1,0:T(8,128)} %get-tuple-element.48) | copy-start | bytes 4718596
  472.2 12.3 %copy-start.7 = (bf16[512,768]{1,0:T(8,128)(2,1)S(1)}, bf16[512,768]{1,0:T(8,128)(2,1)}, u32[]{:S(2)}) copy-start(bf16[512,768]{1,0:T(8,128)(2,1)} %get-tuple-element.57) | copy-start | bytes 2359300
  480.9 16.3 %collective-permute-start.31 = (bf16[96,1728]{1,0:T(8,128)(2,1)S(1)}, bf16[96,1728]{1,0:T(8,128)(2,1)S(1)}, u32[]{:S(2)}, u32[]{:S(2)}) collective-permute-start(bf16[96,1728]{1,0:T(8,128)(2,1)S(1)} %fusion.4), channel_id=1, source_target_pairs={{0,16},{4,20},{8,24},{12,28},{16,0},{20,4},{24,8},{28,12},{1,17},{... | collective-permute-start | bytes 995336 | tf_op jit(solution)/shard_map/ppermute | solution.py:43
  (9 other events, 19.0 us)

commit v2 on v1

v2 whole, which is shorter than its diff:
```python
import functools

import jax
import jax.numpy as jnp
from jax import lax
from jax.experimental import pallas as pl
from jax.experimental.pallas import tpu as pltpu
from jax.sharding import PartitionSpec as P

HEAD_DIM = 64
LANES = 128
EPSILON = 1e-12
MASKED = -1e30
BF16 = jnp.bfloat16
F32 = jnp.float32
NT = (((1,), (1,)), ((), ()))
TN = (((0,), (0,)), ((), ()))
VMEM_LIMIT = 64 << 20


def dot(left, right):
    return jnp.dot(left, right, preferred_element_type=F32)


def dot_nt(left, right):
    return lax.dot_general(left, right, NT, preferred_element_type=F32)


def dot_tn(left, right):
    return lax.dot_general(left, right, TN, preferred_element_type=F32)


def place_of(mask, height, placed):
    start = (lax.axis_index("dp") ^ mask) * height if placed else 0
    return pl.ds(pl.multiple_of(start, height), height)


def valid_row(positions_ref, lengths_ref, j, rows):
    start = (lax.axis_index("tensor") ^ j) * rows
    own = positions_ref[:, pl.ds(pl.multiple_of(start, rows), rows)]
    return own < lengths_ref[lax.axis_index("dp")]


def in_three(column):
    first = column.astype(BF16)
    rest = column - first.astype(F32)
    second = rest.astype(BF16)
    third = (rest - second.astype(F32)).astype(BF16)
    return first, second, third


def swap(value, axis, bits):
    size = lax.axis_size(axis)
    return lax.ppermute(value, axis, [(i, i ^ bits) for i in range(size)])


def bit_of(axis, bit):
    return (lax.axis_index(axis) >> bit) & 1


def gather_bits(block, axis, order, at):
    done = []
    for bit in order:
        place = at + sum(other > bit for other in done)
        got = swap(block, axis, 1 << bit)
        upper = bit_of(axis, bit) == 1
        low = jnp.where(upper, got, block)
        high = jnp.where(upper, block, got)
        block = jnp.stack([low, high], axis=place)
        done.append(bit)
    return block


def scatter_bits(partial, axis, order, at):
    left = sorted(order, reverse=True)
    for bit in order:
        place = at + left.index(bit)
        mine = bit_of(axis, bit)
        away = lax.dynamic_index_in_dim(partial, 1 - mine, place, keepdims=False)
        keep = lax.dynamic_index_in_dim(partial, mine, place, keepdims=False)
        got = swap(away.astype(BF16), axis, 1 << bit)
        partial = keep.astype(F32) + got.astype(F32)
        left.remove(bit)
    return partial


def after(value, *others):
    return lax.optimization_barrier((value,) + others)[0]


def params():
    return pltpu.CompilerParams(vmem_limit_bytes=VMEM_LIMIT - (1 << 20))


def cost(flops, moved, exps=0):
    return pl.CostEstimate(flops=flops, bytes_accessed=moved, transcendentals=exps)


SMEM_SPEC = pl.BlockSpec(memory_space=pltpu.SMEM)
VMEM_SPEC = pl.BlockSpec(memory_space=pltpu.VMEM)
ANY_SPEC = pl.BlockSpec(memory_space=pl.ANY)


def project_kernel(*refs, masks, heads, placed):
    x_refs, w_refs = refs[:4], refs[4 : 4 + len(masks)]
    bq_ref, bv_ref, positions_ref, lengths_ref, q_out, k_out, v_out, w_s = refs[4 + len(masks) :]
    rows = x_refs[0].shape[0]
    for ref, entries in zip(w_refs, masks, strict=True):
        for z, mask in enumerate(entries):
            w_s[place_of(mask, ref.shape[1], placed), :] = ref[z]
    lane = lax.broadcasted_iota(jnp.int32, (1, LANES), 1)
    head_lane = lane < HEAD_DIM
    one_q = jnp.where(lane == HEAD_DIM, 1.0, 0.0)
    one_k = jnp.where((lane > HEAD_DIM) & (lane <= HEAD_DIM + 3), 1.0, 0.0)
    one_v = jnp.where((lane >= HEAD_DIM) & (lane < HEAD_DIM + 3), 1.0, 0.0)
    b_query = bq_ref[...].astype(F32)
    bias = jnp.concatenate([b_query, jnp.zeros_like(b_query), bv_ref[...].astype(F32)], axis=1)
    for j in range(4):
        part = pl.ds(j * rows, rows)
        whole = dot(x_refs[j][...], w_s[...]) + bias
        masked = jnp.where(valid_row(positions_ref, lengths_ref, j, rows), 0.0, MASKED)
        masked = jnp.broadcast_to(masked, (LANES, rows)).T

        def columns(group):
            start = group // 2 * LANES
            both = whole[:, start : start + LANES]
            if both.shape[1] < LANES:
                both = jnp.concatenate([both, both], axis=1)
            return pltpu.roll(both, HEAD_DIM, 1) if group % 2 else both

        for h in range(heads):
            query = columns(h).astype(BF16).astype(F32) * (HEAD_DIM**-0.5)
            q_out[h, part, :] = jnp.where(head_lane, query, one_q).astype(BF16)
            key = jnp.where(head_lane, columns(heads + h), one_k)
            k_out[h, part, :] = jnp.where(lane == HEAD_DIM, masked, key).astype(BF16)
            value = jnp.where(head_lane, columns(2 * heads + h), one_v)
            v_out[h, part, :] = value.astype(BF16)


def project(parts, pieces, masks, b_query, b_value, positions, lengths, heads, placed):
    rows, width = parts[0].shape
    seq = 4 * rows
    return pl.pallas_call(
        functools.partial(project_kernel, masks=masks, heads=heads, placed=placed),
        in_specs=[VMEM_SPEC] * (7 + len(pieces)) + [SMEM_SPEC],
        out_specs=[VMEM_SPEC] * 3,
        out_shape=[jax.ShapeDtypeStruct((heads, seq, LANES), BF16)] * 3,
        scratch_shapes=[pltpu.VMEM((width, pieces[0].shape[2]), BF16)],
        compiler_params=params(),
        cost_estimate=cost(1000, 1000),
        name="project",
    )(*parts, *pieces, b_query, b_value, positions, lengths)


def forward_kernel(q_ref, k_ref, v_ref, *refs, unroll):
    q_out, o_out, own, near, far, packed = refs[-6:]
    seq = q_ref.shape[1]
    block = seq // 8
    lane = lax.broadcasted_iota(jnp.int32, (1, LANES), 1)
    head_lane = lane < HEAD_DIM

    def place(i):
        return pl.ds(pl.multiple_of(i * block, block), block)

    def scores_of(i):
        query = q_ref[0, place(i), :]
        scores = dot_nt(query, k_ref[0])
        return query, scores, jnp.max(scores, axis=-1, keepdims=True)

    def attend(i, query, scores, top):
        expon = jnp.exp(scores - top).astype(BF16)
        total = dot(expon, v_ref[0])
        row_sum = total[:, HEAD_DIM : HEAD_DIM + 1]
        out = total * (1.0 / row_sum)
        o_out[place(i), :] = out
        one, two, three = in_three(-(top + jnp.log(row_sum)))
        q_out[place(i), :] = jnp.where(
            lane == HEAD_DIM + 1,
            one,
            jnp.where(lane == HEAD_DIM + 2, two, jnp.where(lane == HEAD_DIM + 3, three, query)),
        )
        return out

    @pl.loop(0, 8 // unroll)
    def _(step):
        held = scores_of(step * unroll)
        even = None
        for u in range(unroll):
            i = step * unroll + u
            following = scores_of(i + 1) if u < unroll - 1 else None
            out = attend(i, *held)
            if u % 2 == 0:
                even = out
            else:
                pair = jnp.where(head_lane, even, pltpu.roll(out, HEAD_DIM, 1))
                packed[step * (unroll // 2) + u // 2] = pair.astype(BF16)
            held = following

    own[0] = packed[0]
    near[0] = packed[1]
    far[0, 0] = packed[2]
    far[1, 0] = packed[3]


def attention_forward(head, q, k, v, packed):
    heads, seq, _ = q.shape
    block = seq // 8
    one = pl.BlockSpec((1, seq, LANES), lambda i: (head, 0, 0))
    flat = pl.BlockSpec((seq, LANES), lambda i: (0, 0))
    piece = pl.BlockSpec((1, block, LANES), lambda i: (head, 0, 0))
    pieces = pl.BlockSpec((2, 1, block, LANES), lambda i: (0, head, 0, 0))
    shape = jax.ShapeDtypeStruct
    q_kept, out, *packed = pl.pallas_call(
        functools.partial(forward_kernel, unroll=4),
        grid=(1,),
        in_specs=[one] * 3 + [ANY_SPEC] * len(packed),
        out_specs=[flat, flat, piece, piece, pieces],
        out_shape=[shape((seq, LANES), BF16), shape((seq, LANES), F32)]
        + [shape((heads, block, LANES), BF16)] * 2
        + [shape((2, heads, block, LANES), BF16)],
        scratch_shapes=[pltpu.VMEM((4, block, LANES), BF16)],
        input_output_aliases={3 + i: 2 + i for i in range(len(packed))},
        compiler_params=params(),
        cost_estimate=cost(1000, 1000),
        name="attention_forward",
    )(q, k, v, *packed)
    return q_kept, out, packed


def backward_kernel(q_ref, k_ref, v_ref, o_ref, *refs, placed):
    d_refs, x_refs = refs[:4], refs[4:8]
    g_ref, gb_ref, gw_ref, dk_s, dv_s, gw_s, d_s = refs[-7:]
    seq = q_ref.shape[0]
    block = seq // 8
    rows = seq // 4
    lane = lax.broadcasted_iota(jnp.int32, (1, LANES), 1)
    head_lane = lane < HEAD_DIM
    scale = HEAD_DIM**-0.5
    for j in range(4):
        d_s[j] = d_refs[j][0]
    dk_s[...] = jnp.zeros_like(dk_s)
    dv_s[...] = jnp.zeros_like(dv_s)

    @pl.loop(0, 4)
    def _(j):
        for half in range(2):
            place = pl.ds(pl.multiple_of((2 * j + half) * block, block), block)
            query = q_ref[place, :]
            grad = d_s[j].astype(F32)
            if half == 1:
                grad = pltpu.roll(grad, HEAD_DIM, 1)
            grad = jnp.where(head_lane, grad, 0.0)
            delta = jnp.sum(grad * o_ref[place, :], axis=-1, keepdims=True)
            one, two, three = in_three(-delta)
            grad = grad.astype(BF16)
            grad_and = jnp.where(
                lane == HEAD_DIM,
                one,
                jnp.where(lane == HEAD_DIM + 1, two, jnp.where(lane == HEAD_DIM + 2, three, grad)),
            )
            probs = jnp.exp(dot_nt(k_ref[0], query))
            lifted = dot_nt(v_ref[0], grad_and)
            grad_scores = (probs * lifted).astype(BF16)
            dv_s[...] += dot(probs.astype(BF16), grad)
            dk_s[...] += dot(grad_scores, query)
            grad_query = dot_tn(grad_scores, k_ref[0]) * scale
            g_ref[0, place, :LANES] = jnp.where(head_lane, grad_query, 0.0).astype(BF16)

    both = jnp.where(head_lane, g_ref[0, :, :LANES].astype(F32), pltpu.roll(dk_s[...], HEAD_DIM, 1))
    g_ref[0, :, :LANES] = both.astype(BF16)
    g_ref[0, :, LANES:] = dv_s[:, :HEAD_DIM].astype(BF16)
    grads = g_ref[0]
    gb_ref[...] = jnp.sum(grads.astype(F32), axis=0, keepdims=True)
    total = dot_tn(grads[:rows], x_refs[0][...])
    for j in range(1, 4):
        total += dot_tn(grads[j * rows : (j + 1) * rows], x_refs[j][...])
    gw_s[...] = total.T.astype(BF16)
    for i in range(gw_ref.shape[1]):
        gw_ref[0, i] = gw_s[place_of(i, gw_ref.shape[2], placed), :]


def attention_backward(head, q, k, v, out, grads, parts, blocks, before):
    heads, seq, _ = k.shape
    rows, width = parts[0].shape
    one = pl.BlockSpec((1, seq, LANES), lambda i: (head, 0, 0))
    flat = pl.BlockSpec((seq, LANES), lambda i: (0, 0))
    piece = pl.BlockSpec((1, seq // 8, LANES), lambda i: (head, 0, 0))
    whole = pl.BlockSpec((rows, width), lambda i: (0, 0))
    three = 3 * HEAD_DIM
    share = width // blocks
    shape = jax.ShapeDtypeStruct
    alias = {12: 0, 13: 2} if before else {}
    return pl.pallas_call(
        functools.partial(backward_kernel, placed=blocks > 1),
        grid=(1,),
        in_specs=[flat, one, one, flat] + [piece] * 4 + [whole] * 4 + [ANY_SPEC] * len(before),
        out_specs=[
            pl.BlockSpec((1, seq, three), lambda i: (head, 0, 0)),
            pl.BlockSpec((1, three), lambda i: (0, 0)),
            pl.BlockSpec((1, blocks, share, three), lambda i: (head, 0, 0, 0)),
        ],
        out_shape=[
            shape((heads, seq, three), BF16),
            shape((1, three), F32),
            shape((heads, blocks, share, three), BF16),
        ],
        scratch_shapes=[
            pltpu.VMEM((seq, LANES), F32),
            pltpu.VMEM((seq, LANES), F32),
            pltpu.VMEM((width, three), BF16),
            pltpu.VMEM((4, seq // 8, LANES), BF16),
        ],
        input_output_aliases=alias,
        compiler_params=params(),
        cost_estimate=cost(1000, 1000),
        name="attention_backward",
    )(q, k, v, out, *grads, *parts, *before)


def input_kernel(g_ref, *refs, masks, which, placed):
    w_refs = refs[: len(masks)]
    outs, w_s = refs[len(masks) : -1], refs[-1]
    heads, seq, three = g_ref.shape
    rows = seq // 4
    for ref, entries in zip(w_refs, masks, strict=True):
        for z, mask in enumerate(entries):
            place = place_of(mask, ref.shape[1], placed)
            for h in range(heads):
                for kind in range(3):
                    start = (kind * heads + h) * HEAD_DIM
                    stop = (h * 3 + kind) * HEAD_DIM
                    w_s[place, stop : stop + HEAD_DIM] = ref[z, :, start : start + HEAD_DIM]
    for out, j in zip(outs, which, strict=True):
        part = pl.ds(j * rows, rows)
        total = dot_nt(g_ref[0, part, :], w_s[:, :three])
        for h in range(1, heads):
            total += dot_nt(g_ref[h, part, :], w_s[:, h * three : (h + 1) * three])
        out[...] = total.astype(out.dtype)


def input_part(g_all, pieces, masks, which, placed):
    heads, seq, three = g_all.shape
    width = pieces[0].shape[0] * pieces[0].shape[1] * len(pieces)
    return pl.pallas_call(
        functools.partial(input_kernel, masks=masks, which=which, placed=placed),
        in_specs=[VMEM_SPEC] * (1 + len(pieces)),
        out_specs=[VMEM_SPEC] * len(which),
        out_shape=[jax.ShapeDtypeStruct((seq // 4, width), BF16)] * len(which),
        scratch_shapes=[pltpu.VMEM((width, heads * three), BF16)],
        compiler_params=params(),
        cost_estimate=cost(1000, 1000),
        name="input_part",
    )(g_all, *pieces)


def middle_kernel(*refs, plan, blocks):
    w_refs = refs[: len(plan)]
    refs = refs[len(plan) :]
    own_ref, near_ref, far_ref = refs[:3]
    x_ref, og_ref, positions_ref, lengths_ref, vec_ref = refs[3:8]
    lo_ref, done_ref, sums_ref, gbup_ref, sent, kept = refs[8:14]
    ga = refs[14:18]
    w1_s, w2_s, att_s, wo_s, hid_s, slope_s, nrm_s, nb_s, n1_s, rs_s, ffn_s = refs[18:29]
    gf_s, gft_s, nbt_s, acc_s, pre_s, g_s, bup_s, mask_s, in_sem, down_sem, up_sem, out_sem = refs[29:]
    rows, width = x_ref.shape
    hidden = w2_s.shape[2]
    pieces = 4
    cols = width // pieces
    placed = blocks > 1
    chunk = 128
    share = width // blocks
    half = rows // 2
    b_out, b_down, gain_a, shift_a, gain_f, shift_f = (vec_ref[i : i + 1, :] for i in range(6))

    count = cols // HEAD_DIM
    att = [[own_ref[h] for h in range(count)]]
    for ref, i in ((near_ref, 0), (far_ref, 0), (near_ref, 1)):
        att.append([ref[i, h] for h in range(count)])

    loads = []
    for ref, entries in zip(w_refs, plan, strict=True):
        for index, second, j, row in entries:
            source = ref.at[index]
            target = (w2_s if second else w1_s).at[j].at[place_of(row, source.shape[0], placed)]
            copy = pltpu.make_async_copy(source, target, in_sem.at[len(loads)])
            loads.append((second, copy))
            copy.start()

    def row_loop(work):
        @pl.loop(0, rows // chunk)
        def _(i):
            work(pl.ds(pl.multiple_of(i * chunk, chunk), chunk))

    def add_sum(index, value):
        sums_ref[index : index + 1, :] += jnp.sum(value, axis=0, keepdims=True)

    def mean(value):
        return jnp.mean(value, axis=-1, keepdims=True)

    def normal(value):
        centred = value - mean(value)
        inverse = lax.rsqrt(mean(centred * centred) + EPSILON)
        return centred * inverse, inverse

    def norm_back(grad, unit, inverse, gain):
        scaled = grad * gain
        return (scaled - mean(scaled) - unit * mean(scaled * unit)) * inverse

    sums_ref[...] = jnp.zeros_like(sums_ref)
    own_valid = jnp.where(valid_row(positions_ref, lengths_ref, 0, rows), 1.0, 0.0)
    mask_s[...] = jnp.broadcast_to(own_valid, (LANES, rows)).T
    for j in range(pieces):
        for h in range(cols // HEAD_DIM):
            at = j * cols + h * HEAD_DIM
            att_s[:half, at : at + HEAD_DIM] = att[j][h][:, :HEAD_DIM]
            att_s[half:, at : at + HEAD_DIM] = att[j][h][:, HEAD_DIM:]
    for second, copy in loads:
        if not second:
            copy.wait()
    for j in range(pieces):
        wo_s[:, j * cols : (j + 1) * cols] = w1_s[j, :, hidden : hidden + cols]
        last = w1_s[j, :, hidden + cols - HEAD_DIM :].astype(F32)
        bup_s[j] = last.T[HEAD_DIM : HEAD_DIM + 1, :]
    ffn_s[...] = dot_nt(att_s[...], wo_s[...])

    def first_norm(r):
        value = x_ref[r, :].astype(F32)
        attn = ffn_s[r, :] + b_out
        valid = mask_s[r, :1] > 0.0
        add_sum(6, jnp.where(valid, value * value, 0.0))
        add_sum(7, jnp.where(valid, attn * attn, 0.0))
        unit, inverse = normal(value + attn)
        normed = unit * gain_a + shift_a
        n1_s[r, :] = unit
        rs_s[r, :] = jnp.broadcast_to(inverse, (chunk, LANES))
        nrm_s[r, :] = normed
        nb_s[r, :] = normed.astype(BF16)

    row_loop(first_norm)
    ffn_s[...] = jnp.zeros_like(ffn_s)
    for second, copy in loads:
        if second:
            copy.wait()

    @pl.loop(0, pieces)
    def _(j):
        pre_s[...] = dot(nb_s[...], w1_s[j, :, :hidden]) + bup_s[j]

        def gelu(r):
            pre = pre_s[r, :]
            cdf = 0.5 * (1.0 + lax.erf(pre * (0.5**0.5)))
            pdf = jnp.exp(pre * pre * -0.5) * (2.0 * jnp.pi) ** -0.5
            hid_s[j, r, :] = (pre * cdf).astype(BF16)
            slope_s[j, r, :] = cdf + pre * pdf

        row_loop(gelu)
        ffn_s[...] += dot_nt(hid_s[j], w2_s[j])

    def second_norm(r):
        ffn = ffn_s[r, :] + b_down
        valid = mask_s[r, :1] > 0.0
        add_sum(8, jnp.where(valid, ffn * ffn, 0.0))
        unit, inverse = normal(nrm_s[r, :] + ffn)
        lo_ref[r, :] = (unit * gain_f + shift_f).astype(BF16)
        grad = og_ref[r, :].astype(F32)
        add_sum(4, grad * unit)
        add_sum(5, grad)
        d_two = norm_back(grad, unit, inverse, gain_f)
        low = d_two.astype(BF16)
        add_sum(1, low.astype(F32))
        acc_s[r, :] = d_two
        gf_s[r, :] = low

    row_loop(second_norm)
    gft_s[...] = gf_s[...].T
    nbt_s[...] = nb_s[...].T

    places = [place_of(i, share, placed) for i in range(blocks)]

    def copies(j, lanes, target, place, sem):
        return [
            pltpu.make_async_copy(
                g_s.at[j].at[places[i], lanes], target.at[place, i, :, lanes], sem.at[j, i]
            )
            for i in range(blocks)
        ]

    lanes_d, lanes_u, lanes_o = (
        pl.ds(0, hidden),
        pl.ds(hidden, hidden),
        pl.ds(2 * hidden, cols),
    )
    for away, target in ((1, sent), (0, kept)):

        @pl.loop(0, pieces // 2)
        def _(place):
            j = 2 * place + away
            pre_s[...] = dot(gf_s[...], w2_s[j]) * slope_s[j]
            low = pre_s[...].astype(BF16)
            gbup_ref[j] = jnp.sum(low.astype(F32), axis=0, keepdims=True)
            g_s[j, :, lanes_d] = dot(gft_s[...], hid_s[j]).astype(BF16)
            for copy in copies(j, lanes_d, target, place, down_sem):
                copy.start()
            g_s[j, :, lanes_u] = dot(nbt_s[...], low).astype(BF16)
            for copy in copies(j, lanes_u, target, place, up_sem):
                copy.start()
            acc_s[...] += dot_nt(low, w1_s[j, :, :hidden])

    def first_back(r):
        grad = acc_s[r, :]
        unit = n1_s[r, :]
        add_sum(2, grad * unit)
        add_sum(3, grad)
        d_one = norm_back(grad, unit, rs_s[r, :1], gain_a)
        low = d_one.astype(BF16)
        add_sum(0, low.astype(F32))
        done_ref[r, :] = d_one
        gf_s[r, :] = low

    row_loop(first_back)
    low = gf_s[...]
    gout = dot_tn(low, att_s[...]).astype(BF16)
    for j in range(pieces):
        g_s[j, :, 2 * hidden : 2 * hidden + cols] = gout[:, j * cols : (j + 1) * cols]
        for copy in copies(j, lanes_o, sent if j % 2 else kept, j // 2, out_sem):
            copy.start()
    back = dot(low, wo_s[...]).astype(BF16)
    for j in range(pieces):
        for h in range(cols // HEAD_DIM):
            at = j * cols + h * HEAD_DIM
            ga[j][h, :, :HEAD_DIM] = back[:half, at : at + HEAD_DIM]
            ga[j][h, :, HEAD_DIM:] = back[half:, at : at + HEAD_DIM]
    for j in range(pieces):
        target = sent if j % 2 else kept
        for lanes, sem in ((lanes_d, down_sem), (lanes_u, up_sem), (lanes_o, out_sem)):
            for copy in copies(j, lanes, target, j // 2, sem):
                copy.wait()


def middle(blocks, weights, plan, att, tokens, out_grad, positions, lengths, vectors, hidden):
    rows, width = tokens.shape
    cols = width // 4
    share = width // blocks
    shape = jax.ShapeDtypeStruct
    vmem = pltpu.VMEM
    loads = sum(len(entries) for entries in plan)
    return pl.pallas_call(
        functools.partial(middle_kernel, plan=plan, blocks=blocks),
        in_specs=[ANY_SPEC] * len(weights) + [VMEM_SPEC] * 6 + [SMEM_SPEC, VMEM_SPEC],
        out_specs=[VMEM_SPEC] * 4 + [ANY_SPEC] * 2 + [VMEM_SPEC] * 4,
        out_shape=[
            shape((rows, width), BF16),
            shape((rows, width), F32),
            shape((16, width), F32),
            shape((4, 1, hidden), F32),
        ]
        + [shape((2, blocks, share, 2 * hidden + cols), BF16)] * 2
        + [shape(att[0].shape, BF16)] * 4,
        scratch_shapes=[
            vmem((4, width, weights[0].shape[-1]), BF16),
            vmem((4, width, hidden), BF16),
            vmem((rows, width), BF16),
            vmem((width, width), BF16),
            vmem((4, rows, hidden), BF16),
            vmem((4, rows, hidden), F32),
            vmem((rows, width), F32),
            vmem((rows, width), BF16),
            vmem((rows, width), F32),
            vmem((rows, LANES), F32),
            vmem((rows, width), F32),
            vmem((rows, width), BF16),
            vmem((width, rows), BF16),
            vmem((width, rows), BF16),
            vmem((rows, width), F32),
            vmem((rows, hidden), F32),
            vmem((4, width, 2 * hidden + cols), BF16),
            vmem((4, 1, hidden), F32),
            vmem((rows, LANES), F32),
            pltpu.SemaphoreType.DMA((loads,)),
            pltpu.SemaphoreType.DMA((4, blocks)),
            pltpu.SemaphoreType.DMA((4, blocks)),
            pltpu.SemaphoreType.DMA((4, blocks)),
        ],
        compiler_params=params(),
        cost_estimate=cost(1000, 1000),
        name="middle",
    )(*weights, *att, tokens, out_grad, positions, lengths, vectors)


def body(
    tokens,
    seq_lengths,
    positions,
    w_query,
    w_key,
    w_value,
    w_out,
    w_up,
    w_down,
    b_query,
    b_value,
    b_out,
    b_up,
    b_down,
    gain_attn,
    shift_attn,
    gain_ffn,
    shift_ffn,
    out_grad,
):
    group = lax.axis_index("dp")
    member = lax.axis_index("tensor")
    dp_count = lax.axis_size("dp")
    bits = dp_count.bit_length() - 1
    rows, width = tokens.shape
    own_cols = w_query.shape[1]
    heads = own_cols // HEAD_DIM
    share = w_query.shape[0]
    hidden = w_up.shape[1]
    placed = share % 16 == 0 and bits >= 2
    blocks = dp_count if placed else 1
    def core(value):
        return swap(value, "tensor", 1)

    def cross(value):
        return swap(value, "tensor", 2)

    def grow(value, masks, bit, *hold):
        got = after(swap(value, "dp", 1 << bit), *hold)
        both = jnp.stack([value, got], axis=1).reshape((-1,) + value.shape[1:])
        return both, [m ^ b for m in masks for b in (0, 1 << bit)]

    across = cross(tokens)
    parts = [tokens, core(tokens), across, core(across)]
    own_qkv = jnp.concatenate([w_query, w_key, w_value], axis=1)[None]
    own_b_up = lax.dynamic_slice_in_dim(b_up, group * share, share, 0)[:, None]
    spare = -(hidden + own_cols) % LANES
    one = jnp.concatenate([w_up, w_out.T, jnp.broadcast_to(own_b_up, (share, spare))], axis=1)[None]
    two = w_down.T[None]
    biases = [b_query.reshape(1, -1), b_value.reshape(1, -1)]
    vectors = [b_out, b_down, gain_attn, shift_attn, gain_ffn, shift_ffn]
    vectors = jnp.stack([vec.astype(F32) for vec in vectors] + [jnp.zeros((width,), F32)] * 2)

    kept = []
    if placed:
        top = bits - 1
        masks = [0]
        w_part, masks = grow(own_qkv, masks, top, one, two, biases, vectors)
        one = after(one, w_part)
        for bit in range(top - 1, 0, -1):
            w_part, masks = grow(w_part, masks, bit)
        one, one_masks = grow(one, [0], top, w_part)
        two = after(two, across)
        two = jnp.stack([two, cross(two)], axis=1)
        w_qkv = [w_part, swap(w_part, "dp", 1)]
        w_masks = [masks, [m ^ 1 for m in masks]]
        positions = after(positions, two)
        q, k, v = project(parts, w_qkv, w_masks, *biases, positions, seq_lengths, heads, placed)

        for bit in range(top - 1, 0, -1):
            one, one_masks = grow(one, one_masks, bit, q)
        even = (one, one_masks)
        odd = (swap(one, "dp", 1), [m ^ 1 for m in one_masks])
        even_far = (cross(one), one_masks)
        q = after(q, one)
        q_kept, out, packed = attention_forward(0, q, k, v, [])
        kept.append((q_kept, out))
        two, two_masks = grow(two, [0], top, q_kept)
        twos = [(two, two_masks)]
        packed = list(after(packed, two))
        for h in range(1, heads):
            q_kept, out, packed = attention_forward(h, q, k, v, packed)
            kept.append((q_kept, out))
            if h == 1:
                for bit in range(top - 1, 0, -1):
                    twos += [(swap(w, "dp", 1 << bit), [m ^ (1 << bit) for m in ms]) for w, ms in twos]
                odd = (after(odd[0], q_kept), odd[1])
                odd_far = (cross(odd[0]), odd[1])
                first = len(twos)
                twos.append((swap(after(two, q_kept), "dp", 1), [m ^ 1 for m in two_masks]))
                packed = list(after(packed, odd[0]))
        later = [(after(w, q_kept), ms) for w, ms in twos[1:first]]
        twos = [twos[0]] + later + twos[first:] + [(swap(w, "dp", 1), [m ^ 1 for m in ms]) for w, ms in later]
        ones = [even, odd, even_far, odd_far]
    else:
        w_qkv = [gather_bits(own_qkv[0], "dp", range(bits), 0).reshape(1, width, -1)]
        w_masks = [[0]]
        one = gather_bits(one[0], "dp", range(bits), 0).reshape(1, width, -1)
        two = gather_bits(two[0], "dp", range(bits), 0).reshape(1, width, -1)
        q, k, v = project(parts, w_qkv, w_masks, *biases, positions, seq_lengths, heads, placed)
        packed = []
        for h in range(heads):
            q_kept, out, packed = attention_forward(h, q, k, v, packed)
            kept.append((q_kept, out))
        ones = [(one, [0]), (cross(one), [0])]
        twos = [(jnp.stack([two, cross(two)], axis=1), [0])]
    att_far = cross(packed[2])
    att = [packed[0], core(jnp.stack([packed[1], att_far[1]])), att_far]
    weights, plan = [], []
    for near in range(2):
        for a, (array, masks) in enumerate(ones):
            weights.append(core(after(array, q_kept)) if near else array)
            far = a // (len(ones) // 2)
            plan.append([((z,), False, near + 2 * far, mask) for z, mask in enumerate(masks)])
        for array, masks in twos:
            weights.append(core(after(array, q_kept)) if near else array)
            plan.append(
                [
                    ((z, far), True, near + 2 * far, mask)
                    for z, mask in enumerate(masks)
                    for far in range(2)
                ]
            )
    layer_out, d_one, sums, g_b_up, sent, own_sum, *back = middle(
        blocks, weights, plan, att, tokens, out_grad, positions, seq_lengths, vectors, hidden
    )
    grads = [back[0]] + [swap(back[j], "tensor", j) for j in (1, 2, 3)]

    def add(*terms):
        total = terms[0].astype(F32)
        for term in terms[1:]:
            total = total + term.astype(F32)
        return total

    def axes_of(array, lead):
        return array.reshape(array.shape[:lead] + (2,) * bits + array.shape[lead + 1 :])

    class Sum:
        def __init__(self, terms, names):
            self.terms, self.names = terms, list(names)

        def split(self, name):
            at = self.names.index(name)
            pick = functools.partial(lax.index_in_dim, axis=at, keepdims=False)
            away = add(*[pick(t, 1) for t in self.terms]).astype(BF16)
            self.terms = [pick(t, 0) for t in self.terms]
            self.names.remove(name)
            return away

        def join(self, got):
            self.terms.append(got)

    def send(away, name):
        return cross(away) if name == "x" else swap(away, "dp", 1 << name)

    names = list(range(bits))[::-1]
    late = list(range(1, bits))
    got_sum = core(sent)
    if placed:
        terms = [axes_of(own_sum, 1), axes_of(got_sum, 1)]
        down = Sum([t[..., :hidden] for t in terms], ["x"] + names)
        up = Sum([t[..., hidden:] for t in terms], ["x"] + names)
        pair = down.split("x"), up.split(0)
        grads, pair = after((grads, pair), d_one)

    small = jnp.concatenate([sums[:9], jnp.zeros((1, width), F32)])
    ups = g_b_up[:, 0]
    got_small = core(jnp.concatenate([small, ups[1:2], ups[3:4]]))

    g_bias, before = [], []
    for h in range(heads):
        q_kept = kept[h][0]
        if placed and h == heads - 1:
            down.join(after(send(pair[0], "x"), *before[:1]))
            up.join(after(send(pair[1], 0), *before[:1]))
            pair = down.split(0), up.split("x")
            q_kept, pair = after((q_kept, pair), *before[:1])
        g_all, b_head, g_w = attention_backward(
            h, q_kept, k, v, kept[h][1], grads, parts, blocks, before
        )
        before = [g_all, g_w]
        g_bias.append(b_head)
        if h == 0:
            got = after(got_small, g_all)
            small, ups = small + got[:10], ups[0::2] + got[10:]
            got_small = cross(jnp.concatenate([small, ups[1:2]]))
    got_small = after(got_small, g_all)
    if placed:
        down.join(after(send(pair[0], 0), g_all))
        up.join(after(send(pair[1], "x"), g_all))

        def both(name):
            return jnp.concatenate([down.split(name), up.split(name)], axis=-1)

        def join_both(got):
            down.join(got[..., :hidden])
            up.join(got[..., hidden:])

        move = both(late[0])
        g_w, got_small, g_bias, g_all = after((g_w, got_small, g_bias, g_all), move)
        qkv = Sum([axes_of(g_w, 1)], ["h"] + names)
        qkv_move = qkv.split(0)
        g_all, qkv_move = after((g_all, qkv_move), move)
    small = jnp.concatenate([small + got_small[:10], ups[:1] + got_small[10:]])
    spare = width - heads * 3 * HEAD_DIM
    bias_row = jnp.pad(jnp.concatenate(g_bias, axis=1), ((0, 0), (0, spare)))
    small = jnp.concatenate([small, bias_row])
    g_all, small = after((g_all, small), d_one)
    first = input_part(g_all, w_qkv, w_masks, (3, 2), placed)
    crossed = add(first[1], core(first[0])).astype(BF16)
    g_all, crossed = after((g_all, crossed), *first)
    second = input_part(g_all, w_qkv, w_masks, (1, 0), placed)
    crossed = cross(crossed)
    if placed:
        qkv.join(after(send(qkv_move, 0), *second))
        qkv_move = qkv.split(late[0])
        join_both(after(send(move, late[0]), qkv_move))
        for at, name in enumerate(late[1:]):
            move = both(name)
            qkv.join(after(send(qkv_move, late[at]), move))
            qkv_move = qkv.split(name)
            join_both(after(send(move, name), qkv_move))
        qkv.join(send(qkv_move, late[-1]))
    small = small + after(swap(small, "dp", 1), *second)
    for bit in range(1, bits):
        small = small + swap(small, "dp", 1 << bit)
    near = core(second[0])
    input_grad = add(d_one, second[1], near, crossed).astype(BF16)
    if placed:
        g_down = add(*down.terms)
        g_up = add(*up.terms)
        g_qkv = add(*qkv.terms).reshape(heads, share, 3, HEAD_DIM)
    else:
        two_s = (2,) * bits
        total = add(own_sum, got_sum)
        total = total[0] + cross(total[1].astype(BF16)).astype(F32)
        total = scatter_bits(total.reshape(two_s + (share, -1)), "dp", range(bits), 0)
        g_down, g_up = total[:, :hidden], total[:, hidden:]
        g_qkv = g_w.reshape((heads,) + two_s + (share, -1))
        g_qkv = scatter_bits(g_qkv, "dp", range(bits), 1).reshape(heads, share, 3, HEAD_DIM)
    g_q, g_k, g_v = (g_qkv[:, :, i].transpose(1, 0, 2).reshape(share, own_cols) for i in range(3))
    bias_rows = small[11, : heads * 3 * HEAD_DIM].reshape(heads, 3, HEAD_DIM)
    count = jnp.sum(seq_lengths).astype(F32) * width
    rms = jnp.sqrt(jnp.sum(small[6:9], axis=-1) / count)
    return (
        layer_out,
        input_grad,
        g_q,
        g_k,
        g_v,
        g_up[:, hidden:].T,
        g_up[:, :hidden],
        g_down.T,
        bias_rows[:, 0].reshape(own_cols),
        bias_rows[:, 2].reshape(own_cols),
        small[0],
        small[10],
        small[1],
        small[2],
        small[3],
        small[4],
        small[5],
        rms,
    )


def solution(mesh):
    in_specs = (
        P(("dp", "tensor"), None),
        P(),
        P("dp", None),
        P("dp", "tensor"),
        P("dp", "tensor"),
        P("dp", "tensor"),
        P("tensor", "dp"),
        P("dp", "tensor"),
        P("tensor", "dp"),
        P("tensor"),
        P("tensor"),
        P(),
        P("tensor"),
        P(),
        P(),
        P(),
        P(),
        P(),
        P(("dp", "tensor"), None),
    )
    out_specs = (
        P(("dp", "tensor"), None),
        P(("dp", "tensor"), None),
        P("dp", "tensor"),
        P("dp", "tensor"),
        P("dp", "tensor"),
        P("tensor", "dp"),
        P("dp", "tensor"),
        P("tensor", "dp"),
        P("tensor"),
        P("tensor"),
        P(),
        P("tensor"),
        P(),
        P(),
        P(),
        P(),
        P(),
        P(),
    )
    return jax.shard_map(body, mesh=mesh, in_specs=in_specs, out_specs=out_specs, check_vma=False)
```

time: 504 us -> 327 us (0.65)
  waiting for transfers between devices: 191 us -> 65.6 us
  local copies, waits for them, and re-layouts: 103 us -> 37.6 us
  Pallas kernels: 123 us -> 131 us
  other arithmetic: 36.3 us -> 41.4 us
    ppermute x40 -> x47, waiting for transfers between devices: 191 us -> 65.6 us  [swap(): return lax.ppermute(value, axis, [(i, i ^ bits) for i in range(size)])]
    unnamed x88 -> x90, local copies, waits for them, and re-layouts: 38.1 us -> 11.9 us
    slice x10 -> x8, local copies, waits for them, and re-layouts: 24.3 us -> 5.49 us  [the longest x2 3.12 us: split(): away = add(*[pick(t, 1) for t in self.terms]).astype(BF16)]
    convert_element_type x3 -> x10, other arithmetic: 4.67 us -> 20.2 us  [the longest x8 15.8 us: split(): away = add(*[pick(t, 1) for t in self.terms]).astype(BF16)]
    ppermute x2 -> x0, local copies, waits for them, and re-layouts: 11.2 us -> none  [swap(): return lax.ppermute(value, axis, [(i, i ^ bits) for i in range(size)])]
    another operation x17 -> x7, other arithmetic: 14.2 us -> 4.74 us  [the longest x6 3.78 us: grow(): both = jnp.stack([value, got], axis=1).reshape((-1,) + value.shape[1:])]
    squeeze x0 -> x7, local copies, waits for them, and re-layouts: none -> 9.3 us  [split(): self.terms = [pick(t, 0) for t in self.terms]]
    convert_element_type x7 -> x0, local copies, waits for them, and re-layouts: 8.8 us -> none  [the longest x2 6.41 us: body(): pack = packs[0] + swap(packs[1].astype(BF16), 'tensor', 2).astype(F32)]
  transfers between devices with their start and end apart: 40 -> 47, of which waited for: 17 -> 14; matrix products, arithmetic and copies ran while one was open for 20% -> 20% of each run, Pallas kernels for 17% -> 27%
where the time goes in v2:
time: 327 us; the launch traced here: 322 us
  Pallas kernels  131 us (40%)
  waiting for transfers between devices  65.6 us (20%)
  starting transfers between devices  44.4 us (14%)
  other arithmetic  41.4 us (13%)
  local copies, waits for them, and re-layouts  37.6 us (11%)
    ppermute x47, waiting for transfers between devices, swap(): return lax.ppermute(value, axis, [(i, i ^ bits) for i in range(size)])  65.6 us
    pallas_call x3, Pallas kernels, attention_backward(): pl.pallas_call(functools.partial(backward_kernel, placed=blocks > 1), gri...  50.7 us
    ppermute x47, starting transfers between devices, swap(): return lax.ppermute(value, axis, [(i, i ^ bits) for i in range(size)])  44.4 us
    pallas_call x1, Pallas kernels, middle(): pl.pallas_call(functools.partial(middle_kernel, plan=plan, blocks=blocks)...  37.5 us
    pallas_call x3, Pallas kernels, attention_forward(): pl.pallas_call(functools.partial(forward_kernel, unroll=4), grid=(1,), in...  25.6 us
    convert_element_type x8, other arithmetic, split(): away = add(*[pick(t, 1) for t in self.terms]).astype(BF16)  15.8 us
    unnamed x90, local copies, waits for them, and re-layouts  11.9 us
    pallas_call x2, Pallas kernels, input_part(): pl.pallas_call(functools.partial(input_kernel, masks=masks, which=which,...  10.1 us
  transfers between devices with their start and end apart: 47, of which 14 were waited for; matrix products, arithmetic and copies ran while one was open for 20% of the time, Pallas kernels for 27%

profile of v2, /device:TPU:0, one launch (start us, length us, event | category | flops | bytes accessed | tf_op | source)
XLA Modules:
  0.0 321.9 jit_solution(7800847727976486702)
XLA Ops:
  0.7 3.0 collective-permute-start.5
  4.6 2.7 collective-permute-start
  8.2 1.2 reshape.207.refs_6_
  9.4 1.2 reshape.208.refs_7_
  17.3 1.6 collective-permute-start.2
  18.9 2.5 collective-permute-done.5.refs_2_.refs_6_
  21.4 2.8 collective-permute-start.1
  24.6 1.6 collective-permute-start.7
  26.2 7.9 %collective-permute-done.1 = bf16[1,96,1024]{2,1,0:T(8,128)(2,1)S(1)} collective-permute-done((bf16[1,96,1024]{2,1,0:T(8,128)(2,1)S(1)}, bf16[1,96,1024]{2,1,0:T(8,128)(2,1)S(1)}, u32[]{:S(2)}, u32[]{:S(2)}) %collective-permute-start.1) | collective-permute-done | bytes 196640 | tf_op jit(solution)/shard_map/ppermute | solution.py:54
  35.6 1.5 collective-permute-start.8
  37.1 4.0 %collective-permute-done.8 = bf16[1,96,768]{2,1,0:T(8,128)(2,1)S(1)} collective-permute-done((bf16[1,96,768]{2,1,0:T(8,128)(2,1)S(1)}, bf16[1,96,768]{2,1,0:T(8,128)(2,1)S(1)}, u32[]{:S(2)}, u32[]{:S(2)}) %collective-permute-start.8) | collective-permute-done | bytes 147488 | tf_op jit(solution)/shard_map/ppermute | solution.py:54
  43.0 6.8 %project.1 = (bf16[3,2048,128]{2,1,0:T(8,128)(2,1)}, bf16[3,2048,128]{2,1,0:T(8,128)(2,1)}, bf16[3,2048,128]{2,1,0:T(8,128)(2,1)}) custom-call(bf16[512,768]{1,0:T(8,128)(2,1)} %refs_4_.5, bf16[512,768]{1,0:T(8,128)(2,1)} %copy-done.2, bf16[512,768]{1,0:T(8,128)(2,1)} %copy-done.1, bf16[512,768]{1,0:T(8,128)(2,1)} %collective-permute-done.6.refs_3_.refs_7_, ...), custom_call_target="tpu_custom_call" | custom-call | flops 1000 | bytes 1000 | tf_op jit(solution)/shard_map/project/pallas_call | solution.py:143
  51.0 1.6 collective-permute-start.9
  52.5 3.4 %collective-permute-start.10 = (bf16[1,2,96,768]{3,2,1,0:T(8,128)(2,1)}, bf16[1,2,96,768]{3,2,1,0:T(8,128)(2,1)}, u32[]{:S(2)}, u32[]{:S(2)}) collective-permute-start(bf16[1,2,96,768]{3,2,1,0:T(8,128)(2,1)} %get-tuple-element.271), channel_id=1, source_target_pairs={{0,16},{4,20},{8,24},{12,28},{16,0},{20,4},{24,8},{28,12},{1,17},{... | collective-permute-start | bytes 884744 | tf_op jit(solution)/shard_map/ppermute | solution.py:54
  55.9 1.5 collective-permute-start.11
  57.4 8.8 %attention_forward.3 = (bf16[2048,128]{1,0:T(8,128)(2,1)}, f32[2048,128]{1,0:T(8,128)}, bf16[3,256,128]{2,1,0:T(8,128)(2,1)}, bf16[3,256,128]{2,1,0:T(8,128)(2,1)}, bf16[2,3,256,128]{3,2,1,0:T(8,128)(2,1)}) custom-call(bf16[3,2048,128]{2,1,0:T(8,128)(2,1)} %get-tuple-element.123.q_ref, bf16[3,2048,128]{2,1,0:T(8,128)(2,1)} %get-tuple-element.124.k_ref, ...), custom_call_target="tpu_custom_call" | custom-call | flops 1000 | bytes 1000 | tf_op jit(solution)/shard_map/attention_forward/pallas_call | solution.py:213
  66.2 2.2 collective-permute-done.10
  68.5 1.9 maximum_bitcast_fusion.refs_4_
  70.4 8.4 %attention_forward.4 = (bf16[2048,128]{1,0:T(8,128)(2,1)}, f32[2048,128]{1,0:T(8,128)}, bf16[3,256,128]{2,1,0:T(8,128)(2,1)}, bf16[3,256,128]{2,1,0:T(8,128)(2,1)}, bf16[2,3,256,128]{3,2,1,0:T(8,128)(2,1)}) custom-call(bf16[3,2048,128]{2,1,0:T(8,128)(2,1)} %get-tuple-element.123.q_ref, ...), custom_call_target="tpu_custom_call", output_to_operand_aliasing={{2}: (3, {}), {3}: (4, {}), {4}: (5, {})} | custom-call | flops 1000 | bytes 1000 | tf_op jit(solution)/shard_map/attention_forward/pallas_call | solution.py:213
  79.3 1.5 collective-permute-start.12
  80.8 8.4 %attention_forward.5 = (bf16[2048,128]{1,0:T(8,128)(2,1)}, f32[2048,128]{1,0:T(8,128)}, bf16[3,256,128]{2,1,0:T(8,128)(2,1)}, bf16[3,256,128]{2,1,0:T(8,128)(2,1)}, bf16[2,3,256,128]{3,2,1,0:T(8,128)(2,1)}) custom-call(bf16[3,2048,128]{2,1,0:T(8,128)(2,1)} %get-tuple-element.123.q_ref, ...), custom_call_target="tpu_custom_call", output_to_operand_aliasing={{2}: (3, {}), {3}: (4, {}), {4}: (5, {})} | custom-call | flops 1000 | bytes 1000 | tf_op jit(solution)/shard_map/attention_forward/pallas_call | solution.py:213
  89.7 1.5 collective-permute-start.15
  91.2 4.1 %collective-permute-done.14.refs_6_ = bf16[2,2,96,768]{3,2,1,0:T(8,128)(2,1)} collective-permute-done((bf16[2,2,96,768]{3,2,1,0:T(8,128)(2,1)}, bf16[2,2,96,768]{3,2,1,0:T(8,128)(2,1)}, u32[]{:S(2)}, u32[]{:S(2)}) %collective-permute-start.14) | collective-permute-done | bytes 589856 | tf_op jit(solution)/shard_map/ppermute | solution.py:54
  95.8 11.2 %collective-permute-done.24.refs_18_ = bf16[2,3,256,128]{3,2,1,0:T(8,128)(2,1)S(1)} collective-permute-done((bf16[2,3,256,128]{3,2,1,0:T(8,128)(2,1)}, bf16[2,3,256,128]{3,2,1,0:T(8,128)(2,1)S(1)}, u32[]{:S(2)}, u32[]{:S(2)}) %collective-permute-start.24) | collective-permute-done | bytes 393248 | tf_op jit(solution)/shard_map/ppermute | solution.py:54
  108.1 2.7 collective-permute-done.22.refs_14_
  114.2 1.5 collective-permute-done.25.refs_17_
  116.7 37.5 %middle.1 = (bf16[512,768]{1,0:T(8,128)(2,1)}, f32[512,768]{1,0:T(8,128)}, f32[16,768]{1,0:T(8,128)}, f32[4,1,768]{2,1,0:T(1,128)}, bf16[2,8,96,1728]{3,2,1,0:T(...) custom-call(bf16[4,96,1024]{2,1,0:T(8,128)(2,1)} %bitcast.170, ...), custom_call_target="tpu_custom_call" | custom-call | flops 1000 | bytes 1000 | tf_op jit(solution)/shard_map/middle/pallas_call | solution.py:547
  155.2 1.5 pad_maximum_fusion.9
  157.2 1.5 collective-permute-start.28
  158.8 1.8 fusion.20
  160.7 2.7 collective-permute-done.26
  163.4 1.3 fusion.21
  164.8 4.1 %fusion = bf16[2,2,2,96,960]{4,3,2,1,0:T(8,128)(2,1)} fusion(bf16[2,2,2,2,96,1728]{5,4,3,2,1,0:T(8,128)(2,1)S(1)} %bitcast.160, bf16[2,2,2,2,96,1728]{5,4,3,2,1,0:T(8,128)(2,1)} %bitcast.156), kind=kLoop, calls=%fused_computation.2 | loop fusion | flops 2949120 | bytes 4423680 | tf_op jit(solution)/shard_map/convert_element_type | solution.py:735
  168.8 1.4 fusion.2
  170.3 1.6 collective-permute-start.30
  171.9 1.5 collective-permute-start.31
  176.1 17.0 %attention_backward.3 = (bf16[3,2048,192]{2,1,0:T(8,128)(2,1)}, f32[1,192]{1,0:T(1,128)}, bf16[3,8,96,192]{3,2,1,0:T(8,128)(2,1)}) custom-call(bf16[2048,128]{1,0:T(8,128)(2,1)} %get-tuple-element.129.q_ref, bf16[3,2048,128]{2,1,0:T(8,128)(2,1)} %get-tuple-element.124.k_ref, bf16[3,2048,128]{2,1,0:T(8,128)(2,1)} %get-tuple-element.125.v_ref, ...), custom_call_target="tpu_custom_call" | custom-call | flops 1000 | bytes 1000 | tf_op jit(solution)/shard_map/attention_backward/pallas_call | solution.py:293
  193.0 16.8 %attention_backward.4 = (bf16[3,2048,192]{2,1,0:T(8,128)(2,1)}, f32[1,192]{1,0:T(1,128)}, bf16[3,8,96,192]{3,2,1,0:T(8,128)(2,1)}) custom-call(bf16[2048,128]{1,0:T(8,128)(2,1)} %get-tuple-element.134.q_ref, bf16[3,2048,128]{2,1,0:T(8,128)(2,1)} %get-tuple-element.124.k_ref, ...), custom_call_target="tpu_custom_call", output_to_operand_aliasing={{0}: (12, {}), {2}: (13, {})} | custom-call | flops 1000 | bytes 1000 | tf_op jit(solution)/shard_map/attention_backward/pallas_call | solution.py:293
  209.8 1.4 copy.106
  212.9 2.1 slice_bitcast_fusion.2
  215.0 2.1 fusion.3
  217.1 2.9 fusion.1
  221.2 1.5 collective-permute-start.35
  222.7 2.2 slice_bitcast_fusion.7
  224.8 17.0 %attention_backward.5 = (bf16[3,2048,192]{2,1,0:T(8,128)(2,1)}, f32[1,192]{1,0:T(1,128)}, bf16[3,8,96,192]{3,2,1,0:T(8,128)(2,1)}) custom-call(bf16[2048,128]{1,0:T(8,128)(2,1)} %get-tuple-element.177.q_ref, bf16[3,2048,128]{2,1,0:T(8,128)(2,1)} %get-tuple-element.124.k_ref, ...), custom_call_target="tpu_custom_call", output_to_operand_aliasing={{0}: (12, {}), {2}: (13, {})} | custom-call | flops 1000 | bytes 1000 | tf_op jit(solution)/shard_map/attention_backward/pallas_call | solution.py:293
  241.9 1.3 slice_bitcast_fusion.6
  243.2 1.6 fusion.7
  244.8 1.3 fusion.4
  249.2 5.0 %input_part.2 = (bf16[512,768]{1,0:T(8,128)(2,1)}, bf16[512,768]{1,0:T(8,128)(2,1)}) custom-call(bf16[3,2048,192]{2,1,0:T(8,128)(2,1)} %get-tuple-element.203.g_ref, bf16[4,96,576]{2,1,0:T(8,128)(2,1)} %bitcast.153, bf16[4,96,576]{2,1,0:T(8,128)(2,1)} %copy-done.8), custom_call_target="tpu_custom_call" | custom-call | flops 1000 | bytes 1000 | tf_op jit(solution)/shard_map/input_part/pallas_call | solution.py:344
  255.5 1.8 collective-permute-start.41
  257.3 1.5 collective-permute-start.39
  258.8 1.4 copy.100
  262.8 5.0 %input_part.3 = (bf16[512,768]{1,0:T(8,128)(2,1)}, bf16[512,768]{1,0:T(8,128)(2,1)}) custom-call(bf16[3,2048,192]{2,1,0:T(8,128)(2,1)} %get-tuple-element.203.g_ref, bf16[4,96,576]{2,1,0:T(8,128)(2,1)} %bitcast.154, bf16[4,96,576]{2,1,0:T(8,128)(2,1)} %copy-done.8), custom_call_target="tpu_custom_call" | custom-call | flops 1000 | bytes 1000 | tf_op jit(solution)/shard_map/input_part/pallas_call | solution.py:344
  268.0 5.7 %collective-permute-done.39 = bf16[3,2,2,96,192]{3,4,0,1,2:T(8,128)(2,1)} collective-permute-done((bf16[3,2,2,96,192]{3,4,0,1,2:T(8,128)(2,1)}, bf16[3,2,2,96,192]{3,4,0,1,2:T(8,128)(2,1)}, u32[]{:S(2)}, u32[]{:S(2)}) %collective-permute-start.39) | collective-permute-done | bytes 442400 | tf_op jit(solution)/shard_map/ppermute | solution.py:54
  273.6 1.8 fusion.8
  275.8 1.4 fusion.6
  278.4 1.7 collective-permute-start.45
  281.7 2.8 collective-permute-done.45
  286.4 1.9 collective-permute-start.43
  288.3 11.2 %collective-permute-done.46 = f32[12,768]{1,0:T(8,128)S(1)} collective-permute-done((f32[12,768]{1,0:T(8,128)S(1)}, f32[12,768]{1,0:T(8,128)S(1)}, u32[]{:S(2)}, u32[]{:S(2)}) %collective-permute-start.46) | collective-permute-done | bytes 36896 | tf_op jit(solution)/shard_map/ppermute | solution.py:54
  303.3 6.8 %collective-permute-done.42 = bf16[3,96,192]{1,2,0:T(8,128)(2,1)S(1)} collective-permute-done((bf16[3,96,192]{1,2,0:T(8,128)(2,1)S(1)}, bf16[3,96,192]{1,2,0:T(8,128)(2,1)S(1)}, u32[]{:S(2)}, u32[]{:S(2)}) %collective-permute-start.42) | collective-permute-done | bytes 110624 | tf_op jit(solution)/shard_map/ppermute | solution.py:54
  313.3 1.5 fusion.5
  316.3 1.9 fusion.10
  318.2 3.3 %add_convert_fusion.2 = bf16[512,768]{1,0:T(8,128)(2,1)} fusion(bf16[512,768]{1,0:T(8,128)(2,1)} %collective-permute-done.38, bf16[512,768]{1,0:T(8,128)(2,1)} %collective-permute-done.37, f32[512,768]{1,0:T(8,128)} %get-tuple-element.157, bf16[512,768]{1,0:T(8,128)(2,1)} %get-tuple-element.204), kind=kLoop, calls=%fused_computation.7 | loop fusion | flops 2752512 | bytes 4718592 | tf_op jit(solution)/shard_map/convert_element_type | solution.py:818
  (208 shorter events, 47.3 us)
Async XLA Ops:
  0.7 18.2 %copy-start = (bf16[512,768]{1,0:T(8,128)(2,1)S(1)}, bf16[512,768]{1,0:T(8,128)(2,1)}, u32[]{:S(2)}) copy-start(bf16[512,768]{1,0:T(8,128)(2,1)} %refs_4_.5) | copy-start | bytes 2359300
  0.7 20.8 %collective-permute-start.5 = (bf16[512,768]{1,0:T(8,128)(2,1)}, bf16[512,768]{1,0:T(8,128)(2,1)S(1)}, u32[]{:S(2)}, u32[]{:S(2)}) collective-permute-start(bf16[512,768]{1,0:T(8,128)(2,1)} %refs_4_.5), channel_id=1, source_target_pairs={{0,2},{1,3},{2,0},{3,1},{4,6},{5,7},{6,4},{7,5},{8,10},{9,11},{10,... | collective-permute-start | bytes 2359304 | tf_op jit(solution)/shard_map/ppermute | solution.py:54
  4.6 12.6 %collective-permute-start = (bf16[1,96,576]{2,1,0:T(8,128)(2,1)S(1)}, bf16[1,96,576]{2,1,0:T(8,128)(2,1)S(1)}, u32[]{:S(2)}, u32[]{:S(2)}) collective-permute-start(bf16[1,96,576]{2,1,0:T(8,128)(2,1)S(1)} %get-tuple-element.275), channel_id=1, source_target_pairs={{0,16},{4,20},{8,24},{12,28},{16,0},{20,4},{24,8},{28,12},{1,17},{... | collective-permute-start | bytes 331784 | tf_op jit(solution)/shard_map/ppermute | solution.py:54
  17.3 7.2 %collective-permute-start.2 = (bf16[2,96,576]{2,1,0:T(8,128)(2,1)S(1)}, bf16[2,96,576]{2,1,0:T(8,128)(2,1)S(1)}, u32[]{:S(2)}, u32[]{:S(2)}) collective-permute-start(bf16[2,96,576]{2,1,0:T(8,128)(2,1)S(1)} %get-tuple-element.273), channel_id=1, source_target_pairs={{0,8},{4,12},{8,0},{12,4},{16,24},{20,28},{24,16},{28,20},{1,9},{5... | collective-permute-start | bytes 663560 | tf_op jit(solution)/shard_map/ppermute | solution.py:54
  18.9 23.1 %collective-permute-start.4 = (bf16[512,768]{1,0:T(8,128)(2,1)S(1)}, bf16[512,768]{1,0:T(8,128)(2,1)S(1)}, u32[]{:S(2)}, u32[]{:S(2)}) collective-permute-start(bf16[512,768]{1,0:T(8,128)(2,1)S(1)} %copy-done), channel_id=1, source_target_pairs={{0,1},{1,0},{2,3},{3,2},{4,5},{5,4},{6,7},{7,6},{8,9},{9,8},{10,11... | collective-permute-start | bytes 2359304 | tf_op jit(solution)/shard_map/ppermute | solution.py:54
  21.4 13.4 %copy-start.1 = (bf16[512,768]{1,0:T(8,128)(2,1)}, bf16[512,768]{1,0:T(8,128)(2,1)S(1)}, u32[]{:S(2)}) copy-start(bf16[512,768]{1,0:T(8,128)(2,1)S(1)} %collective-permute-done.5.refs_2_.refs_6_) | copy-start | bytes 2359300
  21.4 21.5 %collective-permute-start.6 = (bf16[512,768]{1,0:T(8,128)(2,1)S(1)}, bf16[512,768]{1,0:T(8,128)(2,1)}, u32[]{:S(2)}, u32[]{:S(2)}) collective-permute-start(bf16[512,768]{1,0:T(8,128)(2,1)S(1)} %collective-permute-done.5.refs_2_.refs_6_), channel_id=1, source_target_pairs={{0,1},{1,0},{2,3},{3,2},{4,5},{5,4},{6,7},{7,6},{8,9},{9,8},{10,11... | collective-permute-start | bytes 2359304 | tf_op jit(solution)/shard_map/ppermute | solution.py:54
  21.4 12.6 %collective-permute-start.1 = (bf16[1,96,1024]{2,1,0:T(8,128)(2,1)S(1)}, bf16[1,96,1024]{2,1,0:T(8,128)(2,1)S(1)}, u32[]{:S(2)}, u32[]{:S(2)}) collective-permute-start(bf16[1,96,1024]{2,1,0:T(8,128)(2,1)S(1)} %maximum_bitcast_fusion.1), channel_id=1, source_target_pairs={{0,16},{4,20},{8,24},{12,28},{16,0},{20,4},{24,8},{28,12},{1,17},{... | collective-permute-start | bytes 589832 | tf_op jit(solution)/shard_map/ppermute | solution.py:54
  24.5 11.2 %copy-start.32 = (bf16[768,96]{0,1:T(8,128)(2,1)S(1)}, bf16[768,96]{0,1:T(8,128)(2,1)}, u32[]{:S(2)}) copy-start(bf16[768,96]{0,1:T(8,128)(2,1)} %param.27) | copy-start | bytes 442372
  24.6 17.4 %copy-start.4 = (bf16[2,2,96,576]{3,2,1,0:T(8,128)(2,1)}, bf16[2,2,96,576]{3,2,1,0:T(8,128)(2,1)S(1)}, u32[]{:S(2)}) copy-start(bf16[2,2,96,576]{3,2,1,0:T(8,128)(2,1)S(1)} %copy.70) | copy-start | bytes 1327108
  24.6 17.4 %collective-permute-start.7 = (bf16[4,96,576]{2,1,0:T(8,128)(2,1)S(1)}, bf16[4,96,576]{2,1,0:T(8,128)(2,1)S(1)}, u32[]{:S(2)}, u32[]{:S(2)}) collective-permute-start(bf16[4,96,576]{2,1,0:T(8,128)(2,1)S(1)} %bitcast.151), channel_id=1, source_target_pairs={{0,4},{4,0},{8,12},{12,8},{16,20},{20,16},{24,28},{28,24},{1,5},{5... | collective-permute-start | bytes 1327112 | tf_op jit(solution)/shard_map/ppermute | solution.py:54
  34.9 15.0 %collective-permute-start.3 = (bf16[2,96,1024]{2,1,0:T(8,128)(2,1)}, bf16[2,96,1024]{2,1,0:T(8,128)(2,1)}, u32[]{:S(2)}, u32[]{:S(2)}) collective-permute-start(bf16[2,96,1024]{2,1,0:T(8,128)(2,1)} %get-tuple-element.266), channel_id=1, source_target_pairs={{0,8},{4,12},{8,0},{12,4},{16,24},{20,28},{24,16},{28,20},{1,9},{5... | collective-permute-start | bytes 1179656 | tf_op jit(solution)/shard_map/ppermute | solution.py:54
  35.6 5.5 %collective-permute-start.8 = (bf16[1,96,768]{2,1,0:T(8,128)(2,1)S(1)}, bf16[1,96,768]{2,1,0:T(8,128)(2,1)S(1)}, u32[]{:S(2)}, u32[]{:S(2)}) collective-permute-start(bf16[1,96,768]{2,1,0:T(8,128)(2,1)S(1)} %bitcast.184), channel_id=1, source_target_pairs={{0,2},{1,3},{2,0},{3,1},{4,6},{5,7},{6,4},{7,5},{8,10},{9,11},{10,... | collective-permute-start | bytes 442376 | tf_op jit(solution)/shard_map/ppermute | solution.py:54
  50.9 56.1 %copy-start.11 = (bf16[2,2,96,1024]{3,2,1,0:T(8,128)(2,1)}, bf16[2,2,96,1024]{3,2,1,0:T(8,128)(2,1)S(1)}, u32[]{:S(2)}) copy-start(bf16[2,2,96,1024]{3,2,1,0:T(8,128)(2,1)S(1)} %copy.71) | copy-start | bytes 2359300
  51.0 28.3 %collective-permute-start.9 = (bf16[4,96,1024]{2,1,0:T(8,128)(2,1)S(1)}, bf16[4,96,1024]{2,1,0:T(8,128)(2,1)}, u32[]{:S(2)}, u32[]{:S(2)}) collective-permute-start(bf16[4,96,1024]{2,1,0:T(8,128)(2,1)S(1)} %bitcast.167), channel_id=1, source_target_pairs={{0,4},{4,0},{8,12},{12,8},{16,20},{20,16},{24,28},{28,24},{1,5},{5... | collective-permute-start | bytes 2359304 | tf_op jit(solution)/shard_map/ppermute | solution.py:54
  52.5 15.9 %collective-permute-start.10 = (bf16[1,2,96,768]{3,2,1,0:T(8,128)(2,1)}, bf16[1,2,96,768]{3,2,1,0:T(8,128)(2,1)}, u32[]{:S(2)}, u32[]{:S(2)}) collective-permute-start(bf16[1,2,96,768]{3,2,1,0:T(8,128)(2,1)} %get-tuple-element.271), channel_id=1, source_target_pairs={{0,16},{4,20},{8,24},{12,28},{16,0},{20,4},{24,8},{28,12},{1,17},{... | collective-permute-start | bytes 884744 | tf_op jit(solution)/shard_map/ppermute | solution.py:54
  55.9 39.4 %collective-permute-start.11 = (bf16[4,96,1024]{2,1,0:T(8,128)(2,1)S(1)}, bf16[4,96,1024]{2,1,0:T(8,128)(2,1)}, u32[]{:S(2)}, u32[]{:S(2)}) collective-permute-start(bf16[4,96,1024]{2,1,0:T(8,128)(2,1)S(1)} %bitcast.168), channel_id=1, source_target_pairs={{0,2},{1,3},{2,0},{3,1},{4,6},{5,7},{6,4},{7,5},{8,10},{9,11},{10,... | collective-permute-start | bytes 2359304 | tf_op jit(solution)/shard_map/ppermute | solution.py:54
  70.4 19.3 %collective-permute-start.13 = (bf16[2,2,96,768]{3,2,1,0:T(8,128)(2,1)}, bf16[2,2,96,768]{3,2,1,0:T(8,128)(2,1)}, u32[]{:S(2)}, u32[]{:S(2)}) collective-permute-start(bf16[2,2,96,768]{3,2,1,0:T(8,128)(2,1)} %maximum_bitcast_fusion.refs_4_), channel_id=1, source_target_pairs={{0,8},{4,12},{8,0},{12,4},{16,24},{20,28},{24,16},{28,20},{1,9},{5... | collective-permute-start | bytes 1769480 | tf_op jit(solution)/shard_map/ppermute | solution.py:54
  78.8 16.5 %collective-permute-start.14 = (bf16[2,2,96,768]{3,2,1,0:T(8,128)(2,1)}, bf16[2,2,96,768]{3,2,1,0:T(8,128)(2,1)}, u32[]{:S(2)}, u32[]{:S(2)}) collective-permute-start(bf16[2,2,96,768]{3,2,1,0:T(8,128)(2,1)} %maximum_bitcast_fusion.refs_4_), channel_id=1, source_target_pairs={{0,4},{4,0},{8,12},{12,8},{16,20},{20,16},{24,28},{28,24},{1,5},{5... | collective-permute-start | bytes 1769480 | tf_op jit(solution)/shard_map/ppermute | solution.py:54
  79.3 27.7 %collective-permute-start.12 = (bf16[4,96,1024]{2,1,0:T(8,128)(2,1)}, bf16[4,96,1024]{2,1,0:T(8,128)(2,1)}, u32[]{:S(2)}, u32[]{:S(2)}) collective-permute-start(bf16[4,96,1024]{2,1,0:T(8,128)(2,1)} %collective-permute-done.9.refs_1_), channel_id=1, source_target_pairs={{0,2},{1,3},{2,0},{3,1},{4,6},{5,7},{6,4},{7,5},{8,10},{9,11},{10,... | collective-permute-start | bytes 2359304 | tf_op jit(solution)/shard_map/ppermute | solution.py:54
  89.2 17.8 %collective-permute-start.24 = (bf16[2,3,256,128]{3,2,1,0:T(8,128)(2,1)}, bf16[2,3,256,128]{3,2,1,0:T(8,128)(2,1)S(1)}, u32[]{:S(2)}, u32[]{:S(2)}) collective-permute-start(bf16[2,3,256,128]{3,2,1,0:T(8,128)(2,1)} %get-tuple-element.155), channel_id=1, source_target_pairs={{0,2},{1,3},{2,0},{3,1},{4,6},{5,7},{6,4},{7,5},{8,10},{9,11},{10,... | collective-permute-start | bytes 1179656 | tf_op jit(solution)/shard_map/ppermute | solution.py:54
  89.7 17.8 %collective-permute-start.15 = (bf16[2,2,96,768]{3,2,1,0:T(8,128)(2,1)}, bf16[2,2,96,768]{3,2,1,0:T(8,128)(2,1)S(1)}, u32[]{:S(2)}, u32[]{:S(2)}) collective-permute-start(bf16[2,2,96,768]{3,2,1,0:T(8,128)(2,1)} %collective-permute-done.13.refs_5_), channel_id=1, source_target_pairs={{0,4},{4,0},{8,12},{12,8},{16,20},{20,16},{24,28},{28,24},{1,5},{5... | collective-permute-start | bytes 1769480 | tf_op jit(solution)/shard_map/ppermute | solution.py:54
  95.3 12.3 %collective-permute-start.20 = (bf16[2,2,96,768]{3,2,1,0:T(8,128)(2,1)}, bf16[2,2,96,768]{3,2,1,0:T(8,128)(2,1)S(1)}, u32[]{:S(2)}, u32[]{:S(2)}) collective-permute-start(bf16[2,2,96,768]{3,2,1,0:T(8,128)(2,1)} %maximum_bitcast_fusion.refs_4_), channel_id=1, source_target_pairs={{0,1},{1,0},{2,3},{3,2},{4,5},{5,4},{6,7},{7,6},{8,9},{9,8},{10,11... | collective-permute-start | bytes 1769480 | tf_op jit(solution)/shard_map/ppermute | solution.py:54
  95.3 12.7 %collective-permute-start.21 = (bf16[2,2,96,768]{3,2,1,0:T(8,128)(2,1)}, bf16[2,2,96,768]{3,2,1,0:T(8,128)(2,1)S(1)}, u32[]{:S(2)}, u32[]{:S(2)}) collective-permute-start(bf16[2,2,96,768]{3,2,1,0:T(8,128)(2,1)} %collective-permute-done.13.refs_5_), channel_id=1, source_target_pairs={{0,1},{1,0},{2,3},{3,2},{4,5},{5,4},{6,7},{7,6},{8,9},{9,8},{10,11... | collective-permute-start | bytes 1769480 | tf_op jit(solution)/shard_map/ppermute | solution.py:54
  107.0 6.0 %collective-permute-start.16 = (bf16[4,96,1024]{2,1,0:T(8,128)(2,1)S(1)}, bf16[4,96,1024]{2,1,0:T(8,128)(2,1)S(1)}, u32[]{:S(2)}, u32[]{:S(2)}) collective-permute-start(bf16[4,96,1024]{2,1,0:T(8,128)(2,1)S(1)} %bitcast.169), channel_id=1, source_target_pairs={{0,1},{1,0},{2,3},{3,2},{4,5},{5,4},{6,7},{7,6},{8,9},{9,8},{10,11... | collective-permute-start | bytes 2359304 | tf_op jit(solution)/shard_map/ppermute | solution.py:54
  107.0 3.9 %collective-permute-start.22 = (bf16[2,2,96,768]{3,2,1,0:T(8,128)(2,1)}, bf16[2,2,96,768]{3,2,1,0:T(8,128)(2,1)S(1)}, u32[]{:S(2)}, u32[]{:S(2)}) collective-permute-start(bf16[2,2,96,768]{3,2,1,0:T(8,128)(2,1)} %collective-permute-done.14.refs_6_), channel_id=1, source_target_pairs={{0,1},{1,0},{2,3},{3,2},{4,5},{5,4},{6,7},{7,6},{8,9},{9,8},{10,11... | collective-permute-start | bytes 1769480 | tf_op jit(solution)/shard_map/ppermute | solution.py:54
  107.5 6.6 %copy-start.25 = (bf16[2,2,96,768]{3,2,1,0:T(8,128)(2,1)}, bf16[2,2,96,768]{3,2,1,0:T(8,128)(2,1)S(1)}, u32[]{:S(2)}) copy-start(bf16[2,2,96,768]{3,2,1,0:T(8,128)(2,1)S(1)} %collective-permute-done.15.refs_7_) | copy-start | bytes 1769476
  107.5 6.6 %collective-permute-start.17 = (bf16[4,96,1024]{2,1,0:T(8,128)(2,1)}, bf16[4,96,1024]{2,1,0:T(8,128)(2,1)}, u32[]{:S(2)}, u32[]{:S(2)}) collective-permute-start(bf16[4,96,1024]{2,1,0:T(8,128)(2,1)} %collective-permute-done.9.refs_1_), channel_id=1, source_target_pairs={{0,1},{1,0},{2,3},{3,2},{4,5},{5,4},{6,7},{7,6},{8,9},{9,8},{10,11... | collective-permute-start | bytes 2359304 | tf_op jit(solution)/shard_map/ppermute | solution.py:54
  107.6 6.6 %collective-permute-start.18 = (bf16[4,96,1024]{2,1,0:T(8,128)(2,1)}, bf16[4,96,1024]{2,1,0:T(8,128)(2,1)}, u32[]{:S(2)}, u32[]{:S(2)}) collective-permute-start(bf16[4,96,1024]{2,1,0:T(8,128)(2,1)} %collective-permute-done.11.refs_2_), channel_id=1, source_target_pairs={{0,1},{1,0},{2,3},{3,2},{4,5},{5,4},{6,7},{7,6},{8,9},{9,8},{10,11... | collective-permute-start | bytes 2359304 | tf_op jit(solution)/shard_map/ppermute | solution.py:54
  108.1 8.5 %collective-permute-start.19 = (bf16[4,96,1024]{2,1,0:T(8,128)(2,1)}, bf16[4,96,1024]{2,1,0:T(8,128)(2,1)}, u32[]{:S(2)}, u32[]{:S(2)}) collective-permute-start(bf16[4,96,1024]{2,1,0:T(8,128)(2,1)} %collective-permute-done.12.refs_3_), channel_id=1, source_target_pairs={{0,1},{1,0},{2,3},{3,2},{4,5},{5,4},{6,7},{7,6},{8,9},{9,8},{10,11... | collective-permute-start | bytes 2359304 | tf_op jit(solution)/shard_map/ppermute | solution.py:54
  111.7 4.0 %collective-permute-start.23 = (bf16[2,2,96,768]{3,2,1,0:T(8,128)(2,1)S(1)}, bf16[2,2,96,768]{3,2,1,0:T(8,128)(2,1)S(1)}, u32[]{:S(2)}, u32[]{:S(2)}) collective-permute-start(bf16[2,2,96,768]{3,2,1,0:T(8,128)(2,1)S(1)} %collective-permute-done.15.refs_7_), channel_id=1, source_target_pairs={{0,1},{1,0},{2,3},{3,2},{4,5},{5,4},{6,7},{7,6},{8,9},{9,8},{10,11... | collective-permute-start | bytes 1769480 | tf_op jit(solution)/shard_map/ppermute | solution.py:54
  114.0 1.7 collective-permute-start.25
  154.1 9.3 %collective-permute-start.26 = (bf16[2,8,96,1728]{3,2,1,0:T(8,128)(2,1)}, bf16[2,8,96,1728]{3,2,1,0:T(8,128)(2,1)S(1)}, u32[]{:S(2)}, u32[]{:S(2)}) collective-permute-start(bf16[2,8,96,1728]{3,2,1,0:T(8,128)(2,1)} %get-tuple-element.159), channel_id=1, source_target_pairs={{0,1},{1,0},{2,3},{3,2},{4,5},{5,4},{6,7},{7,6},{8,9},{9,8},{10,11... | collective-permute-start | bytes 15925256 | tf_op jit(solution)/shard_map/ppermute | solution.py:54
  156.6 36.4 %collective-permute-start.32 = (f32[12,768]{1,0:T(8,128)}, f32[12,768]{1,0:T(8,128)}, u32[]{:S(2)}, u32[]{:S(2)}) collective-permute-start(f32[12,768]{1,0:T(8,128)} %pad_maximum_fusion.9), channel_id=1, source_target_pairs={{0,1},{1,0},{2,3},{3,2},{4,5},{5,4},{6,7},{7,6},{8,9},{9,8},{10,11... | collective-permute-start | bytes 110600 | tf_op jit(solution)/shard_map/ppermute | solution.py:54
  157.0 13.3 %collective-permute-start.27 = (bf16[3,256,128]{2,1,0:T(8,128)(2,1)}, bf16[3,256,128]{2,1,0:T(8,128)(2,1)S(1)}, u32[]{:S(2)}, u32[]{:S(2)}) collective-permute-start(bf16[3,256,128]{2,1,0:T(8,128)(2,1)} %get-tuple-element.161), channel_id=1, source_target_pairs={{0,1},{1,0},{2,3},{3,2},{4,5},{5,4},{6,7},{7,6},{8,9},{9,8},{10,11... | collective-permute-start | bytes 589832 | tf_op jit(solution)/shard_map/ppermute | solution.py:54
  157.2 13.1 %collective-permute-start.28 = (bf16[3,256,128]{2,1,0:T(8,128)(2,1)}, bf16[3,256,128]{2,1,0:T(8,128)(2,1)S(1)}, u32[]{:S(2)}, u32[]{:S(2)}) collective-permute-start(bf16[3,256,128]{2,1,0:T(8,128)(2,1)} %get-tuple-element.162), channel_id=1, source_target_pairs={{0,2},{1,3},{2,0},{3,1},{4,6},{5,7},{6,4},{7,5},{8,10},{9,11},{10,... | collective-permute-start | bytes 589832 | tf_op jit(solution)/shard_map/ppermute | solution.py:54
  158.6 11.6 %collective-permute-start.29 = (bf16[3,256,128]{2,1,0:T(8,128)(2,1)}, bf16[3,256,128]{2,1,0:T(8,128)(2,1)S(1)}, u32[]{:S(2)}, u32[]{:S(2)}) collective-permute-start(bf16[3,256,128]{2,1,0:T(8,128)(2,1)} %get-tuple-element.163), channel_id=1, source_target_pairs={{0,3},{1,2},{2,1},{3,0},{4,7},{5,6},{6,5},{7,4},{8,11},{9,10},{10,... | collective-permute-start | bytes 589832 | tf_op jit(solution)/shard_map/ppermute | solution.py:54
  160.7 13.9 %copy-start.6 = (bf16[1,2,2,2,96,768]{5,4,2,1,3,0:T(8,128)(2,1)}, bf16[1,2,2,2,96,768]{5,4,2,1,3,0:T(8,128)(2,1)S(1)}, u32[]{:S(2)}) copy-start(bf16[1,2,2,2,96,768]{5,4,2,1,3,0:T(8,128)(2,1)S(1)} %copy.107) | copy-start | bytes 3538948
  163.4 5.4 %copy-start.5 = (bf16[2,8,96,1728]{3,2,1,0:T(8,128)(2,1)}, bf16[2,8,96,1728]{3,2,1,0:T(8,128)(2,1)S(1)}, u32[]{:S(2)}) copy-start(bf16[2,8,96,1728]{3,2,1,0:T(8,128)(2,1)S(1)} %collective-permute-done.26) | copy-start | bytes 15925252
  170.2 5.2 %copy-start.33 = (f32[4,1,768]{2,1,0:T(1,128)S(1)}, f32[4,1,768]{2,1,0:T(1,128)}, u32[]{:S(2)}) copy-start(f32[4,1,768]{2,1,0:T(1,128)} %get-tuple-element.182) | copy-start | bytes 36868
  170.3 5.8 %copy-start.17 = (bf16[3,256,128]{2,1,0:T(8,128)(2,1)}, bf16[3,256,128]{2,1,0:T(8,128)(2,1)S(1)}, u32[]{:S(2)}) copy-start(bf16[3,256,128]{2,1,0:T(8,128)(2,1)S(1)} %collective-permute-done.27.refs_1_) | copy-start | bytes 589828
  170.3 44.7 %collective-permute-start.30 = (bf16[2,2,2,96,768]{4,3,1,0,2:T(8,128)(2,1)}, bf16[2,2,2,96,768]{4,3,1,0,2:T(8,128)(2,1)}, u32[]{:S(2)}, u32[]{:S(2)}) collective-permute-start(bf16[2,2,2,96,768]{4,3,1,0,2:T(8,128)(2,1)} %fusion.2), channel_id=1, source_target_pairs={{0,2},{1,3},{2,0},{3,1},{4,6},{5,7},{6,4},{7,5},{8,10},{9,11},{10,... | collective-permute-start | bytes 3538952 | tf_op jit(solution)/shard_map/ppermute | solution.py:54
  171.9 45.3 %collective-permute-start.31 = (bf16[2,2,2,96,960]{4,3,2,1,0:T(8,128)(2,1)}, bf16[2,2,2,96,960]{4,3,2,1,0:T(8,128)(2,1)}, u32[]{:S(2)}, u32[]{:S(2)}) collective-permute-start(bf16[2,2,2,96,960]{4,3,2,1,0:T(8,128)(2,1)} %fusion), channel_id=1, source_target_pairs={{0,4},{4,0},{8,12},{12,8},{16,20},{20,16},{24,28},{28,24},{1,5},{5... | collective-permute-start | bytes 4423688 | tf_op jit(solution)/shard_map/ppermute | solution.py:54
  209.8 5.2 %copy-start.7 = (bf16[1,2,2,2,96,768]{5,4,2,1,3,0:T(8,128)(2,1)S(1)}, bf16[1,2,2,2,96,768]{5,4,2,1,3,0:T(8,128)(2,1)}, u32[]{:S(2)}) copy-start(bf16[1,2,2,2,96,768]{5,4,2,1,3,0:T(8,128)(2,1)} %copy-done.6) | copy-start | bytes 3538948
  220.1 23.1 %collective-permute-start.34 = (bf16[2,2,96,768]{3,2,1,0:T(8,128)(2,1)}, bf16[2,2,96,768]{3,2,1,0:T(8,128)(2,1)}, u32[]{:S(2)}, u32[]{:S(2)}) collective-permute-start(bf16[2,2,96,768]{3,2,1,0:T(8,128)(2,1)} %fusion.3), channel_id=1, source_target_pairs={{0,4},{4,0},{8,12},{12,8},{16,20},{20,16},{24,28},{28,24},{1,5},{5... | collective-permute-start | bytes 1769480 | tf_op jit(solution)/shard_map/ppermute | solution.py:54
  220.6 21.3 %collective-permute-start.33 = (f32[11,768]{1,0:T(8,128)S(1)}, f32[11,768]{1,0:T(8,128)S(1)}, u32[]{:S(2)}, u32[]{:S(2)}) collective-permute-start(f32[11,768]{1,0:T(8,128)S(1)} %pad_maximum_fusion.10), channel_id=1, source_target_pairs={{0,2},{1,3},{2,0},{3,1},{4,6},{5,7},{6,4},{7,5},{8,10},{9,11},{10,... | collective-permute-start | bytes 101384 | tf_op jit(solution)/shard_map/ppermute | solution.py:54
  221.2 23.6 %collective-permute-start.35 = (bf16[2,2,96,960]{3,2,1,0:T(8,128)(2,1)}, bf16[2,2,96,960]{3,2,1,0:T(8,128)(2,1)}, u32[]{:S(2)}, u32[]{:S(2)}) collective-permute-start(bf16[2,2,96,960]{3,2,1,0:T(8,128)(2,1)} %fusion.1), channel_id=1, source_target_pairs={{0,2},{1,3},{2,0},{3,1},{4,6},{5,7},{6,4},{7,5},{8,10},{9,11},{10,... | collective-permute-start | bytes 2211848 | tf_op jit(solution)/shard_map/ppermute | solution.py:54
  254.2 7.6 %copy-start.23 = (bf16[512,768]{1,0:T(8,128)(2,1)S(1)}, bf16[512,768]{1,0:T(8,128)(2,1)}, u32[]{:S(2)}) copy-start(bf16[512,768]{1,0:T(8,128)(2,1)} %get-tuple-element.201) | copy-start | bytes 2359300
  254.2 7.6 %collective-permute-start.36 = (bf16[512,768]{1,0:T(8,128)(2,1)}, bf16[512,768]{1,0:T(8,128)(2,1)S(1)}, u32[]{:S(2)}, u32[]{:S(2)}) collective-permute-start(bf16[512,768]{1,0:T(8,128)(2,1)} %get-tuple-element.202), channel_id=1, source_target_pairs={{0,1},{1,0},{2,3},{3,2},{4,5},{5,4},{6,7},{7,6},{8,9},{9,8},{10,11... | collective-permute-start | bytes 2359304 | tf_op jit(solution)/shard_map/ppermute | solution.py:54
  255.5 20.3 %collective-permute-start.41 = (bf16[2,96,1728]{2,1,0:T(8,128)(2,1)}, bf16[2,96,1728]{2,1,0:T(8,128)(2,1)}, u32[]{:S(2)}, u32[]{:S(2)}) collective-permute-start(bf16[2,96,1728]{2,1,0:T(8,128)(2,1)} %pad_maximum_fusion.1), channel_id=1, source_target_pairs={{0,8},{4,12},{8,0},{12,4},{16,24},{20,28},{24,16},{28,20},{1,9},{5... | collective-permute-start | bytes 1990664 | tf_op jit(solution)/shard_map/ppermute | solution.py:54
  257.3 16.3 %collective-permute-start.39 = (bf16[3,2,2,96,192]{3,4,0,1,2:T(8,128)(2,1)}, bf16[3,2,2,96,192]{3,4,0,1,2:T(8,128)(2,1)}, u32[]{:S(2)}, u32[]{:S(2)}) collective-permute-start(bf16[3,2,2,96,192]{3,4,0,1,2:T(8,128)(2,1)} %bitcast.176), channel_id=1, source_target_pairs={{0,4},{4,0},{8,12},{12,8},{16,20},{20,16},{24,28},{28,24},{1,5},{5... | collective-permute-start | bytes 1327112 | tf_op jit(solution)/shard_map/ppermute | solution.py:54
  260.2 18.2 %collective-permute-start.44 = (f32[12,768]{1,0:T(8,128)S(1)}, f32[12,768]{1,0:T(8,128)S(1)}, u32[]{:S(2)}, u32[]{:S(2)}) collective-permute-start(f32[12,768]{1,0:T(8,128)S(1)} %pad_maximum_fusion.11), channel_id=1, source_target_pairs={{0,4},{4,0},{8,12},{12,8},{16,20},{20,16},{24,28},{28,24},{1,5},{5... | collective-permute-start | bytes 110600 | tf_op jit(solution)/shard_map/ppermute | solution.py:54
  267.9 9.3 %copy-start.13 = (bf16[2,2,96,768]{3,2,1,0:T(8,128)(2,1)S(1)}, bf16[2,2,96,768]{3,2,1,0:T(8,128)(2,1)}, u32[]{:S(2)}) copy-start(bf16[2,2,96,768]{3,2,1,0:T(8,128)(2,1)} %slice_bitcast_fusion.8) | copy-start | bytes 1769476
  267.9 9.3 %copy-start.15 = (bf16[2,2,96,768]{3,2,1,0:T(8,128)(2,1)S(1)}, bf16[2,2,96,768]{3,2,1,0:T(8,128)(2,1)}, u32[]{:S(2)}) copy-start(bf16[2,2,96,768]{3,2,1,0:T(8,128)(2,1)} %get-tuple-element.278) | copy-start | bytes 1769476
  267.9 9.3 %copy-start.16 = (bf16[2,2,96,768]{3,2,1,0:T(8,128)(2,1)S(1)}, bf16[2,2,96,768]{3,2,1,0:T(8,128)(2,1)}, u32[]{:S(2)}) copy-start(bf16[2,2,96,768]{3,2,1,0:T(8,128)(2,1)} %get-tuple-element.279) | copy-start | bytes 1769476
  267.9 50.3 %collective-permute-start.37 = (bf16[512,768]{1,0:T(8,128)(2,1)}, bf16[512,768]{1,0:T(8,128)(2,1)}, u32[]{:S(2)}, u32[]{:S(2)}) collective-permute-start(bf16[512,768]{1,0:T(8,128)(2,1)} %get-tuple-element.205), channel_id=1, source_target_pairs={{0,1},{1,0},{2,3},{3,2},{4,5},{5,4},{6,7},{7,6},{8,9},{9,8},{10,11... | collective-permute-start | bytes 2359304 | tf_op jit(solution)/shard_map/ppermute | solution.py:54
  275.5 26.1 %collective-permute-start.40 = (bf16[3,2,96,192]{2,3,0,1:T(8,128)(2,1)}, bf16[3,2,96,192]{2,3,0,1:T(8,128)(2,1)}, u32[]{:S(2)}, u32[]{:S(2)}) collective-permute-start(bf16[3,2,96,192]{2,3,0,1:T(8,128)(2,1)} %fusion.8), channel_id=1, source_target_pairs={{0,8},{4,12},{8,0},{12,4},{16,24},{20,28},{24,16},{28,20},{1,9},{5... | collective-permute-start | bytes 663560 | tf_op jit(solution)/shard_map/ppermute | solution.py:54
  277.2 24.3 %copy-start.20 = (bf16[3,2,96,192]{2,3,0,1:T(8,128)(2,1)S(1)}, bf16[3,2,96,192]{2,3,0,1:T(8,128)(2,1)}, u32[]{:S(2)}) copy-start(bf16[3,2,96,192]{2,3,0,1:T(8,128)(2,1)} %slice_bitcast_fusion.10) | copy-start | bytes 663556
  278.4 6.1 %collective-permute-start.45 = (f32[12,768]{1,0:T(8,128)S(1)}, f32[12,768]{1,0:T(8,128)S(1)}, u32[]{:S(2)}, u32[]{:S(2)}) collective-permute-start(f32[12,768]{1,0:T(8,128)S(1)} %add.243), channel_id=1, source_target_pairs={{0,8},{4,12},{8,0},{12,4},{16,24},{20,28},{24,16},{28,20},{1,9},{5... | collective-permute-start | bytes 110600 | tf_op jit(solution)/shard_map/ppermute | solution.py:54
  281.1 22.2 %copy-start.21 = (bf16[3,2,96,192]{2,3,0,1:T(8,128)(2,1)}, bf16[3,2,96,192]{2,3,0,1:T(8,128)(2,1)S(1)}, u32[]{:S(2)}) copy-start(bf16[3,2,96,192]{2,3,0,1:T(8,128)(2,1)S(1)} %slice_bitcast_fusion.11) | copy-start | bytes 663556
  281.1 37.0 %collective-permute-start.38 = (bf16[512,768]{1,0:T(8,128)(2,1)}, bf16[512,768]{1,0:T(8,128)(2,1)}, u32[]{:S(2)}, u32[]{:S(2)}) collective-permute-start(bf16[512,768]{1,0:T(8,128)(2,1)} %add_convert_fusion.3), channel_id=1, source_target_pairs={{0,2},{1,3},{2,0},{3,1},{4,6},{5,7},{6,4},{7,5},{8,10},{9,11},{10,... | collective-permute-start | bytes 2359304 | tf_op jit(solution)/shard_map/ppermute | solution.py:54
  284.5 15.0 %collective-permute-start.46 = (f32[12,768]{1,0:T(8,128)S(1)}, f32[12,768]{1,0:T(8,128)S(1)}, u32[]{:S(2)}, u32[]{:S(2)}) collective-permute-start(f32[12,768]{1,0:T(8,128)S(1)} %add.244), channel_id=1, source_target_pairs={{0,16},{4,20},{8,24},{12,28},{16,0},{20,4},{24,8},{28,12},{1,17},{... | collective-permute-start | bytes 110600 | tf_op jit(solution)/shard_map/ppermute | solution.py:54
  286.4 27.0 %collective-permute-start.43 = (bf16[96,1728]{1,0:T(8,128)(2,1)}, bf16[96,1728]{1,0:T(8,128)(2,1)}, u32[]{:S(2)}, u32[]{:S(2)}) collective-permute-start(bf16[96,1728]{1,0:T(8,128)(2,1)} %pad_maximum_fusion.5), channel_id=1, source_target_pairs={{0,16},{4,20},{8,24},{12,28},{16,0},{20,4},{24,8},{28,12},{1,17},{... | collective-permute-start | bytes 995336 | tf_op jit(solution)/shard_map/ppermute | solution.py:54
  302.5 7.5 %collective-permute-start.42 = (bf16[3,96,192]{1,2,0:T(8,128)(2,1)S(1)}, bf16[3,96,192]{1,2,0:T(8,128)(2,1)S(1)}, u32[]{:S(2)}, u32[]{:S(2)}) collective-permute-start(bf16[3,96,192]{1,2,0:T(8,128)(2,1)S(1)} %fusion.16), channel_id=1, source_target_pairs={{0,16},{4,20},{8,24},{12,28},{16,0},{20,4},{24,8},{28,12},{1,17},{... | collective-permute-start | bytes 331784 | tf_op jit(solution)/shard_map/ppermute | solution.py:54
  (23 other events, 56.8 us)

commit v3 on v2

--- a/solution.py
+++ b/solution.py
@@ -1,4 +1,5 @@
 import functools
+import itertools
 
 import jax
 import jax.numpy as jnp
@@ -16,6 +17,7 @@
 NT = (((1,), (1,)), ((), ()))
 TN = (((0,), (0,)), ((), ()))
 VMEM_LIMIT = 64 << 20
+EXTRA = 16
 
 
 def dot(left, right):
@@ -99,6 +101,7 @@
 SMEM_SPEC = pl.BlockSpec(memory_space=pltpu.SMEM)
 VMEM_SPEC = pl.BlockSpec(memory_space=pltpu.VMEM)
 ANY_SPEC = pl.BlockSpec(memory_space=pl.ANY)
+HBM_SPEC = pl.BlockSpec(memory_space=pltpu.HBM)
 
 
 def project_kernel(*refs, masks, heads, placed):
@@ -229,7 +232,7 @@
 
 def backward_kernel(q_ref, k_ref, v_ref, o_ref, *refs, placed):
     d_refs, x_refs = refs[:4], refs[4:8]
-    g_ref, gb_ref, gw_ref, dk_s, dv_s, gw_s, d_s = refs[-7:]
+    g_ref, gw_ref, dk_s, dv_s, gw_s, d_s = refs[-6:]
     seq = q_ref.shape[0]
     block = seq // 8
     rows = seq // 4
@@ -270,13 +273,18 @@
     g_ref[0, :, :LANES] = both.astype(BF16)
     g_ref[0, :, LANES:] = dv_s[:, :HEAD_DIM].astype(BF16)
     grads = g_ref[0]
-    gb_ref[...] = jnp.sum(grads.astype(F32), axis=0, keepdims=True)
+    bias = jnp.sum(grads.astype(F32), axis=0, keepdims=True)
+    share = gw_ref.shape[2]
+    line = lax.broadcasted_iota(jnp.int32, (share, 1), 0)
+    side = jnp.where(line < 8, bias[:, :HEAD_DIM], 0.0)
+    side = jnp.where((line >= 8) & (line < 16), bias[:, LANES:], side).astype(BF16)
     total = dot_tn(grads[:rows], x_refs[0][...])
     for j in range(1, 4):
         total += dot_tn(grads[j * rows : (j + 1) * rows], x_refs[j][...])
     gw_s[...] = total.T.astype(BF16)
     for i in range(gw_ref.shape[1]):
-        gw_ref[0, i] = gw_s[place_of(i, gw_ref.shape[2], placed), :]
+        gw_ref[0, i, :, : 3 * HEAD_DIM] = gw_s[place_of(i, share, placed), :]
+        gw_ref[0, i, :, 3 * HEAD_DIM :] = side
 
 
 def attention_backward(head, q, k, v, out, grads, parts, blocks, before):
@@ -289,20 +297,18 @@
     three = 3 * HEAD_DIM
     share = width // blocks
     shape = jax.ShapeDtypeStruct
-    alias = {12: 0, 13: 2} if before else {}
+    alias = {12: 0, 13: 1} if before else {}
     return pl.pallas_call(
         functools.partial(backward_kernel, placed=blocks > 1),
         grid=(1,),
         in_specs=[flat, one, one, flat] + [piece] * 4 + [whole] * 4 + [ANY_SPEC] * len(before),
         out_specs=[
             pl.BlockSpec((1, seq, three), lambda i: (head, 0, 0)),
-            pl.BlockSpec((1, three), lambda i: (0, 0)),
-            pl.BlockSpec((1, blocks, share, three), lambda i: (head, 0, 0, 0)),
+            pl.BlockSpec((1, blocks, share, 4 * HEAD_DIM), lambda i: (head, 0, 0, 0)),
         ],
         out_shape=[
             shape((heads, seq, three), BF16),
-            shape((1, three), F32),
-            shape((heads, blocks, share, three), BF16),
+            shape((heads, blocks, share, 4 * HEAD_DIM), BF16),
         ],
         scratch_shapes=[
             pltpu.VMEM((seq, LANES), F32),
@@ -321,7 +327,6 @@
     w_refs = refs[: len(masks)]
     outs, w_s = refs[len(masks) : -1], refs[-1]
     heads, seq, three = g_ref.shape
-    rows = seq // 4
     for ref, entries in zip(w_refs, masks, strict=True):
         for z, mask in enumerate(entries):
             place = place_of(mask, ref.shape[1], placed)
@@ -330,8 +335,8 @@
                     start = (kind * heads + h) * HEAD_DIM
                     stop = (h * 3 + kind) * HEAD_DIM
                     w_s[place, stop : stop + HEAD_DIM] = ref[z, :, start : start + HEAD_DIM]
-    for out, j in zip(outs, which, strict=True):
-        part = pl.ds(j * rows, rows)
+    for out, (start, count) in zip(outs, which, strict=True):
+        part = pl.ds(start, count)
         total = dot_nt(g_ref[0, part, :], w_s[:, :three])
         for h in range(1, heads):
             total += dot_nt(g_ref[h, part, :], w_s[:, h * three : (h + 1) * three])
@@ -345,7 +350,7 @@
         functools.partial(input_kernel, masks=masks, which=which, placed=placed),
         in_specs=[VMEM_SPEC] * (1 + len(pieces)),
         out_specs=[VMEM_SPEC] * len(which),
-        out_shape=[jax.ShapeDtypeStruct((seq // 4, width), BF16)] * len(which),
+        out_shape=[jax.ShapeDtypeStruct((count, width), BF16) for _, count in which],
         scratch_shapes=[pltpu.VMEM((width, heads * three), BF16)],
         compiler_params=params(),
         cost_estimate=cost(1000, 1000),
@@ -358,10 +363,10 @@
     refs = refs[len(plan) :]
     own_ref, near_ref, far_ref = refs[:3]
     x_ref, og_ref, positions_ref, lengths_ref, vec_ref = refs[3:8]
-    lo_ref, done_ref, sums_ref, gbup_ref, sent, kept = refs[8:14]
+    lo_ref, done_ref, sent_d, kept_d, sent_u, kept_u = refs[8:14]
     ga = refs[14:18]
     w1_s, w2_s, att_s, wo_s, hid_s, slope_s, nrm_s, nb_s, n1_s, rs_s, ffn_s = refs[18:29]
-    gf_s, gft_s, nbt_s, acc_s, pre_s, g_s, bup_s, mask_s, in_sem, down_sem, up_sem, out_sem = refs[29:]
+    gf_s, gft_s, nbt_s, acc_s, pre_s, g_s, bup_s, mask_s, sums_ref, low_s, in_sem, down_sem, up_sem, out_sem, low_sem = refs[29:]
     rows, width = x_ref.shape
     hidden = w2_s.shape[2]
     pieces = 4
@@ -477,10 +482,10 @@
 
     places = [place_of(i, share, placed) for i in range(blocks)]
 
-    def copies(j, lanes, target, place, sem):
+    def copies(j, lanes, target, place, sem, to):
         return [
             pltpu.make_async_copy(
-                g_s.at[j].at[places[i], lanes], target.at[place, i, :, lanes], sem.at[j, i]
+                g_s.at[j].at[places[i], lanes], target.at[place, i, pl.ds(0, share), to], sem.at[j, i]
             )
             for i in range(blocks)
         ]
@@ -490,19 +495,20 @@
         pl.ds(hidden, hidden),
         pl.ds(2 * hidden, cols),
     )
-    for away, target in ((1, sent), (0, kept)):
+    to_d, to_u, to_o = pl.ds(0, hidden), pl.ds(0, hidden), pl.ds(hidden, cols)
+    for away, target_d, target_u in ((1, sent_d, sent_u), (0, kept_d, kept_u)):
 
         @pl.loop(0, pieces // 2)
         def _(place):
             j = 2 * place + away
             pre_s[...] = dot(gf_s[...], w2_s[j]) * slope_s[j]
             low = pre_s[...].astype(BF16)
-            gbup_ref[j] = jnp.sum(low.astype(F32), axis=0, keepdims=True)
+            sums_ref[pl.ds(10 + j, 1), :] = jnp.sum(low.astype(F32), axis=0, keepdims=True)
             g_s[j, :, lanes_d] = dot(gft_s[...], hid_s[j]).astype(BF16)
-            for copy in copies(j, lanes_d, target, place, down_sem):
+            for copy in copies(j, lanes_d, target_d, place, down_sem, to_d):
                 copy.start()
             g_s[j, :, lanes_u] = dot(nbt_s[...], low).astype(BF16)
-            for copy in copies(j, lanes_u, target, place, up_sem):
+            for copy in copies(j, lanes_u, target_u, place, up_sem, to_u):
                 copy.start()
             acc_s[...] += dot_nt(low, w1_s[j, :, :hidden])
 
@@ -522,8 +528,16 @@
     gout = dot_tn(low, att_s[...]).astype(BF16)
     for j in range(pieces):
         g_s[j, :, 2 * hidden : 2 * hidden + cols] = gout[:, j * cols : (j + 1) * cols]
-        for copy in copies(j, lanes_o, sent if j % 2 else kept, j // 2, out_sem):
+        for copy in copies(j, lanes_o, sent_u if j % 2 else kept_u, j // 2, out_sem, to_o):
             copy.start()
+    small = []
+    for j in range(pieces):
+        low_s[j] = jnp.concatenate([sums_ref[:9], sums_ref[10 + j : 11 + j], sums_ref[9:15]]).astype(BF16)
+        target = sent_d if j % 2 else kept_d
+        for i in range(blocks):
+            under = target.at[j // 2, i, pl.ds(share, EXTRA), :]
+            small.append(pltpu.make_async_copy(low_s.at[j], under, low_sem.at[j, i]))
+            small[-1].start()
     back = dot(low, wo_s[...]).astype(BF16)
     for j in range(pieces):
         for h in range(cols // HEAD_DIM):
@@ -531,10 +545,15 @@
             ga[j][h, :, :HEAD_DIM] = back[:half, at : at + HEAD_DIM]
             ga[j][h, :, HEAD_DIM:] = back[half:, at : at + HEAD_DIM]
     for j in range(pieces):
-        target = sent if j % 2 else kept
-        for lanes, sem in ((lanes_d, down_sem), (lanes_u, up_sem), (lanes_o, out_sem)):
-            for copy in copies(j, lanes, target, j // 2, sem):
-                copy.wait()
+        target_d, target_u = (sent_d, sent_u) if j % 2 else (kept_d, kept_u)
+        for copy in copies(j, lanes_d, target_d, j // 2, down_sem, to_d):
+            copy.wait()
+        for copy in copies(j, lanes_u, target_u, j // 2, up_sem, to_u):
+            copy.wait()
+        for copy in copies(j, lanes_o, target_u, j // 2, out_sem, to_o):
+            copy.wait()
+    for copy in small:
+        copy.wait()
 
 
 def middle(blocks, weights, plan, att, tokens, out_grad, positions, lengths, vectors, hidden):
@@ -547,14 +566,13 @@
     return pl.pallas_call(
         functools.partial(middle_kernel, plan=plan, blocks=blocks),
         in_specs=[ANY_SPEC] * len(weights) + [VMEM_SPEC] * 6 + [SMEM_SPEC, VMEM_SPEC],
-        out_specs=[VMEM_SPEC] * 4 + [ANY_SPEC] * 2 + [VMEM_SPEC] * 4,
+        out_specs=[VMEM_SPEC] * 2 + [ANY_SPEC] * 4 + [VMEM_SPEC] * 4,
         out_shape=[
             shape((rows, width), BF16),
             shape((rows, width), F32),
-            shape((16, width), F32),
-            shape((4, 1, hidden), F32),
         ]
-        + [shape((2, blocks, share, 2 * hidden + cols), BF16)] * 2
+        + [shape((2, blocks, share + EXTRA, hidden), BF16)] * 2
+        + [shape((2, blocks, share, hidden + cols), BF16)] * 2
         + [shape(att[0].shape, BF16)] * 4,
         scratch_shapes=[
             vmem((4, width, weights[0].shape[-1]), BF16),
@@ -576,7 +594,10 @@
             vmem((4, width, 2 * hidden + cols), BF16),
             vmem((4, 1, hidden), F32),
             vmem((rows, LANES), F32),
+            vmem((16, width), F32),
+            vmem((4, EXTRA, width), BF16),
             pltpu.SemaphoreType.DMA((loads,)),
+            pltpu.SemaphoreType.DMA((4, blocks)),
             pltpu.SemaphoreType.DMA((4, blocks)),
             pltpu.SemaphoreType.DMA((4, blocks)),
             pltpu.SemaphoreType.DMA((4, blocks)),
@@ -585,6 +606,108 @@
         cost_estimate=cost(1000, 1000),
         name="middle",
     )(*weights, *att, tokens, out_grad, positions, lengths, vectors)
+
+
+def reduce_kernel(*refs, jobs, inputs, outputs, terms, extra, extra_in):
+    ins = refs[:inputs]
+    more = refs[inputs : inputs + extra_in]
+    outs = refs[inputs + extra_in : inputs + extra_in + outputs]
+    rest = refs[inputs + extra_in + outputs :]
+    extra_out = rest[: len(rest) - terms - 1]
+    held, sems = rest[len(extra_out) : -1], rest[-1]
+    loads = []
+    for _, _, _, parts in jobs:
+        for source, index, start, size in parts:
+            at = len(loads)
+            picked = ins[source].at[index + (slice(None), pl.ds(start, size))]
+            loads.append(pltpu.make_async_copy(picked, held[at], sems.at[at]))
+            loads[-1].start()
+    at = 0
+    for out, start, lead, parts in jobs:
+        mine = range(at, at + len(parts))
+        at += len(parts)
+        for i in mine:
+            loads[i].wait()
+        size = parts[0][3]
+        for index in itertools.product(*map(range, lead)):
+            total = held[mine[0]][index].astype(F32)
+            for i in mine[1:]:
+                total += held[i][index].astype(F32)
+            target = outs[out]
+            target[index + (slice(None), slice(start, start + size))] = total.astype(target.dtype)
+    if extra is not None:
+        extra(outs, more, extra_out)
+
+
+class Sum:
+    def __init__(self, names, width):
+        self.names, self.width, self.terms, self.picks = list(names), width, [], {}
+
+    def join(self, array, start=0, names=None):
+        self.terms.append((array, start, list(self.names if names is None else names)))
+
+    def parts(self, picks):
+        return [
+            (array, tuple(picks.get(name, slice(None)) for name in names), start, self.width)
+            for array, start, names in self.terms
+        ]
+
+    def away(self, name):
+        parts = self.parts({**self.picks, name: 1})
+        self.picks[name] = 0
+        self.names.remove(name)
+        return parts
+
+    def all(self):
+        return self.parts(self.picks)
+
+
+def reduce_call(name, groups, dtype, extra=None, extra_in=(), extra_out=(), keep=True):
+    arrays, jobs, shapes, scratch = [], [], [], []
+    for out, columns in enumerate(groups):
+        start = 0
+        for parts in columns:
+            coded = []
+            for array, index, first, size in parts:
+                known = [i for i, other in enumerate(arrays) if other is array]
+                if not known:
+                    arrays.append(array)
+                coded.append((known[0] if known else len(arrays) - 1, index, first, size))
+                sizes = [n for n, i in zip(array.shape, index) if isinstance(i, slice)]
+                sizes += [array.shape[-2], size]
+                scratch.append(pltpu.VMEM(tuple(sizes), array.dtype))
+            jobs.append((out, start, tuple(sizes[:-2]), coded))
+            start += coded[0][3]
+        shapes.append(tuple(sizes[:-1]) + (start,))
+    outs = [jax.ShapeDtypeStruct(shape, dtype) for shape in shapes]
+    held = [] if keep else [pltpu.VMEM(shape, dtype) for shape in shapes]
+    result = pl.pallas_call(
+        functools.partial(
+            reduce_kernel if keep else reduce_inside,
+            jobs=jobs,
+            inputs=len(arrays),
+            outputs=len(outs),
+            terms=len(scratch),
+            extra=extra,
+            extra_in=len(extra_in),
+        ),
+        in_specs=[HBM_SPEC] * len(arrays) + [VMEM_SPEC] * len(extra_in),
+        out_specs=[VMEM_SPEC] * (len(outs) * keep + len(extra_out)),
+        out_shape=outs * keep + list(extra_out),
+        scratch_shapes=held + scratch + [pltpu.SemaphoreType.DMA((len(scratch),))],
+        compiler_params=params(),
+        cost_estimate=cost(1000, 1000),
+        name=name,
+    )(*arrays, *extra_in)
+    return result
+
+
+def reduce_inside(*refs, inputs, extra_in, outputs, terms, **rest):
+    front = inputs + extra_in
+    results = refs[front : len(refs) - outputs - terms - 1]
+    held = refs[len(refs) - outputs - terms - 1 : len(refs) - terms - 1]
+    order = refs[:front] + held + results + refs[len(refs) - terms - 1 :]
+    reduce_kernel(*order, inputs=inputs, extra_in=extra_in, outputs=outputs, terms=terms, **rest)
 
 
 def body(
@@ -617,7 +740,7 @@
     heads = own_cols // HEAD_DIM
     share = w_query.shape[0]
     hidden = w_up.shape[1]
-    placed = share % 16 == 0 and bits >= 2
+    placed = share % 16 == 0 and bits == 3 and heads == 3
     blocks = dp_count if placed else 1
     def core(value):
         return swap(value, "tensor", 1)
@@ -625,13 +748,12 @@
     def cross(value):
         return swap(value, "tensor", 2)
 
-    def grow(value, masks, bit, *hold):
-        got = after(swap(value, "dp", 1 << bit), *hold)
+    def grow(value, got, masks, bit):
         both = jnp.stack([value, got], axis=1).reshape((-1,) + value.shape[1:])
-        return both, [m ^ b for m in masks for b in (0, 1 << bit)]
+        return both, [m ^ b for m in masks for b in (0, bit)]
 
     across = cross(tokens)
-    parts = [tokens, core(tokens), across, core(across)]
+    beside = core(tokens)
     own_qkv = jnp.concatenate([w_query, w_key, w_value], axis=1)[None]
     own_b_up = lax.dynamic_slice_in_dim(b_up, group * share, share, 0)[:, None]
     spare = -(hidden + own_cols) % LANES
@@ -643,50 +765,60 @@
 
     kept = []
     if placed:
-        top = bits - 1
-        masks = [0]
-        w_part, masks = grow(own_qkv, masks, top, one, two, biases, vectors)
+        got_w = after(swap(own_qkv, "dp", 4), one, two)
+        w_part, w_mask = grow(own_qkv, got_w, [0], 4)
         one = after(one, w_part)
-        for bit in range(top - 1, 0, -1):
-            w_part, masks = grow(w_part, masks, bit)
-        one, one_masks = grow(one, [0], top, w_part)
+        got_w, got_one, across = after((swap(w_part, "dp", 2), swap(one, "dp", 4), across), w_part)
+        w_part, w_mask = grow(w_part, got_w, w_mask, 2)
+        one, one_mask = grow(one, got_one, [0], 4)
+
         two = after(two, across)
-        two = jnp.stack([two, cross(two)], axis=1)
-        w_qkv = [w_part, swap(w_part, "dp", 1)]
-        w_masks = [masks, [m ^ 1 for m in masks]]
-        positions = after(positions, two)
+        round_three = (swap(w_part, "dp", 1), swap(one, "dp", 2), cross(two), core(across))
+        round_three = after((round_three, biases, vectors), w_part)
+        (got_w, got_one, got_two, beyond), biases, vectors = round_three
+        w_qkv, w_masks = [w_part, got_w], [w_mask, [m ^ 1 for m in w_mask]]
+        one, one_mask = grow(one, got_one, one_mask, 2)
+        two = jnp.stack([two, got_two], axis=1)
+        parts = [tokens, beside, across, beyond]
+
+        round_four = (swap(two, "dp", 4), swap(one, "dp", 1), cross(one), core(one))
+        positions = after(positions, one, two)
         q, k, v = project(parts, w_qkv, w_masks, *biases, positions, seq_lengths, heads, placed)
-
-        for bit in range(top - 1, 0, -1):
-            one, one_masks = grow(one, one_masks, bit, q)
-        even = (one, one_masks)
-        odd = (swap(one, "dp", 1), [m ^ 1 for m in one_masks])
-        even_far = (cross(one), one_masks)
-        q = after(q, one)
         q_kept, out, packed = attention_forward(0, q, k, v, [])
         kept.append((q_kept, out))
-        two, two_masks = grow(two, [0], top, q_kept)
-        twos = [(two, two_masks)]
-        packed = list(after(packed, two))
-        for h in range(1, heads):
-            q_kept, out, packed = attention_forward(h, q, k, v, packed)
-            kept.append((q_kept, out))
-            if h == 1:
-                for bit in range(top - 1, 0, -1):
-                    twos += [(swap(w, "dp", 1 << bit), [m ^ (1 << bit) for m in ms]) for w, ms in twos]
-                odd = (after(odd[0], q_kept), odd[1])
-                odd_far = (cross(odd[0]), odd[1])
-                first = len(twos)
-                twos.append((swap(after(two, q_kept), "dp", 1), [m ^ 1 for m in two_masks]))
-                packed = list(after(packed, odd[0]))
-        later = [(after(w, q_kept), ms) for w, ms in twos[1:first]]
-        twos = [twos[0]] + later + twos[first:] + [(swap(w, "dp", 1), [m ^ 1 for m in ms]) for w, ms in later]
-        ones = [even, odd, even_far, odd_far]
+        got_two, odd, even_far, even_near = after(round_four, q_kept)
+        two, two_mask = grow(two, got_two, [0], 4)
+
+        round_five = (swap(two, "dp", 2), cross(odd), swap(two, "dp", 1), core(even_far))
+        packed, odd, two, even_far = after((packed, odd, two, even_far), q_kept)
+        q_kept, out, packed = attention_forward(1, q, k, v, packed)
+        kept.append((q_kept, out))
+        q = after(q, q_kept)
+        q_kept, out, packed = attention_forward(2, q, k, v, packed)
+        kept.append((q_kept, out))
+        two_late, odd_far, two_odd, both_near = after(round_five, q_kept)
+
+        far_odd = [m ^ 1 for m in one_mask]
+        two_mask_odd = [m ^ 1 for m in two_mask]
+        late_mask, last_mask = [m ^ 2 for m in two_mask], [m ^ 3 for m in two_mask]
+        two_last = swap(two_late, "dp", 1)
+        att_far = cross(packed[2])
+        odd, two = after((odd, two), two_late)
+        two_near, odd_near = core(two), core(odd)
+        odd_far, two_late, two_odd = after((odd_far, two_late, two_odd), two_near, odd_near)
+        odd_far_near, late_near, two_odd_near = core(odd_far), core(two_late), core(two_odd)
+        two_last, att_far = after((two_last, att_far), odd_far_near, late_near, two_odd_near)
+        att_near = core(jnp.stack([packed[1], att_far[1]]))
+        ones = [(one, one_mask), (odd, far_odd), (even_far, one_mask), (odd_far, far_odd)]
+        twos = [(two, two_mask), (two_odd, two_mask_odd), (two_late, late_mask), (two_last, last_mask)]
+        early = [even_near, odd_near, both_near, odd_far_near, two_near, two_odd_near, late_near]
+        early.append(core(two_last))
     else:
         w_qkv = [gather_bits(own_qkv[0], "dp", range(bits), 0).reshape(1, width, -1)]
         w_masks = [[0]]
         one = gather_bits(one[0], "dp", range(bits), 0).reshape(1, width, -1)
         two = gather_bits(two[0], "dp", range(bits), 0).reshape(1, width, -1)
+        parts = [tokens, beside, across, core(across)]
         q, k, v = project(parts, w_qkv, w_masks, *biases, positions, seq_lengths, heads, placed)
         packed = []
         for h in range(heads):
@@ -694,16 +826,17 @@
             kept.append((q_kept, out))
         ones = [(one, [0]), (cross(one), [0])]
         twos = [(jnp.stack([two, cross(two)], axis=1), [0])]
-    att_far = cross(packed[2])
-    att = [packed[0], core(jnp.stack([packed[1], att_far[1]])), att_far]
-    weights, plan = [], []
+        early = [core(array) for array, _ in ones + twos]
+        att_far = cross(packed[2])
+        att_near = core(jnp.stack([packed[1], att_far[1]]))
+    att = [packed[0], att_near, att_far]
+    weights = [array for array, _ in ones + twos] + early
+    plan = []
     for near in range(2):
-        for a, (array, masks) in enumerate(ones):
-            weights.append(core(after(array, q_kept)) if near else array)
+        for a, (_, masks) in enumerate(ones):
             far = a // (len(ones) // 2)
             plan.append([((z,), False, near + 2 * far, mask) for z, mask in enumerate(masks)])
-        for array, masks in twos:
-            weights.append(core(after(array, q_kept)) if near else array)
+        for _, masks in twos:
             plan.append(
                 [
                     ((z, far), True, near + 2 * far, mask)
@@ -711,7 +844,7 @@
                     for far in range(2)
                 ]
             )
-    layer_out, d_one, sums, g_b_up, sent, own_sum, *back = middle(
+    layer_out, d_one, sent_d, kept_d, sent_u, kept_u, *back = middle(
         blocks, weights, plan, att, tokens, out_grad, positions, seq_lengths, vectors, hidden
     )
     grads = [back[0]] + [swap(back[j], "tensor", j) for j in (1, 2, 3)]
@@ -722,114 +855,164 @@
             total = total + term.astype(F32)
         return total
 
+    def send(away, name):
+        return cross(away) if name == "x" else swap(away, "dp", 1 << name)
+
     def axes_of(array, lead):
         return array.reshape(array.shape[:lead] + (2,) * bits + array.shape[lead + 1 :])
 
-    class Sum:
-        def __init__(self, terms, names):
-            self.terms, self.names = terms, list(names)
-
-        def split(self, name):
-            at = self.names.index(name)
-            pick = functools.partial(lax.index_in_dim, axis=at, keepdims=False)
-            away = add(*[pick(t, 1) for t in self.terms]).astype(BF16)
-            self.terms = [pick(t, 0) for t in self.terms]
-            self.names.remove(name)
-            return away
-
-        def join(self, got):
-            self.terms.append(got)
-
-    def send(away, name):
-        return cross(away) if name == "x" else swap(away, "dp", 1 << name)
-
     names = list(range(bits))[::-1]
     late = list(range(1, bits))
-    got_sum = core(sent)
+    shape = jax.ShapeDtypeStruct
+    three = 3 * HEAD_DIM
+
+    got_d, got_u = core(sent_d), core(sent_u)
+    before = []
     if placed:
-        terms = [axes_of(own_sum, 1), axes_of(got_sum, 1)]
-        down = Sum([t[..., :hidden] for t in terms], ["x"] + names)
-        up = Sum([t[..., hidden:] for t in terms], ["x"] + names)
-        pair = down.split("x"), up.split(0)
-        grads, pair = after((grads, pair), d_one)
-
-    small = jnp.concatenate([sums[:9], jnp.zeros((1, width), F32)])
-    ups = g_b_up[:, 0]
-    got_small = core(jnp.concatenate([small, ups[1:2], ups[3:4]]))
-
-    g_bias, before = [], []
+        down, up = Sum(["x"] + names, hidden), Sum(["x"] + names, hidden + own_cols)
+        for total, arrays in ((down, (kept_d, got_d)), (up, (kept_u, got_u))):
+            for array in arrays:
+                total.join(axes_of(array, 1))
+        move_d, move_u = reduce_call("sum_first", [[down.away("x")], [up.away(0)]], BF16)
+        move_d, move_u = after((move_d, move_u), grads)
+        grads = after(grads, move_d)
+        down_names, up_names = ["x"] + late + [0], [0, "x"] + late
     for h in range(heads):
         q_kept = kept[h][0]
         if placed and h == heads - 1:
-            down.join(after(send(pair[0], "x"), *before[:1]))
-            up.join(after(send(pair[1], 0), *before[:1]))
-            pair = down.split(0), up.split("x")
-            q_kept, pair = after((q_kept, pair), *before[:1])
-        g_all, b_head, g_w = attention_backward(
+            last = before[:1]
+            down.join(after(send(move_d, down_names.pop(0)), *last))
+            up.join(after(send(move_u, up_names.pop(0)), *last))
+            groups = [[down.away(down_names[0])], [up.away(up_names[0])]]
+            move_d, move_u = reduce_call("sum_second", groups, BF16)
+            q_kept = after(q_kept, move_d)
+        g_all, g_w = attention_backward(
             h, q_kept, k, v, kept[h][1], grads, parts, blocks, before
         )
         before = [g_all, g_w]
-        g_bias.append(b_head)
-        if h == 0:
-            got = after(got_small, g_all)
-            small, ups = small + got[:10], ups[0::2] + got[10:]
-            got_small = cross(jnp.concatenate([small, ups[1:2]]))
-    got_small = after(got_small, g_all)
     if placed:
-        down.join(after(send(pair[0], 0), g_all))
-        up.join(after(send(pair[1], "x"), g_all))
-
-        def both(name):
-            return jnp.concatenate([down.split(name), up.split(name)], axis=-1)
-
-        def join_both(got):
-            down.join(got[..., :hidden])
-            up.join(got[..., hidden:])
-
-        move = both(late[0])
-        g_w, got_small, g_bias, g_all = after((g_w, got_small, g_bias, g_all), move)
-        qkv = Sum([axes_of(g_w, 1)], ["h"] + names)
-        qkv_move = qkv.split(0)
-        g_all, qkv_move = after((g_all, qkv_move), move)
-    small = jnp.concatenate([small + got_small[:10], ups[:1] + got_small[10:]])
-    spare = width - heads * 3 * HEAD_DIM
-    bias_row = jnp.pad(jnp.concatenate(g_bias, axis=1), ((0, 0), (0, spare)))
-    small = jnp.concatenate([small, bias_row])
-    g_all, small = after((g_all, small), d_one)
-    first = input_part(g_all, w_qkv, w_masks, (3, 2), placed)
-    crossed = add(first[1], core(first[0])).astype(BF16)
-    g_all, crossed = after((g_all, crossed), *first)
-    second = input_part(g_all, w_qkv, w_masks, (1, 0), placed)
-    crossed = cross(crossed)
+        got_d = after(send(move_d, down_names.pop(0)), g_all)
+        got_u = after(send(move_u, up_names.pop(0)), g_all)
+        down.join(got_d)
+        up.join(got_u)
+        g_all, got_d, got_u = after((g_all, got_d, got_u), g_w)
+        g_all = after(g_all, got_d, got_u)
+    half = rows // 2
+    first = input_part(g_all, w_qkv, w_masks, ((3 * rows, rows), (2 * rows, rows)), placed)
+    got_part = core(first[0])
+    own_parts = ((rows, half), (rows + half, half), (0, rows))
     if placed:
-        qkv.join(after(send(qkv_move, 0), *second))
-        qkv_move = qkv.split(late[0])
-        join_both(after(send(move, late[0]), qkv_move))
-        for at, name in enumerate(late[1:]):
-            move = both(name)
-            qkv.join(after(send(qkv_move, late[at]), move))
-            qkv_move = qkv.split(name)
-            join_both(after(send(move, name), qkv_move))
-        qkv.join(send(qkv_move, late[-1]))
-    small = small + after(swap(small, "dp", 1), *second)
-    for bit in range(1, bits):
-        small = small + swap(small, "dp", 1 << bit)
-    near = core(second[0])
-    input_grad = add(d_one, second[1], near, crossed).astype(BF16)
+        qkv = Sum(["h"] + names, 4 * HEAD_DIM)
+        qkv.join(axes_of(g_w, 1))
+        groups = [[down.away(down_names[0])], [up.away(up_names[0])], [qkv.away(0)]]
+        groups.append([[(first[1], (), 0, width), (got_part, (), 0, width)]])
+        move_d, move_u, move_qkv, crossed = reduce_call("sum_third", groups, BF16)
+        crossed = cross(crossed)
+        g_all = after(g_all, move_d)
+        second = input_part(g_all, w_qkv, w_masks, own_parts, placed)
+        near = [core(part) for part in second[:2]]
+        down.join(after(send(move_d, down_names.pop(0)), *second))
+        up.join(after(send(move_u, up_names.pop(0)), *second))
+        qkv.join(after(send(move_qkv, 0), *second))
+        crossed = after(crossed, *second)
+        others = list(itertools.product(range(2), repeat=len(late)))[1:]
+        groups = [[down.away(down_names[0])], [up.away(up_names[0])]]
+        groups += [[qkv.parts({**qkv.picks, **dict(zip(late, pick))})] for pick in others]
+        move_d, move_u, *moves_qkv = reduce_call("sum_fourth", groups, BF16)
+        down.join(send(move_d, down_names.pop(0)))
+        got_u = send(move_u, up_names.pop(0))
+        gots_qkv = [
+            swap(move, "dp", sum(bit << name for bit, name in zip(pick, late)))
+            for move, pick in zip(moves_qkv, others)
+        ]
+        qkv.picks.update(dict.fromkeys(late, 0))
+        for name in late:
+            qkv.names.remove(name)
+
+        def finish_down(totals, ins, outs):
+            outs[0][...] = totals[0][:share]
+            outs[1][...] = totals[0][share:]
+            for i in range(2):
+                part = pl.ds(i * half, half)
+                total = ins[0][part, :]
+                for term in (ins[1][part, :], ins[2][part, :], ins[3 + i][...]):
+                    total += term.astype(F32)
+                outs[2][part, :] = total.astype(BF16)
+
+        g_down, small, input_grad = reduce_call(
+            "finish_down",
+            [[down.all()]],
+            F32,
+            finish_down,
+            (d_one, second[2], crossed, *near),
+            (
+                shape((share, hidden), F32),
+                shape((EXTRA, width), F32),
+                shape((rows, width), BF16),
+            ),
+            keep=False,
+        )
+        g_down = g_down.T
+        got_u, gots_qkv = after((got_u, gots_qkv), small)
+        up.join(got_u)
+        for got in gots_qkv:
+            qkv.join(got)
+    else:
+        crossed = cross(add(first[1], got_part).astype(BF16))
+        second = input_part(g_all, w_qkv, w_masks, own_parts, placed)
+        near = jnp.concatenate([core(part) for part in second[:2]])
+
     if placed:
-        g_down = add(*down.terms)
-        g_up = add(*up.terms)
-        g_qkv = add(*qkv.terms).reshape(heads, share, 3, HEAD_DIM)
+
+        def finish(totals, _, outs):
+            g_up, g_qkv = totals
+            q_out, k_out, v_out, o_out, up_out, bq_out, bv_out = outs
+            for h in range(heads):
+                at = pl.ds(h * HEAD_DIM, HEAD_DIM)
+                for kind, out in enumerate((q_out, k_out, v_out)):
+                    out[:, at] = g_qkv[h, :, kind * HEAD_DIM : (kind + 1) * HEAD_DIM]
+                bq_out[:, at] = g_qkv[h, 0:1, three:]
+                bv_out[:, at] = g_qkv[h, 8:9, three:]
+            up_out[...] = g_up[:, :hidden]
+            o_out[...] = g_up[:, hidden:].T
+
+        g_q, g_k, g_v, g_out, g_up, bias_q, bias_v = reduce_call(
+            "finish",
+            [[up.all()], [qkv.all()]],
+            F32,
+            finish,
+            (),
+            (
+                [shape((share, own_cols), F32)] * 3
+                + [shape((own_cols, share), F32), shape((share, hidden), F32)]
+                + [shape((1, own_cols), F32)] * 2
+            ),
+            keep=False,
+        )
+        bias_q, bias_v = bias_q[0], bias_v[0]
     else:
+        input_grad = add(d_one, second[2], near, crossed).astype(BF16)
         two_s = (2,) * bits
-        total = add(own_sum, got_sum)
-        total = total[0] + cross(total[1].astype(BF16)).astype(F32)
-        total = scatter_bits(total.reshape(two_s + (share, -1)), "dp", range(bits), 0)
-        g_down, g_up = total[:, :hidden], total[:, hidden:]
-        g_qkv = g_w.reshape((heads,) + two_s + (share, -1))
-        g_qkv = scatter_bits(g_qkv, "dp", range(bits), 1).reshape(heads, share, 3, HEAD_DIM)
-    g_q, g_k, g_v = (g_qkv[:, :, i].transpose(1, 0, 2).reshape(share, own_cols) for i in range(3))
-    bias_rows = small[11, : heads * 3 * HEAD_DIM].reshape(heads, 3, HEAD_DIM)
+
+        def whole_sum(mine, got):
+            total = add(mine, got)
+            return total[0, 0] + cross(total[1, 0].astype(BF16)).astype(F32)
+
+        def home(total, lead):
+            shaped = total.reshape(total.shape[:lead] + two_s + (share, total.shape[-1]))
+            return scatter_bits(shaped, "dp", range(bits), lead)
+
+        total = whole_sum(kept_d, got_d)
+        g_down, small = home(total[:width], 0).T, total[width:]
+        total = home(whole_sum(kept_u, got_u), 0)
+        g_up, g_out = total[:, :hidden], total[:, hidden:].T
+        g_qkv = home(g_w[:, 0, :, :three].astype(F32), 1).reshape(heads, share, 3, HEAD_DIM)
+        g_q, g_k, g_v = (g_qkv[:, :, i].transpose(1, 0, 2).reshape(share, own_cols) for i in range(3))
+        bias_rows = g_w[:, 0, 0:16:8, three:].astype(F32)
+        for bit in range(bits):
+            small = small + swap(small, "dp", 1 << bit)
+            bias_rows = bias_rows + swap(bias_rows, "dp", 1 << bit)
+        bias_q, bias_v = bias_rows[:, 0].reshape(own_cols), bias_rows[:, 1].reshape(own_cols)
     count = jnp.sum(seq_lengths).astype(F32) * width
     rms = jnp.sqrt(jnp.sum(small[6:9], axis=-1) / count)
     return (
@@ -838,13 +1021,13 @@
         g_q,
         g_k,
         g_v,
-        g_up[:, hidden:].T,
-        g_up[:, :hidden],
-        g_down.T,
-        bias_rows[:, 0].reshape(own_cols),
-        bias_rows[:, 2].reshape(own_cols),
+        g_out,
+        g_up,
+        g_down,
+        bias_q,
+        bias_v,
         small[0],
-        small[10],
+        small[9],
         small[1],
         small[2],
         small[3],

time: 327 us -> 295 us (0.902)
  other arithmetic: 41.4 us -> 10.4 us
  local copies, waits for them, and re-layouts: 37.6 us -> 13.9 us
  Pallas kernels: 131 us -> 154 us
    pallas_call x0 -> x6, Pallas kernels: none -> 21.8 us  [reduce_call(): pl.pallas_call(functools.partial(reduce_kernel if keep else reduce_inside...]
    convert_element_type x10 -> x0, other arithmetic: 20.2 us -> none  [the longest x8 15.8 us: split(): away = add(*[pick(t, 1) for t in self.terms]).astype(BF16)]
    squeeze x7 -> x0, local copies, waits for them, and re-layouts: 9.3 us -> none  [split(): self.terms = [pick(t, 0) for t in self.terms]]
    add x11 -> x0, other arithmetic: 7.08 us -> none  [the longest x4 5.42 us: add(): total = total + term.astype(F32)]
    slice x11 -> x1, local copies, waits for them, and re-layouts: 6.15 us -> 0.01 us  [body(): att_near = core(jnp.stack([packed[1], att_far[1]]))]
    another operation x8, local copies, waits for them, and re-layouts: 4.75 us -> 0.68 us  [body(): jnp.stack([vec.astype(F32) for vec in vectors] + [jnp.zeros((width,), F32...]
    unnamed x90 -> x77, local copies, waits for them, and re-layouts: 11.9 us -> 8.64 us
  transfers between devices with their start and end apart: 47 -> 47, of which waited for: 14 -> 18; matrix products, arithmetic and copies ran while one was open for 20% -> 6% of each run, Pallas kernels for 27% -> 35%
where the time goes in v3:
time: 295 us; the launch traced here: 289 us
  Pallas kernels  154 us (52%)
  waiting for transfers between devices  65.2 us (22%)
  starting transfers between devices  43.6 us (15%)
  local copies, waits for them, and re-layouts  13.9 us (5%)
  other arithmetic  10.4 us (4%)
    ppermute x47, waiting for transfers between devices, swap(): return lax.ppermute(value, axis, [(i, i ^ bits) for i in range(size)])  65.2 us
    pallas_call x3, Pallas kernels, attention_backward(): pl.pallas_call(functools.partial(backward_kernel, placed=blocks > 1), gri...  51.7 us
    ppermute x47, starting transfers between devices, swap(): return lax.ppermute(value, axis, [(i, i ^ bits) for i in range(size)])  43.6 us
    pallas_call x1, Pallas kernels, middle(): pl.pallas_call(functools.partial(middle_kernel, plan=plan, blocks=blocks)...  38.5 us
    pallas_call x3, Pallas kernels, attention_forward(): pl.pallas_call(functools.partial(forward_kernel, unroll=4), grid=(1,), in...  25.3 us
    pallas_call x6, Pallas kernels, reduce_call(): pl.pallas_call(functools.partial(reduce_kernel if keep else reduce_inside...  21.8 us
    pallas_call x2, Pallas kernels, input_part(): pl.pallas_call(functools.partial(input_kernel, masks=masks, which=which,...  10.1 us
    unnamed x77, local copies, waits for them, and re-layouts  8.64 us
  transfers between devices with their start and end apart: 47, of which 18 were waited for; matrix products, arithmetic and copies ran while one was open for 6% of the time, Pallas kernels for 35%

profile of v3, /device:TPU:0, one launch (start us, length us, event | category | flops | bytes accessed | tf_op | source)
XLA Modules:
  0.0 289.5 jit_solution(13246220552152241238)
XLA Ops:
  0.7 3.0 %collective-permute-start.3 = (bf16[512,768]{1,0:T(8,128)(2,1)}, bf16[512,768]{1,0:T(8,128)(2,1)S(1)}, u32[]{:S(2)}, u32[]{:S(2)}) collective-permute-start(bf16[512,768]{1,0:T(8,128)(2,1)} %refs_4_.5), channel_id=1, source_target_pairs={{0,2},{1,3},{2,0},{3,1},{4,6},{5,7},{6,4},{7,5},{8,10},{9,11},{10,... | collective-permute-start | bytes 2359304 | tf_op jit(solution)/shard_map/ppermute | solution.py:56
  3.7 0.9 fusion.5
  4.6 2.7 collective-permute-start
  7.3 0.9 copy.47
  9.0 1.0 maximum_bitcast_fusion.1
  10.0 3.0 %collective-permute-done = bf16[1,96,576]{2,1,0:T(8,128)(2,1)S(1)} collective-permute-done((bf16[1,96,576]{2,1,0:T(8,128)(2,1)S(1)}, bf16[1,96,576]{2,1,0:T(8,128)(2,1)S(1)}, u32[]{:S(2)}, u32[]{:S(2)}) %collective-permute-start) | collective-permute-done | bytes 110624 | tf_op jit(solution)/shard_map/ppermute | solution.py:56
  13.8 3.4 %collective-permute-start.2 = (bf16[1,96,1024]{2,1,0:T(8,128)(2,1)S(1)}, bf16[1,96,1024]{2,1,0:T(8,128)(2,1)S(1)}, u32[]{:S(2)}, u32[]{:S(2)}) collective-permute-start(bf16[1,96,1024]{2,1,0:T(8,128)(2,1)S(1)} %maximum_bitcast_fusion.1), channel_id=1, source_target_pairs={{0,16},{4,20},{8,24},{12,28},{16,0},{20,4},{24,8},{28,12},{1,17},{... | collective-permute-start | bytes 589832 | tf_op jit(solution)/shard_map/ppermute | solution.py:56
  17.1 6.3 %collective-permute-done.2 = bf16[1,96,1024]{2,1,0:T(8,128)(2,1)S(1)} collective-permute-done((bf16[1,96,1024]{2,1,0:T(8,128)(2,1)S(1)}, bf16[1,96,1024]{2,1,0:T(8,128)(2,1)S(1)}, u32[]{:S(2)}, u32[]{:S(2)}) %collective-permute-start.2) | collective-permute-done | bytes 196640 | tf_op jit(solution)/shard_map/ppermute | solution.py:56
  24.4 1.6 collective-permute-start.4
  26.0 0.9 fusion.1
  26.9 3.5 %collective-permute-start.5 = (bf16[2,96,1024]{2,1,0:T(8,128)(2,1)}, bf16[2,96,1024]{2,1,0:T(8,128)(2,1)}, u32[]{:S(2)}, u32[]{:S(2)}) collective-permute-start(bf16[2,96,1024]{2,1,0:T(8,128)(2,1)} %get-tuple-element.264), channel_id=1, source_target_pairs={{0,8},{4,12},{8,0},{12,4},{16,24},{20,28},{24,16},{28,20},{1,9},{5... | collective-permute-start | bytes 1179656 | tf_op jit(solution)/shard_map/ppermute | solution.py:56
  32.8 3.3 %collective-permute-done.6 = bf16[1,96,768]{2,1,0:T(8,128)(2,1)} collective-permute-done((bf16[1,96,768]{2,1,0:T(8,128)(2,1)S(1)}, bf16[1,96,768]{2,1,0:T(8,128)(2,1)}, u32[]{:S(2)}, u32[]{:S(2)}) %collective-permute-start.6) | collective-permute-done | bytes 147488 | tf_op jit(solution)/shard_map/ppermute | solution.py:56
  36.1 4.0 %collective-permute-done.5 = bf16[2,96,1024]{2,1,0:T(8,128)(2,1)} collective-permute-done((bf16[2,96,1024]{2,1,0:T(8,128)(2,1)}, bf16[2,96,1024]{2,1,0:T(8,128)(2,1)}, u32[]{:S(2)}, u32[]{:S(2)}) %collective-permute-start.5) | collective-permute-done | bytes 393248 | tf_op jit(solution)/shard_map/ppermute | solution.py:56
  40.2 1.7 pad_maximum_fusion
  41.8 0.9 copy.49
  43.9 0.9 fusion.6
  44.8 1.8 collective-permute-start.9
  46.7 6.8 %project.1 = (bf16[3,2048,128]{2,1,0:T(8,128)(2,1)}, bf16[3,2048,128]{2,1,0:T(8,128)(2,1)}, bf16[3,2048,128]{2,1,0:T(8,128)(2,1)}) custom-call(bf16[512,768]{1,0:T(8,128)(2,1)} %refs_4_.5, bf16[512,768]{1,0:T(8,128)(2,1)} %collective-permute-done.8.refs_1_.refs_5_, bf16[512,768]{1,0:T(8,128)(2,1)} %copy-done.1, bf16[512,768]{1,0:T(8,128)(2,1)} %copy-done.2, ...), custom_call_target="tpu_custom_call" | custom-call | flops 1000 | bytes 1000 | tf_op jit(solution)/shard_map/project/pallas_call | solution.py:146
  53.4 8.5 %attention_forward.3 = (bf16[2048,128]{1,0:T(8,128)(2,1)}, f32[2048,128]{1,0:T(8,128)}, bf16[3,256,128]{2,1,0:T(8,128)(2,1)}, bf16[3,256,128]{2,1,0:T(8,128)(2,1)}, bf16[2,3,256,128]{3,2,1,0:T(8,128)(2,1)}) custom-call(bf16[3,2048,128]{2,1,0:T(8,128)(2,1)} %get-tuple-element.166.q_ref, bf16[3,2048,128]{2,1,0:T(8,128)(2,1)} %get-tuple-element.151.k_ref, ...), custom_call_target="tpu_custom_call" | custom-call | flops 1000 | bytes 1000 | tf_op jit(solution)/shard_map/attention_forward/pallas_call | solution.py:216
  62.5 1.1 collective-permute-start.14
  63.6 1.0 maximum_bitcast_fusion.refs_4_
  64.6 2.4 collective-permute-start.13
  67.0 0.9 collective-permute-start.15
  67.9 8.4 %attention_forward.4 = (bf16[2048,128]{1,0:T(8,128)(2,1)}, f32[2048,128]{1,0:T(8,128)}, bf16[3,256,128]{2,1,0:T(8,128)(2,1)}, bf16[3,256,128]{2,1,0:T(8,128)(2,1)}, bf16[2,3,256,128]{3,2,1,0:T(8,128)(2,1)}) custom-call(bf16[3,2048,128]{2,1,0:T(8,128)(2,1)} %get-tuple-element.166.q_ref, ...), custom_call_target="tpu_custom_call", output_to_operand_aliasing={{2}: (3, {}), {3}: (4, {}), {4}: (5, {})} | custom-call | flops 1000 | bytes 1000 | tf_op jit(solution)/shard_map/attention_forward/pallas_call | solution.py:216
  76.3 8.4 %attention_forward.5 = (bf16[2048,128]{1,0:T(8,128)(2,1)}, f32[2048,128]{1,0:T(8,128)}, bf16[3,256,128]{2,1,0:T(8,128)(2,1)}, bf16[3,256,128]{2,1,0:T(8,128)(2,1)}, bf16[2,3,256,128]{3,2,1,0:T(8,128)(2,1)}) custom-call(bf16[3,2048,128]{2,1,0:T(8,128)(2,1)} %get-tuple-element.166.q_ref, ...), custom_call_target="tpu_custom_call", output_to_operand_aliasing={{2}: (3, {}), {3}: (4, {}), {4}: (5, {})} | custom-call | flops 1000 | bytes 1000 | tf_op jit(solution)/shard_map/attention_forward/pallas_call | solution.py:216
  85.3 2.6 collective-permute-done.17.refs_12_
  87.9 0.9 copy-done.16
  88.9 1.1 collective-permute-start.19
  90.5 1.0 collective-permute-start.20
  91.5 10.3 %collective-permute-done.20.refs_18_ = bf16[2,3,256,128]{3,2,1,0:T(8,128)(2,1)S(1)} collective-permute-done((bf16[2,3,256,128]{3,2,1,0:T(8,128)(2,1)}, bf16[2,3,256,128]{3,2,1,0:T(8,128)(2,1)S(1)}, u32[]{:S(2)}, u32[]{:S(2)}) %collective-permute-start.20) | collective-permute-done | bytes 393248 | tf_op jit(solution)/shard_map/ppermute | solution.py:56
  101.9 2.9 collective-permute-done.19.refs_7_
  105.8 0.9 copy-done.15
  106.7 1.0 pad_maximum_fusion.3
  108.2 1.3 collective-permute-done.25.refs_17_
  111.1 38.5 %middle.1 = (bf16[512,768]{1,0:T(8,128)(2,1)}, f32[512,768]{1,0:T(8,128)}, bf16[2,8,112,768]{3,2,1,0:T(8,128)(2,1)}, bf16[2,8,112,768]{3,2,1,0:T(8,128)(2,1)}, b...) custom-call(bf16[4,96,1024]{2,1,0:T(8,128)(2,1)} %bitcast.17.refs_0_, ...), custom_call_target="tpu_custom_call" | custom-call | flops 1000 | bytes 1000 | tf_op jit(solution)/shard_map/middle/pallas_call | solution.py:566
  152.1 7.9 %collective-permute-done.26 = bf16[2,8,112,768]{3,2,1,0:T(8,128)(2,1)} collective-permute-done((bf16[2,8,112,768]{3,2,1,0:T(8,128)(2,1)}, bf16[2,8,112,768]{3,2,1,0:T(8,128)(2,1)}, u32[]{:S(2)}, u32[]{:S(2)}) %collective-permute-start.26) | collective-permute-done | bytes 2752544 | tf_op jit(solution)/shard_map/ppermute | solution.py:56
  160.0 4.3 %sum_first.1 = (bf16[2,2,2,112,768]{4,3,2,1,0:T(8,128)(2,1)}, bf16[2,2,2,96,960]{4,3,2,1,0:T(8,128)(2,1)}) custom-call(bf16[2,2,2,2,112,768]{5,4,3,2,1,0:T(8,128)(2,1)} %bitcast.46, bf16[2,2,2,2,112,768]{5,4,3,2,1,0:T(8,128)(2,1)} %bitcast.25.refs_1_, bf16[2,2,2,2,96,960]{5,4,3,2,1,0:T(8,128)(2,1)} %bitcast.41, ...), custom_call_target="tpu_custom_call" | custom-call | flops 1000 | bytes 1000 | tf_op jit(solution)/shard_map/sum_first/pallas_call | solution.py:684
  164.4 1.2 collective-permute-start.32
  165.5 1.0 collective-permute-start.31
  166.5 17.4 %attention_backward.3 = (bf16[3,2048,192]{2,1,0:T(8,128)(2,1)}, bf16[3,8,96,256]{3,2,1,0:T(8,128)(2,1)}) custom-call(bf16[2048,128]{1,0:T(8,128)(2,1)} %get-tuple-element.156.q_ref, bf16[3,2048,128]{2,1,0:T(8,128)(2,1)} %get-tuple-element.151.k_ref, bf16[3,2048,128]{2,1,0:T(8,128)(2,1)} %get-tuple-element.152.v_ref, f32[2048,128]{1,0:T(8,128)} %get-tuple-element.205.o_ref, ...), custom_call_target="tpu_custom_call" | custom-call | flops 1000 | bytes 1000 | tf_op jit(solution)/shard_map/attention_backward/pallas_call | solution.py:301
  184.0 17.1 %attention_backward.4 = (bf16[3,2048,192]{2,1,0:T(8,128)(2,1)}, bf16[3,8,96,256]{3,2,1,0:T(8,128)(2,1)}) custom-call(bf16[2048,128]{1,0:T(8,128)(2,1)} %get-tuple-element.165.q_ref, bf16[3,2048,128]{2,1,0:T(8,128)(2,1)} %get-tuple-element.151.k_ref, bf16[3,2048,128]{2,1,0:T(8,128)(2,1)} %get-tuple-element.152.v_ref, ...), custom_call_target="tpu_custom_call", output_to_operand_aliasing={{0}: (12, {}), {1}: (13, {})} | custom-call | flops 1000 | bytes 1000 | tf_op jit(solution)/shard_map/attention_backward/pallas_call | solution.py:301
  201.4 3.4 %sum_second.1 = (bf16[2,2,112,768]{3,2,1,0:T(8,128)(2,1)}, bf16[2,2,96,960]{3,2,1,0:T(8,128)(2,1)}) custom-call(bf16[2,2,2,2,112,768]{5,4,3,2,1,0:T(8,128)(2,1)} %bitcast.47, bf16[2,2,2,2,112,768]{5,4,3,2,1,0:T(8,128)(2,1)} %bitcast.25.refs_1_, bf16[2,2,2,112,768]{4,3,2,1,0:T(8,128)(2,1)} %collective-permute-done.31.refs_2_, ...), custom_call_target="tpu_custom_call" | custom-call | flops 1000 | bytes 1000 | tf_op jit(solution)/shard_map/sum_second/pallas_call | solution.py:684
  206.2 17.2 %attention_backward.5 = (bf16[3,2048,192]{2,1,0:T(8,128)(2,1)}, bf16[3,8,96,256]{3,2,1,0:T(8,128)(2,1)}) custom-call(bf16[2048,128]{1,0:T(8,128)(2,1)} %get-tuple-element.213.q_ref, bf16[3,2048,128]{2,1,0:T(8,128)(2,1)} %get-tuple-element.151.k_ref, bf16[3,2048,128]{2,1,0:T(8,128)(2,1)} %get-tuple-element.152.v_ref, ...), custom_call_target="tpu_custom_call", output_to_operand_aliasing={{0}: (12, {}), {1}: (13, {})} | custom-call | flops 1000 | bytes 1000 | tf_op jit(solution)/shard_map/attention_backward/pallas_call | solution.py:301
  224.1 5.3 %input_part.2 = (bf16[512,768]{1,0:T(8,128)(2,1)}, bf16[512,768]{1,0:T(8,128)(2,1)}) custom-call(bf16[3,2048,192]{2,1,0:T(8,128)(2,1)} %get-tuple-element.225.g_ref, bf16[4,96,576]{2,1,0:T(8,128)(2,1)} %bitcast.56, bf16[4,96,576]{2,1,0:T(8,128)(2,1)} %copy-done.5), custom_call_target="tpu_custom_call" | custom-call | flops 1000 | bytes 1000 | tf_op jit(solution)/shard_map/input_part/pallas_call | solution.py:349
  229.5 2.5 collective-permute-done.35.refs_10_
  232.0 0.9 copy-done.13
  232.8 3.9 %sum_third.1 = (bf16[2,112,768]{2,1,0:T(8,128)(2,1)}, bf16[2,96,960]{2,1,0:T(8,128)(2,1)}, bf16[3,2,2,96,256]{4,3,2,1,0:T(8,128)(2,1)}, bf16[512,768]{1,0:T(8,128)(2,1)}) custom-call(bf16[2,2,2,2,112,768]{5,4,3,2,1,0:T(8,128)(2,1)} %bitcast.48, bf16[2,2,2,2,112,768]{5,4,3,2,1,0:T(8,128)(2,1)} %bitcast.25.refs_1_, ...), custom_call_target="tpu_custom_call" | custom-call | flops 1000 | bytes 1000 | tf_op jit(solution)/shard_map/sum_third/pallas_call | solution.py:684
  236.7 1.0 collective-permute-start.40
  237.7 1.2 collective-permute-start.38
  238.9 1.7 collective-permute-start.36
  241.2 4.8 %input_part.3 = (bf16[256,768]{1,0:T(8,128)(2,1)}, bf16[256,768]{1,0:T(8,128)(2,1)}, bf16[512,768]{1,0:T(8,128)(2,1)}) custom-call(bf16[3,2048,192]{2,1,0:T(8,128)(2,1)} %get-tuple-element.225.g_ref, bf16[4,96,576]{2,1,0:T(8,128)(2,1)} %bitcast.57, bf16[4,96,576]{2,1,0:T(8,128)(2,1)} %copy-done.5), custom_call_target="tpu_custom_call" | custom-call | flops 1000 | bytes 1000 | tf_op jit(solution)/shard_map/input_part/pallas_call | solution.py:349
  246.0 11.1 %collective-permute-done.36.refs_4_ = bf16[2,112,768]{2,1,0:T(8,128)(2,1)} collective-permute-done((bf16[2,112,768]{2,1,0:T(8,128)(2,1)}, bf16[2,112,768]{2,1,0:T(8,128)(2,1)}, u32[]{:S(2)}, u32[]{:S(2)}) %collective-permute-start.36) | collective-permute-done | bytes 344096 | tf_op jit(solution)/shard_map/ppermute | solution.py:56
  257.1 0.8 collective-permute-done.37.refs_9_.refs_4_
  259.6 2.8 sum_fourth.1
  262.4 0.9 collective-permute-start.39
  263.3 1.3 reduce_sum.19
  265.2 1.3 collective-permute-start.43
  266.5 1.7 collective-permute-start.44
  268.9 2.0 collective-permute-start.46
  271.6 4.8 %finish_down.1 = (f32[96,768]{1,0:T(8,128)}, f32[16,768]{1,0:T(8,128)}, bf16[512,768]{1,0:T(8,128)(2,1)}) custom-call(bf16[2,2,2,2,112,768]{5,4,3,2,1,0:T(8,128)(2,1)} %bitcast.50, bf16[2,2,2,2,112,768]{5,4,3,2,1,0:T(8,128)(2,1)} %bitcast.25.refs_1_, bf16[2,2,2,112,768]{4,3,2,1,0:T(8,128)(2,1)} %collective-permute-done.31.refs_2_, ...), custom_call_target="tpu_custom_call" | custom-call | flops 1000 | bytes 1000 | tf_op jit(solution)/shard_map/finish_down/pallas_call | solution.py:684
  276.4 0.9 slice_reduce_fusion
  277.3 1.6 slice_reduce_fusion.1
  278.9 6.8 %collective-permute-done.44.refs_8_ = bf16[3,96,256]{2,1,0:T(8,128)(2,1)S(1)} collective-permute-done((bf16[3,96,256]{2,1,0:T(8,128)(2,1)}, bf16[3,96,256]{2,1,0:T(8,128)(2,1)S(1)}, u32[]{:S(2)}, u32[]{:S(2)}) %collective-permute-start.44) | collective-permute-done | bytes 147488 | tf_op jit(solution)/shard_map/ppermute | solution.py:56
  286.6 2.6 finish.1
  (151 shorter events, 20.1 us)
Async XLA Ops:
  0.7 23.5 %collective-permute-start.3 = (bf16[512,768]{1,0:T(8,128)(2,1)}, bf16[512,768]{1,0:T(8,128)(2,1)S(1)}, u32[]{:S(2)}, u32[]{:S(2)}) collective-permute-start(bf16[512,768]{1,0:T(8,128)(2,1)} %refs_4_.5), channel_id=1, source_target_pairs={{0,2},{1,3},{2,0},{3,1},{4,6},{5,7},{6,4},{7,5},{8,10},{9,11},{10,... | collective-permute-start | bytes 2359304 | tf_op jit(solution)/shard_map/ppermute | solution.py:56
  4.6 8.4 %collective-permute-start = (bf16[1,96,576]{2,1,0:T(8,128)(2,1)S(1)}, bf16[1,96,576]{2,1,0:T(8,128)(2,1)S(1)}, u32[]{:S(2)}, u32[]{:S(2)}) collective-permute-start(bf16[1,96,576]{2,1,0:T(8,128)(2,1)S(1)} %get-tuple-element.270), channel_id=1, source_target_pairs={{0,16},{4,20},{8,24},{12,28},{16,0},{20,4},{24,8},{28,12},{1,17},{... | collective-permute-start | bytes 331784 | tf_op jit(solution)/shard_map/ppermute | solution.py:56
  13.0 11.1 %collective-permute-start.1 = (bf16[2,96,576]{2,1,0:T(8,128)(2,1)S(1)}, bf16[2,96,576]{2,1,0:T(8,128)(2,1)S(1)}, u32[]{:S(2)}, u32[]{:S(2)}) collective-permute-start(bf16[2,96,576]{2,1,0:T(8,128)(2,1)S(1)} %get-tuple-element.268), channel_id=1, source_target_pairs={{0,8},{4,12},{8,0},{12,4},{16,24},{20,28},{24,16},{28,20},{1,9},{5... | collective-permute-start | bytes 663560 | tf_op jit(solution)/shard_map/ppermute | solution.py:56
  13.8 9.7 %collective-permute-start.2 = (bf16[1,96,1024]{2,1,0:T(8,128)(2,1)S(1)}, bf16[1,96,1024]{2,1,0:T(8,128)(2,1)S(1)}, u32[]{:S(2)}, u32[]{:S(2)}) collective-permute-start(bf16[1,96,1024]{2,1,0:T(8,128)(2,1)S(1)} %maximum_bitcast_fusion.1), channel_id=1, source_target_pairs={{0,16},{4,20},{8,24},{12,28},{16,0},{20,4},{24,8},{28,12},{1,17},{... | collective-permute-start | bytes 589832 | tf_op jit(solution)/shard_map/ppermute | solution.py:56
  24.1 16.0 %collective-permute-start.7 = (bf16[512,768]{1,0:T(8,128)(2,1)S(1)}, bf16[512,768]{1,0:T(8,128)(2,1)S(1)}, u32[]{:S(2)}, u32[]{:S(2)}) collective-permute-start(bf16[512,768]{1,0:T(8,128)(2,1)S(1)} %collective-permute-done.3.refs_2_.refs_6_), channel_id=1, source_target_pairs={{0,1},{1,0},{2,3},{3,2},{4,5},{5,4},{6,7},{7,6},{8,9},{9,8},{10,11... | collective-permute-start | bytes 2359304 | tf_op jit(solution)/shard_map/ppermute | solution.py:56
  24.1 6.2 %copy-start.25 = (bf16[768,96]{0,1:T(8,128)(2,1)S(1)}, bf16[768,96]{0,1:T(8,128)(2,1)}, u32[]{:S(2)}) copy-start(bf16[768,96]{0,1:T(8,128)(2,1)} %param.27) | copy-start | bytes 442372
  24.1 6.8 %copy-start = (bf16[512,768]{1,0:T(8,128)(2,1)S(1)}, bf16[512,768]{1,0:T(8,128)(2,1)}, u32[]{:S(2)}) copy-start(bf16[512,768]{1,0:T(8,128)(2,1)} %refs_4_.5) | copy-start | bytes 2359300
  24.2 6.8 %copy-start.30 = (bf16[768]{0:T(1024)(128)(2,1)S(1)}, bf16[768]{0:T(1024)(128)(2,1)}, u32[]{:S(2)}) copy-start(bf16[768]{0:T(1024)(128)(2,1)} %param.30) | copy-start | bytes 4612
  24.2 6.8 %copy-start.31 = (bf16[768]{0:T(1024)(128)(2,1)S(1)}, bf16[768]{0:T(1024)(128)(2,1)}, u32[]{:S(2)}) copy-start(bf16[768]{0:T(1024)(128)(2,1)} %param.32) | copy-start | bytes 4612
  24.2 6.8 %copy-start.32 = (bf16[768]{0:T(1024)(128)(2,1)S(1)}, bf16[768]{0:T(1024)(128)(2,1)}, u32[]{:S(2)}) copy-start(bf16[768]{0:T(1024)(128)(2,1)} %param.33) | copy-start | bytes 4612
  24.2 6.8 %copy-start.33 = (bf16[768]{0:T(1024)(128)(2,1)S(1)}, bf16[768]{0:T(1024)(128)(2,1)}, u32[]{:S(2)}) copy-start(bf16[768]{0:T(1024)(128)(2,1)} %param.34) | copy-start | bytes 4612
  24.2 6.8 %copy-start.34 = (bf16[768]{0:T(1024)(128)(2,1)S(1)}, bf16[768]{0:T(1024)(128)(2,1)}, u32[]{:S(2)}) copy-start(bf16[768]{0:T(1024)(128)(2,1)} %param.35) | copy-start | bytes 4612
  24.2 6.8 %copy-start.35 = (bf16[768]{0:T(1024)(128)(2,1)S(1)}, bf16[768]{0:T(1024)(128)(2,1)}, u32[]{:S(2)}) copy-start(bf16[768]{0:T(1024)(128)(2,1)} %param.36) | copy-start | bytes 4612
  24.2 6.8 %copy-start.36 = (bf16[192]{0:T(256)(128)(2,1)S(1)}, bf16[192]{0:T(256)(128)(2,1)}, u32[]{:S(2)}) copy-start(bf16[192]{0:T(256)(128)(2,1)} %param.28) | copy-start | bytes 1156
  24.2 7.4 %copy-start.37 = (bf16[192]{0:T(256)(128)(2,1)S(1)}, bf16[192]{0:T(256)(128)(2,1)}, u32[]{:S(2)}) copy-start(bf16[192]{0:T(256)(128)(2,1)} %param.29) | copy-start | bytes 1156
  24.4 18.4 %copy-start.3 = (bf16[2,2,96,576]{3,2,1,0:T(8,128)(2,1)}, bf16[2,2,96,576]{3,2,1,0:T(8,128)(2,1)S(1)}, u32[]{:S(2)}) copy-start(bf16[2,2,96,576]{3,2,1,0:T(8,128)(2,1)S(1)} %copy.48) | copy-start | bytes 1327108
  24.4 15.7 %collective-permute-start.4 = (bf16[4,96,576]{2,1,0:T(8,128)(2,1)S(1)}, bf16[4,96,576]{2,1,0:T(8,128)(2,1)S(1)}, u32[]{:S(2)}, u32[]{:S(2)}) collective-permute-start(bf16[4,96,576]{2,1,0:T(8,128)(2,1)S(1)} %bitcast.54), channel_id=1, source_target_pairs={{0,4},{4,0},{8,12},{12,8},{16,20},{20,16},{24,28},{28,24},{1,5},{5... | collective-permute-start | bytes 1327112 | tf_op jit(solution)/shard_map/ppermute | solution.py:56
  26.9 13.2 %collective-permute-start.5 = (bf16[2,96,1024]{2,1,0:T(8,128)(2,1)}, bf16[2,96,1024]{2,1,0:T(8,128)(2,1)}, u32[]{:S(2)}, u32[]{:S(2)}) collective-permute-start(bf16[2,96,1024]{2,1,0:T(8,128)(2,1)} %get-tuple-element.264), channel_id=1, source_target_pairs={{0,8},{4,12},{8,0},{12,4},{16,24},{20,28},{24,16},{28,20},{1,9},{5... | collective-permute-start | bytes 1179656 | tf_op jit(solution)/shard_map/ppermute | solution.py:56
  30.4 5.8 %collective-permute-start.6 = (bf16[1,96,768]{2,1,0:T(8,128)(2,1)S(1)}, bf16[1,96,768]{2,1,0:T(8,128)(2,1)}, u32[]{:S(2)}, u32[]{:S(2)}) collective-permute-start(bf16[1,96,768]{2,1,0:T(8,128)(2,1)S(1)} %bitcast.64), channel_id=1, source_target_pairs={{0,2},{1,3},{2,0},{3,1},{4,6},{5,7},{6,4},{7,5},{8,10},{9,11},{10,... | collective-permute-start | bytes 442376 | tf_op jit(solution)/shard_map/ppermute | solution.py:56
  30.9 15.7 %collective-permute-start.8 = (bf16[512,768]{1,0:T(8,128)(2,1)S(1)}, bf16[512,768]{1,0:T(8,128)(2,1)}, u32[]{:S(2)}, u32[]{:S(2)}) collective-permute-start(bf16[512,768]{1,0:T(8,128)(2,1)S(1)} %copy-done), channel_id=1, source_target_pairs={{0,1},{1,0},{2,3},{3,2},{4,5},{5,4},{6,7},{7,6},{8,9},{9,8},{10,11... | collective-permute-start | bytes 2359304 | tf_op jit(solution)/shard_map/ppermute | solution.py:56
  40.2 3.7 %copy-start.26 = (bf16[768,96]{0,1:T(8,128)(2,1)S(1)}, bf16[768,96]{0,1:T(8,128)(2,1)}, u32[]{:S(2)}) copy-start(bf16[768,96]{0,1:T(8,128)(2,1)} %param.27) | copy-start | bytes 442372
  42.8 19.5 %collective-permute-start.10 = (bf16[4,96,1024]{2,1,0:T(8,128)(2,1)}, bf16[4,96,1024]{2,1,0:T(8,128)(2,1)}, u32[]{:S(2)}, u32[]{:S(2)}) collective-permute-start(bf16[4,96,1024]{2,1,0:T(8,128)(2,1)} %bitcast.17.refs_0_), channel_id=1, source_target_pairs={{0,4},{4,0},{8,12},{12,8},{16,20},{20,16},{24,28},{28,24},{1,5},{5... | collective-permute-start | bytes 2359304 | tf_op jit(solution)/shard_map/ppermute | solution.py:56
  43.4 19.1 %collective-permute-start.11 = (bf16[4,96,1024]{2,1,0:T(8,128)(2,1)}, bf16[4,96,1024]{2,1,0:T(8,128)(2,1)}, u32[]{:S(2)}, u32[]{:S(2)}) collective-permute-start(bf16[4,96,1024]{2,1,0:T(8,128)(2,1)} %bitcast.17.refs_0_), channel_id=1, source_target_pairs={{0,2},{1,3},{2,0},{3,1},{4,6},{5,7},{6,4},{7,5},{8,10},{9,11},{10,... | collective-permute-start | bytes 2359304 | tf_op jit(solution)/shard_map/ppermute | solution.py:56
  43.9 18.6 %collective-permute-start.12 = (bf16[4,96,1024]{2,1,0:T(8,128)(2,1)}, bf16[4,96,1024]{2,1,0:T(8,128)(2,1)}, u32[]{:S(2)}, u32[]{:S(2)}) collective-permute-start(bf16[4,96,1024]{2,1,0:T(8,128)(2,1)} %bitcast.17.refs_0_), channel_id=1, source_target_pairs={{0,1},{1,0},{2,3},{3,2},{4,5},{5,4},{6,7},{7,6},{8,9},{9,8},{10,11... | collective-permute-start | bytes 2359304 | tf_op jit(solution)/shard_map/ppermute | solution.py:56
  44.8 17.1 %collective-permute-start.9 = (bf16[1,2,96,768]{3,2,1,0:T(8,128)(2,1)S(1)}, bf16[1,2,96,768]{3,2,1,0:T(8,128)(2,1)S(1)}, u32[]{:S(2)}, u32[]{:S(2)}) collective-permute-start(bf16[1,2,96,768]{3,2,1,0:T(8,128)(2,1)S(1)} %get-tuple-element.266), channel_id=1, source_target_pairs={{0,16},{4,20},{8,24},{12,28},{16,0},{20,4},{24,8},{28,12},{1,17},{... | collective-permute-start | bytes 884744 | tf_op jit(solution)/shard_map/ppermute | solution.py:56
  62.5 22.2 %collective-permute-start.14 = (bf16[4,96,1024]{2,1,0:T(8,128)(2,1)}, bf16[4,96,1024]{2,1,0:T(8,128)(2,1)}, u32[]{:S(2)}, u32[]{:S(2)}) collective-permute-start(bf16[4,96,1024]{2,1,0:T(8,128)(2,1)} %collective-permute-done.10.refs_1_), channel_id=1, source_target_pairs={{0,2},{1,3},{2,0},{3,1},{4,6},{5,7},{6,4},{7,5},{8,10},{9,11},{10,... | collective-permute-start | bytes 2359304 | tf_op jit(solution)/shard_map/ppermute | solution.py:56
  63.5 21.2 %collective-permute-start.16 = (bf16[4,96,1024]{2,1,0:T(8,128)(2,1)}, bf16[4,96,1024]{2,1,0:T(8,128)(2,1)}, u32[]{:S(2)}, u32[]{:S(2)}) collective-permute-start(bf16[4,96,1024]{2,1,0:T(8,128)(2,1)} %collective-permute-done.11.refs_2_), channel_id=1, source_target_pairs={{0,1},{1,0},{2,3},{3,2},{4,5},{5,4},{6,7},{7,6},{8,9},{9,8},{10,11... | collective-permute-start | bytes 2359304 | tf_op jit(solution)/shard_map/ppermute | solution.py:56
  64.6 20.2 %copy-start.6 = (bf16[2,2,96,768]{3,2,1,0:T(8,128)(2,1)}, bf16[2,2,96,768]{3,2,1,0:T(8,128)(2,1)S(1)}, u32[]{:S(2)}) copy-start(bf16[2,2,96,768]{3,2,1,0:T(8,128)(2,1)S(1)} %maximum_bitcast_fusion.refs_4_) | copy-start | bytes 1769476
  64.6 20.1 %collective-permute-start.13 = (bf16[2,2,96,768]{3,2,1,0:T(8,128)(2,1)S(1)}, bf16[2,2,96,768]{3,2,1,0:T(8,128)(2,1)}, u32[]{:S(2)}, u32[]{:S(2)}) collective-permute-start(bf16[2,2,96,768]{3,2,1,0:T(8,128)(2,1)S(1)} %maximum_bitcast_fusion.refs_4_), channel_id=1, source_target_pairs={{0,8},{4,12},{8,0},{12,4},{16,24},{20,28},{24,16},{28,20},{1,9},{5... | collective-permute-start | bytes 1769480 | tf_op jit(solution)/shard_map/ppermute | solution.py:56
  67.0 17.7 %collective-permute-start.15 = (bf16[2,2,96,768]{3,2,1,0:T(8,128)(2,1)S(1)}, bf16[2,2,96,768]{3,2,1,0:T(8,128)(2,1)}, u32[]{:S(2)}, u32[]{:S(2)}) collective-permute-start(bf16[2,2,96,768]{3,2,1,0:T(8,128)(2,1)S(1)} %maximum_bitcast_fusion.refs_4_), channel_id=1, source_target_pairs={{0,4},{4,0},{8,12},{12,8},{16,20},{20,16},{24,28},{28,24},{1,5},{5... | collective-permute-start | bytes 1769480 | tf_op jit(solution)/shard_map/ppermute | solution.py:56
  84.7 4.1 %collective-permute-start.18 = (bf16[4,96,1024]{2,1,0:T(8,128)(2,1)}, bf16[4,96,1024]{2,1,0:T(8,128)(2,1)S(1)}, u32[]{:S(2)}, u32[]{:S(2)}) collective-permute-start(bf16[4,96,1024]{2,1,0:T(8,128)(2,1)} %collective-permute-done.10.refs_1_), channel_id=1, source_target_pairs={{0,1},{1,0},{2,3},{3,2},{4,5},{5,4},{6,7},{7,6},{8,9},{9,8},{10,11... | collective-permute-start | bytes 2359304 | tf_op jit(solution)/shard_map/ppermute | solution.py:56
  84.8 3.1 %collective-permute-start.17 = (bf16[2,2,96,768]{3,2,1,0:T(8,128)(2,1)S(1)}, bf16[2,2,96,768]{3,2,1,0:T(8,128)(2,1)S(1)}, u32[]{:S(2)}, u32[]{:S(2)}) collective-permute-start(bf16[2,2,96,768]{3,2,1,0:T(8,128)(2,1)S(1)} %maximum_bitcast_fusion.refs_4_), channel_id=1, source_target_pairs={{0,1},{1,0},{2,3},{3,2},{4,5},{5,4},{6,7},{7,6},{8,9},{9,8},{10,11... | collective-permute-start | bytes 1769480 | tf_op jit(solution)/shard_map/ppermute | solution.py:56
  88.8 16.0 %copy-start.14 = (bf16[4,96,1024]{2,1,0:T(8,128)(2,1)}, bf16[4,96,1024]{2,1,0:T(8,128)(2,1)S(1)}, u32[]{:S(2)}) copy-start(bf16[4,96,1024]{2,1,0:T(8,128)(2,1)S(1)} %collective-permute-done.18.refs_9_) | copy-start | bytes 2359300
  88.8 16.0 %collective-permute-start.21 = (bf16[4,96,1024]{2,1,0:T(8,128)(2,1)}, bf16[4,96,1024]{2,1,0:T(8,128)(2,1)S(1)}, u32[]{:S(2)}, u32[]{:S(2)}) collective-permute-start(bf16[4,96,1024]{2,1,0:T(8,128)(2,1)} %collective-permute-done.14.refs_3_), channel_id=1, source_target_pairs={{0,1},{1,0},{2,3},{3,2},{4,5},{5,4},{6,7},{7,6},{8,9},{9,8},{10,11... | collective-permute-start | bytes 2359304 | tf_op jit(solution)/shard_map/ppermute | solution.py:56
  88.9 15.8 %collective-permute-start.19 = (bf16[2,2,96,768]{3,2,1,0:T(8,128)(2,1)}, bf16[2,2,96,768]{3,2,1,0:T(8,128)(2,1)S(1)}, u32[]{:S(2)}, u32[]{:S(2)}) collective-permute-start(bf16[2,2,96,768]{3,2,1,0:T(8,128)(2,1)} %collective-permute-done.13.refs_6_), channel_id=1, source_target_pairs={{0,4},{4,0},{8,12},{12,8},{16,20},{20,16},{24,28},{28,24},{1,5},{5... | collective-permute-start | bytes 1769480 | tf_op jit(solution)/shard_map/ppermute | solution.py:56
  90.0 14.7 %collective-permute-start.22 = (bf16[2,2,96,768]{3,2,1,0:T(8,128)(2,1)}, bf16[2,2,96,768]{3,2,1,0:T(8,128)(2,1)S(1)}, u32[]{:S(2)}, u32[]{:S(2)}) collective-permute-start(bf16[2,2,96,768]{3,2,1,0:T(8,128)(2,1)} %collective-permute-done.13.refs_6_), channel_id=1, source_target_pairs={{0,1},{1,0},{2,3},{3,2},{4,5},{5,4},{6,7},{7,6},{8,9},{9,8},{10,11... | collective-permute-start | bytes 1769480 | tf_op jit(solution)/shard_map/ppermute | solution.py:56
  90.1 14.6 %collective-permute-start.23 = (bf16[2,2,96,768]{3,2,1,0:T(8,128)(2,1)}, bf16[2,2,96,768]{3,2,1,0:T(8,128)(2,1)S(1)}, u32[]{:S(2)}, u32[]{:S(2)}) collective-permute-start(bf16[2,2,96,768]{3,2,1,0:T(8,128)(2,1)} %collective-permute-done.15.refs_5_), channel_id=1, source_target_pairs={{0,1},{1,0},{2,3},{3,2},{4,5},{5,4},{6,7},{7,6},{8,9},{9,8},{10,11... | collective-permute-start | bytes 1769480 | tf_op jit(solution)/shard_map/ppermute | solution.py:56
  90.5 11.3 %collective-permute-start.20 = (bf16[2,3,256,128]{3,2,1,0:T(8,128)(2,1)}, bf16[2,3,256,128]{3,2,1,0:T(8,128)(2,1)S(1)}, u32[]{:S(2)}, u32[]{:S(2)}) collective-permute-start(bf16[2,3,256,128]{3,2,1,0:T(8,128)(2,1)} %get-tuple-element.180), channel_id=1, source_target_pairs={{0,2},{1,3},{2,0},{3,1},{4,6},{5,7},{6,4},{7,5},{8,10},{9,11},{10,... | collective-permute-start | bytes 1179656 | tf_op jit(solution)/shard_map/ppermute | solution.py:56
  101.9 9.3 %copy-start.12 = (bf16[2,3,256,128]{3,2,1,0:T(8,128)(2,1)}, bf16[2,3,256,128]{3,2,1,0:T(8,128)(2,1)S(1)}, u32[]{:S(2)}) copy-start(bf16[2,3,256,128]{3,2,1,0:T(8,128)(2,1)S(1)} %collective-permute-done.20.refs_18_) | copy-start | bytes 1179652
  104.7 6.4 %copy-start.17 = (bf16[2,2,96,768]{3,2,1,0:T(8,128)(2,1)}, bf16[2,2,96,768]{3,2,1,0:T(8,128)(2,1)S(1)}, u32[]{:S(2)}) copy-start(bf16[2,2,96,768]{3,2,1,0:T(8,128)(2,1)S(1)} %collective-permute-done.19.refs_7_) | copy-start | bytes 1769476
  106.6 2.9 %collective-permute-start.24 = (bf16[2,2,96,768]{3,2,1,0:T(8,128)(2,1)S(1)}, bf16[2,2,96,768]{3,2,1,0:T(8,128)(2,1)S(1)}, u32[]{:S(2)}, u32[]{:S(2)}) collective-permute-start(bf16[2,2,96,768]{3,2,1,0:T(8,128)(2,1)S(1)} %collective-permute-done.19.refs_7_), channel_id=1, source_target_pairs={{0,1},{1,0},{2,3},{3,2},{4,5},{5,4},{6,7},{7,6},{8,9},{9,8},{10,11... | collective-permute-start | bytes 1769480 | tf_op jit(solution)/shard_map/ppermute | solution.py:56
  107.6 1.9 collective-permute-start.25
  149.7 10.3 %collective-permute-start.27 = (bf16[2,8,96,960]{3,2,1,0:T(8,128)(2,1)}, bf16[2,8,96,960]{3,2,1,0:T(8,128)(2,1)}, u32[]{:S(2)}, u32[]{:S(2)}) collective-permute-start(bf16[2,8,96,960]{3,2,1,0:T(8,128)(2,1)} %get-tuple-element.192), channel_id=1, source_target_pairs={{0,1},{1,0},{2,3},{3,2},{4,5},{5,4},{6,7},{7,6},{8,9},{9,8},{10,11... | collective-permute-start | bytes 8847368 | tf_op jit(solution)/shard_map/ppermute | solution.py:56
  150.1 9.8 %collective-permute-start.26 = (bf16[2,8,112,768]{3,2,1,0:T(8,128)(2,1)}, bf16[2,8,112,768]{3,2,1,0:T(8,128)(2,1)}, u32[]{:S(2)}, u32[]{:S(2)}) collective-permute-start(bf16[2,8,112,768]{3,2,1,0:T(8,128)(2,1)} %get-tuple-element.190), channel_id=1, source_target_pairs={{0,1},{1,0},{2,3},{3,2},{4,5},{5,4},{6,7},{7,6},{8,9},{9,8},{10,11... | collective-permute-start | bytes 8257544 | tf_op jit(solution)/shard_map/ppermute | solution.py:56
  150.2 14.0 %collective-permute-start.28 = (bf16[3,256,128]{2,1,0:T(8,128)(2,1)}, bf16[3,256,128]{2,1,0:T(8,128)(2,1)S(1)}, u32[]{:S(2)}, u32[]{:S(2)}) collective-permute-start(bf16[3,256,128]{2,1,0:T(8,128)(2,1)} %get-tuple-element.196), channel_id=1, source_target_pairs={{0,1},{1,0},{2,3},{3,2},{4,5},{5,4},{6,7},{7,6},{8,9},{9,8},{10,11... | collective-permute-start | bytes 589832 | tf_op jit(solution)/shard_map/ppermute | solution.py:56
  150.6 13.7 %collective-permute-start.29 = (bf16[3,256,128]{2,1,0:T(8,128)(2,1)}, bf16[3,256,128]{2,1,0:T(8,128)(2,1)S(1)}, u32[]{:S(2)}, u32[]{:S(2)}) collective-permute-start(bf16[3,256,128]{2,1,0:T(8,128)(2,1)} %get-tuple-element.197), channel_id=1, source_target_pairs={{0,2},{1,3},{2,0},{3,1},{4,6},{5,7},{6,4},{7,5},{8,10},{9,11},{10,... | collective-permute-start | bytes 589832 | tf_op jit(solution)/shard_map/ppermute | solution.py:56
  151.3 13.0 %collective-permute-start.30 = (bf16[3,256,128]{2,1,0:T(8,128)(2,1)}, bf16[3,256,128]{2,1,0:T(8,128)(2,1)S(1)}, u32[]{:S(2)}, u32[]{:S(2)}) collective-permute-start(bf16[3,256,128]{2,1,0:T(8,128)(2,1)} %get-tuple-element.198), channel_id=1, source_target_pairs={{0,3},{1,2},{2,1},{3,0},{4,7},{5,6},{6,5},{7,4},{8,11},{9,10},{10,... | collective-permute-start | bytes 589832 | tf_op jit(solution)/shard_map/ppermute | solution.py:56
  164.4 37.1 %collective-permute-start.32 = (bf16[2,2,2,96,960]{4,3,2,1,0:T(8,128)(2,1)}, bf16[2,2,2,96,960]{4,3,2,1,0:T(8,128)(2,1)}, u32[]{:S(2)}, u32[]{:S(2)}) collective-permute-start(bf16[2,2,2,96,960]{4,3,2,1,0:T(8,128)(2,1)} %get-tuple-element.210), channel_id=1, source_target_pairs={{0,4},{4,0},{8,12},{12,8},{16,20},{20,16},{24,28},{28,24},{1,5},{5... | collective-permute-start | bytes 4423688 | tf_op jit(solution)/shard_map/ppermute | solution.py:56
  165.5 35.5 %collective-permute-start.31 = (bf16[2,2,2,112,768]{4,3,2,1,0:T(8,128)(2,1)}, bf16[2,2,2,112,768]{4,3,2,1,0:T(8,128)(2,1)}, u32[]{:S(2)}, u32[]{:S(2)}) collective-permute-start(bf16[2,2,2,112,768]{4,3,2,1,0:T(8,128)(2,1)} %get-tuple-element.199), channel_id=1, source_target_pairs={{0,2},{1,3},{2,0},{3,1},{4,6},{5,7},{6,4},{7,5},{8,10},{9,11},{10,... | collective-permute-start | bytes 4128776 | tf_op jit(solution)/shard_map/ppermute | solution.py:56
  204.9 19.3 %collective-permute-start.34 = (bf16[2,2,96,960]{3,2,1,0:T(8,128)(2,1)}, bf16[2,2,96,960]{3,2,1,0:T(8,128)(2,1)S(1)}, u32[]{:S(2)}, u32[]{:S(2)}) collective-permute-start(bf16[2,2,96,960]{3,2,1,0:T(8,128)(2,1)} %get-tuple-element.218), channel_id=1, source_target_pairs={{0,2},{1,3},{2,0},{3,1},{4,6},{5,7},{6,4},{7,5},{8,10},{9,11},{10,... | collective-permute-start | bytes 2211848 | tf_op jit(solution)/shard_map/ppermute | solution.py:56
  205.6 17.8 %collective-permute-start.33 = (bf16[2,2,112,768]{3,2,1,0:T(8,128)(2,1)}, bf16[2,2,112,768]{3,2,1,0:T(8,128)(2,1)}, u32[]{:S(2)}, u32[]{:S(2)}) collective-permute-start(bf16[2,2,112,768]{3,2,1,0:T(8,128)(2,1)} %get-tuple-element.212), channel_id=1, source_target_pairs={{0,8},{4,12},{8,0},{12,4},{16,24},{20,28},{24,16},{28,20},{1,9},{5... | collective-permute-start | bytes 2064392 | tf_op jit(solution)/shard_map/ppermute | solution.py:56
  224.1 5.3 %copy-start.4 = (bf16[2,2,96,960]{3,2,1,0:T(8,128)(2,1)}, bf16[2,2,96,960]{3,2,1,0:T(8,128)(2,1)S(1)}, u32[]{:S(2)}) copy-start(bf16[2,2,96,960]{3,2,1,0:T(8,128)(2,1)S(1)} %collective-permute-done.34.refs_7_.refs_8_.refs_3_) | copy-start | bytes 2211844
  229.5 2.5 collective-permute-start.35
  236.7 29.8 %collective-permute-start.40 = (bf16[512,768]{1,0:T(8,128)(2,1)}, bf16[512,768]{1,0:T(8,128)(2,1)}, u32[]{:S(2)}, u32[]{:S(2)}) collective-permute-start(bf16[512,768]{1,0:T(8,128)(2,1)} %get-tuple-element.236), channel_id=1, source_target_pairs={{0,2},{1,3},{2,0},{3,1},{4,6},{5,7},{6,4},{7,5},{8,10},{9,11},{10,... | collective-permute-start | bytes 2359304 | tf_op jit(solution)/shard_map/ppermute | solution.py:56
  237.7 20.3 %collective-permute-start.38 = (bf16[3,2,2,96,256]{4,3,2,1,0:T(8,128)(2,1)}, bf16[3,2,2,96,256]{4,3,2,1,0:T(8,128)(2,1)S(1)}, u32[]{:S(2)}, u32[]{:S(2)}) collective-permute-start(bf16[3,2,2,96,256]{4,3,2,1,0:T(8,128)(2,1)} %get-tuple-element.232), channel_id=1, source_target_pairs={{0,4},{4,0},{8,12},{12,8},{16,20},{20,16},{24,28},{28,24},{1,5},{5... | collective-permute-start | bytes 1769480 | tf_op jit(solution)/shard_map/ppermute | solution.py:56
  238.9 18.2 %collective-permute-start.36 = (bf16[2,112,768]{2,1,0:T(8,128)(2,1)}, bf16[2,112,768]{2,1,0:T(8,128)(2,1)}, u32[]{:S(2)}, u32[]{:S(2)}) collective-permute-start(bf16[2,112,768]{2,1,0:T(8,128)(2,1)} %get-tuple-element.224), channel_id=1, source_target_pairs={{0,16},{4,20},{8,24},{12,28},{16,0},{20,4},{24,8},{28,12},{1,17},{... | collective-permute-start | bytes 1032200 | tf_op jit(solution)/shard_map/ppermute | solution.py:56
  240.6 17.3 %collective-permute-start.37 = (bf16[2,96,960]{2,1,0:T(8,128)(2,1)}, bf16[2,96,960]{2,1,0:T(8,128)(2,1)S(1)}, u32[]{:S(2)}, u32[]{:S(2)}) collective-permute-start(bf16[2,96,960]{2,1,0:T(8,128)(2,1)} %get-tuple-element.230), channel_id=1, source_target_pairs={{0,8},{4,12},{8,0},{12,4},{16,24},{20,28},{24,16},{28,20},{1,9},{5... | collective-permute-start | bytes 1105928 | tf_op jit(solution)/shard_map/ppermute | solution.py:56
  246.0 22.2 %collective-permute-start.41 = (bf16[256,768]{1,0:T(8,128)(2,1)}, bf16[256,768]{1,0:T(8,128)(2,1)}, u32[]{:S(2)}, u32[]{:S(2)}) collective-permute-start(bf16[256,768]{1,0:T(8,128)(2,1)} %get-tuple-element.226), channel_id=1, source_target_pairs={{0,1},{1,0},{2,3},{3,2},{4,5},{5,4},{6,7},{7,6},{8,9},{9,8},{10,11... | collective-permute-start | bytes 1179656 | tf_op jit(solution)/shard_map/ppermute | solution.py:56
  257.1 11.8 %collective-permute-start.42 = (bf16[256,768]{1,0:T(8,128)(2,1)}, bf16[256,768]{1,0:T(8,128)(2,1)}, u32[]{:S(2)}, u32[]{:S(2)}) collective-permute-start(bf16[256,768]{1,0:T(8,128)(2,1)} %get-tuple-element.227), channel_id=1, source_target_pairs={{0,1},{1,0},{2,3},{3,2},{4,5},{5,4},{6,7},{7,6},{8,9},{9,8},{10,11... | collective-permute-start | bytes 1179656 | tf_op jit(solution)/shard_map/ppermute | solution.py:56
  262.4 8.5 %collective-permute-start.39 = (bf16[112,768]{1,0:T(8,128)(2,1)}, bf16[112,768]{1,0:T(8,128)(2,1)S(1)}, u32[]{:S(2)}, u32[]{:S(2)}) collective-permute-start(bf16[112,768]{1,0:T(8,128)(2,1)} %get-tuple-element.234), channel_id=1, source_target_pairs={{0,4},{4,0},{8,12},{12,8},{16,20},{20,16},{24,28},{28,24},{1,5},{5... | collective-permute-start | bytes 516104 | tf_op jit(solution)/shard_map/ppermute | solution.py:56
  265.2 20.6 %collective-permute-start.43 = (bf16[96,960]{1,0:T(8,128)(2,1)}, bf16[96,960]{1,0:T(8,128)(2,1)S(1)}, u32[]{:S(2)}, u32[]{:S(2)}) collective-permute-start(bf16[96,960]{1,0:T(8,128)(2,1)} %get-tuple-element.239), channel_id=1, source_target_pairs={{0,16},{4,20},{8,24},{12,28},{16,0},{20,4},{24,8},{28,12},{1,17},{... | collective-permute-start | bytes 552968 | tf_op jit(solution)/shard_map/ppermute | solution.py:56
  266.5 19.2 %collective-permute-start.44 = (bf16[3,96,256]{2,1,0:T(8,128)(2,1)}, bf16[3,96,256]{2,1,0:T(8,128)(2,1)S(1)}, u32[]{:S(2)}, u32[]{:S(2)}) collective-permute-start(bf16[3,96,256]{2,1,0:T(8,128)(2,1)} %get-tuple-element.240), channel_id=1, source_target_pairs={{0,16},{4,20},{8,24},{12,28},{16,0},{20,4},{24,8},{28,12},{1,17},{... | collective-permute-start | bytes 442376 | tf_op jit(solution)/shard_map/ppermute | solution.py:56
  268.2 17.5 %collective-permute-start.45 = (bf16[3,96,256]{2,1,0:T(8,128)(2,1)}, bf16[3,96,256]{2,1,0:T(8,128)(2,1)S(1)}, u32[]{:S(2)}, u32[]{:S(2)}) collective-permute-start(bf16[3,96,256]{2,1,0:T(8,128)(2,1)} %get-tuple-element.241), channel_id=1, source_target_pairs={{0,8},{4,12},{8,0},{12,4},{16,24},{20,28},{24,16},{28,20},{1,9},{5... | collective-permute-start | bytes 442376 | tf_op jit(solution)/shard_map/ppermute | solution.py:56
  268.9 16.9 %collective-permute-start.46 = (bf16[3,96,256]{2,1,0:T(8,128)(2,1)}, bf16[3,96,256]{2,1,0:T(8,128)(2,1)S(1)}, u32[]{:S(2)}, u32[]{:S(2)}) collective-permute-start(bf16[3,96,256]{2,1,0:T(8,128)(2,1)} %get-tuple-element.242), channel_id=1, source_target_pairs={{0,24},{4,28},{8,16},{12,20},{16,8},{20,12},{24,0},{28,4},{1,25},{... | collective-permute-start | bytes 442376 | tf_op jit(solution)/shard_map/ppermute | solution.py:56
  (21 other events, 27.6 us)

commit v4 on v3

--- a/solution.py
+++ b/solution.py
@@ -16,7 +16,6 @@
 F32 = jnp.float32
 NT = (((1,), (1,)), ((), ()))
 TN = (((0,), (0,)), ((), ()))
-VMEM_LIMIT = 64 << 20
 EXTRA = 16
 
 
@@ -90,8 +89,8 @@
     return lax.optimization_barrier((value,) + others)[0]
 
 
-def params():
-    return pltpu.CompilerParams(vmem_limit_bytes=VMEM_LIMIT - (1 << 20))
+def params(mebibytes=63):
+    return pltpu.CompilerParams(vmem_limit_bytes=mebibytes << 20)
 
 
 def cost(flops, moved, exps=0):
@@ -106,8 +105,13 @@
 
 def project_kernel(*refs, masks, heads, placed):
     x_refs, w_refs = refs[:4], refs[4 : 4 + len(masks)]
-    bq_ref, bv_ref, positions_ref, lengths_ref, q_out, k_out, v_out, w_s = refs[4 + len(masks) :]
+    bq_ref, bv_ref, positions_ref, lengths_ref, q_out, k_out, v_out, w_s, x_s, m_s, sems = refs[
+        4 + len(masks) :
+    ]
     rows = x_refs[0].shape[0]
+    loads = [pltpu.make_async_copy(x_refs[j], x_s.at[j], sems.at[j]) for j in range(4)]
+    for load in loads:
+        load.start()
     for ref, entries in zip(w_refs, masks, strict=True):
         for z, mask in enumerate(entries):
             w_s[place_of(mask, ref.shape[1], placed), :] = ref[z]
@@ -119,10 +123,16 @@
     b_query = bq_ref[...].astype(F32)
     bias = jnp.concatenate([b_query, jnp.zeros_like(b_query), bv_ref[...].astype(F32)], axis=1)
     for j in range(4):
-        part = pl.ds(j * rows, rows)
-        whole = dot(x_refs[j][...], w_s[...]) + bias
         masked = jnp.where(valid_row(positions_ref, lengths_ref, j, rows), 0.0, MASKED)
-        masked = jnp.broadcast_to(masked, (LANES, rows)).T
+        m_s[j] = jnp.broadcast_to(masked, (8, rows))
+    for load in loads:
+        load.wait()
+
+    @pl.loop(0, 4)
+    def _(j):
+        part = pl.ds(pl.multiple_of(j * rows, rows), rows)
+        whole = dot(x_s[j], w_s[...]) + bias
+        masked = jnp.broadcast_to(m_s[j, 0:1, :], (LANES, rows)).T
 
         def columns(group):
             start = group // 2 * LANES
@@ -145,11 +155,16 @@
     seq = 4 * rows
     return pl.pallas_call(
         functools.partial(project_kernel, masks=masks, heads=heads, placed=placed),
-        in_specs=[VMEM_SPEC] * (7 + len(pieces)) + [SMEM_SPEC],
+        in_specs=[ANY_SPEC] * 4 + [VMEM_SPEC] * (3 + len(pieces)) + [SMEM_SPEC],
         out_specs=[VMEM_SPEC] * 3,
         out_shape=[jax.ShapeDtypeStruct((heads, seq, LANES), BF16)] * 3,
-        scratch_shapes=[pltpu.VMEM((width, pieces[0].shape[2]), BF16)],
-        compiler_params=params(),
+        scratch_shapes=[
+            pltpu.VMEM((width, pieces[0].shape[2]), BF16),
+            pltpu.VMEM((4, rows, width), BF16),
+            pltpu.VMEM((4, 8, rows), F32),
+            pltpu.SemaphoreType.DMA((4,)),
+        ],
+        compiler_params=params(32),
         cost_estimate=cost(1000, 1000),
         name="project",
     )(*parts, *pieces, b_query, b_value, positions, lengths)
@@ -175,9 +190,9 @@
         total = dot(expon, v_ref[0])
         row_sum = total[:, HEAD_DIM : HEAD_DIM + 1]
         out = total * (1.0 / row_sum)
-        o_out[place(i), :] = out
+        o_out[0, place(i), :] = out
         one, two, three = in_three(-(top + jnp.log(row_sum)))
-        q_out[place(i), :] = jnp.where(
+        q_out[0, place(i), :] = jnp.where(
             lane == HEAD_DIM + 1,
             one,
             jnp.where(lane == HEAD_DIM + 2, two, jnp.where(lane == HEAD_DIM + 3, three, query)),
@@ -205,35 +220,33 @@
     far[1, 0] = packed[3]
 
 
-def attention_forward(head, q, k, v, packed):
+def attention_forward(first, count, q, k, v, before):
     heads, seq, _ = q.shape
     block = seq // 8
-    one = pl.BlockSpec((1, seq, LANES), lambda i: (head, 0, 0))
-    flat = pl.BlockSpec((seq, LANES), lambda i: (0, 0))
-    piece = pl.BlockSpec((1, block, LANES), lambda i: (head, 0, 0))
-    pieces = pl.BlockSpec((2, 1, block, LANES), lambda i: (0, head, 0, 0))
+    one = pl.BlockSpec((1, seq, LANES), lambda i: (first + i, 0, 0))
+    piece = pl.BlockSpec((1, block, LANES), lambda i: (first + i, 0, 0))
+    pieces = pl.BlockSpec((2, 1, block, LANES), lambda i: (0, first + i, 0, 0))
     shape = jax.ShapeDtypeStruct
-    q_kept, out, *packed = pl.pallas_call(
+    return pl.pallas_call(
         functools.partial(forward_kernel, unroll=4),
-        grid=(1,),
-        in_specs=[one] * 3 + [ANY_SPEC] * len(packed),
-        out_specs=[flat, flat, piece, piece, pieces],
-        out_shape=[shape((seq, LANES), BF16), shape((seq, LANES), F32)]
+        grid=(count,),
+        in_specs=[one] * 3 + [ANY_SPEC] * len(before),
+        out_specs=[one, one, piece, piece, pieces],
+        out_shape=[shape((heads, seq, LANES), BF16), shape((heads, seq, LANES), F32)]
         + [shape((heads, block, LANES), BF16)] * 2
         + [shape((2, heads, block, LANES), BF16)],
         scratch_shapes=[pltpu.VMEM((4, block, LANES), BF16)],
-        input_output_aliases={3 + i: 2 + i for i in range(len(packed))},
-        compiler_params=params(),
+        input_output_aliases={3 + i: i for i in range(len(before))},
+        compiler_params=params(32),
         cost_estimate=cost(1000, 1000),
         name="attention_forward",
-    )(q, k, v, *packed)
-    return q_kept, out, packed
+    )(q, k, v, *before)
 
 
 def backward_kernel(q_ref, k_ref, v_ref, o_ref, *refs, placed):
     d_refs, x_refs = refs[:4], refs[4:8]
     g_ref, gw_ref, dk_s, dv_s, gw_s, d_s = refs[-6:]
-    seq = q_ref.shape[0]
+    seq = q_ref.shape[1]
     block = seq // 8
     rows = seq // 4
     lane = lax.broadcasted_iota(jnp.int32, (1, LANES), 1)
@@ -248,12 +261,12 @@
     def _(j):
         for half in range(2):
             place = pl.ds(pl.multiple_of((2 * j + half) * block, block), block)
-            query = q_ref[place, :]
+            query = q_ref[0, place, :]
             grad = d_s[j].astype(F32)
             if half == 1:
                 grad = pltpu.roll(grad, HEAD_DIM, 1)
             grad = jnp.where(head_lane, grad, 0.0)
-            delta = jnp.sum(grad * o_ref[place, :], axis=-1, keepdims=True)
+            delta = jnp.sum(grad * o_ref[0, place, :], axis=-1, keepdims=True)
             one, two, three = in_three(-delta)
             grad = grad.astype(BF16)
             grad_and = jnp.where(
@@ -287,12 +300,11 @@
         gw_ref[0, i, :, 3 * HEAD_DIM :] = side
 
 
-def attention_backward(head, q, k, v, out, grads, parts, blocks, before):
+def attention_backward(first, count, q, k, v, out, grads, parts, blocks, before):
     heads, seq, _ = k.shape
     rows, width = parts[0].shape
-    one = pl.BlockSpec((1, seq, LANES), lambda i: (head, 0, 0))
-    flat = pl.BlockSpec((seq, LANES), lambda i: (0, 0))
-    piece = pl.BlockSpec((1, seq // 8, LANES), lambda i: (head, 0, 0))
+    one = pl.BlockSpec((1, seq, LANES), lambda i: (first + i, 0, 0))
+    piece = pl.BlockSpec((1, seq // 8, LANES), lambda i: (first + i, 0, 0))
     whole = pl.BlockSpec((rows, width), lambda i: (0, 0))
     three = 3 * HEAD_DIM
     share = width // blocks
@@ -300,11 +312,11 @@
     alias = {12: 0, 13: 1} if before else {}
     return pl.pallas_call(
         functools.partial(backward_kernel, placed=blocks > 1),
-        grid=(1,),
-        in_specs=[flat, one, one, flat] + [piece] * 4 + [whole] * 4 + [ANY_SPEC] * len(before),
+        grid=(count,),
+        in_specs=[one] * 4 + [piece] * 4 + [whole] * 4 + [ANY_SPEC] * len(before),
         out_specs=[
-            pl.BlockSpec((1, seq, three), lambda i: (head, 0, 0)),
-            pl.BlockSpec((1, blocks, share, 4 * HEAD_DIM), lambda i: (head, 0, 0, 0)),
+            pl.BlockSpec((1, seq, three), lambda i: (first + i, 0, 0)),
+            pl.BlockSpec((1, blocks, share, 4 * HEAD_DIM), lambda i: (first + i, 0, 0, 0)),
         ],
         out_shape=[
             shape((heads, seq, three), BF16),
@@ -366,7 +378,7 @@
     lo_ref, done_ref, sent_d, kept_d, sent_u, kept_u = refs[8:14]
     ga = refs[14:18]
     w1_s, w2_s, att_s, wo_s, hid_s, slope_s, nrm_s, nb_s, n1_s, rs_s, ffn_s = refs[18:29]
-    gf_s, gft_s, nbt_s, acc_s, pre_s, g_s, bup_s, mask_s, sums_ref, low_s, in_sem, down_sem, up_sem, out_sem, low_sem = refs[29:]
+    gf_s, gft_s, nbt_s, acc_s, pre_s, g_s, bup_s, mask_s, sums_ref, low_s, two_s, act_s, in_sem, down_sem, up_sem, out_sem, low_sem = refs[29:]
     rows, width = x_ref.shape
     hidden = w2_s.shape[2]
     pieces = 4
@@ -447,19 +459,36 @@
         if second:
             copy.wait()
 
-    @pl.loop(0, pieces)
-    def _(j):
-        pre_s[...] = dot(nb_s[...], w1_s[j, :, :hidden]) + bup_s[j]
-
-        def gelu(r):
-            pre = pre_s[r, :]
-            cdf = 0.5 * (1.0 + lax.erf(pre * (0.5**0.5)))
-            pdf = jnp.exp(pre * pre * -0.5) * (2.0 * jnp.pi) ** -0.5
-            hid_s[j, r, :] = (pre * cdf).astype(BF16)
-            slope_s[j, r, :] = cdf + pre * pdf
-
-        row_loop(gelu)
-        ffn_s[...] += dot_nt(hid_s[j], w2_s[j])
+    wide = 256
+    per = hidden // wide
+
+    def chunk_of(c):
+        return c // per, pl.ds(pl.multiple_of(c % per * wide, wide), wide)
+
+    def product_of(c):
+        j, at = chunk_of(c)
+        return dot(nb_s[...], w1_s[j, :, at]) + bup_s[j, :, at]
+
+    act_s[...] = jnp.zeros_like(act_s)
+    two_s[0] = product_of(0)
+    count = pieces * per
+
+    @pl.loop(0, count)
+    def _(c):
+        j, at = chunk_of(c)
+        back, behind = chunk_of(jnp.maximum(c - 1, 0))
+        now = c % 2
+        two_s[1 - now] = product_of(jnp.minimum(c + 1, count - 1))
+        ffn_s[...] += dot_nt(act_s[...], w2_s[back, :, behind])
+        pre = two_s[now]
+        cdf = 0.5 * (1.0 + lax.erf(pre * (0.5**0.5)))
+        pdf = jnp.exp(pre * pre * -0.5) * (2.0 * jnp.pi) ** -0.5
+        act = (pre * cdf).astype(BF16)
+        hid_s[j, :, at] = act
+        slope_s[j, :, at] = cdf + pre * pdf
+        act_s[...] = act
+
+    ffn_s[...] += dot_nt(act_s[...], w2_s[pieces - 1, :, (per - 1) * wide :])
 
     def second_norm(r):
         ffn = ffn_s[r, :] + b_down
@@ -496,21 +525,27 @@
         pl.ds(2 * hidden, cols),
     )
     to_d, to_u, to_o = pl.ds(0, hidden), pl.ds(0, hidden), pl.ds(hidden, cols)
-    for away, target_d, target_u in ((1, sent_d, sent_u), (0, kept_d, kept_u)):
-
-        @pl.loop(0, pieces // 2)
-        def _(place):
-            j = 2 * place + away
-            pre_s[...] = dot(gf_s[...], w2_s[j]) * slope_s[j]
-            low = pre_s[...].astype(BF16)
-            sums_ref[pl.ds(10 + j, 1), :] = jnp.sum(low.astype(F32), axis=0, keepdims=True)
-            g_s[j, :, lanes_d] = dot(gft_s[...], hid_s[j]).astype(BF16)
-            for copy in copies(j, lanes_d, target_d, place, down_sem, to_d):
-                copy.start()
-            g_s[j, :, lanes_u] = dot(nbt_s[...], low).astype(BF16)
-            for copy in copies(j, lanes_u, target_u, place, up_sem, to_u):
-                copy.start()
-            acc_s[...] += dot_nt(low, w1_s[j, :, :hidden])
+    def start_all(j, place, lanes, to, sem, targets):
+        for away in (1, 0):
+
+            @pl.when(j % 2 == away)
+            def _():
+                for copy in copies(j, lanes, targets[1 - away], place, sem, to):
+                    copy.start()
+
+    @pl.loop(0, pieces)
+    def _(step):
+        away = 1 - step // (pieces // 2)
+        place = step % (pieces // 2)
+        j = 2 * place + away
+        pre_s[...] = dot(gf_s[...], w2_s[j]) * slope_s[j]
+        low = pre_s[...].astype(BF16)
+        sums_ref[pl.ds(10 + j, 1), :] = jnp.sum(low.astype(F32), axis=0, keepdims=True)
+        g_s[j, :, lanes_d] = dot(gft_s[...], hid_s[j]).astype(BF16)
+        start_all(j, place, lanes_d, to_d, down_sem, (sent_d, kept_d))
+        g_s[j, :, lanes_u] = dot(nbt_s[...], low).astype(BF16)
+        start_all(j, place, lanes_u, to_u, up_sem, (sent_u, kept_u))
+        acc_s[...] += dot_nt(low, w1_s[j, :, :hidden])
 
     def first_back(r):
         grad = acc_s[r, :]
@@ -596,6 +631,8 @@
             vmem((rows, LANES), F32),
             vmem((16, width), F32),
             vmem((4, EXTRA, width), BF16),
+            vmem((2, rows, 256), F32),
+            vmem((rows, 256), BF16),
             pltpu.SemaphoreType.DMA((loads,)),
             pltpu.SemaphoreType.DMA((4, blocks)),
             pltpu.SemaphoreType.DMA((4, blocks)),
@@ -763,7 +800,6 @@
     vectors = [b_out, b_down, gain_attn, shift_attn, gain_ffn, shift_ffn]
     vectors = jnp.stack([vec.astype(F32) for vec in vectors] + [jnp.zeros((width,), F32)] * 2)
 
-    kept = []
     if placed:
         got_w = after(swap(own_qkv, "dp", 4), one, two)
         w_part, w_mask = grow(own_qkv, got_w, [0], 4)
@@ -784,18 +820,15 @@
         round_four = (swap(two, "dp", 4), swap(one, "dp", 1), cross(one), core(one))
         positions = after(positions, one, two)
         q, k, v = project(parts, w_qkv, w_masks, *biases, positions, seq_lengths, heads, placed)
-        q_kept, out, packed = attention_forward(0, q, k, v, [])
-        kept.append((q_kept, out))
+        kept = attention_forward(0, 1, q, k, v, [])
+        q_kept = kept[0]
         got_two, odd, even_far, even_near = after(round_four, q_kept)
         two, two_mask = grow(two, got_two, [0], 4)
 
         round_five = (swap(two, "dp", 2), cross(odd), swap(two, "dp", 1), core(even_far))
-        packed, odd, two, even_far = after((packed, odd, two, even_far), q_kept)
-        q_kept, out, packed = attention_forward(1, q, k, v, packed)
-        kept.append((q_kept, out))
-        q = after(q, q_kept)
-        q_kept, out, packed = attention_forward(2, q, k, v, packed)
-        kept.append((q_kept, out))
+        kept, odd, two, even_far = after((kept, odd, two, even_far), q_kept)
+        q_kept, out, *packed = attention_forward(1, 2, q, k, v, kept)
+        kept = [q_kept, out]
         two_late, odd_far, two_odd, both_near = after(round_five, q_kept)
 
         far_odd = [m ^ 1 for m in one_mask]
@@ -820,10 +853,8 @@
         two = gather_bits(two[0], "dp", range(bits), 0).reshape(1, width, -1)
         parts = [tokens, beside, across, core(across)]
         q, k, v = project(parts, w_qkv, w_masks, *biases, positions, seq_lengths, heads, placed)
-        packed = []
-        for h in range(heads):
-            q_kept, out, packed = attention_forward(h, q, k, v, packed)
-            kept.append((q_kept, out))
+        q_kept, out, *packed = attention_forward(0, heads, q, k, v, [])
+        kept = [q_kept, out]
         ones = [(one, [0]), (cross(one), [0])]
         twos = [(jnp.stack([two, cross(two)], axis=1), [0])]
         early = [core(array) for array, _ in ones + twos]
@@ -867,7 +898,6 @@
     three = 3 * HEAD_DIM
 
     got_d, got_u = core(sent_d), core(sent_u)
-    before = []
     if placed:
         down, up = Sum(["x"] + names, hidden), Sum(["x"] + names, hidden + own_cols)
         for total, arrays in ((down, (kept_d, got_d)), (up, (kept_u, got_u))):
@@ -877,19 +907,20 @@
         move_d, move_u = after((move_d, move_u), grads)
         grads = after(grads, move_d)
         down_names, up_names = ["x"] + late + [0], [0, "x"] + late
-    for h in range(heads):
-        q_kept = kept[h][0]
-        if placed and h == heads - 1:
-            last = before[:1]
-            down.join(after(send(move_d, down_names.pop(0)), *last))
-            up.join(after(send(move_u, up_names.pop(0)), *last))
-            groups = [[down.away(down_names[0])], [up.away(up_names[0])]]
-            move_d, move_u = reduce_call("sum_second", groups, BF16)
-            q_kept = after(q_kept, move_d)
+    q_kept, out = kept
+    if placed:
+        before = attention_backward(0, heads - 1, q_kept, k, v, out, grads, parts, blocks, [])
+        last = before[0]
+        down.join(after(send(move_d, down_names.pop(0)), last))
+        up.join(after(send(move_u, up_names.pop(0)), last))
+        groups = [[down.away(down_names[0])], [up.away(up_names[0])]]
+        move_d, move_u = reduce_call("sum_second", groups, BF16)
+        q_kept = after(q_kept, move_d)
         g_all, g_w = attention_backward(
-            h, q_kept, k, v, kept[h][1], grads, parts, blocks, before
+            heads - 1, 1, q_kept, k, v, out, grads, parts, blocks, before
         )
-        before = [g_all, g_w]
+    else:
+        g_all, g_w = attention_backward(0, heads, q_kept, k, v, out, grads, parts, blocks, [])
     if placed:
         got_d = after(send(move_d, down_names.pop(0)), g_all)
         got_u = after(send(move_u, up_names.pop(0)), g_all)

time: 295 us -> 283 us (0.959); the launches traced: 289 us -> 282 us
  Pallas kernels: 154 us -> 142 us
  waiting for transfers between devices: 65.2 us -> 72.3 us
    pallas_call x3 -> x2, Pallas kernels: 25.3 us -> 17.7 us  [attention_forward(): pl.pallas_call(functools.partial(forward_kernel, unroll=4), grid=(count,)...]
    ppermute x47, waiting for transfers between devices: 65.2 us -> 72.3 us  [swap(): return lax.ppermute(value, axis, [(i, i ^ bits) for i in range(size)])]
    pallas_call x3 -> x2, Pallas kernels: 51.7 us -> 48 us  [attention_backward(): pl.pallas_call(functools.partial(backward_kernel, placed=blocks > 1), gri...]
    unnamed x77 -> x105, local copies, waits for them, and re-layouts: 8.64 us -> 8.23 us
  transfers between devices with their start and end apart: 47 -> 47, of which waited for: 18 -> 21; matrix products, arithmetic and copies ran while one was open for 6% -> 4% of each run, Pallas kernels for 35% -> 31%
where the time goes in v4:
time: 283 us; the launch traced here: 282 us
  Pallas kernels  142 us (50%)
  waiting for transfers between devices  72.3 us (26%)
  starting transfers between devices  46.1 us (16%)
  local copies, waits for them, and re-layouts  11.5 us (4%)
  other arithmetic  7.83 us (3%)
    ppermute x47, waiting for transfers between devices, swap(): return lax.ppermute(value, axis, [(i, i ^ bits) for i in range(size)])  72.3 us
    pallas_call x2, Pallas kernels, attention_backward(): pl.pallas_call(functools.partial(backward_kernel, placed=blocks > 1), gri...  48 us
    ppermute x47, starting transfers between devices, swap(): return lax.ppermute(value, axis, [(i, i ^ bits) for i in range(size)])  46.1 us
    pallas_call x1, Pallas kernels, middle(): pl.pallas_call(functools.partial(middle_kernel, plan=plan, blocks=blocks)...  39.1 us
    pallas_call x6, Pallas kernels, reduce_call(): pl.pallas_call(functools.partial(reduce_kernel if keep else reduce_inside...  21.9 us
    pallas_call x2, Pallas kernels, attention_forward(): pl.pallas_call(functools.partial(forward_kernel, unroll=4), grid=(count,)...  17.7 us
    pallas_call x2, Pallas kernels, input_part(): pl.pallas_call(functools.partial(input_kernel, masks=masks, which=which,...  10 us
    unnamed x105, local copies, waits for them, and re-layouts  8.23 us
  transfers between devices with their start and end apart: 47, of which 21 were waited for; matrix products, arithmetic and copies ran while one was open for 4% of the time, Pallas kernels for 31%

profile of v4, /device:TPU:0, one launch (start us, length us, event | category | flops | bytes accessed | tf_op | source)
XLA Modules:
  0.0 281.9 jit_solution(14375714059296834719)
XLA Ops:
  0.7 3.0 %collective-permute-start.3 = (bf16[512,768]{1,0:T(8,128)(2,1)}, bf16[512,768]{1,0:T(8,128)(2,1)S(1)}, u32[]{:S(2)}, u32[]{:S(2)}) collective-permute-start(bf16[512,768]{1,0:T(8,128)(2,1)} %refs_4_.3), channel_id=1, source_target_pairs={{0,2},{1,3},{2,0},{3,1},{4,6},{5,7},{6,4},{7,5},{8,10},{9,11},{10,... | collective-permute-start | bytes 2359304 | tf_op jit(solution)/shard_map/ppermute | solution.py:55
  3.7 0.9 fusion.5
  4.6 2.7 collective-permute-start
  7.3 0.9 copy.44
  9.0 1.0 maximum_bitcast_fusion.1
  10.0 3.0 %collective-permute-done = bf16[1,96,576]{2,1,0:T(8,128)(2,1)S(1)} collective-permute-done((bf16[1,96,576]{2,1,0:T(8,128)(2,1)S(1)}, bf16[1,96,576]{2,1,0:T(8,128)(2,1)S(1)}, u32[]{:S(2)}, u32[]{:S(2)}) %collective-permute-start) | collective-permute-done | bytes 110624 | tf_op jit(solution)/shard_map/ppermute | solution.py:55
  13.8 3.4 %collective-permute-start.2 = (bf16[1,96,1024]{2,1,0:T(8,128)(2,1)S(1)}, bf16[1,96,1024]{2,1,0:T(8,128)(2,1)S(1)}, u32[]{:S(2)}, u32[]{:S(2)}) collective-permute-start(bf16[1,96,1024]{2,1,0:T(8,128)(2,1)S(1)} %maximum_bitcast_fusion.1), channel_id=1, source_target_pairs={{0,16},{4,20},{8,24},{12,28},{16,0},{20,4},{24,8},{28,12},{1,17},{... | collective-permute-start | bytes 589832 | tf_op jit(solution)/shard_map/ppermute | solution.py:55
  17.1 6.3 %collective-permute-done.2 = bf16[1,96,1024]{2,1,0:T(8,128)(2,1)S(1)} collective-permute-done((bf16[1,96,1024]{2,1,0:T(8,128)(2,1)S(1)}, bf16[1,96,1024]{2,1,0:T(8,128)(2,1)S(1)}, u32[]{:S(2)}, u32[]{:S(2)}) %collective-permute-start.2) | collective-permute-done | bytes 196640 | tf_op jit(solution)/shard_map/ppermute | solution.py:55
  24.4 1.6 collective-permute-start.4
  26.0 0.9 fusion.1
  26.9 3.5 %collective-permute-start.5 = (bf16[2,96,1024]{2,1,0:T(8,128)(2,1)}, bf16[2,96,1024]{2,1,0:T(8,128)(2,1)}, u32[]{:S(2)}, u32[]{:S(2)}) collective-permute-start(bf16[2,96,1024]{2,1,0:T(8,128)(2,1)} %get-tuple-element.252), channel_id=1, source_target_pairs={{0,8},{4,12},{8,0},{12,4},{16,24},{20,28},{24,16},{28,20},{1,9},{5... | collective-permute-start | bytes 1179656 | tf_op jit(solution)/shard_map/ppermute | solution.py:55
  31.7 4.4 %collective-permute-done.6 = bf16[1,96,768]{2,1,0:T(8,128)(2,1)} collective-permute-done((bf16[1,96,768]{2,1,0:T(8,128)(2,1)S(1)}, bf16[1,96,768]{2,1,0:T(8,128)(2,1)}, u32[]{:S(2)}, u32[]{:S(2)}) %collective-permute-start.6) | collective-permute-done | bytes 147488 | tf_op jit(solution)/shard_map/ppermute | solution.py:55
  36.1 4.0 %collective-permute-done.5 = bf16[2,96,1024]{2,1,0:T(8,128)(2,1)} collective-permute-done((bf16[2,96,1024]{2,1,0:T(8,128)(2,1)}, bf16[2,96,1024]{2,1,0:T(8,128)(2,1)}, u32[]{:S(2)}, u32[]{:S(2)}) %collective-permute-start.5) | collective-permute-done | bytes 393248 | tf_op jit(solution)/shard_map/ppermute | solution.py:55
  40.2 1.7 pad_maximum_fusion
  43.0 0.9 fusion.6
  44.0 1.8 collective-permute-start.9
  45.8 5.3 %project.1 = (bf16[3,2048,128]{2,1,0:T(8,128)(2,1)S(1)}, bf16[3,2048,128]{2,1,0:T(8,128)(2,1)S(1)}, bf16[3,2048,128]{2,1,0:T(8,128)(2,1)S(1)}) custom-call(bf16[512,768]{1,0:T(8,128)(2,1)S(1)} %copy-done.4, bf16[512,768]{1,0:T(8,128)(2,1)} %collective-permute-done.8.refs_1_.refs_5_, bf16[512,768]{1,0:T(8,128)(2,1)S(1)} %collective-permute-done.3.refs_2_.refs_6_, ...), custom_call_target="tpu_custom_call" | custom-call | flops 1000 | bytes 1000 | tf_op jit(solution)/shard_map/project/pallas_call | solution.py:156
  51.1 5.9 %attention_forward.2 = (bf16[3,2048,128]{2,1,0:T(8,128)(2,1)S(1)}, f32[3,2048,128]{2,1,0:T(8,128)S(1)}, bf16[3,256,128]{2,1,0:T(8,128)(2,1)S(1)}, bf16[3,256,128...) custom-call(bf16[3,2048,128]{2,1,0:T(8,128)(2,1)S(1)} %get-tuple-element.144.q_ref, ...), custom_call_target="tpu_custom_call" | custom-call | flops 1000 | bytes 1000 | tf_op jit(solution)/shard_map/attention_forward/pallas_call | solution.py:230
  57.0 3.7 %collective-permute-done.9 = bf16[1,2,96,768]{3,2,1,0:T(8,128)(2,1)S(1)} collective-permute-done((bf16[1,2,96,768]{3,2,1,0:T(8,128)(2,1)S(1)}, bf16[1,2,96,768]{3,2,1,0:T(8,128)(2,1)S(1)}, u32[]{:S(2)}, u32[]{:S(2)}) %collective-permute-start.9) | collective-permute-done | bytes 294944 | tf_op jit(solution)/shard_map/ppermute | solution.py:55
  61.3 0.9 collective-permute-start.14
  62.3 2.1 collective-permute-start.13
  65.0 11.8 %attention_forward.3 = (bf16[3,2048,128]{2,1,0:T(8,128)(2,1)S(1)}, f32[3,2048,128]{2,1,0:T(8,128)S(1)}, bf16[3,256,128]{2,1,0:T(8,128)(2,1)S(1)}, bf16[3,256,128...) custom-call(bf16[3,2048,128]{2,1,0:T(8,128)(2,1)S(1)} %get-tuple-ele, ...), custom_call_target="tpu_custom_call", output_to_operand_aliasing={{0}: (3, {}), {1}: (4, {}), {2}: (5, {}), {3}: (6, {}), {4}... | custom-call | flops 1000 | bytes 1000 | tf_op jit(solution)/shard_map/attention_forward/pallas_call | solution.py:230
  76.9 1.7 copy-done
  78.6 1.2 copy-done.3
  80.5 2.6 collective-permute-done.17.refs_12_
  83.2 0.8 copy-done.32
  84.1 1.5 collective-permute-start.19
  86.1 1.5 collective-permute-start.20
  87.6 9.6 %collective-permute-done.20.refs_18_ = bf16[2,3,256,128]{3,2,1,0:T(8,128)(2,1)S(1)} collective-permute-done((bf16[2,3,256,128]{3,2,1,0:T(8,128)(2,1)S(1)}, bf16[2,3,256,128]{3,2,1,0:T(8,128)(2,1)S(1)}, u32[]{:S(2)}, u32[]{:S(2)}) %collective-permute-start.20) | collective-permute-done | bytes 393248 | tf_op jit(solution)/shard_map/ppermute | solution.py:55
  97.2 2.5 collective-permute-done.19.refs_7_
  100.5 1.9 collective-permute-done.25.refs_17_
  102.5 0.9 copy-done.36
  103.4 39.1 %middle.1 = (bf16[512,768]{1,0:T(8,128)(2,1)}, f32[512,768]{1,0:T(8,128)}, bf16[2,8,112,768]{3,2,1,0:T(8,128)(2,1)}, bf16[2,8,112,768]{3,2,1,0:T(8,128)(2,1)}, b...) custom-call(bf16[4,96,1024]{2,1,0:T(8,128)(2,1)} %bitcast.62, ...), custom_call_target="tpu_custom_call" | custom-call | flops 1000 | bytes 1000 | tf_op jit(solution)/shard_map/middle/pallas_call | solution.py:601
  143.1 1.5 collective-permute-start.29
  144.9 7.8 %collective-permute-done.26 = bf16[2,8,112,768]{3,2,1,0:T(8,128)(2,1)} collective-permute-done((bf16[2,8,112,768]{3,2,1,0:T(8,128)(2,1)}, bf16[2,8,112,768]{3,2,1,0:T(8,128)(2,1)}, u32[]{:S(2)}, u32[]{:S(2)}) %collective-permute-start.26) | collective-permute-done | bytes 2752544 | tf_op jit(solution)/shard_map/ppermute | solution.py:55
  152.7 4.4 %sum_first.1 = (bf16[2,2,2,112,768]{4,3,2,1,0:T(8,128)(2,1)}, bf16[2,2,2,96,960]{4,3,2,1,0:T(8,128)(2,1)}) custom-call(bf16[2,2,2,2,112,768]{5,4,3,2,1,0:T(8,128)(2,1)} %bitcast.51, bf16[2,2,2,2,112,768]{5,4,3,2,1,0:T(8,128)(2,1)} %bitcast.25.refs_1_, bf16[2,2,2,2,96,960]{5,4,3,2,1,0:T(8,128)(2,1)} %bitcast.46, ...), custom_call_target="tpu_custom_call" | custom-call | flops 1000 | bytes 1000 | tf_op jit(solution)/shard_map/sum_first/pallas_call | solution.py:721
  157.2 1.6 collective-permute-start.32
  158.7 1.5 collective-permute-start.31
  160.2 30.7 %attention_backward.2 = (bf16[3,2048,192]{2,1,0:T(8,128)(2,1)}, bf16[3,8,96,256]{3,2,1,0:T(8,128)(2,1)}) custom-call(bf16[3,2048,128]{2,1,0:T(8,128)(2,1)} %copy-done.3, bf16[3,2048,128]{2,1,0:T(8,128)(2,1)} %copy-done.1, bf16[3,2048,128]{2,1,0:T(8,128)(2,1)} %copy-done.2, f32[3,2048,128]{2,1,0:T(8,128)} %copy-done, ...), custom_call_target="tpu_custom_call" | custom-call | flops 1000 | bytes 1000 | tf_op jit(solution)/shard_map/attention_backward/pallas_call | solution.py:313
  191.0 3.0 %collective-permute-done.32.refs_5_.refs_6_.refs_7_.refs_2_ = bf16[2,2,2,96,960]{4,3,2,1,0:T(8,128)(2,1)} collective-permute-done((bf16[2,2,2,96,960]{4,3,2,1,0:T(8,128)(2,1)}, bf16[2,2,2,96,960]{4,3,2,1,0:T(8,128)(2,1)}, u32[]{:S(2)}, u32[]{:S(2)}) %collective-permute-start.32) | collective-permute-done | bytes 1474592 | tf_op jit(solution)/shard_map/ppermute | solution.py:55
  194.0 3.4 %sum_second.1 = (bf16[2,2,112,768]{3,2,1,0:T(8,128)(2,1)}, bf16[2,2,96,960]{3,2,1,0:T(8,128)(2,1)}) custom-call(bf16[2,2,2,2,112,768]{5,4,3,2,1,0:T(8,128)(2,1)} %bitcast.52, bf16[2,2,2,2,112,768]{5,4,3,2,1,0:T(8,128)(2,1)} %bitcast.25.refs_1_, bf16[2,2,2,112,768]{4,3,2,1,0:T(8,128)(2,1)} %collective-permute-done.31.refs_2_, ...), custom_call_target="tpu_custom_call" | custom-call | flops 1000 | bytes 1000 | tf_op jit(solution)/shard_map/sum_second/pallas_call | solution.py:721
  197.4 1.5 collective-permute-start.34
  199.7 17.3 %attention_backward.3 = (bf16[3,2048,192]{2,1,0:T(8,128)(2,1)}, bf16[3,8,96,256]{3,2,1,0:T(8,128)(2,1)}) custom-call(bf16[3,2048,128]{2,1,0:T(8,128)(2,1)} %copy-done.3, bf16[3,2048,128]{2,1,0:T(8,128)(2,1)} %copy-done.1, bf16[3,2048,128]{2,1,0:T(8,128)(2,1)} %copy-done.2, f32[3,2048,128]{2,1,0:T(8,128)} %copy-done, ...), custom_call_target="tpu_custom_call", output_to_operand_aliasing={{0}: (12, {}), {1}: (13, {})} | custom-call | flops 1000 | bytes 1000 | tf_op jit(solution)/shard_map/attention_backward/pallas_call | solution.py:313
  217.0 5.3 %input_part.2 = (bf16[512,768]{1,0:T(8,128)(2,1)}, bf16[512,768]{1,0:T(8,128)(2,1)}) custom-call(bf16[3,2048,192]{2,1,0:T(8,128)(2,1)} %get-tuple-element.213.g_ref, bf16[4,96,576]{2,1,0:T(8,128)(2,1)} %bitcast.43, bf16[4,96,576]{2,1,0:T(8,128)(2,1)} %copy-done.8), custom_call_target="tpu_custom_call" | custom-call | flops 1000 | bytes 1000 | tf_op jit(solution)/shard_map/input_part/pallas_call | solution.py:361
  222.3 2.5 collective-permute-done.35.refs_10_
  224.8 0.9 copy-done.19
  225.7 3.9 %sum_third.1 = (bf16[2,112,768]{2,1,0:T(8,128)(2,1)}, bf16[2,96,960]{2,1,0:T(8,128)(2,1)}, bf16[3,2,2,96,256]{4,3,2,1,0:T(8,128)(2,1)}, bf16[512,768]{1,0:T(8,128)(2,1)}) custom-call(bf16[2,2,2,2,112,768]{5,4,3,2,1,0:T(8,128)(2,1)} %bitcast.53, bf16[2,2,2,2,112,768]{5,4,3,2,1,0:T(8,128)(2,1)} %bitcast.25.refs_1_, ...), custom_call_target="tpu_custom_call" | custom-call | flops 1000 | bytes 1000 | tf_op jit(solution)/shard_map/sum_third/pallas_call | solution.py:721
  229.6 1.6 collective-permute-start.40
  231.2 0.9 collective-permute-start.38
  232.1 2.4 collective-permute-start.36
  234.5 1.1 collective-permute-start.37
  235.7 4.7 %input_part.3 = (bf16[256,768]{1,0:T(8,128)(2,1)}, bf16[256,768]{1,0:T(8,128)(2,1)}, bf16[512,768]{1,0:T(8,128)(2,1)}) custom-call(bf16[3,2048,192]{2,1,0:T(8,128)(2,1)} %get-tuple-element.213.g_ref, bf16[4,96,576]{2,1,0:T(8,128)(2,1)} %bitcast.44, bf16[4,96,576]{2,1,0:T(8,128)(2,1)} %copy-done.8), custom_call_target="tpu_custom_call" | custom-call | flops 1000 | bytes 1000 | tf_op jit(solution)/shard_map/input_part/pallas_call | solution.py:361
  240.4 9.8 %collective-permute-done.36.refs_4_ = bf16[2,112,768]{2,1,0:T(8,128)(2,1)S(1)} collective-permute-done((bf16[2,112,768]{2,1,0:T(8,128)(2,1)}, bf16[2,112,768]{2,1,0:T(8,128)(2,1)S(1)}, u32[]{:S(2)}, u32[]{:S(2)}) %collective-permute-start.36) | collective-permute-done | bytes 344096 | tf_op jit(solution)/shard_map/ppermute | solution.py:55
  250.3 1.8 collective-permute-done.37.refs_9_.refs_4_
  252.1 0.8 copy-done.16
  252.9 2.8 %sum_fourth.1 = (bf16[112,768]{1,0:T(8,128)(2,1)}, bf16[96,960]{1,0:T(8,128)(2,1)}, bf16[3,96,256]{2,1,0:T(8,128)(2,1)}, bf16[3,96,256]{2,1,0:T(8,128)(2,1)}, bf16[3,96,256]{2,1,0:T(8,128)(2,1)}) custom-call(bf16[2,2,2,2,112,768]{5,4,3,2,1,0:T(8,128)(2,1)} %bitcast.54, bf16[2,2,2,2,112,768]{5,4,3,2,1,0:T(8,128)(2,1)} %bitcast.25.refs_1_, ...), custom_call_target="tpu_custom_call" | custom-call | flops 1000 | bytes 1000 | tf_op jit(solution)/shard_map/sum_fourth/pallas_call | solution.py:721
  255.8 1.0 collective-permute-start.39
  258.1 2.9 %collective-permute-start.44 = (bf16[3,96,256]{2,1,0:T(8,128)(2,1)}, bf16[3,96,256]{2,1,0:T(8,128)(2,1)S(1)}, u32[]{:S(2)}, u32[]{:S(2)}) collective-permute-start(bf16[3,96,256]{2,1,0:T(8,128)(2,1)} %get-tuple-element.228), channel_id=1, source_target_pairs={{0,16},{4,20},{8,24},{12,28},{16,0},{20,4},{24,8},{28,12},{1,17},{... | collective-permute-start | bytes 442376 | tf_op jit(solution)/shard_map/ppermute | solution.py:55
  261.4 1.2 collective-permute-start.46
  263.2 4.8 %finish_down.1 = (f32[96,768]{1,0:T(8,128)}, f32[16,768]{1,0:T(8,128)}, bf16[512,768]{1,0:T(8,128)(2,1)}) custom-call(bf16[2,2,2,2,112,768]{5,4,3,2,1,0:T(8,128)(2,1)} %bitcast.55, bf16[2,2,2,2,112,768]{5,4,3,2,1,0:T(8,128)(2,1)} %bitcast.25.refs_1_, bf16[2,2,2,112,768]{4,3,2,1,0:T(8,128)(2,1)} %collective-permute-done.31.refs_2_, ...), custom_call_target="tpu_custom_call" | custom-call | flops 1000 | bytes 1000 | tf_op jit(solution)/shard_map/finish_down/pallas_call | solution.py:721
  268.0 0.9 slice_reduce_fusion
  268.9 1.6 slice_reduce_fusion.1
  270.6 7.7 %collective-permute-done.44.refs_8_ = bf16[3,96,256]{2,1,0:T(8,128)(2,1)S(1)} collective-permute-done((bf16[3,96,256]{2,1,0:T(8,128)(2,1)}, bf16[3,96,256]{2,1,0:T(8,128)(2,1)S(1)}, u32[]{:S(2)}, u32[]{:S(2)}) %collective-permute-start.44) | collective-permute-done | bytes 147488 | tf_op jit(solution)/shard_map/ppermute | solution.py:55
  279.1 2.6 finish.1
  (177 shorter events, 12.8 us)
Async XLA Ops:
  0.7 23.5 %collective-permute-start.3 = (bf16[512,768]{1,0:T(8,128)(2,1)}, bf16[512,768]{1,0:T(8,128)(2,1)S(1)}, u32[]{:S(2)}, u32[]{:S(2)}) collective-permute-start(bf16[512,768]{1,0:T(8,128)(2,1)} %refs_4_.3), channel_id=1, source_target_pairs={{0,2},{1,3},{2,0},{3,1},{4,6},{5,7},{6,4},{7,5},{8,10},{9,11},{10,... | collective-permute-start | bytes 2359304 | tf_op jit(solution)/shard_map/ppermute | solution.py:55
  4.6 8.4 %collective-permute-start = (bf16[1,96,576]{2,1,0:T(8,128)(2,1)S(1)}, bf16[1,96,576]{2,1,0:T(8,128)(2,1)S(1)}, u32[]{:S(2)}, u32[]{:S(2)}) collective-permute-start(bf16[1,96,576]{2,1,0:T(8,128)(2,1)S(1)} %get-tuple-element.258), channel_id=1, source_target_pairs={{0,16},{4,20},{8,24},{12,28},{16,0},{20,4},{24,8},{28,12},{1,17},{... | collective-permute-start | bytes 331784 | tf_op jit(solution)/shard_map/ppermute | solution.py:55
  13.0 11.1 %collective-permute-start.1 = (bf16[2,96,576]{2,1,0:T(8,128)(2,1)S(1)}, bf16[2,96,576]{2,1,0:T(8,128)(2,1)S(1)}, u32[]{:S(2)}, u32[]{:S(2)}) collective-permute-start(bf16[2,96,576]{2,1,0:T(8,128)(2,1)S(1)} %get-tuple-element.256), channel_id=1, source_target_pairs={{0,8},{4,12},{8,0},{12,4},{16,24},{20,28},{24,16},{28,20},{1,9},{5... | collective-permute-start | bytes 663560 | tf_op jit(solution)/shard_map/ppermute | solution.py:55
  13.8 9.7 %collective-permute-start.2 = (bf16[1,96,1024]{2,1,0:T(8,128)(2,1)S(1)}, bf16[1,96,1024]{2,1,0:T(8,128)(2,1)S(1)}, u32[]{:S(2)}, u32[]{:S(2)}) collective-permute-start(bf16[1,96,1024]{2,1,0:T(8,128)(2,1)S(1)} %maximum_bitcast_fusion.1), channel_id=1, source_target_pairs={{0,16},{4,20},{8,24},{12,28},{16,0},{20,4},{24,8},{28,12},{1,17},{... | collective-permute-start | bytes 589832 | tf_op jit(solution)/shard_map/ppermute | solution.py:55
  24.1 21.7 %copy-start.6 = (bf16[512,768]{1,0:T(8,128)(2,1)}, bf16[512,768]{1,0:T(8,128)(2,1)S(1)}, u32[]{:S(2)}) copy-start(bf16[512,768]{1,0:T(8,128)(2,1)S(1)} %collective-permute-done.3.refs_2_.refs_6_) | copy-start | bytes 2359300
  24.1 16.0 %collective-permute-start.7 = (bf16[512,768]{1,0:T(8,128)(2,1)S(1)}, bf16[512,768]{1,0:T(8,128)(2,1)S(1)}, u32[]{:S(2)}, u32[]{:S(2)}) collective-permute-start(bf16[512,768]{1,0:T(8,128)(2,1)S(1)} %collective-permute-done.3.refs_2_.refs_6_), channel_id=1, source_target_pairs={{0,1},{1,0},{2,3},{3,2},{4,5},{5,4},{6,7},{7,6},{8,9},{9,8},{10,11... | collective-permute-start | bytes 2359304 | tf_op jit(solution)/shard_map/ppermute | solution.py:55
  24.2 6.8 %copy-start.50 = (bf16[192]{0:T(256)(128)(2,1)S(1)}, bf16[192]{0:T(256)(128)(2,1)}, u32[]{:S(2)}) copy-start(bf16[192]{0:T(256)(128)(2,1)} %param.28) | copy-start | bytes 1156
  24.2 6.8 %copy-start.51 = (bf16[192]{0:T(256)(128)(2,1)S(1)}, bf16[192]{0:T(256)(128)(2,1)}, u32[]{:S(2)}) copy-start(bf16[192]{0:T(256)(128)(2,1)} %param.29) | copy-start | bytes 1156
  24.4 21.4 %copy-start.5 = (bf16[2,2,96,576]{3,2,1,0:T(8,128)(2,1)}, bf16[2,2,96,576]{3,2,1,0:T(8,128)(2,1)S(1)}, u32[]{:S(2)}) copy-start(bf16[2,2,96,576]{3,2,1,0:T(8,128)(2,1)S(1)} %copy.45) | copy-start | bytes 1327108
  24.4 15.7 %collective-permute-start.4 = (bf16[4,96,576]{2,1,0:T(8,128)(2,1)S(1)}, bf16[4,96,576]{2,1,0:T(8,128)(2,1)S(1)}, u32[]{:S(2)}, u32[]{:S(2)}) collective-permute-start(bf16[4,96,576]{2,1,0:T(8,128)(2,1)S(1)} %bitcast.41), channel_id=1, source_target_pairs={{0,4},{4,0},{8,12},{12,8},{16,20},{20,16},{24,28},{28,24},{1,5},{5... | collective-permute-start | bytes 1327112 | tf_op jit(solution)/shard_map/ppermute | solution.py:55
  26.9 13.2 %collective-permute-start.5 = (bf16[2,96,1024]{2,1,0:T(8,128)(2,1)}, bf16[2,96,1024]{2,1,0:T(8,128)(2,1)}, u32[]{:S(2)}, u32[]{:S(2)}) collective-permute-start(bf16[2,96,1024]{2,1,0:T(8,128)(2,1)} %get-tuple-element.252), channel_id=1, source_target_pairs={{0,8},{4,12},{8,0},{12,4},{16,24},{20,28},{24,16},{28,20},{1,9},{5... | collective-permute-start | bytes 1179656 | tf_op jit(solution)/shard_map/ppermute | solution.py:55
  30.4 5.8 %collective-permute-start.6 = (bf16[1,96,768]{2,1,0:T(8,128)(2,1)S(1)}, bf16[1,96,768]{2,1,0:T(8,128)(2,1)}, u32[]{:S(2)}, u32[]{:S(2)}) collective-permute-start(bf16[1,96,768]{2,1,0:T(8,128)(2,1)S(1)} %bitcast.68), channel_id=1, source_target_pairs={{0,2},{1,3},{2,0},{3,1},{4,6},{5,7},{6,4},{7,5},{8,10},{9,11},{10,... | collective-permute-start | bytes 442376 | tf_op jit(solution)/shard_map/ppermute | solution.py:55
  30.9 14.9 %collective-permute-start.8 = (bf16[512,768]{1,0:T(8,128)(2,1)S(1)}, bf16[512,768]{1,0:T(8,128)(2,1)}, u32[]{:S(2)}, u32[]{:S(2)}) collective-permute-start(bf16[512,768]{1,0:T(8,128)(2,1)S(1)} %copy-done.4), channel_id=1, source_target_pairs={{0,1},{1,0},{2,3},{3,2},{4,5},{5,4},{6,7},{7,6},{8,9},{9,8},{10,11... | collective-permute-start | bytes 2359304 | tf_op jit(solution)/shard_map/ppermute | solution.py:55
  41.9 9.2 %copy-start.14 = (bf16[2,2,96,1024]{3,2,1,0:T(8,128)(2,1)}, bf16[2,2,96,1024]{3,2,1,0:T(8,128)(2,1)S(1)}, u32[]{:S(2)}) copy-start(bf16[2,2,96,1024]{3,2,1,0:T(8,128)(2,1)S(1)} %copy.46) | copy-start | bytes 2359300
  41.9 19.2 %collective-permute-start.10 = (bf16[4,96,1024]{2,1,0:T(8,128)(2,1)S(1)}, bf16[4,96,1024]{2,1,0:T(8,128)(2,1)S(1)}, u32[]{:S(2)}, u32[]{:S(2)}) collective-permute-start(bf16[4,96,1024]{2,1,0:T(8,128)(2,1)S(1)} %bitcast.59), channel_id=1, source_target_pairs={{0,4},{4,0},{8,12},{12,8},{16,20},{20,16},{24,28},{28,24},{1,5},{5... | collective-permute-start | bytes 2359304 | tf_op jit(solution)/shard_map/ppermute | solution.py:55
  42.5 18.8 %collective-permute-start.11 = (bf16[4,96,1024]{2,1,0:T(8,128)(2,1)S(1)}, bf16[4,96,1024]{2,1,0:T(8,128)(2,1)S(1)}, u32[]{:S(2)}, u32[]{:S(2)}) collective-permute-start(bf16[4,96,1024]{2,1,0:T(8,128)(2,1)S(1)} %bitcast.60), channel_id=1, source_target_pairs={{0,2},{1,3},{2,0},{3,1},{4,6},{5,7},{6,4},{7,5},{8,10},{9,11},{10,... | collective-permute-start | bytes 2359304 | tf_op jit(solution)/shard_map/ppermute | solution.py:55
  43.0 18.3 %collective-permute-start.12 = (bf16[4,96,1024]{2,1,0:T(8,128)(2,1)S(1)}, bf16[4,96,1024]{2,1,0:T(8,128)(2,1)S(1)}, u32[]{:S(2)}, u32[]{:S(2)}) collective-permute-start(bf16[4,96,1024]{2,1,0:T(8,128)(2,1)S(1)} %bitcast.61), channel_id=1, source_target_pairs={{0,1},{1,0},{2,3},{3,2},{4,5},{5,4},{6,7},{7,6},{8,9},{9,8},{10,11... | collective-permute-start | bytes 2359304 | tf_op jit(solution)/shard_map/ppermute | solution.py:55
  44.0 16.7 %collective-permute-start.9 = (bf16[1,2,96,768]{3,2,1,0:T(8,128)(2,1)S(1)}, bf16[1,2,96,768]{3,2,1,0:T(8,128)(2,1)S(1)}, u32[]{:S(2)}, u32[]{:S(2)}) collective-permute-start(bf16[1,2,96,768]{3,2,1,0:T(8,128)(2,1)S(1)} %get-tuple-element.254), channel_id=1, source_target_pairs={{0,16},{4,20},{8,24},{12,28},{16,0},{20,4},{24,8},{28,12},{1,17},{... | collective-permute-start | bytes 884744 | tf_op jit(solution)/shard_map/ppermute | solution.py:55
  51.1 13.9 %copy-start.1 = (bf16[3,2048,128]{2,1,0:T(8,128)(2,1)}, bf16[3,2048,128]{2,1,0:T(8,128)(2,1)S(1)}, u32[]{:S(2)}) copy-start(bf16[3,2048,128]{2,1,0:T(8,128)(2,1)S(1)} %get-tuple-element.145.k_ref) | copy-start | bytes 4718596
  51.1 13.9 %copy-start.2 = (bf16[3,2048,128]{2,1,0:T(8,128)(2,1)}, bf16[3,2048,128]{2,1,0:T(8,128)(2,1)S(1)}, u32[]{:S(2)}) copy-start(bf16[3,2048,128]{2,1,0:T(8,128)(2,1)S(1)} %get-tuple-element.146.v_ref) | copy-start | bytes 4718596
  61.1 18.9 %copy-start.23 = (bf16[4,96,1024]{2,1,0:T(8,128)(2,1)}, bf16[4,96,1024]{2,1,0:T(8,128)(2,1)S(1)}, u32[]{:S(2)}) copy-start(bf16[4,96,1024]{2,1,0:T(8,128)(2,1)S(1)} %collective-permute-done.10.refs_1_) | copy-start | bytes 2359300
  61.3 15.6 %copy-start.24 = (bf16[4,96,1024]{2,1,0:T(8,128)(2,1)}, bf16[4,96,1024]{2,1,0:T(8,128)(2,1)S(1)}, u32[]{:S(2)}) copy-start(bf16[4,96,1024]{2,1,0:T(8,128)(2,1)S(1)} %collective-permute-done.11.refs_2_) | copy-start | bytes 2359300
  61.3 15.6 %copy-start.25 = (bf16[4,96,1024]{2,1,0:T(8,128)(2,1)}, bf16[4,96,1024]{2,1,0:T(8,128)(2,1)S(1)}, u32[]{:S(2)}) copy-start(bf16[4,96,1024]{2,1,0:T(8,128)(2,1)S(1)} %collective-permute-done.12.refs_8_) | copy-start | bytes 2359300
  61.3 18.6 %collective-permute-start.14 = (bf16[4,96,1024]{2,1,0:T(8,128)(2,1)S(1)}, bf16[4,96,1024]{2,1,0:T(8,128)(2,1)S(1)}, u32[]{:S(2)}, u32[]{:S(2)}) collective-permute-start(bf16[4,96,1024]{2,1,0:T(8,128)(2,1)S(1)} %collective-permute-done.10.refs_1_), channel_id=1, source_target_pairs={{0,2},{1,3},{2,0},{3,1},{4,6},{5,7},{6,4},{7,5},{8,10},{9,11},{10,... | collective-permute-start | bytes 2359304 | tf_op jit(solution)/shard_map/ppermute | solution.py:55
  62.3 17.7 %collective-permute-start.16 = (bf16[4,96,1024]{2,1,0:T(8,128)(2,1)S(1)}, bf16[4,96,1024]{2,1,0:T(8,128)(2,1)S(1)}, u32[]{:S(2)}, u32[]{:S(2)}) collective-permute-start(bf16[4,96,1024]{2,1,0:T(8,128)(2,1)S(1)} %collective-permute-done.11.refs_2_), channel_id=1, source_target_pairs={{0,1},{1,0},{2,3},{3,2},{4,5},{5,4},{6,7},{7,6},{8,9},{9,8},{10,11... | collective-permute-start | bytes 2359304 | tf_op jit(solution)/shard_map/ppermute | solution.py:55
  62.3 17.7 %copy-start.15 = (bf16[2,2,96,768]{3,2,1,0:T(8,128)(2,1)}, bf16[2,2,96,768]{3,2,1,0:T(8,128)(2,1)S(1)}, u32[]{:S(2)}) copy-start(bf16[2,2,96,768]{3,2,1,0:T(8,128)(2,1)S(1)} %maximum_bitcast_fusion.refs_4_) | copy-start | bytes 1769476
  62.3 17.5 %collective-permute-start.13 = (bf16[2,2,96,768]{3,2,1,0:T(8,128)(2,1)S(1)}, bf16[2,2,96,768]{3,2,1,0:T(8,128)(2,1)S(1)}, u32[]{:S(2)}, u32[]{:S(2)}) collective-permute-start(bf16[2,2,96,768]{3,2,1,0:T(8,128)(2,1)S(1)} %maximum_bitcast_fusion.refs_4_), channel_id=1, source_target_pairs={{0,8},{4,12},{8,0},{12,4},{16,24},{20,28},{24,16},{28,20},{1,9},{5... | collective-permute-start | bytes 1769480 | tf_op jit(solution)/shard_map/ppermute | solution.py:55
  64.4 15.5 %collective-permute-start.15 = (bf16[2,2,96,768]{3,2,1,0:T(8,128)(2,1)S(1)}, bf16[2,2,96,768]{3,2,1,0:T(8,128)(2,1)S(1)}, u32[]{:S(2)}, u32[]{:S(2)}) collective-permute-start(bf16[2,2,96,768]{3,2,1,0:T(8,128)(2,1)S(1)} %maximum_bitcast_fusion.refs_4_), channel_id=1, source_target_pairs={{0,4},{4,0},{8,12},{12,8},{16,20},{20,16},{24,28},{28,24},{1,5},{5... | collective-permute-start | bytes 1769480 | tf_op jit(solution)/shard_map/ppermute | solution.py:55
  79.8 23.6 %copy-start.9 = (bf16[3,256,128]{2,1,0:T(8,128)(2,1)}, bf16[3,256,128]{2,1,0:T(8,128)(2,1)S(1)}, u32[]{:S(2)}) copy-start(bf16[3,256,128]{2,1,0:T(8,128)(2,1)S(1)} %get-tuple-element.176.refs_16_) | copy-start | bytes 589828
  79.8 22.6 %copy-start.30 = (bf16[2,2,96,768]{3,2,1,0:T(8,128)(2,1)}, bf16[2,2,96,768]{3,2,1,0:T(8,128)(2,1)S(1)}, u32[]{:S(2)}) copy-start(bf16[2,2,96,768]{3,2,1,0:T(8,128)(2,1)S(1)} %collective-permute-done.13.refs_6_) | copy-start | bytes 1769476
  79.9 22.5 %copy-start.31 = (bf16[2,2,96,768]{3,2,1,0:T(8,128)(2,1)}, bf16[2,2,96,768]{3,2,1,0:T(8,128)(2,1)S(1)}, u32[]{:S(2)}) copy-start(bf16[2,2,96,768]{3,2,1,0:T(8,128)(2,1)S(1)} %collective-permute-done.15.refs_5_) | copy-start | bytes 1769476
  80.0 19.9 %copy-start.26 = (bf16[4,96,1024]{2,1,0:T(8,128)(2,1)}, bf16[4,96,1024]{2,1,0:T(8,128)(2,1)S(1)}, u32[]{:S(2)}) copy-start(bf16[4,96,1024]{2,1,0:T(8,128)(2,1)S(1)} %collective-permute-done.14.refs_3_) | copy-start | bytes 2359300
  80.0 20.5 %copy-start.27 = (bf16[4,96,1024]{2,1,0:T(8,128)(2,1)}, bf16[4,96,1024]{2,1,0:T(8,128)(2,1)S(1)}, u32[]{:S(2)}) copy-start(bf16[4,96,1024]{2,1,0:T(8,128)(2,1)S(1)} %collective-permute-done.16.refs_10_) | copy-start | bytes 2359300
  80.0 4.0 %collective-permute-start.18 = (bf16[4,96,1024]{2,1,0:T(8,128)(2,1)S(1)}, bf16[4,96,1024]{2,1,0:T(8,128)(2,1)S(1)}, u32[]{:S(2)}, u32[]{:S(2)}) collective-permute-start(bf16[4,96,1024]{2,1,0:T(8,128)(2,1)S(1)} %collective-permute-done.10.refs_1_), channel_id=1, source_target_pairs={{0,1},{1,0},{2,3},{3,2},{4,5},{5,4},{6,7},{7,6},{8,9},{9,8},{10,11... | collective-permute-start | bytes 2359304 | tf_op jit(solution)/shard_map/ppermute | solution.py:55
  80.1 3.1 %collective-permute-start.17 = (bf16[2,2,96,768]{3,2,1,0:T(8,128)(2,1)S(1)}, bf16[2,2,96,768]{3,2,1,0:T(8,128)(2,1)S(1)}, u32[]{:S(2)}, u32[]{:S(2)}) collective-permute-start(bf16[2,2,96,768]{3,2,1,0:T(8,128)(2,1)S(1)} %maximum_bitcast_fusion.refs_4_), channel_id=1, source_target_pairs={{0,1},{1,0},{2,3},{3,2},{4,5},{5,4},{6,7},{7,6},{8,9},{9,8},{10,11... | collective-permute-start | bytes 1769480 | tf_op jit(solution)/shard_map/ppermute | solution.py:55
  84.0 18.4 %copy-start.28 = (bf16[4,96,1024]{2,1,0:T(8,128)(2,1)}, bf16[4,96,1024]{2,1,0:T(8,128)(2,1)S(1)}, u32[]{:S(2)}) copy-start(bf16[4,96,1024]{2,1,0:T(8,128)(2,1)S(1)} %collective-permute-done.18.refs_9_) | copy-start | bytes 2359300
  84.0 15.8 %collective-permute-start.21 = (bf16[4,96,1024]{2,1,0:T(8,128)(2,1)S(1)}, bf16[4,96,1024]{2,1,0:T(8,128)(2,1)S(1)}, u32[]{:S(2)}, u32[]{:S(2)}) collective-permute-start(bf16[4,96,1024]{2,1,0:T(8,128)(2,1)S(1)} %collective-permute-done.14.refs_3_), channel_id=1, source_target_pairs={{0,1},{1,0},{2,3},{3,2},{4,5},{5,4},{6,7},{7,6},{8,9},{9,8},{10,11... | collective-permute-start | bytes 2359304 | tf_op jit(solution)/shard_map/ppermute | solution.py:55
  84.1 15.6 %collective-permute-start.19 = (bf16[2,2,96,768]{3,2,1,0:T(8,128)(2,1)S(1)}, bf16[2,2,96,768]{3,2,1,0:T(8,128)(2,1)S(1)}, u32[]{:S(2)}, u32[]{:S(2)}) collective-permute-start(bf16[2,2,96,768]{3,2,1,0:T(8,128)(2,1)S(1)} %collective-permute-done.13.refs_6_), channel_id=1, source_target_pairs={{0,4},{4,0},{8,12},{12,8},{16,20},{20,16},{24,28},{28,24},{1,5},{5... | collective-permute-start | bytes 1769480 | tf_op jit(solution)/shard_map/ppermute | solution.py:55
  85.6 14.1 %collective-permute-start.22 = (bf16[2,2,96,768]{3,2,1,0:T(8,128)(2,1)S(1)}, bf16[2,2,96,768]{3,2,1,0:T(8,128)(2,1)S(1)}, u32[]{:S(2)}, u32[]{:S(2)}) collective-permute-start(bf16[2,2,96,768]{3,2,1,0:T(8,128)(2,1)S(1)} %collective-permute-done.13.refs_6_), channel_id=1, source_target_pairs={{0,1},{1,0},{2,3},{3,2},{4,5},{5,4},{6,7},{7,6},{8,9},{9,8},{10,11... | collective-permute-start | bytes 1769480 | tf_op jit(solution)/shard_map/ppermute | solution.py:55
  85.7 14.0 %collective-permute-start.23 = (bf16[2,2,96,768]{3,2,1,0:T(8,128)(2,1)S(1)}, bf16[2,2,96,768]{3,2,1,0:T(8,128)(2,1)S(1)}, u32[]{:S(2)}, u32[]{:S(2)}) collective-permute-start(bf16[2,2,96,768]{3,2,1,0:T(8,128)(2,1)S(1)} %collective-permute-done.15.refs_5_), channel_id=1, source_target_pairs={{0,1},{1,0},{2,3},{3,2},{4,5},{5,4},{6,7},{7,6},{8,9},{9,8},{10,11... | collective-permute-start | bytes 1769480 | tf_op jit(solution)/shard_map/ppermute | solution.py:55
  86.1 11.1 %collective-permute-start.20 = (bf16[2,3,256,128]{3,2,1,0:T(8,128)(2,1)S(1)}, bf16[2,3,256,128]{3,2,1,0:T(8,128)(2,1)S(1)}, u32[]{:S(2)}, u32[]{:S(2)}) collective-permute-start(bf16[2,3,256,128]{3,2,1,0:T(8,128)(2,1)S(1)} %get-tuple-element.172), channel_id=1, source_target_pairs={{0,2},{1,3},{2,0},{3,1},{4,6},{5,7},{6,4},{7,5},{8,10},{9,11},{10,... | collective-permute-start | bytes 1179656 | tf_op jit(solution)/shard_map/ppermute | solution.py:55
  99.8 2.6 collective-permute-start.24
  99.9 2.5 collective-permute-start.25
  142.4 10.3 %collective-permute-start.27 = (bf16[2,8,96,960]{3,2,1,0:T(8,128)(2,1)}, bf16[2,8,96,960]{3,2,1,0:T(8,128)(2,1)}, u32[]{:S(2)}, u32[]{:S(2)}) collective-permute-start(bf16[2,8,96,960]{3,2,1,0:T(8,128)(2,1)} %get-tuple-element.184), channel_id=1, source_target_pairs={{0,1},{1,0},{2,3},{3,2},{4,5},{5,4},{6,7},{7,6},{8,9},{9,8},{10,11... | collective-permute-start | bytes 8847368 | tf_op jit(solution)/shard_map/ppermute | solution.py:55
  142.6 10.1 %collective-permute-start.26 = (bf16[2,8,112,768]{3,2,1,0:T(8,128)(2,1)}, bf16[2,8,112,768]{3,2,1,0:T(8,128)(2,1)}, u32[]{:S(2)}, u32[]{:S(2)}) collective-permute-start(bf16[2,8,112,768]{3,2,1,0:T(8,128)(2,1)} %get-tuple-element.182), channel_id=1, source_target_pairs={{0,1},{1,0},{2,3},{3,2},{4,5},{5,4},{6,7},{7,6},{8,9},{9,8},{10,11... | collective-permute-start | bytes 8257544 | tf_op jit(solution)/shard_map/ppermute | solution.py:55
  143.0 14.1 %collective-permute-start.28 = (bf16[3,256,128]{2,1,0:T(8,128)(2,1)}, bf16[3,256,128]{2,1,0:T(8,128)(2,1)S(1)}, u32[]{:S(2)}, u32[]{:S(2)}) collective-permute-start(bf16[3,256,128]{2,1,0:T(8,128)(2,1)} %get-tuple-element.188), channel_id=1, source_target_pairs={{0,1},{1,0},{2,3},{3,2},{4,5},{5,4},{6,7},{7,6},{8,9},{9,8},{10,11... | collective-permute-start | bytes 589832 | tf_op jit(solution)/shard_map/ppermute | solution.py:55
  143.1 14.0 %collective-permute-start.29 = (bf16[3,256,128]{2,1,0:T(8,128)(2,1)}, bf16[3,256,128]{2,1,0:T(8,128)(2,1)S(1)}, u32[]{:S(2)}, u32[]{:S(2)}) collective-permute-start(bf16[3,256,128]{2,1,0:T(8,128)(2,1)} %get-tuple-element.189), channel_id=1, source_target_pairs={{0,2},{1,3},{2,0},{3,1},{4,6},{5,7},{6,4},{7,5},{8,10},{9,11},{10,... | collective-permute-start | bytes 589832 | tf_op jit(solution)/shard_map/ppermute | solution.py:55
  144.7 12.5 %collective-permute-start.30 = (bf16[3,256,128]{2,1,0:T(8,128)(2,1)}, bf16[3,256,128]{2,1,0:T(8,128)(2,1)S(1)}, u32[]{:S(2)}, u32[]{:S(2)}) collective-permute-start(bf16[3,256,128]{2,1,0:T(8,128)(2,1)} %get-tuple-element.190), channel_id=1, source_target_pairs={{0,3},{1,2},{2,1},{3,0},{4,7},{5,6},{6,5},{7,4},{8,11},{9,10},{10,... | collective-permute-start | bytes 589832 | tf_op jit(solution)/shard_map/ppermute | solution.py:55
  157.2 36.8 %collective-permute-start.32 = (bf16[2,2,2,96,960]{4,3,2,1,0:T(8,128)(2,1)}, bf16[2,2,2,96,960]{4,3,2,1,0:T(8,128)(2,1)}, u32[]{:S(2)}, u32[]{:S(2)}) collective-permute-start(bf16[2,2,2,96,960]{4,3,2,1,0:T(8,128)(2,1)} %get-tuple-element.199), channel_id=1, source_target_pairs={{0,4},{4,0},{8,12},{12,8},{16,20},{20,16},{24,28},{28,24},{1,5},{5... | collective-permute-start | bytes 4423688 | tf_op jit(solution)/shard_map/ppermute | solution.py:55
  158.7 32.3 %collective-permute-start.31 = (bf16[2,2,2,112,768]{4,3,2,1,0:T(8,128)(2,1)}, bf16[2,2,2,112,768]{4,3,2,1,0:T(8,128)(2,1)}, u32[]{:S(2)}, u32[]{:S(2)}) collective-permute-start(bf16[2,2,2,112,768]{4,3,2,1,0:T(8,128)(2,1)} %get-tuple-element.191), channel_id=1, source_target_pairs={{0,2},{1,3},{2,0},{3,1},{4,6},{5,7},{6,4},{7,5},{8,10},{9,11},{10,... | collective-permute-start | bytes 4128776 | tf_op jit(solution)/shard_map/ppermute | solution.py:55
  197.4 19.6 %collective-permute-start.34 = (bf16[2,2,96,960]{3,2,1,0:T(8,128)(2,1)}, bf16[2,2,96,960]{3,2,1,0:T(8,128)(2,1)S(1)}, u32[]{:S(2)}, u32[]{:S(2)}) collective-permute-start(bf16[2,2,96,960]{3,2,1,0:T(8,128)(2,1)} %get-tuple-element.206), channel_id=1, source_target_pairs={{0,2},{1,3},{2,0},{3,1},{4,6},{5,7},{6,4},{7,5},{8,10},{9,11},{10,... | collective-permute-start | bytes 2211848 | tf_op jit(solution)/shard_map/ppermute | solution.py:55
  199.0 18.0 %collective-permute-start.33 = (bf16[2,2,112,768]{3,2,1,0:T(8,128)(2,1)}, bf16[2,2,112,768]{3,2,1,0:T(8,128)(2,1)}, u32[]{:S(2)}, u32[]{:S(2)}) collective-permute-start(bf16[2,2,112,768]{3,2,1,0:T(8,128)(2,1)} %get-tuple-element.201), channel_id=1, source_target_pairs={{0,8},{4,12},{8,0},{12,4},{16,24},{20,28},{24,16},{28,20},{1,9},{5... | collective-permute-start | bytes 2064392 | tf_op jit(solution)/shard_map/ppermute | solution.py:55
  222.3 2.5 collective-permute-start.35
  229.6 28.5 %collective-permute-start.40 = (bf16[512,768]{1,0:T(8,128)(2,1)}, bf16[512,768]{1,0:T(8,128)(2,1)}, u32[]{:S(2)}, u32[]{:S(2)}) collective-permute-start(bf16[512,768]{1,0:T(8,128)(2,1)} %get-tuple-element.224), channel_id=1, source_target_pairs={{0,2},{1,3},{2,0},{3,1},{4,6},{5,7},{6,4},{7,5},{8,10},{9,11},{10,... | collective-permute-start | bytes 2359304 | tf_op jit(solution)/shard_map/ppermute | solution.py:55
  231.2 20.9 %collective-permute-start.38 = (bf16[3,2,2,96,256]{4,3,2,1,0:T(8,128)(2,1)}, bf16[3,2,2,96,256]{4,3,2,1,0:T(8,128)(2,1)S(1)}, u32[]{:S(2)}, u32[]{:S(2)}) collective-permute-start(bf16[3,2,2,96,256]{4,3,2,1,0:T(8,128)(2,1)} %get-tuple-element.220), channel_id=1, source_target_pairs={{0,4},{4,0},{8,12},{12,8},{16,20},{20,16},{24,28},{28,24},{1,5},{5... | collective-permute-start | bytes 1769480 | tf_op jit(solution)/shard_map/ppermute | solution.py:55
  232.1 18.1 %collective-permute-start.36 = (bf16[2,112,768]{2,1,0:T(8,128)(2,1)}, bf16[2,112,768]{2,1,0:T(8,128)(2,1)S(1)}, u32[]{:S(2)}, u32[]{:S(2)}) collective-permute-start(bf16[2,112,768]{2,1,0:T(8,128)(2,1)} %get-tuple-element.212), channel_id=1, source_target_pairs={{0,16},{4,20},{8,24},{12,28},{16,0},{20,4},{24,8},{28,12},{1,17},{... | collective-permute-start | bytes 1032200 | tf_op jit(solution)/shard_map/ppermute | solution.py:55
  234.5 17.6 %collective-permute-start.37 = (bf16[2,96,960]{2,1,0:T(8,128)(2,1)}, bf16[2,96,960]{2,1,0:T(8,128)(2,1)}, u32[]{:S(2)}, u32[]{:S(2)}) collective-permute-start(bf16[2,96,960]{2,1,0:T(8,128)(2,1)} %get-tuple-element.218), channel_id=1, source_target_pairs={{0,8},{4,12},{8,0},{12,4},{16,24},{20,28},{24,16},{28,20},{1,9},{5... | collective-permute-start | bytes 1105928 | tf_op jit(solution)/shard_map/ppermute | solution.py:55
  240.4 20.6 %collective-permute-start.41 = (bf16[256,768]{1,0:T(8,128)(2,1)}, bf16[256,768]{1,0:T(8,128)(2,1)}, u32[]{:S(2)}, u32[]{:S(2)}) collective-permute-start(bf16[256,768]{1,0:T(8,128)(2,1)} %get-tuple-element.214), channel_id=1, source_target_pairs={{0,1},{1,0},{2,3},{3,2},{4,5},{5,4},{6,7},{7,6},{8,9},{9,8},{10,11... | collective-permute-start | bytes 1179656 | tf_op jit(solution)/shard_map/ppermute | solution.py:55
  250.3 11.2 %collective-permute-start.42 = (bf16[256,768]{1,0:T(8,128)(2,1)}, bf16[256,768]{1,0:T(8,128)(2,1)}, u32[]{:S(2)}, u32[]{:S(2)}) collective-permute-start(bf16[256,768]{1,0:T(8,128)(2,1)} %get-tuple-element.215), channel_id=1, source_target_pairs={{0,1},{1,0},{2,3},{3,2},{4,5},{5,4},{6,7},{7,6},{8,9},{9,8},{10,11... | collective-permute-start | bytes 1179656 | tf_op jit(solution)/shard_map/ppermute | solution.py:55
  255.8 6.8 %collective-permute-start.39 = (bf16[112,768]{1,0:T(8,128)(2,1)}, bf16[112,768]{1,0:T(8,128)(2,1)S(1)}, u32[]{:S(2)}, u32[]{:S(2)}) collective-permute-start(bf16[112,768]{1,0:T(8,128)(2,1)} %get-tuple-element.222), channel_id=1, source_target_pairs={{0,4},{4,0},{8,12},{12,8},{16,20},{20,16},{24,28},{28,24},{1,5},{5... | collective-permute-start | bytes 516104 | tf_op jit(solution)/shard_map/ppermute | solution.py:55
  258.0 20.3 %collective-permute-start.43 = (bf16[96,960]{1,0:T(8,128)(2,1)}, bf16[96,960]{1,0:T(8,128)(2,1)S(1)}, u32[]{:S(2)}, u32[]{:S(2)}) collective-permute-start(bf16[96,960]{1,0:T(8,128)(2,1)} %get-tuple-element.227), channel_id=1, source_target_pairs={{0,16},{4,20},{8,24},{12,28},{16,0},{20,4},{24,8},{28,12},{1,17},{... | collective-permute-start | bytes 552968 | tf_op jit(solution)/shard_map/ppermute | solution.py:55
  258.1 20.2 %collective-permute-start.44 = (bf16[3,96,256]{2,1,0:T(8,128)(2,1)}, bf16[3,96,256]{2,1,0:T(8,128)(2,1)S(1)}, u32[]{:S(2)}, u32[]{:S(2)}) collective-permute-start(bf16[3,96,256]{2,1,0:T(8,128)(2,1)} %get-tuple-element.228), channel_id=1, source_target_pairs={{0,16},{4,20},{8,24},{12,28},{16,0},{20,4},{24,8},{28,12},{1,17},{... | collective-permute-start | bytes 442376 | tf_op jit(solution)/shard_map/ppermute | solution.py:55
  261.0 17.3 %collective-permute-start.45 = (bf16[3,96,256]{2,1,0:T(8,128)(2,1)}, bf16[3,96,256]{2,1,0:T(8,128)(2,1)S(1)}, u32[]{:S(2)}, u32[]{:S(2)}) collective-permute-start(bf16[3,96,256]{2,1,0:T(8,128)(2,1)} %get-tuple-element.229), channel_id=1, source_target_pairs={{0,8},{4,12},{8,0},{12,4},{16,24},{20,28},{24,16},{28,20},{1,9},{5... | collective-permute-start | bytes 442376 | tf_op jit(solution)/shard_map/ppermute | solution.py:55
  261.4 16.9 %collective-permute-start.46 = (bf16[3,96,256]{2,1,0:T(8,128)(2,1)}, bf16[3,96,256]{2,1,0:T(8,128)(2,1)S(1)}, u32[]{:S(2)}, u32[]{:S(2)}) collective-permute-start(bf16[3,96,256]{2,1,0:T(8,128)(2,1)} %get-tuple-element.230), channel_id=1, source_target_pairs={{0,24},{4,28},{8,16},{12,20},{16,8},{20,12},{24,0},{28,4},{1,25},{... | collective-permute-start | bytes 442376 | tf_op jit(solution)/shard_map/ppermute | solution.py:55
  (35 other events, 123.8 us)

commit v5 on v4

--- a/solution.py
+++ b/solution.py
@@ -1,5 +1,6 @@
 import functools
 import itertools
+import math
 
 import jax
 import jax.numpy as jnp
@@ -228,7 +229,7 @@
     pieces = pl.BlockSpec((2, 1, block, LANES), lambda i: (0, first + i, 0, 0))
     shape = jax.ShapeDtypeStruct
     return pl.pallas_call(
-        functools.partial(forward_kernel, unroll=4),
+        functools.partial(forward_kernel, unroll=4 if first else 2),
         grid=(count,),
         in_specs=[one] * 3 + [ANY_SPEC] * len(before),
         out_specs=[one, one, piece, piece, pieces],
@@ -243,9 +244,35 @@
     )(q, k, v, *before)
 
 
-def backward_kernel(q_ref, k_ref, v_ref, o_ref, *refs, placed):
+def by_head(w_refs, masks, heads, placed, target):
+    for ref, entries in zip(w_refs, masks, strict=True):
+        for z, mask in enumerate(entries):
+            place = place_of(mask, ref.shape[1], placed)
+            for h in range(heads):
+                for kind in range(3):
+                    start = (kind * heads + h) * HEAD_DIM
+                    stop = (h * 3 + kind) * HEAD_DIM
+                    target[place, stop : stop + HEAD_DIM] = ref[z, :, start : start + HEAD_DIM]
+
+
+def through_weights(g_refs, part, w_s):
+    three = 3 * HEAD_DIM
+    total, h = None, 0
+    for ref in g_refs:
+        for i in range(ref.shape[0]):
+            term = dot_nt(ref[i, part, :], w_s[:, h * three : (h + 1) * three])
+            total = term if total is None else total + term
+            h += 1
+    return total
+
+
+def backward_kernel(q_ref, k_ref, v_ref, o_ref, *refs, placed, masks, heads):
     d_refs, x_refs = refs[:4], refs[4:8]
-    g_ref, gw_ref, dk_s, dv_s, gw_s, d_s = refs[-6:]
+    if masks:
+        g_ref, gw_ref, *dx_refs, dk_s, dv_s, gw_s, d_s, w_s = refs[-10:]
+        by_head(refs[9 : 9 + len(masks)], masks, heads, placed, w_s)
+    else:
+        g_ref, gw_ref, dk_s, dv_s, gw_s, d_s = refs[-6:]
     seq = q_ref.shape[1]
     block = seq // 8
     rows = seq // 4
@@ -298,9 +325,16 @@
     for i in range(gw_ref.shape[1]):
         gw_ref[0, i, :, : 3 * HEAD_DIM] = gw_s[place_of(i, share, placed), :]
         gw_ref[0, i, :, 3 * HEAD_DIM :] = side
-
-
-def attention_backward(first, count, q, k, v, out, grads, parts, blocks, before):
+    if masks:
+        half = rows // 2
+        spread = (3 * rows, 3 * rows + half, 2 * rows)
+        for out, start in zip(dx_refs, spread, strict=True):
+            count = math.prod(out.shape[:-1])
+            total = through_weights((refs[8], g_ref), pl.ds(start, count), w_s)
+            out[...] = total.astype(BF16).reshape(out.shape)
+
+
+def attention_backward(first, count, q, k, v, out, grads, parts, blocks, before, more=()):
     heads, seq, _ = k.shape
     rows, width = parts[0].shape
     one = pl.BlockSpec((1, seq, LANES), lambda i: (first + i, 0, 0))
@@ -309,65 +343,69 @@
     three = 3 * HEAD_DIM
     share = width // blocks
     shape = jax.ShapeDtypeStruct
-    alias = {12: 0, 13: 1} if before else {}
+
+    def fixed(array):
+        return pl.BlockSpec(array.shape, lambda i: (0,) * len(array.shape))
+
+    others, pieces, masks = more if more else (None, [], ())
+    extra = [others, *pieces] if more else []
+    dx = [shape((rows // 2, width), BF16)] * 2 + [shape((2, rows // 2, width), BF16)] if more else []
     return pl.pallas_call(
-        functools.partial(backward_kernel, placed=blocks > 1),
+        functools.partial(backward_kernel, placed=blocks > 1, masks=masks, heads=heads),
         grid=(count,),
-        in_specs=[one] * 4 + [piece] * 4 + [whole] * 4 + [ANY_SPEC] * len(before),
+        in_specs=[one] * 4
+        + [piece] * 4
+        + [whole] * 4
+        + [fixed(array) for array in extra]
+        + [ANY_SPEC] * len(before),
         out_specs=[
-            pl.BlockSpec((1, seq, three), lambda i: (first + i, 0, 0)),
+            pl.BlockSpec((1, seq, three), lambda i: (i, 0, 0)),
             pl.BlockSpec((1, blocks, share, 4 * HEAD_DIM), lambda i: (first + i, 0, 0, 0)),
-        ],
+        ]
+        + [fixed(array) for array in dx],
         out_shape=[
-            shape((heads, seq, three), BF16),
+            shape((count, seq, three), BF16),
             shape((heads, blocks, share, 4 * HEAD_DIM), BF16),
-        ],
+        ]
+        + dx,
         scratch_shapes=[
             pltpu.VMEM((seq, LANES), F32),
             pltpu.VMEM((seq, LANES), F32),
             pltpu.VMEM((width, three), BF16),
             pltpu.VMEM((4, seq // 8, LANES), BF16),
-        ],
-        input_output_aliases=alias,
+        ]
+        + ([pltpu.VMEM((width, heads * three), BF16)] if more else []),
+        input_output_aliases={12 + len(extra): 1} if before else {},
         compiler_params=params(),
         cost_estimate=cost(1000, 1000),
         name="attention_backward",
-    )(q, k, v, out, *grads, *parts, *before)
-
-
-def input_kernel(g_ref, *refs, masks, which, placed):
-    w_refs = refs[: len(masks)]
-    outs, w_s = refs[len(masks) : -1], refs[-1]
-    heads, seq, three = g_ref.shape
-    for ref, entries in zip(w_refs, masks, strict=True):
-        for z, mask in enumerate(entries):
-            place = place_of(mask, ref.shape[1], placed)
-            for h in range(heads):
-                for kind in range(3):
-                    start = (kind * heads + h) * HEAD_DIM
-                    stop = (h * 3 + kind) * HEAD_DIM
-                    w_s[place, stop : stop + HEAD_DIM] = ref[z, :, start : start + HEAD_DIM]
-    for out, (start, count) in zip(outs, which, strict=True):
-        part = pl.ds(start, count)
-        total = dot_nt(g_ref[0, part, :], w_s[:, :three])
-        for h in range(1, heads):
-            total += dot_nt(g_ref[h, part, :], w_s[:, h * three : (h + 1) * three])
-        out[...] = total.astype(out.dtype)
-
-
-def input_part(g_all, pieces, masks, which, placed):
-    heads, seq, three = g_all.shape
+    )(q, k, v, out, *grads, *parts, *extra, *before)
+
+
+def input_kernel(*refs, masks, which, placed, count, heads):
+    g_refs, w_refs = refs[:count], refs[count : count + len(masks)]
+    outs, w_s = refs[count + len(masks) : -1], refs[-1]
+    by_head(w_refs, masks, heads, placed, w_s)
+    for out, (start, size) in zip(outs, which, strict=True):
+        out[...] = through_weights(g_refs, pl.ds(start, size), w_s).astype(out.dtype)
+
+
+def input_part(g_parts, pieces, masks, which, placed):
+    heads = sum(part.shape[0] for part in g_parts)
+    three = g_parts[0].shape[2]
     width = pieces[0].shape[0] * pieces[0].shape[1] * len(pieces)
     return pl.pallas_call(
-        functools.partial(input_kernel, masks=masks, which=which, placed=placed),
-        in_specs=[VMEM_SPEC] * (1 + len(pieces)),
+        functools.partial(
+            input_kernel, masks=masks, which=which, placed=placed, count=len(g_parts), heads=heads
+        ),
+        in_specs=[VMEM_SPEC] * (len(g_parts) + len(pieces)),
         out_specs=[VMEM_SPEC] * len(which),
-        out_shape=[jax.ShapeDtypeStruct((count, width), BF16) for _, count in which],
+        out_shape=[jax.ShapeDtypeStruct((size, width), BF16) for _, size in which],
         scratch_shapes=[pltpu.VMEM((width, heads * three), BF16)],
         compiler_params=params(),
         cost_estimate=cost(1000, 1000),
         name="input_part",
-    )(g_all, *pieces)
+    )(*g_parts, *pieces)
 
 
 def middle_kernel(*refs, plan, blocks):
@@ -653,14 +691,14 @@
     extra_out = rest[: len(rest) - terms - 1]
     held, sems = rest[len(extra_out) : -1], rest[-1]
     loads = []
-    for _, _, _, parts in jobs:
+    for _, _, _, parts, _ in jobs:
         for source, index, start, size in parts:
             at = len(loads)
             picked = ins[source].at[index + (slice(None), pl.ds(start, size))]
             loads.append(pltpu.make_async_copy(picked, held[at], sems.at[at]))
             loads[-1].start()
     at = 0
-    for out, start, lead, parts in jobs:
+    for out, start, lead, parts, base in jobs:
         mine = range(at, at + len(parts))
         at += len(parts)
         for i in mine:
@@ -671,7 +709,7 @@
             for i in mine[1:]:
                 total += held[i][index].astype(F32)
             target = outs[out]
-            target[index + (slice(None), slice(start, start + size))] = total.astype(target.dtype)
+            target[base + index + (slice(None), slice(start, start + size))] = total.astype(target.dtype)
     if extra is not None:
         extra(outs, more, extra_out)
 
@@ -703,7 +741,8 @@
     arrays, jobs, shapes, scratch = [], [], [], []
     for out, columns in enumerate(groups):
         start = 0
-        for parts in columns:
+        stacked = isinstance(columns, tuple)
+        for at, parts in enumerate(columns):
             coded = []
             for array, index, first, size in parts:
                 known = [i for i, other in enumerate(arrays) if other is array]
@@ -713,9 +752,10 @@
                 sizes = [n for n, i in zip(array.shape, index) if isinstance(i, slice)]
                 sizes += [array.shape[-2], size]
                 scratch.append(pltpu.VMEM(tuple(sizes), array.dtype))
-            jobs.append((out, start, tuple(sizes[:-2]), coded))
-            start += coded[0][3]
-        shapes.append(tuple(sizes[:-1]) + (start,))
+            jobs.append((out, start, tuple(sizes[:-2]), coded, (at,) if stacked else ()))
+            start += 0 if stacked else coded[0][3]
+        front = (len(columns),) if stacked else ()
+        shapes.append(front + tuple(sizes[:-1]) + (coded[0][3] if stacked else start,))
     outs = [jax.ShapeDtypeStruct(shape, dtype) for shape in shapes]
     held = [] if keep else [pltpu.VMEM(shape, dtype) for shape in shapes]
     result = pl.pallas_call(
@@ -916,31 +956,28 @@
         groups = [[down.away(down_names[0])], [up.away(up_names[0])]]
         move_d, move_u = reduce_call("sum_second", groups, BF16)
         q_kept = after(q_kept, move_d)
-        g_all, g_w = attention_backward(
-            heads - 1, 1, q_kept, k, v, out, grads, parts, blocks, before
+        more = (before[0], w_qkv, w_masks)
+        g_last, g_w, *first = attention_backward(
+            heads - 1, 1, q_kept, k, v, out, grads, parts, blocks, before[1:], more
         )
+        g_parts = [before[0], g_last]
     else:
         g_all, g_w = attention_backward(0, heads, q_kept, k, v, out, grads, parts, blocks, [])
     if placed:
-        got_d = after(send(move_d, down_names.pop(0)), g_all)
-        got_u = after(send(move_u, up_names.pop(0)), g_all)
-        down.join(got_d)
-        up.join(got_u)
-        g_all, got_d, got_u = after((g_all, got_d, got_u), g_w)
-        g_all = after(g_all, got_d, got_u)
+        down.join(after(send(move_d, down_names.pop(0)), g_last))
+        up.join(after(send(move_u, up_names.pop(0)), g_last))
+        got_part = [core(part) for part in first[:2]]
     half = rows // 2
-    first = input_part(g_all, w_qkv, w_masks, ((3 * rows, rows), (2 * rows, rows)), placed)
-    got_part = core(first[0])
     own_parts = ((rows, half), (rows + half, half), (0, rows))
     if placed:
         qkv = Sum(["h"] + names, 4 * HEAD_DIM)
         qkv.join(axes_of(g_w, 1))
         groups = [[down.away(down_names[0])], [up.away(up_names[0])], [qkv.away(0)]]
-        groups.append([[(first[1], (), 0, width), (got_part, (), 0, width)]])
+        groups.append(tuple([(first[2], (i,), 0, width), (got_part[i], (), 0, width)] for i in range(2)))
         move_d, move_u, move_qkv, crossed = reduce_call("sum_third", groups, BF16)
         crossed = cross(crossed)
-        g_all = after(g_all, move_d)
-        second = input_part(g_all, w_qkv, w_masks, own_parts, placed)
+        g_parts = after(g_parts, move_d)
+        second = input_part(g_parts, w_qkv, w_masks, own_parts, placed)
         near = [core(part) for part in second[:2]]
         down.join(after(send(move_d, down_names.pop(0)), *second))
         up.join(after(send(move_u, up_names.pop(0)), *second))
@@ -966,7 +1003,7 @@
             for i in range(2):
                 part = pl.ds(i * half, half)
                 total = ins[0][part, :]
-                for term in (ins[1][part, :], ins[2][part, :], ins[3 + i][...]):
+                for term in (ins[1][part, :], ins[2][i], ins[3 + i][...]):
                     total += term.astype(F32)
                 outs[2][part, :] = total.astype(BF16)
 
@@ -989,8 +1026,9 @@
         for got in gots_qkv:
             qkv.join(got)
     else:
-        crossed = cross(add(first[1], got_part).astype(BF16))
-        second = input_part(g_all, w_qkv, w_masks, own_parts, placed)
+        first = input_part([g_all], w_qkv, w_masks, ((3 * rows, rows), (2 * rows, rows)), placed)
+        crossed = cross(add(first[1], core(first[0])).astype(BF16))
+        second = input_part([g_all], w_qkv, w_masks, own_parts, placed)
         near = jnp.concatenate([core(part) for part in second[:2]])
 
     if placed:

time: 283 us -> 280 us (0.989)
    pallas_call x2 -> x1, Pallas kernels: 10 us -> 4.76 us  [input_part(): pl.pallas_call(functools.partial(input_kernel, masks=masks, which=which,...]
    pallas_call x4, Pallas kernels: 65.7 us -> 69 us  [the longest x2 50.9 us: attention_backward(): pl.pallas_call(functools.partial(backward_kernel, placed=blocks > 1, mask...]
    unnamed x105 -> x103, local copies, waits for them, and re-layouts: 8.23 us -> 7.4 us
    ppermute x47 -> x48, starting transfers between devices: 46.1 us -> 45.7 us  [swap(): return lax.ppermute(value, axis, [(i, i ^ bits) for i in range(size)])]
    ppermute x47 -> x48, waiting for transfers between devices: 72.3 us -> 72.1 us  [swap(): return lax.ppermute(value, axis, [(i, i ^ bits) for i in range(size)])]
  transfers between devices with their start and end apart: 47 -> 48, of which waited for: 21 -> 21; matrix products, arithmetic and copies ran while one was open for 4% -> 4% of each run, Pallas kernels for 31% -> 33%
where the time goes in v5:
time: 280 us; the launch traced here: 278 us
  Pallas kernels  140 us (50%)
  waiting for transfers between devices  72.1 us (26%)
  starting transfers between devices  45.7 us (16%)
  local copies, waits for them, and re-layouts  10.7 us (4%)
  other arithmetic  7.83 us (3%)
    ppermute x48, waiting for transfers between devices, swap(): return lax.ppermute(value, axis, [(i, i ^ bits) for i in range(size)])  72.1 us
    pallas_call x2, Pallas kernels, attention_backward(): pl.pallas_call(functools.partial(backward_kernel, placed=blocks > 1, mask...  50.9 us
    ppermute x48, starting transfers between devices, swap(): return lax.ppermute(value, axis, [(i, i ^ bits) for i in range(size)])  45.7 us
    pallas_call x1, Pallas kernels, middle(): pl.pallas_call(functools.partial(middle_kernel, plan=plan, blocks=blocks)...  39 us
    pallas_call x6, Pallas kernels, reduce_call(): pl.pallas_call(functools.partial(reduce_kernel if keep else reduce_inside...  21.9 us
    pallas_call x2, Pallas kernels, attention_forward(): pl.pallas_call(functools.partial(forward_kernel, unroll=4 if first else 2...  18.1 us
    unnamed x103, local copies, waits for them, and re-layouts  7.4 us
  transfers between devices with their start and end apart: 48, of which 21 were waited for; matrix products, arithmetic and copies ran while one was open for 4% of the time, Pallas kernels for 33%

profile of v5, /device:TPU:0, one launch (start us, length us, event | category | flops | bytes accessed | tf_op | source)
XLA Modules:
  0.0 278.5 jit_solution(13644731206790900294)
XLA Ops:
  0.7 3.0 %collective-permute-start.3 = (bf16[512,768]{1,0:T(8,128)(2,1)}, bf16[512,768]{1,0:T(8,128)(2,1)S(1)}, u32[]{:S(2)}, u32[]{:S(2)}) collective-permute-start(bf16[512,768]{1,0:T(8,128)(2,1)} %refs_4_.3), channel_id=1, source_target_pairs={{0,2},{1,3},{2,0},{3,1},{4,6},{5,7},{6,4},{7,5},{8,10},{9,11},{10,... | collective-permute-start | bytes 2359304 | tf_op jit(solution)/shard_map/ppermute | solution.py:56
  3.7 0.9 fusion.5
  4.6 2.7 collective-permute-start
  7.3 0.9 copy.43
  8.1 0.8 dynamic_slice.3
  9.0 1.0 maximum_bitcast_fusion.1
  10.0 3.0 %collective-permute-done = bf16[1,96,576]{2,1,0:T(8,128)(2,1)S(1)} collective-permute-done((bf16[1,96,576]{2,1,0:T(8,128)(2,1)S(1)}, bf16[1,96,576]{2,1,0:T(8,128)(2,1)S(1)}, u32[]{:S(2)}, u32[]{:S(2)}) %collective-permute-start) | collective-permute-done | bytes 110624 | tf_op jit(solution)/shard_map/ppermute | solution.py:56
  13.0 0.7 collective-permute-start.1
  13.8 3.4 %collective-permute-start.2 = (bf16[1,96,1024]{2,1,0:T(8,128)(2,1)S(1)}, bf16[1,96,1024]{2,1,0:T(8,128)(2,1)S(1)}, u32[]{:S(2)}, u32[]{:S(2)}) collective-permute-start(bf16[1,96,1024]{2,1,0:T(8,128)(2,1)S(1)} %maximum_bitcast_fusion.1), channel_id=1, source_target_pairs={{0,16},{4,20},{8,24},{12,28},{16,0},{20,4},{24,8},{28,12},{1,17},{... | collective-permute-start | bytes 589832 | tf_op jit(solution)/shard_map/ppermute | solution.py:56
  17.1 6.3 %collective-permute-done.2 = bf16[1,96,1024]{2,1,0:T(8,128)(2,1)S(1)} collective-permute-done((bf16[1,96,1024]{2,1,0:T(8,128)(2,1)S(1)}, bf16[1,96,1024]{2,1,0:T(8,128)(2,1)S(1)}, u32[]{:S(2)}, u32[]{:S(2)}) %collective-permute-start.2) | collective-permute-done | bytes 196640 | tf_op jit(solution)/shard_map/ppermute | solution.py:56
  23.4 0.7 collective-permute-done.1
  24.4 1.6 collective-permute-start.4
  26.0 0.9 fusion.1
  26.9 3.5 %collective-permute-start.5 = (bf16[2,96,1024]{2,1,0:T(8,128)(2,1)}, bf16[2,96,1024]{2,1,0:T(8,128)(2,1)}, u32[]{:S(2)}, u32[]{:S(2)}) collective-permute-start(bf16[2,96,1024]{2,1,0:T(8,128)(2,1)} %get-tuple-element.254), channel_id=1, source_target_pairs={{0,8},{4,12},{8,0},{12,4},{16,24},{20,28},{24,16},{28,20},{1,9},{5... | collective-permute-start | bytes 1179656 | tf_op jit(solution)/shard_map/ppermute | solution.py:56
  31.7 4.4 %collective-permute-done.6 = bf16[1,96,768]{2,1,0:T(8,128)(2,1)} collective-permute-done((bf16[1,96,768]{2,1,0:T(8,128)(2,1)S(1)}, bf16[1,96,768]{2,1,0:T(8,128)(2,1)}, u32[]{:S(2)}, u32[]{:S(2)}) %collective-permute-start.6) | collective-permute-done | bytes 147488 | tf_op jit(solution)/shard_map/ppermute | solution.py:56
  36.1 4.0 %collective-permute-done.5 = bf16[2,96,1024]{2,1,0:T(8,128)(2,1)} collective-permute-done((bf16[2,96,1024]{2,1,0:T(8,128)(2,1)}, bf16[2,96,1024]{2,1,0:T(8,128)(2,1)}, u32[]{:S(2)}, u32[]{:S(2)}) %collective-permute-start.5) | collective-permute-done | bytes 393248 | tf_op jit(solution)/shard_map/ppermute | solution.py:56
  40.2 1.7 pad_maximum_fusion
  43.0 0.9 fusion.6
  44.0 1.8 collective-permute-start.9
  45.8 5.3 %project.1 = (bf16[3,2048,128]{2,1,0:T(8,128)(2,1)S(1)}, bf16[3,2048,128]{2,1,0:T(8,128)(2,1)S(1)}, bf16[3,2048,128]{2,1,0:T(8,128)(2,1)S(1)}) custom-call(bf16[512,768]{1,0:T(8,128)(2,1)S(1)} %copy-done.4, bf16[512,768]{1,0:T(8,128)(2,1)} %collective-permute-done.8.refs_1_.refs_5_, bf16[512,768]{1,0:T(8,128)(2,1)S(1)} %collective-permute-done.3.refs_2_.refs_6_, ...), custom_call_target="tpu_custom_call" | custom-call | flops 1000 | bytes 1000 | tf_op jit(solution)/shard_map/project/pallas_call | solution.py:157
  51.1 6.2 %attention_forward.2 = (bf16[3,2048,128]{2,1,0:T(8,128)(2,1)S(1)}, f32[3,2048,128]{2,1,0:T(8,128)S(1)}, bf16[3,256,128]{2,1,0:T(8,128)(2,1)S(1)}, bf16[3,256,128...) custom-call(bf16[3,2048,128]{2,1,0:T(8,128)(2,1)S(1)} %get-tuple-element.145.q_ref, ...), custom_call_target="tpu_custom_call" | custom-call | flops 1000 | bytes 1000 | tf_op jit(solution)/shard_map/attention_forward/pallas_call | solution.py:231
  57.3 3.3 %collective-permute-done.9 = bf16[1,2,96,768]{3,2,1,0:T(8,128)(2,1)S(1)} collective-permute-done((bf16[1,2,96,768]{3,2,1,0:T(8,128)(2,1)S(1)}, bf16[1,2,96,768]{3,2,1,0:T(8,128)(2,1)S(1)}, u32[]{:S(2)}, u32[]{:S(2)}) %collective-permute-start.9) | collective-permute-done | bytes 294944 | tf_op jit(solution)/shard_map/ppermute | solution.py:56
  61.3 0.9 collective-permute-start.14
  62.3 2.1 collective-permute-start.13
  65.0 11.8 %attention_forward.3 = (bf16[3,2048,128]{2,1,0:T(8,128)(2,1)S(1)}, f32[3,2048,128]{2,1,0:T(8,128)S(1)}, bf16[3,256,128]{2,1,0:T(8,128)(2,1)S(1)}, bf16[3,256,128...) custom-call(bf16[3,2048,128]{2,1,0:T(8,128)(2,1)S(1)} %get-tuple-ele, ...), custom_call_target="tpu_custom_call", output_to_operand_aliasing={{0}: (3, {}), {1}: (4, {}), {2}: (5, {}), {3}: (6, {}), {4}... | custom-call | flops 1000 | bytes 1000 | tf_op jit(solution)/shard_map/attention_forward/pallas_call | solution.py:231
  76.9 1.7 copy-done
  78.7 1.2 copy-done.3
  80.5 2.6 collective-permute-done.17.refs_12_
  83.2 0.8 copy-done.31
  84.1 1.5 collective-permute-start.19
  86.2 1.5 collective-permute-start.20
  87.6 9.6 %collective-permute-done.20.refs_18_ = bf16[2,3,256,128]{3,2,1,0:T(8,128)(2,1)S(1)} collective-permute-done((bf16[2,3,256,128]{3,2,1,0:T(8,128)(2,1)S(1)}, bf16[2,3,256,128]{3,2,1,0:T(8,128)(2,1)S(1)}, u32[]{:S(2)}, u32[]{:S(2)}) %collective-permute-start.20) | collective-permute-done | bytes 393248 | tf_op jit(solution)/shard_map/ppermute | solution.py:56
  97.3 2.5 collective-permute-done.19.refs_7_
  100.5 1.9 collective-permute-done.25.refs_17_
  102.5 0.9 copy-done.35
  103.3 39.0 %middle.1 = (bf16[512,768]{1,0:T(8,128)(2,1)}, f32[512,768]{1,0:T(8,128)}, bf16[2,8,112,768]{3,2,1,0:T(8,128)(2,1)}, bf16[2,8,112,768]{3,2,1,0:T(8,128)(2,1)}, b...) custom-call(bf16[4,96,1024]{2,1,0:T(8,128)(2,1)} %bitcast.62, ...), custom_call_target="tpu_custom_call" | custom-call | flops 1000 | bytes 1000 | tf_op jit(solution)/shard_map/middle/pallas_call | solution.py:639
  143.1 1.5 collective-permute-start.29
  144.8 7.8 %collective-permute-done.26 = bf16[2,8,112,768]{3,2,1,0:T(8,128)(2,1)} collective-permute-done((bf16[2,8,112,768]{3,2,1,0:T(8,128)(2,1)}, bf16[2,8,112,768]{3,2,1,0:T(8,128)(2,1)}, u32[]{:S(2)}, u32[]{:S(2)}) %collective-permute-start.26) | collective-permute-done | bytes 2752544 | tf_op jit(solution)/shard_map/ppermute | solution.py:56
  152.6 4.4 %sum_first.1 = (bf16[2,2,2,112,768]{4,3,2,1,0:T(8,128)(2,1)}, bf16[2,2,2,96,960]{4,3,2,1,0:T(8,128)(2,1)}) custom-call(bf16[2,2,2,2,112,768]{5,4,3,2,1,0:T(8,128)(2,1)} %bitcast.51, bf16[2,2,2,2,112,768]{5,4,3,2,1,0:T(8,128)(2,1)} %bitcast.25.refs_1_, bf16[2,2,2,2,96,960]{5,4,3,2,1,0:T(8,128)(2,1)} %bitcast.46, ...), custom_call_target="tpu_custom_call" | custom-call | flops 1000 | bytes 1000 | tf_op jit(solution)/shard_map/sum_first/pallas_call | solution.py:761
  157.1 1.6 collective-permute-start.32
  158.7 1.5 collective-permute-start.31
  160.2 30.7 %attention_backward.2 = (bf16[2,2048,192]{2,1,0:T(8,128)(2,1)}, bf16[3,8,96,256]{3,2,1,0:T(8,128)(2,1)}) custom-call(bf16[3,2048,128]{2,1,0:T(8,128)(2,1)} %copy-done.3, bf16[3,2048,128]{2,1,0:T(8,128)(2,1)} %copy-done.1, bf16[3,2048,128]{2,1,0:T(8,128)(2,1)} %copy-done.2, f32[3,2048,128]{2,1,0:T(8,128)} %copy-done, ...), custom_call_target="tpu_custom_call" | custom-call | flops 1000 | bytes 1000 | tf_op jit(solution)/shard_map/attention_backward/pallas_call | solution.py:353
  191.0 3.0 %collective-permute-done.32.refs_5_.refs_6_.refs_7_.refs_2_ = bf16[2,2,2,96,960]{4,3,2,1,0:T(8,128)(2,1)} collective-permute-done((bf16[2,2,2,96,960]{4,3,2,1,0:T(8,128)(2,1)}, bf16[2,2,2,96,960]{4,3,2,1,0:T(8,128)(2,1)}, u32[]{:S(2)}, u32[]{:S(2)}) %collective-permute-start.32) | collective-permute-done | bytes 1474592 | tf_op jit(solution)/shard_map/ppermute | solution.py:56
  194.0 3.4 %sum_second.1 = (bf16[2,2,112,768]{3,2,1,0:T(8,128)(2,1)}, bf16[2,2,96,960]{3,2,1,0:T(8,128)(2,1)}) custom-call(bf16[2,2,2,2,112,768]{5,4,3,2,1,0:T(8,128)(2,1)} %bitcast.52, bf16[2,2,2,2,112,768]{5,4,3,2,1,0:T(8,128)(2,1)} %bitcast.25.refs_1_, bf16[2,2,2,112,768]{4,3,2,1,0:T(8,128)(2,1)} %collective-permute-done.31.refs_2_, ...), custom_call_target="tpu_custom_call" | custom-call | flops 1000 | bytes 1000 | tf_op jit(solution)/shard_map/sum_second/pallas_call | solution.py:761
  197.4 1.6 collective-permute-start.34
  199.0 0.7 collective-permute-start.33
  199.7 20.2 %attention_backward.3 = (bf16[1,2048,192]{2,1,0:T(8,128)(2,1)}, bf16[3,8,96,256]{3,2,1,0:T(8,128)(2,1)}, bf16[256,768]{1,0:T(8,128)(2,1)}, bf16[256,768]{1,0:T(8,128)(2,1)}, bf16[2,256,768]{2,1,0:T(8,128)(2,1)}) custom-call(bf16[3,2048,128]{2,1,0:T(8,128)(2,1)} %copy-done.3, bf16[3,2048,128]{2,1,0:T(8,128)(2,1)} %copy-done.1, ...), custom_call_target="tpu_custom_call", output_to_operand_aliasing={{1}: (15, {})} | custom-call | flops 1000 | bytes 1000 | tf_op jit(solution)/shard_map/attention_backward/pallas_call | solution.py:353
  220.4 1.5 collective-permute-done.35.refs_10_
  222.5 3.8 %sum_third.1 = (bf16[2,112,768]{2,1,0:T(8,128)(2,1)}, bf16[2,96,960]{2,1,0:T(8,128)(2,1)}, bf16[3,2,2,96,256]{4,3,2,1,0:T(8,128)(2,1)}, bf16[2,256,768]{2,1,0:T(8,128)(2,1)}) custom-call(bf16[2,2,2,2,112,768]{5,4,3,2,1,0:T(8,128)(2,1)} %bitcast.53, bf16[2,2,2,2,112,768]{5,4,3,2,1,0:T(8,128)(2,1)} %bitcast.25.refs_1_, ...), custom_call_target="tpu_custom_call" | custom-call | flops 1000 | bytes 1000 | tf_op jit(solution)/shard_map/sum_third/pallas_call | solution.py:761
  226.4 1.6 collective-permute-start.41
  228.5 2.7 collective-permute-start.37
  231.3 4.8 %input_part.1 = (bf16[256,768]{1,0:T(8,128)(2,1)}, bf16[256,768]{1,0:T(8,128)(2,1)}, bf16[512,768]{1,0:T(8,128)(2,1)}) custom-call(bf16[2,2048,192]{2,1,0:T(8,128)(2,1)} %get-tuple-element.214.refs_8_.refs_0_, bf16[1,2048,192]{2,1,0:T(8,128)(2,1)} %get-tuple-element.215.refs_1_, bf16[4,96,576]{2,1,0:T(8,128)(2,1)} %bitcast.44, bf16[4,96,576]{2,1,0:T(8,128)(2,1)} %copy-done.8), custom_call_target="tpu_custom_call" | custom-call | flops 1000 | bytes 1000 | tf_op jit(solution)/shard_map/input_part/pallas_call | solution.py:397
  236.1 10.7 %collective-permute-done.37.refs_4_ = bf16[2,112,768]{2,1,0:T(8,128)(2,1)S(1)} collective-permute-done((bf16[2,112,768]{2,1,0:T(8,128)(2,1)}, bf16[2,112,768]{2,1,0:T(8,128)(2,1)S(1)}, u32[]{:S(2)}, u32[]{:S(2)}) %collective-permute-start.37) | collective-permute-done | bytes 344096 | tf_op jit(solution)/shard_map/ppermute | solution.py:56
  246.8 1.8 collective-permute-done.38.refs_9_.refs_4_
  248.6 0.9 copy-done.16
  249.5 2.8 %sum_fourth.1 = (bf16[112,768]{1,0:T(8,128)(2,1)}, bf16[96,960]{1,0:T(8,128)(2,1)}, bf16[3,96,256]{2,1,0:T(8,128)(2,1)}, bf16[3,96,256]{2,1,0:T(8,128)(2,1)}, bf16[3,96,256]{2,1,0:T(8,128)(2,1)}) custom-call(bf16[2,2,2,2,112,768]{5,4,3,2,1,0:T(8,128)(2,1)} %bitcast.54, bf16[2,2,2,2,112,768]{5,4,3,2,1,0:T(8,128)(2,1)} %bitcast.25.refs_1_, ...), custom_call_target="tpu_custom_call" | custom-call | flops 1000 | bytes 1000 | tf_op jit(solution)/shard_map/sum_fourth/pallas_call | solution.py:761
  252.3 1.2 collective-permute-start.40
  254.9 2.9 %collective-permute-start.45 = (bf16[3,96,256]{2,1,0:T(8,128)(2,1)}, bf16[3,96,256]{2,1,0:T(8,128)(2,1)S(1)}, u32[]{:S(2)}, u32[]{:S(2)}) collective-permute-start(bf16[3,96,256]{2,1,0:T(8,128)(2,1)} %get-tuple-element.230), channel_id=1, source_target_pairs={{0,16},{4,20},{8,24},{12,28},{16,0},{20,4},{24,8},{28,12},{1,17},{... | collective-permute-start | bytes 442376 | tf_op jit(solution)/shard_map/ppermute | solution.py:56
  258.2 1.2 collective-permute-start.47
  260.0 4.8 %finish_down.1 = (f32[96,768]{1,0:T(8,128)}, f32[16,768]{1,0:T(8,128)}, bf16[512,768]{1,0:T(8,128)(2,1)}) custom-call(bf16[2,2,2,2,112,768]{5,4,3,2,1,0:T(8,128)(2,1)} %bitcast.55, bf16[2,2,2,2,112,768]{5,4,3,2,1,0:T(8,128)(2,1)} %bitcast.25.refs_1_, bf16[2,2,2,112,768]{4,3,2,1,0:T(8,128)(2,1)} %collective-permute-done.31.refs_2_, ...), custom_call_target="tpu_custom_call" | custom-call | flops 1000 | bytes 1000 | tf_op jit(solution)/shard_map/finish_down/pallas_call | solution.py:761
  264.8 0.9 slice_reduce_fusion
  265.7 1.6 slice_reduce_fusion.1
  267.3 7.5 %collective-permute-done.45.refs_8_ = bf16[3,96,256]{2,1,0:T(8,128)(2,1)S(1)} collective-permute-done((bf16[3,96,256]{2,1,0:T(8,128)(2,1)}, bf16[3,96,256]{2,1,0:T(8,128)(2,1)S(1)}, u32[]{:S(2)}, u32[]{:S(2)}) %collective-permute-start.45) | collective-permute-done | bytes 147488 | tf_op jit(solution)/shard_map/ppermute | solution.py:56
  275.7 2.6 finish.1
  (176 shorter events, 11.5 us)
Async XLA Ops:
  0.7 23.5 %collective-permute-start.3 = (bf16[512,768]{1,0:T(8,128)(2,1)}, bf16[512,768]{1,0:T(8,128)(2,1)S(1)}, u32[]{:S(2)}, u32[]{:S(2)}) collective-permute-start(bf16[512,768]{1,0:T(8,128)(2,1)} %refs_4_.3), channel_id=1, source_target_pairs={{0,2},{1,3},{2,0},{3,1},{4,6},{5,7},{6,4},{7,5},{8,10},{9,11},{10,... | collective-permute-start | bytes 2359304 | tf_op jit(solution)/shard_map/ppermute | solution.py:56
  4.6 8.4 %collective-permute-start = (bf16[1,96,576]{2,1,0:T(8,128)(2,1)S(1)}, bf16[1,96,576]{2,1,0:T(8,128)(2,1)S(1)}, u32[]{:S(2)}, u32[]{:S(2)}) collective-permute-start(bf16[1,96,576]{2,1,0:T(8,128)(2,1)S(1)} %get-tuple-element.260), channel_id=1, source_target_pairs={{0,16},{4,20},{8,24},{12,28},{16,0},{20,4},{24,8},{28,12},{1,17},{... | collective-permute-start | bytes 331784 | tf_op jit(solution)/shard_map/ppermute | solution.py:56
  13.0 11.1 %collective-permute-start.1 = (bf16[2,96,576]{2,1,0:T(8,128)(2,1)S(1)}, bf16[2,96,576]{2,1,0:T(8,128)(2,1)S(1)}, u32[]{:S(2)}, u32[]{:S(2)}) collective-permute-start(bf16[2,96,576]{2,1,0:T(8,128)(2,1)S(1)} %get-tuple-element.258), channel_id=1, source_target_pairs={{0,8},{4,12},{8,0},{12,4},{16,24},{20,28},{24,16},{28,20},{1,9},{5... | collective-permute-start | bytes 663560 | tf_op jit(solution)/shard_map/ppermute | solution.py:56
  13.8 9.7 %collective-permute-start.2 = (bf16[1,96,1024]{2,1,0:T(8,128)(2,1)S(1)}, bf16[1,96,1024]{2,1,0:T(8,128)(2,1)S(1)}, u32[]{:S(2)}, u32[]{:S(2)}) collective-permute-start(bf16[1,96,1024]{2,1,0:T(8,128)(2,1)S(1)} %maximum_bitcast_fusion.1), channel_id=1, source_target_pairs={{0,16},{4,20},{8,24},{12,28},{16,0},{20,4},{24,8},{28,12},{1,17},{... | collective-permute-start | bytes 589832 | tf_op jit(solution)/shard_map/ppermute | solution.py:56
  24.1 21.7 %copy-start.6 = (bf16[512,768]{1,0:T(8,128)(2,1)}, bf16[512,768]{1,0:T(8,128)(2,1)S(1)}, u32[]{:S(2)}) copy-start(bf16[512,768]{1,0:T(8,128)(2,1)S(1)} %collective-permute-done.3.refs_2_.refs_6_) | copy-start | bytes 2359300
  24.1 16.0 %collective-permute-start.7 = (bf16[512,768]{1,0:T(8,128)(2,1)S(1)}, bf16[512,768]{1,0:T(8,128)(2,1)S(1)}, u32[]{:S(2)}, u32[]{:S(2)}) collective-permute-start(bf16[512,768]{1,0:T(8,128)(2,1)S(1)} %collective-permute-done.3.refs_2_.refs_6_), channel_id=1, source_target_pairs={{0,1},{1,0},{2,3},{3,2},{4,5},{5,4},{6,7},{7,6},{8,9},{9,8},{10,11... | collective-permute-start | bytes 2359304 | tf_op jit(solution)/shard_map/ppermute | solution.py:56
  24.2 6.8 %copy-start.50 = (bf16[192]{0:T(256)(128)(2,1)S(1)}, bf16[192]{0:T(256)(128)(2,1)}, u32[]{:S(2)}) copy-start(bf16[192]{0:T(256)(128)(2,1)} %param.29) | copy-start | bytes 1156
  24.4 21.4 %copy-start.5 = (bf16[2,2,96,576]{3,2,1,0:T(8,128)(2,1)}, bf16[2,2,96,576]{3,2,1,0:T(8,128)(2,1)S(1)}, u32[]{:S(2)}) copy-start(bf16[2,2,96,576]{3,2,1,0:T(8,128)(2,1)S(1)} %copy.44) | copy-start | bytes 1327108
  24.4 15.7 %collective-permute-start.4 = (bf16[4,96,576]{2,1,0:T(8,128)(2,1)S(1)}, bf16[4,96,576]{2,1,0:T(8,128)(2,1)S(1)}, u32[]{:S(2)}, u32[]{:S(2)}) collective-permute-start(bf16[4,96,576]{2,1,0:T(8,128)(2,1)S(1)} %bitcast.41), channel_id=1, source_target_pairs={{0,4},{4,0},{8,12},{12,8},{16,20},{20,16},{24,28},{28,24},{1,5},{5... | collective-permute-start | bytes 1327112 | tf_op jit(solution)/shard_map/ppermute | solution.py:56
  26.9 13.2 %collective-permute-start.5 = (bf16[2,96,1024]{2,1,0:T(8,128)(2,1)}, bf16[2,96,1024]{2,1,0:T(8,128)(2,1)}, u32[]{:S(2)}, u32[]{:S(2)}) collective-permute-start(bf16[2,96,1024]{2,1,0:T(8,128)(2,1)} %get-tuple-element.254), channel_id=1, source_target_pairs={{0,8},{4,12},{8,0},{12,4},{16,24},{20,28},{24,16},{28,20},{1,9},{5... | collective-permute-start | bytes 1179656 | tf_op jit(solution)/shard_map/ppermute | solution.py:56
  30.4 5.8 %collective-permute-start.6 = (bf16[1,96,768]{2,1,0:T(8,128)(2,1)S(1)}, bf16[1,96,768]{2,1,0:T(8,128)(2,1)}, u32[]{:S(2)}, u32[]{:S(2)}) collective-permute-start(bf16[1,96,768]{2,1,0:T(8,128)(2,1)S(1)} %bitcast.68), channel_id=1, source_target_pairs={{0,2},{1,3},{2,0},{3,1},{4,6},{5,7},{6,4},{7,5},{8,10},{9,11},{10,... | collective-permute-start | bytes 442376 | tf_op jit(solution)/shard_map/ppermute | solution.py:56
  30.9 14.9 %collective-permute-start.8 = (bf16[512,768]{1,0:T(8,128)(2,1)S(1)}, bf16[512,768]{1,0:T(8,128)(2,1)}, u32[]{:S(2)}, u32[]{:S(2)}) collective-permute-start(bf16[512,768]{1,0:T(8,128)(2,1)S(1)} %copy-done.4), channel_id=1, source_target_pairs={{0,1},{1,0},{2,3},{3,2},{4,5},{5,4},{6,7},{7,6},{8,9},{9,8},{10,11... | collective-permute-start | bytes 2359304 | tf_op jit(solution)/shard_map/ppermute | solution.py:56
  41.9 9.2 %copy-start.14 = (bf16[2,2,96,1024]{3,2,1,0:T(8,128)(2,1)}, bf16[2,2,96,1024]{3,2,1,0:T(8,128)(2,1)S(1)}, u32[]{:S(2)}) copy-start(bf16[2,2,96,1024]{3,2,1,0:T(8,128)(2,1)S(1)} %copy.45) | copy-start | bytes 2359300
  41.9 19.2 %collective-permute-start.10 = (bf16[4,96,1024]{2,1,0:T(8,128)(2,1)S(1)}, bf16[4,96,1024]{2,1,0:T(8,128)(2,1)S(1)}, u32[]{:S(2)}, u32[]{:S(2)}) collective-permute-start(bf16[4,96,1024]{2,1,0:T(8,128)(2,1)S(1)} %bitcast.59), channel_id=1, source_target_pairs={{0,4},{4,0},{8,12},{12,8},{16,20},{20,16},{24,28},{28,24},{1,5},{5... | collective-permute-start | bytes 2359304 | tf_op jit(solution)/shard_map/ppermute | solution.py:56
  42.5 18.8 %collective-permute-start.11 = (bf16[4,96,1024]{2,1,0:T(8,128)(2,1)S(1)}, bf16[4,96,1024]{2,1,0:T(8,128)(2,1)S(1)}, u32[]{:S(2)}, u32[]{:S(2)}) collective-permute-start(bf16[4,96,1024]{2,1,0:T(8,128)(2,1)S(1)} %bitcast.60), channel_id=1, source_target_pairs={{0,2},{1,3},{2,0},{3,1},{4,6},{5,7},{6,4},{7,5},{8,10},{9,11},{10,... | collective-permute-start | bytes 2359304 | tf_op jit(solution)/shard_map/ppermute | solution.py:56
  43.0 18.3 %collective-permute-start.12 = (bf16[4,96,1024]{2,1,0:T(8,128)(2,1)S(1)}, bf16[4,96,1024]{2,1,0:T(8,128)(2,1)S(1)}, u32[]{:S(2)}, u32[]{:S(2)}) collective-permute-start(bf16[4,96,1024]{2,1,0:T(8,128)(2,1)S(1)} %bitcast.61), channel_id=1, source_target_pairs={{0,1},{1,0},{2,3},{3,2},{4,5},{5,4},{6,7},{7,6},{8,9},{9,8},{10,11... | collective-permute-start | bytes 2359304 | tf_op jit(solution)/shard_map/ppermute | solution.py:56
  44.0 16.7 %collective-permute-start.9 = (bf16[1,2,96,768]{3,2,1,0:T(8,128)(2,1)S(1)}, bf16[1,2,96,768]{3,2,1,0:T(8,128)(2,1)S(1)}, u32[]{:S(2)}, u32[]{:S(2)}) collective-permute-start(bf16[1,2,96,768]{3,2,1,0:T(8,128)(2,1)S(1)} %get-tuple-element.256), channel_id=1, source_target_pairs={{0,16},{4,20},{8,24},{12,28},{16,0},{20,4},{24,8},{28,12},{1,17},{... | collective-permute-start | bytes 884744 | tf_op jit(solution)/shard_map/ppermute | solution.py:56
  51.1 13.9 %copy-start.1 = (bf16[3,2048,128]{2,1,0:T(8,128)(2,1)}, bf16[3,2048,128]{2,1,0:T(8,128)(2,1)S(1)}, u32[]{:S(2)}) copy-start(bf16[3,2048,128]{2,1,0:T(8,128)(2,1)S(1)} %get-tuple-element.146.k_ref) | copy-start | bytes 4718596
  51.1 13.9 %copy-start.2 = (bf16[3,2048,128]{2,1,0:T(8,128)(2,1)}, bf16[3,2048,128]{2,1,0:T(8,128)(2,1)S(1)}, u32[]{:S(2)}) copy-start(bf16[3,2048,128]{2,1,0:T(8,128)(2,1)S(1)} %get-tuple-element.147.v_ref) | copy-start | bytes 4718596
  61.1 18.9 %copy-start.22 = (bf16[4,96,1024]{2,1,0:T(8,128)(2,1)}, bf16[4,96,1024]{2,1,0:T(8,128)(2,1)S(1)}, u32[]{:S(2)}) copy-start(bf16[4,96,1024]{2,1,0:T(8,128)(2,1)S(1)} %collective-permute-done.10.refs_1_) | copy-start | bytes 2359300
  61.3 15.6 %copy-start.23 = (bf16[4,96,1024]{2,1,0:T(8,128)(2,1)}, bf16[4,96,1024]{2,1,0:T(8,128)(2,1)S(1)}, u32[]{:S(2)}) copy-start(bf16[4,96,1024]{2,1,0:T(8,128)(2,1)S(1)} %collective-permute-done.11.refs_2_) | copy-start | bytes 2359300
  61.3 15.6 %copy-start.24 = (bf16[4,96,1024]{2,1,0:T(8,128)(2,1)}, bf16[4,96,1024]{2,1,0:T(8,128)(2,1)S(1)}, u32[]{:S(2)}) copy-start(bf16[4,96,1024]{2,1,0:T(8,128)(2,1)S(1)} %collective-permute-done.12.refs_8_) | copy-start | bytes 2359300
  61.3 18.6 %collective-permute-start.14 = (bf16[4,96,1024]{2,1,0:T(8,128)(2,1)S(1)}, bf16[4,96,1024]{2,1,0:T(8,128)(2,1)S(1)}, u32[]{:S(2)}, u32[]{:S(2)}) collective-permute-start(bf16[4,96,1024]{2,1,0:T(8,128)(2,1)S(1)} %collective-permute-done.10.refs_1_), channel_id=1, source_target_pairs={{0,2},{1,3},{2,0},{3,1},{4,6},{5,7},{6,4},{7,5},{8,10},{9,11},{10,... | collective-permute-start | bytes 2359304 | tf_op jit(solution)/shard_map/ppermute | solution.py:56
  62.3 17.7 %collective-permute-start.16 = (bf16[4,96,1024]{2,1,0:T(8,128)(2,1)S(1)}, bf16[4,96,1024]{2,1,0:T(8,128)(2,1)S(1)}, u32[]{:S(2)}, u32[]{:S(2)}) collective-permute-start(bf16[4,96,1024]{2,1,0:T(8,128)(2,1)S(1)} %collective-permute-done.11.refs_2_), channel_id=1, source_target_pairs={{0,1},{1,0},{2,3},{3,2},{4,5},{5,4},{6,7},{7,6},{8,9},{9,8},{10,11... | collective-permute-start | bytes 2359304 | tf_op jit(solution)/shard_map/ppermute | solution.py:56
  62.3 17.7 %copy-start.15 = (bf16[2,2,96,768]{3,2,1,0:T(8,128)(2,1)}, bf16[2,2,96,768]{3,2,1,0:T(8,128)(2,1)S(1)}, u32[]{:S(2)}) copy-start(bf16[2,2,96,768]{3,2,1,0:T(8,128)(2,1)S(1)} %maximum_bitcast_fusion.refs_4_) | copy-start | bytes 1769476
  62.3 17.5 %collective-permute-start.13 = (bf16[2,2,96,768]{3,2,1,0:T(8,128)(2,1)S(1)}, bf16[2,2,96,768]{3,2,1,0:T(8,128)(2,1)S(1)}, u32[]{:S(2)}, u32[]{:S(2)}) collective-permute-start(bf16[2,2,96,768]{3,2,1,0:T(8,128)(2,1)S(1)} %maximum_bitcast_fusion.refs_4_), channel_id=1, source_target_pairs={{0,8},{4,12},{8,0},{12,4},{16,24},{20,28},{24,16},{28,20},{1,9},{5... | collective-permute-start | bytes 1769480 | tf_op jit(solution)/shard_map/ppermute | solution.py:56
  64.4 15.5 %collective-permute-start.15 = (bf16[2,2,96,768]{3,2,1,0:T(8,128)(2,1)S(1)}, bf16[2,2,96,768]{3,2,1,0:T(8,128)(2,1)S(1)}, u32[]{:S(2)}, u32[]{:S(2)}) collective-permute-start(bf16[2,2,96,768]{3,2,1,0:T(8,128)(2,1)S(1)} %maximum_bitcast_fusion.refs_4_), channel_id=1, source_target_pairs={{0,4},{4,0},{8,12},{12,8},{16,20},{20,16},{24,28},{28,24},{1,5},{5... | collective-permute-start | bytes 1769480 | tf_op jit(solution)/shard_map/ppermute | solution.py:56
  79.8 23.5 %copy-start.9 = (bf16[3,256,128]{2,1,0:T(8,128)(2,1)}, bf16[3,256,128]{2,1,0:T(8,128)(2,1)S(1)}, u32[]{:S(2)}) copy-start(bf16[3,256,128]{2,1,0:T(8,128)(2,1)S(1)} %get-tuple-element.177.refs_16_) | copy-start | bytes 589828
  79.8 22.6 %copy-start.29 = (bf16[2,2,96,768]{3,2,1,0:T(8,128)(2,1)}, bf16[2,2,96,768]{3,2,1,0:T(8,128)(2,1)S(1)}, u32[]{:S(2)}) copy-start(bf16[2,2,96,768]{3,2,1,0:T(8,128)(2,1)S(1)} %collective-permute-done.13.refs_6_) | copy-start | bytes 1769476
  79.9 22.5 %copy-start.30 = (bf16[2,2,96,768]{3,2,1,0:T(8,128)(2,1)}, bf16[2,2,96,768]{3,2,1,0:T(8,128)(2,1)S(1)}, u32[]{:S(2)}) copy-start(bf16[2,2,96,768]{3,2,1,0:T(8,128)(2,1)S(1)} %collective-permute-done.15.refs_5_) | copy-start | bytes 1769476
  80.0 20.0 %copy-start.25 = (bf16[4,96,1024]{2,1,0:T(8,128)(2,1)}, bf16[4,96,1024]{2,1,0:T(8,128)(2,1)S(1)}, u32[]{:S(2)}) copy-start(bf16[4,96,1024]{2,1,0:T(8,128)(2,1)S(1)} %collective-permute-done.14.refs_3_) | copy-start | bytes 2359300
  80.0 20.5 %copy-start.26 = (bf16[4,96,1024]{2,1,0:T(8,128)(2,1)}, bf16[4,96,1024]{2,1,0:T(8,128)(2,1)S(1)}, u32[]{:S(2)}) copy-start(bf16[4,96,1024]{2,1,0:T(8,128)(2,1)S(1)} %collective-permute-done.16.refs_10_) | copy-start | bytes 2359300
  80.0 4.0 %collective-permute-start.18 = (bf16[4,96,1024]{2,1,0:T(8,128)(2,1)S(1)}, bf16[4,96,1024]{2,1,0:T(8,128)(2,1)S(1)}, u32[]{:S(2)}, u32[]{:S(2)}) collective-permute-start(bf16[4,96,1024]{2,1,0:T(8,128)(2,1)S(1)} %collective-permute-done.10.refs_1_), channel_id=1, source_target_pairs={{0,1},{1,0},{2,3},{3,2},{4,5},{5,4},{6,7},{7,6},{8,9},{9,8},{10,11... | collective-permute-start | bytes 2359304 | tf_op jit(solution)/shard_map/ppermute | solution.py:56
  80.1 3.1 %collective-permute-start.17 = (bf16[2,2,96,768]{3,2,1,0:T(8,128)(2,1)S(1)}, bf16[2,2,96,768]{3,2,1,0:T(8,128)(2,1)S(1)}, u32[]{:S(2)}, u32[]{:S(2)}) collective-permute-start(bf16[2,2,96,768]{3,2,1,0:T(8,128)(2,1)S(1)} %maximum_bitcast_fusion.refs_4_), channel_id=1, source_target_pairs={{0,1},{1,0},{2,3},{3,2},{4,5},{5,4},{6,7},{7,6},{8,9},{9,8},{10,11... | collective-permute-start | bytes 1769480 | tf_op jit(solution)/shard_map/ppermute | solution.py:56
  84.0 18.4 %copy-start.27 = (bf16[4,96,1024]{2,1,0:T(8,128)(2,1)}, bf16[4,96,1024]{2,1,0:T(8,128)(2,1)S(1)}, u32[]{:S(2)}) copy-start(bf16[4,96,1024]{2,1,0:T(8,128)(2,1)S(1)} %collective-permute-done.18.refs_9_) | copy-start | bytes 2359300
  84.0 15.8 %collective-permute-start.21 = (bf16[4,96,1024]{2,1,0:T(8,128)(2,1)S(1)}, bf16[4,96,1024]{2,1,0:T(8,128)(2,1)S(1)}, u32[]{:S(2)}, u32[]{:S(2)}) collective-permute-start(bf16[4,96,1024]{2,1,0:T(8,128)(2,1)S(1)} %collective-permute-done.14.refs_3_), channel_id=1, source_target_pairs={{0,1},{1,0},{2,3},{3,2},{4,5},{5,4},{6,7},{7,6},{8,9},{9,8},{10,11... | collective-permute-start | bytes 2359304 | tf_op jit(solution)/shard_map/ppermute | solution.py:56
  84.1 15.6 %collective-permute-start.19 = (bf16[2,2,96,768]{3,2,1,0:T(8,128)(2,1)S(1)}, bf16[2,2,96,768]{3,2,1,0:T(8,128)(2,1)S(1)}, u32[]{:S(2)}, u32[]{:S(2)}) collective-permute-start(bf16[2,2,96,768]{3,2,1,0:T(8,128)(2,1)S(1)} %collective-permute-done.13.refs_6_), channel_id=1, source_target_pairs={{0,4},{4,0},{8,12},{12,8},{16,20},{20,16},{24,28},{28,24},{1,5},{5... | collective-permute-start | bytes 1769480 | tf_op jit(solution)/shard_map/ppermute | solution.py:56
  85.6 14.1 %collective-permute-start.22 = (bf16[2,2,96,768]{3,2,1,0:T(8,128)(2,1)S(1)}, bf16[2,2,96,768]{3,2,1,0:T(8,128)(2,1)S(1)}, u32[]{:S(2)}, u32[]{:S(2)}) collective-permute-start(bf16[2,2,96,768]{3,2,1,0:T(8,128)(2,1)S(1)} %collective-permute-done.13.refs_6_), channel_id=1, source_target_pairs={{0,1},{1,0},{2,3},{3,2},{4,5},{5,4},{6,7},{7,6},{8,9},{9,8},{10,11... | collective-permute-start | bytes 1769480 | tf_op jit(solution)/shard_map/ppermute | solution.py:56
  85.7 14.0 %collective-permute-start.23 = (bf16[2,2,96,768]{3,2,1,0:T(8,128)(2,1)S(1)}, bf16[2,2,96,768]{3,2,1,0:T(8,128)(2,1)S(1)}, u32[]{:S(2)}, u32[]{:S(2)}) collective-permute-start(bf16[2,2,96,768]{3,2,1,0:T(8,128)(2,1)S(1)} %collective-permute-done.15.refs_5_), channel_id=1, source_target_pairs={{0,1},{1,0},{2,3},{3,2},{4,5},{5,4},{6,7},{7,6},{8,9},{9,8},{10,11... | collective-permute-start | bytes 1769480 | tf_op jit(solution)/shard_map/ppermute | solution.py:56
  86.2 11.1 %collective-permute-start.20 = (bf16[2,3,256,128]{3,2,1,0:T(8,128)(2,1)S(1)}, bf16[2,3,256,128]{3,2,1,0:T(8,128)(2,1)S(1)}, u32[]{:S(2)}, u32[]{:S(2)}) collective-permute-start(bf16[2,3,256,128]{3,2,1,0:T(8,128)(2,1)S(1)} %get-tuple-element.173), channel_id=1, source_target_pairs={{0,2},{1,3},{2,0},{3,1},{4,6},{5,7},{6,4},{7,5},{8,10},{9,11},{10,... | collective-permute-start | bytes 1179656 | tf_op jit(solution)/shard_map/ppermute | solution.py:56
  99.8 2.6 collective-permute-start.24
  99.9 2.5 collective-permute-start.25
  142.4 10.3 %collective-permute-start.27 = (bf16[2,8,96,960]{3,2,1,0:T(8,128)(2,1)}, bf16[2,8,96,960]{3,2,1,0:T(8,128)(2,1)}, u32[]{:S(2)}, u32[]{:S(2)}) collective-permute-start(bf16[2,8,96,960]{3,2,1,0:T(8,128)(2,1)} %get-tuple-element.185), channel_id=1, source_target_pairs={{0,1},{1,0},{2,3},{3,2},{4,5},{5,4},{6,7},{7,6},{8,9},{9,8},{10,11... | collective-permute-start | bytes 8847368 | tf_op jit(solution)/shard_map/ppermute | solution.py:56
  142.6 10.1 %collective-permute-start.26 = (bf16[2,8,112,768]{3,2,1,0:T(8,128)(2,1)}, bf16[2,8,112,768]{3,2,1,0:T(8,128)(2,1)}, u32[]{:S(2)}, u32[]{:S(2)}) collective-permute-start(bf16[2,8,112,768]{3,2,1,0:T(8,128)(2,1)} %get-tuple-element.183), channel_id=1, source_target_pairs={{0,1},{1,0},{2,3},{3,2},{4,5},{5,4},{6,7},{7,6},{8,9},{9,8},{10,11... | collective-permute-start | bytes 8257544 | tf_op jit(solution)/shard_map/ppermute | solution.py:56
  142.9 14.1 %collective-permute-start.28 = (bf16[3,256,128]{2,1,0:T(8,128)(2,1)}, bf16[3,256,128]{2,1,0:T(8,128)(2,1)S(1)}, u32[]{:S(2)}, u32[]{:S(2)}) collective-permute-start(bf16[3,256,128]{2,1,0:T(8,128)(2,1)} %get-tuple-element.189), channel_id=1, source_target_pairs={{0,1},{1,0},{2,3},{3,2},{4,5},{5,4},{6,7},{7,6},{8,9},{9,8},{10,11... | collective-permute-start | bytes 589832 | tf_op jit(solution)/shard_map/ppermute | solution.py:56
  143.1 14.0 %collective-permute-start.29 = (bf16[3,256,128]{2,1,0:T(8,128)(2,1)}, bf16[3,256,128]{2,1,0:T(8,128)(2,1)S(1)}, u32[]{:S(2)}, u32[]{:S(2)}) collective-permute-start(bf16[3,256,128]{2,1,0:T(8,128)(2,1)} %get-tuple-element.190), channel_id=1, source_target_pairs={{0,2},{1,3},{2,0},{3,1},{4,6},{5,7},{6,4},{7,5},{8,10},{9,11},{10,... | collective-permute-start | bytes 589832 | tf_op jit(solution)/shard_map/ppermute | solution.py:56
  144.6 12.5 %collective-permute-start.30 = (bf16[3,256,128]{2,1,0:T(8,128)(2,1)}, bf16[3,256,128]{2,1,0:T(8,128)(2,1)S(1)}, u32[]{:S(2)}, u32[]{:S(2)}) collective-permute-start(bf16[3,256,128]{2,1,0:T(8,128)(2,1)} %get-tuple-element.191), channel_id=1, source_target_pairs={{0,3},{1,2},{2,1},{3,0},{4,7},{5,6},{6,5},{7,4},{8,11},{9,10},{10,... | collective-permute-start | bytes 589832 | tf_op jit(solution)/shard_map/ppermute | solution.py:56
  157.1 36.8 %collective-permute-start.32 = (bf16[2,2,2,96,960]{4,3,2,1,0:T(8,128)(2,1)}, bf16[2,2,2,96,960]{4,3,2,1,0:T(8,128)(2,1)}, u32[]{:S(2)}, u32[]{:S(2)}) collective-permute-start(bf16[2,2,2,96,960]{4,3,2,1,0:T(8,128)(2,1)} %get-tuple-element.200), channel_id=1, source_target_pairs={{0,4},{4,0},{8,12},{12,8},{16,20},{20,16},{24,28},{28,24},{1,5},{5... | collective-permute-start | bytes 4423688 | tf_op jit(solution)/shard_map/ppermute | solution.py:56
  158.7 32.3 %collective-permute-start.31 = (bf16[2,2,2,112,768]{4,3,2,1,0:T(8,128)(2,1)}, bf16[2,2,2,112,768]{4,3,2,1,0:T(8,128)(2,1)}, u32[]{:S(2)}, u32[]{:S(2)}) collective-permute-start(bf16[2,2,2,112,768]{4,3,2,1,0:T(8,128)(2,1)} %get-tuple-element.192), channel_id=1, source_target_pairs={{0,2},{1,3},{2,0},{3,1},{4,6},{5,7},{6,4},{7,5},{8,10},{9,11},{10,... | collective-permute-start | bytes 4128776 | tf_op jit(solution)/shard_map/ppermute | solution.py:56
  197.4 23.0 %collective-permute-start.34 = (bf16[2,2,96,960]{3,2,1,0:T(8,128)(2,1)}, bf16[2,2,96,960]{3,2,1,0:T(8,128)(2,1)S(1)}, u32[]{:S(2)}, u32[]{:S(2)}) collective-permute-start(bf16[2,2,96,960]{3,2,1,0:T(8,128)(2,1)} %get-tuple-element.207), channel_id=1, source_target_pairs={{0,2},{1,3},{2,0},{3,1},{4,6},{5,7},{6,4},{7,5},{8,10},{9,11},{10,... | collective-permute-start | bytes 2211848 | tf_op jit(solution)/shard_map/ppermute | solution.py:56
  199.0 21.4 %collective-permute-start.33 = (bf16[2,2,112,768]{3,2,1,0:T(8,128)(2,1)}, bf16[2,2,112,768]{3,2,1,0:T(8,128)(2,1)}, u32[]{:S(2)}, u32[]{:S(2)}) collective-permute-start(bf16[2,2,112,768]{3,2,1,0:T(8,128)(2,1)} %get-tuple-element.202), channel_id=1, source_target_pairs={{0,8},{4,12},{8,0},{12,4},{16,24},{20,28},{24,16},{28,20},{1,9},{5... | collective-permute-start | bytes 2064392 | tf_op jit(solution)/shard_map/ppermute | solution.py:56
  219.9 2.1 collective-permute-start.35
  219.9 2.6 collective-permute-start.36
  226.4 28.5 %collective-permute-start.41 = (bf16[2,256,768]{2,1,0:T(8,128)(2,1)}, bf16[2,256,768]{2,1,0:T(8,128)(2,1)}, u32[]{:S(2)}, u32[]{:S(2)}) collective-permute-start(bf16[2,256,768]{2,1,0:T(8,128)(2,1)} %get-tuple-element.226), channel_id=1, source_target_pairs={{0,2},{1,3},{2,0},{3,1},{4,6},{5,7},{6,4},{7,5},{8,10},{9,11},{10,... | collective-permute-start | bytes 2359304 | tf_op jit(solution)/shard_map/ppermute | solution.py:56
  227.9 20.7 %collective-permute-start.39 = (bf16[3,2,2,96,256]{4,3,2,1,0:T(8,128)(2,1)}, bf16[3,2,2,96,256]{4,3,2,1,0:T(8,128)(2,1)S(1)}, u32[]{:S(2)}, u32[]{:S(2)}) collective-permute-start(bf16[3,2,2,96,256]{4,3,2,1,0:T(8,128)(2,1)} %get-tuple-element.222), channel_id=1, source_target_pairs={{0,4},{4,0},{8,12},{12,8},{16,20},{20,16},{24,28},{28,24},{1,5},{5... | collective-permute-start | bytes 1769480 | tf_op jit(solution)/shard_map/ppermute | solution.py:56
  228.5 18.2 %collective-permute-start.37 = (bf16[2,112,768]{2,1,0:T(8,128)(2,1)}, bf16[2,112,768]{2,1,0:T(8,128)(2,1)S(1)}, u32[]{:S(2)}, u32[]{:S(2)}) collective-permute-start(bf16[2,112,768]{2,1,0:T(8,128)(2,1)} %get-tuple-element.213), channel_id=1, source_target_pairs={{0,16},{4,20},{8,24},{12,28},{16,0},{20,4},{24,8},{28,12},{1,17},{... | collective-permute-start | bytes 1032200 | tf_op jit(solution)/shard_map/ppermute | solution.py:56
  231.3 17.3 %collective-permute-start.38 = (bf16[2,96,960]{2,1,0:T(8,128)(2,1)}, bf16[2,96,960]{2,1,0:T(8,128)(2,1)}, u32[]{:S(2)}, u32[]{:S(2)}) collective-permute-start(bf16[2,96,960]{2,1,0:T(8,128)(2,1)} %get-tuple-element.220), channel_id=1, source_target_pairs={{0,8},{4,12},{8,0},{12,4},{16,24},{20,28},{24,16},{28,20},{1,9},{5... | collective-permute-start | bytes 1105928 | tf_op jit(solution)/shard_map/ppermute | solution.py:56
  236.1 21.7 %collective-permute-start.42 = (bf16[256,768]{1,0:T(8,128)(2,1)}, bf16[256,768]{1,0:T(8,128)(2,1)}, u32[]{:S(2)}, u32[]{:S(2)}) collective-permute-start(bf16[256,768]{1,0:T(8,128)(2,1)} %get-tuple-element.216), channel_id=1, source_target_pairs={{0,1},{1,0},{2,3},{3,2},{4,5},{5,4},{6,7},{7,6},{8,9},{9,8},{10,11... | collective-permute-start | bytes 1179656 | tf_op jit(solution)/shard_map/ppermute | solution.py:56
  246.8 11.4 %collective-permute-start.43 = (bf16[256,768]{1,0:T(8,128)(2,1)}, bf16[256,768]{1,0:T(8,128)(2,1)}, u32[]{:S(2)}, u32[]{:S(2)}) collective-permute-start(bf16[256,768]{1,0:T(8,128)(2,1)} %get-tuple-element.217), channel_id=1, source_target_pairs={{0,1},{1,0},{2,3},{3,2},{4,5},{5,4},{6,7},{7,6},{8,9},{9,8},{10,11... | collective-permute-start | bytes 1179656 | tf_op jit(solution)/shard_map/ppermute | solution.py:56
  252.3 7.0 %collective-permute-start.40 = (bf16[112,768]{1,0:T(8,128)(2,1)}, bf16[112,768]{1,0:T(8,128)(2,1)S(1)}, u32[]{:S(2)}, u32[]{:S(2)}) collective-permute-start(bf16[112,768]{1,0:T(8,128)(2,1)} %get-tuple-element.224), channel_id=1, source_target_pairs={{0,4},{4,0},{8,12},{12,8},{16,20},{20,16},{24,28},{28,24},{1,5},{5... | collective-permute-start | bytes 516104 | tf_op jit(solution)/shard_map/ppermute | solution.py:56
  254.8 20.0 %collective-permute-start.44 = (bf16[96,960]{1,0:T(8,128)(2,1)}, bf16[96,960]{1,0:T(8,128)(2,1)S(1)}, u32[]{:S(2)}, u32[]{:S(2)}) collective-permute-start(bf16[96,960]{1,0:T(8,128)(2,1)} %get-tuple-element.229), channel_id=1, source_target_pairs={{0,16},{4,20},{8,24},{12,28},{16,0},{20,4},{24,8},{28,12},{1,17},{... | collective-permute-start | bytes 552968 | tf_op jit(solution)/shard_map/ppermute | solution.py:56
  254.9 19.9 %collective-permute-start.45 = (bf16[3,96,256]{2,1,0:T(8,128)(2,1)}, bf16[3,96,256]{2,1,0:T(8,128)(2,1)S(1)}, u32[]{:S(2)}, u32[]{:S(2)}) collective-permute-start(bf16[3,96,256]{2,1,0:T(8,128)(2,1)} %get-tuple-element.230), channel_id=1, source_target_pairs={{0,16},{4,20},{8,24},{12,28},{16,0},{20,4},{24,8},{28,12},{1,17},{... | collective-permute-start | bytes 442376 | tf_op jit(solution)/shard_map/ppermute | solution.py:56
  257.8 17.0 %collective-permute-start.46 = (bf16[3,96,256]{2,1,0:T(8,128)(2,1)}, bf16[3,96,256]{2,1,0:T(8,128)(2,1)S(1)}, u32[]{:S(2)}, u32[]{:S(2)}) collective-permute-start(bf16[3,96,256]{2,1,0:T(8,128)(2,1)} %get-tuple-element.231), channel_id=1, source_target_pairs={{0,8},{4,12},{8,0},{12,4},{16,24},{20,28},{24,16},{28,20},{1,9},{5... | collective-permute-start | bytes 442376 | tf_op jit(solution)/shard_map/ppermute | solution.py:56
  258.2 16.6 %collective-permute-start.47 = (bf16[3,96,256]{2,1,0:T(8,128)(2,1)}, bf16[3,96,256]{2,1,0:T(8,128)(2,1)S(1)}, u32[]{:S(2)}, u32[]{:S(2)}) collective-permute-start(bf16[3,96,256]{2,1,0:T(8,128)(2,1)} %get-tuple-element.232), channel_id=1, source_target_pairs={{0,24},{4,28},{8,16},{12,20},{16,8},{20,12},{24,0},{28,4},{1,25},{... | collective-permute-start | bytes 442376 | tf_op jit(solution)/shard_map/ppermute | solution.py:56
  (35 other events, 126.8 us)

commit v6 on v5

--- a/solution.py
+++ b/solution.py
@@ -940,11 +940,14 @@
     got_d, got_u = core(sent_d), core(sent_u)
     if placed:
         down, up = Sum(["x"] + names, hidden), Sum(["x"] + names, hidden + own_cols)
-        for total, arrays in ((down, (kept_d, got_d)), (up, (kept_u, got_u))):
-            for array in arrays:
-                total.join(axes_of(array, 1))
-        move_d, move_u = reduce_call("sum_first", [[down.away("x")], [up.away(0)]], BF16)
-        move_d, move_u = after((move_d, move_u), grads)
+        for array in (kept_u, got_u):
+            up.join(axes_of(array, 1))
+        (move_u,) = reduce_call("sum_up", [[up.away(0)]], BF16)
+        got_d = after(got_d, move_u)
+        for array in (kept_d, got_d):
+            down.join(axes_of(array, 1))
+        (move_d,) = reduce_call("sum_down", [[down.away("x")]], BF16)
+        move_d = after(move_d, grads)
         grads = after(grads, move_d)
         down_names, up_names = ["x"] + late + [0], [0, "x"] + late
     q_kept, out = kept

time: 280 us -> 275 us (0.982)
  waiting for transfers between devices: 72.1 us -> 65.3 us
    ppermute x48, waiting for transfers between devices: 72.1 us -> 65.3 us  [swap(): return lax.ppermute(value, axis, [(i, i ^ bits) for i in range(size)])]
    pallas_call x6 -> x7, Pallas kernels: 21.9 us -> 24 us  [reduce_call(): pl.pallas_call(functools.partial(reduce_kernel if keep else reduce_inside...]
  transfers between devices with their start and end apart: 48 -> 48, of which waited for: 21 -> 21; matrix products, arithmetic and copies ran while one was open for 4% -> 4% of each run, Pallas kernels for 33% -> 34%
where the time goes in v6:
time: 275 us; the launch traced here: 274 us
  Pallas kernels  142 us (52%)
  waiting for transfers between devices  65.3 us (24%)
  starting transfers between devices  45.6 us (17%)
  local copies, waits for them, and re-layouts  10.6 us (4%)
  other arithmetic  7.83 us (3%)
    ppermute x48, waiting for transfers between devices, swap(): return lax.ppermute(value, axis, [(i, i ^ bits) for i in range(size)])  65.3 us
    pallas_call x2, Pallas kernels, attention_backward(): pl.pallas_call(functools.partial(backward_kernel, placed=blocks > 1, mask...  50.8 us
    ppermute x48, starting transfers between devices, swap(): return lax.ppermute(value, axis, [(i, i ^ bits) for i in range(size)])  45.6 us
    pallas_call x1, Pallas kernels, middle(): pl.pallas_call(functools.partial(middle_kernel, plan=plan, blocks=blocks)...  39 us
    pallas_call x7, Pallas kernels, reduce_call(): pl.pallas_call(functools.partial(reduce_kernel if keep else reduce_inside...  24 us
    pallas_call x2, Pallas kernels, attention_forward(): pl.pallas_call(functools.partial(forward_kernel, unroll=4 if first else 2...  18.1 us
    unnamed x103, local copies, waits for them, and re-layouts  7.33 us
  transfers between devices with their start and end apart: 48, of which 21 were waited for; matrix products, arithmetic and copies ran while one was open for 4% of the time, Pallas kernels for 34%

profile of v6, /device:TPU:0, one launch (start us, length us, event | category | flops | bytes accessed | tf_op | source)
XLA Modules:
  0.0 273.5 jit_solution(1317758381529040480)
XLA Ops:
  0.7 3.0 %collective-permute-start.3 = (bf16[512,768]{1,0:T(8,128)(2,1)}, bf16[512,768]{1,0:T(8,128)(2,1)S(1)}, u32[]{:S(2)}, u32[]{:S(2)}) collective-permute-start(bf16[512,768]{1,0:T(8,128)(2,1)} %refs_4_.3), channel_id=1, source_target_pairs={{0,2},{1,3},{2,0},{3,1},{4,6},{5,7},{6,4},{7,5},{8,10},{9,11},{10,... | collective-permute-start | bytes 2359304 | tf_op jit(solution)/shard_map/ppermute | solution.py:56
  3.7 0.9 fusion.5
  4.6 2.7 collective-permute-start
  7.3 0.9 copy.43
  8.1 0.8 dynamic_slice.3
  9.0 1.0 maximum_bitcast_fusion.1
  10.0 3.0 %collective-permute-done = bf16[1,96,576]{2,1,0:T(8,128)(2,1)S(1)} collective-permute-done((bf16[1,96,576]{2,1,0:T(8,128)(2,1)S(1)}, bf16[1,96,576]{2,1,0:T(8,128)(2,1)S(1)}, u32[]{:S(2)}, u32[]{:S(2)}) %collective-permute-start) | collective-permute-done | bytes 110624 | tf_op jit(solution)/shard_map/ppermute | solution.py:56
  13.0 0.7 collective-permute-start.1
  13.8 3.4 %collective-permute-start.2 = (bf16[1,96,1024]{2,1,0:T(8,128)(2,1)S(1)}, bf16[1,96,1024]{2,1,0:T(8,128)(2,1)S(1)}, u32[]{:S(2)}, u32[]{:S(2)}) collective-permute-start(bf16[1,96,1024]{2,1,0:T(8,128)(2,1)S(1)} %maximum_bitcast_fusion.1), channel_id=1, source_target_pairs={{0,16},{4,20},{8,24},{12,28},{16,0},{20,4},{24,8},{28,12},{1,17},{... | collective-permute-start | bytes 589832 | tf_op jit(solution)/shard_map/ppermute | solution.py:56
  17.1 6.3 %collective-permute-done.2 = bf16[1,96,1024]{2,1,0:T(8,128)(2,1)S(1)} collective-permute-done((bf16[1,96,1024]{2,1,0:T(8,128)(2,1)S(1)}, bf16[1,96,1024]{2,1,0:T(8,128)(2,1)S(1)}, u32[]{:S(2)}, u32[]{:S(2)}) %collective-permute-start.2) | collective-permute-done | bytes 196640 | tf_op jit(solution)/shard_map/ppermute | solution.py:56
  23.4 0.7 collective-permute-done.1
  24.4 1.6 collective-permute-start.4
  26.0 0.9 fusion.1
  26.9 3.5 %collective-permute-start.5 = (bf16[2,96,1024]{2,1,0:T(8,128)(2,1)}, bf16[2,96,1024]{2,1,0:T(8,128)(2,1)}, u32[]{:S(2)}, u32[]{:S(2)}) collective-permute-start(bf16[2,96,1024]{2,1,0:T(8,128)(2,1)} %get-tuple-element.250), channel_id=1, source_target_pairs={{0,8},{4,12},{8,0},{12,4},{16,24},{20,28},{24,16},{28,20},{1,9},{5... | collective-permute-start | bytes 1179656 | tf_op jit(solution)/shard_map/ppermute | solution.py:56
  31.7 4.4 %collective-permute-done.6 = bf16[1,96,768]{2,1,0:T(8,128)(2,1)} collective-permute-done((bf16[1,96,768]{2,1,0:T(8,128)(2,1)S(1)}, bf16[1,96,768]{2,1,0:T(8,128)(2,1)}, u32[]{:S(2)}, u32[]{:S(2)}) %collective-permute-start.6) | collective-permute-done | bytes 147488 | tf_op jit(solution)/shard_map/ppermute | solution.py:56
  36.1 4.0 %collective-permute-done.5 = bf16[2,96,1024]{2,1,0:T(8,128)(2,1)} collective-permute-done((bf16[2,96,1024]{2,1,0:T(8,128)(2,1)}, bf16[2,96,1024]{2,1,0:T(8,128)(2,1)}, u32[]{:S(2)}, u32[]{:S(2)}) %collective-permute-start.5) | collective-permute-done | bytes 393248 | tf_op jit(solution)/shard_map/ppermute | solution.py:56
  40.2 1.7 pad_maximum_fusion
  43.0 0.9 fusion.6
  44.0 1.8 collective-permute-start.9
  45.8 5.3 %project.1 = (bf16[3,2048,128]{2,1,0:T(8,128)(2,1)S(1)}, bf16[3,2048,128]{2,1,0:T(8,128)(2,1)S(1)}, bf16[3,2048,128]{2,1,0:T(8,128)(2,1)S(1)}) custom-call(bf16[512,768]{1,0:T(8,128)(2,1)S(1)} %copy-done.4, bf16[512,768]{1,0:T(8,128)(2,1)} %collective-permute-done.8.refs_1_.refs_5_, bf16[512,768]{1,0:T(8,128)(2,1)S(1)} %collective-permute-done.3.refs_2_.refs_6_, ...), custom_call_target="tpu_custom_call" | custom-call | flops 1000 | bytes 1000 | tf_op jit(solution)/shard_map/project/pallas_call | solution.py:157
  51.1 6.2 %attention_forward.2 = (bf16[3,2048,128]{2,1,0:T(8,128)(2,1)S(1)}, f32[3,2048,128]{2,1,0:T(8,128)S(1)}, bf16[3,256,128]{2,1,0:T(8,128)(2,1)S(1)}, bf16[3,256,128...) custom-call(bf16[3,2048,128]{2,1,0:T(8,128)(2,1)S(1)} %get-tuple-element.143.q_ref, ...), custom_call_target="tpu_custom_call" | custom-call | flops 1000 | bytes 1000 | tf_op jit(solution)/shard_map/attention_forward/pallas_call | solution.py:231
  57.3 3.3 %collective-permute-done.9 = bf16[1,2,96,768]{3,2,1,0:T(8,128)(2,1)S(1)} collective-permute-done((bf16[1,2,96,768]{3,2,1,0:T(8,128)(2,1)S(1)}, bf16[1,2,96,768]{3,2,1,0:T(8,128)(2,1)S(1)}, u32[]{:S(2)}, u32[]{:S(2)}) %collective-permute-start.9) | collective-permute-done | bytes 294944 | tf_op jit(solution)/shard_map/ppermute | solution.py:56
  61.3 0.9 collective-permute-start.14
  62.3 2.1 collective-permute-start.13
  65.0 11.8 %attention_forward.3 = (bf16[3,2048,128]{2,1,0:T(8,128)(2,1)S(1)}, f32[3,2048,128]{2,1,0:T(8,128)S(1)}, bf16[3,256,128]{2,1,0:T(8,128)(2,1)S(1)}, bf16[3,256,128...) custom-call(bf16[3,2048,128]{2,1,0:T(8,128)(2,1)S(1)} %get-tuple-ele, ...), custom_call_target="tpu_custom_call", output_to_operand_aliasing={{0}: (3, {}), {1}: (4, {}), {2}: (5, {}), {3}: (6, {}), {4}... | custom-call | flops 1000 | bytes 1000 | tf_op jit(solution)/shard_map/attention_forward/pallas_call | solution.py:231
  76.9 1.7 copy-done
  78.6 1.1 copy-done.3
  80.5 2.6 collective-permute-done.17.refs_12_
  83.2 0.8 copy-done.31
  84.1 1.5 collective-permute-start.19
  86.2 1.5 collective-permute-start.20
  87.6 9.6 %collective-permute-done.20.refs_18_ = bf16[2,3,256,128]{3,2,1,0:T(8,128)(2,1)S(1)} collective-permute-done((bf16[2,3,256,128]{3,2,1,0:T(8,128)(2,1)S(1)}, bf16[2,3,256,128]{3,2,1,0:T(8,128)(2,1)S(1)}, u32[]{:S(2)}, u32[]{:S(2)}) %collective-permute-start.20) | collective-permute-done | bytes 393248 | tf_op jit(solution)/shard_map/ppermute | solution.py:56
  97.3 2.5 collective-permute-done.19.refs_7_
  100.5 1.9 collective-permute-done.25.refs_17_
  102.5 0.9 copy-done.35
  103.4 39.0 %middle.1 = (bf16[512,768]{1,0:T(8,128)(2,1)}, f32[512,768]{1,0:T(8,128)}, bf16[2,8,112,768]{3,2,1,0:T(8,128)(2,1)}, bf16[2,8,112,768]{3,2,1,0:T(8,128)(2,1)}, b...) custom-call(bf16[4,96,1024]{2,1,0:T(8,128)(2,1)} %bitcast.62, ...), custom_call_target="tpu_custom_call" | custom-call | flops 1000 | bytes 1000 | tf_op jit(solution)/shard_map/middle/pallas_call | solution.py:639
  143.1 1.5 collective-permute-start.29
  144.9 3.6 %collective-permute-done.27 = bf16[2,8,96,960]{3,2,1,0:T(8,128)(2,1)} collective-permute-done((bf16[2,8,96,960]{3,2,1,0:T(8,128)(2,1)}, bf16[2,8,96,960]{3,2,1,0:T(8,128)(2,1)}, u32[]{:S(2)}, u32[]{:S(2)}) %collective-permute-start.27) | collective-permute-done | bytes 2949152 | tf_op jit(solution)/shard_map/ppermute | solution.py:56
  148.5 3.4 %sum_up.1 = bf16[2,2,2,96,960]{4,3,2,1,0:T(8,128)(2,1)} custom-call(bf16[2,2,2,2,96,960]{5,4,3,2,1,0:T(8,128)(2,1)} %bitcast.46, bf16[2,2,2,2,96,960]{5,4,3,2,1,0:T(8,128)(2,1)} %bitcast.26.refs_1_.refs_4_.refs_5_.refs_6_), custom_call_target="tpu_custom_call" | custom-call | flops 1000 | bytes 1000 | tf_op jit(solution)/shard_map/sum_up/pallas_call | solution.py:761
  151.9 1.6 collective-permute-start.32
  153.5 3.1 %sum_down.1 = bf16[2,2,2,112,768]{4,3,2,1,0:T(8,128)(2,1)} custom-call(bf16[2,2,2,2,112,768]{5,4,3,2,1,0:T(8,128)(2,1)} %bitcast.51, bf16[2,2,2,2,112,768]{5,4,3,2,1,0:T(8,128)(2,1)} %bitcast.27.refs_1_), custom_call_target="tpu_custom_call" | custom-call | flops 1000 | bytes 1000 | tf_op jit(solution)/shard_map/sum_down/pallas_call | solution.py:761
  156.7 1.6 collective-permute-start.31
  158.3 30.7 %attention_backward.2 = (bf16[2,2048,192]{2,1,0:T(8,128)(2,1)}, bf16[3,8,96,256]{3,2,1,0:T(8,128)(2,1)}) custom-call(bf16[3,2048,128]{2,1,0:T(8,128)(2,1)} %copy-done.3, bf16[3,2048,128]{2,1,0:T(8,128)(2,1)} %copy-done.1, bf16[3,2048,128]{2,1,0:T(8,128)(2,1)} %copy-done.2, f32[3,2048,128]{2,1,0:T(8,128)} %copy-done, ...), custom_call_target="tpu_custom_call" | custom-call | flops 1000 | bytes 1000 | tf_op jit(solution)/shard_map/attention_backward/pallas_call | solution.py:353
  189.0 3.4 %sum_second.1 = (bf16[2,2,112,768]{3,2,1,0:T(8,128)(2,1)}, bf16[2,2,96,960]{3,2,1,0:T(8,128)(2,1)}) custom-call(bf16[2,2,2,2,112,768]{5,4,3,2,1,0:T(8,128)(2,1)} %bitcast.52, bf16[2,2,2,2,112,768]{5,4,3,2,1,0:T(8,128)(2,1)} %bitcast.27.refs_1_, bf16[2,2,2,112,768]{4,3,2,1,0:T(8,128)(2,1)} %collective-permute-done.31.refs_2_, ...), custom_call_target="tpu_custom_call" | custom-call | flops 1000 | bytes 1000 | tf_op jit(solution)/shard_map/sum_second/pallas_call | solution.py:761
  192.5 1.6 collective-permute-start.34
  194.5 20.1 %attention_backward.3 = (bf16[1,2048,192]{2,1,0:T(8,128)(2,1)}, bf16[3,8,96,256]{3,2,1,0:T(8,128)(2,1)}, bf16[256,768]{1,0:T(8,128)(2,1)}, bf16[256,768]{1,0:T(8,128)(2,1)}, bf16[2,256,768]{2,1,0:T(8,128)(2,1)}) custom-call(bf16[3,2048,128]{2,1,0:T(8,128)(2,1)} %copy-done.3, bf16[3,2048,128]{2,1,0:T(8,128)(2,1)} %copy-done.1, ...), custom_call_target="tpu_custom_call", output_to_operand_aliasing={{1}: (15, {})} | custom-call | flops 1000 | bytes 1000 | tf_op jit(solution)/shard_map/attention_backward/pallas_call | solution.py:353
  215.1 1.5 collective-permute-done.35.refs_10_
  217.2 3.8 %sum_third.1 = (bf16[2,112,768]{2,1,0:T(8,128)(2,1)}, bf16[2,96,960]{2,1,0:T(8,128)(2,1)}, bf16[3,2,2,96,256]{4,3,2,1,0:T(8,128)(2,1)}, bf16[2,256,768]{2,1,0:T(8,128)(2,1)}) custom-call(bf16[2,2,2,2,112,768]{5,4,3,2,1,0:T(8,128)(2,1)} %bitcast.53, bf16[2,2,2,2,112,768]{5,4,3,2,1,0:T(8,128)(2,1)} %bitcast.27.refs_1_, ...), custom_call_target="tpu_custom_call" | custom-call | flops 1000 | bytes 1000 | tf_op jit(solution)/shard_map/sum_third/pallas_call | solution.py:761
  221.1 1.6 collective-permute-start.41
  222.7 0.8 collective-permute-start.39
  223.5 2.5 collective-permute-start.37
  226.0 4.8 %input_part.1 = (bf16[256,768]{1,0:T(8,128)(2,1)}, bf16[256,768]{1,0:T(8,128)(2,1)}, bf16[512,768]{1,0:T(8,128)(2,1)}) custom-call(bf16[2,2048,192]{2,1,0:T(8,128)(2,1)} %get-tuple-element.210.refs_8_.refs_0_, bf16[1,2048,192]{2,1,0:T(8,128)(2,1)} %get-tuple-element.211.refs_1_, bf16[4,96,576]{2,1,0:T(8,128)(2,1)} %bitcast.44, bf16[4,96,576]{2,1,0:T(8,128)(2,1)} %copy-done.8), custom_call_target="tpu_custom_call" | custom-call | flops 1000 | bytes 1000 | tf_op jit(solution)/shard_map/input_part/pallas_call | solution.py:397
  230.8 10.8 %collective-permute-done.37.refs_4_ = bf16[2,112,768]{2,1,0:T(8,128)(2,1)S(1)} collective-permute-done((bf16[2,112,768]{2,1,0:T(8,128)(2,1)}, bf16[2,112,768]{2,1,0:T(8,128)(2,1)S(1)}, u32[]{:S(2)}, u32[]{:S(2)}) %collective-permute-start.37) | collective-permute-done | bytes 344096 | tf_op jit(solution)/shard_map/ppermute | solution.py:56
  241.6 1.9 collective-permute-done.38.refs_9_.refs_4_
  243.5 0.8 copy-done.16
  244.3 2.8 %sum_fourth.1 = (bf16[112,768]{1,0:T(8,128)(2,1)}, bf16[96,960]{1,0:T(8,128)(2,1)}, bf16[3,96,256]{2,1,0:T(8,128)(2,1)}, bf16[3,96,256]{2,1,0:T(8,128)(2,1)}, bf16[3,96,256]{2,1,0:T(8,128)(2,1)}) custom-call(bf16[2,2,2,2,112,768]{5,4,3,2,1,0:T(8,128)(2,1)} %bitcast.54, bf16[2,2,2,2,112,768]{5,4,3,2,1,0:T(8,128)(2,1)} %bitcast.27.refs_1_, ...), custom_call_target="tpu_custom_call" | custom-call | flops 1000 | bytes 1000 | tf_op jit(solution)/shard_map/sum_fourth/pallas_call | solution.py:761
  247.1 1.3 collective-permute-start.40
  249.8 2.9 %collective-permute-start.45 = (bf16[3,96,256]{2,1,0:T(8,128)(2,1)}, bf16[3,96,256]{2,1,0:T(8,128)(2,1)S(1)}, u32[]{:S(2)}, u32[]{:S(2)}) collective-permute-start(bf16[3,96,256]{2,1,0:T(8,128)(2,1)} %get-tuple-element.226), channel_id=1, source_target_pairs={{0,16},{4,20},{8,24},{12,28},{16,0},{20,4},{24,8},{28,12},{1,17},{... | collective-permute-start | bytes 442376 | tf_op jit(solution)/shard_map/ppermute | solution.py:56
  253.2 1.1 collective-permute-start.47
  254.9 4.8 %finish_down.1 = (f32[96,768]{1,0:T(8,128)}, f32[16,768]{1,0:T(8,128)}, bf16[512,768]{1,0:T(8,128)(2,1)}) custom-call(bf16[2,2,2,2,112,768]{5,4,3,2,1,0:T(8,128)(2,1)} %bitcast.55, bf16[2,2,2,2,112,768]{5,4,3,2,1,0:T(8,128)(2,1)} %bitcast.27.refs_1_, bf16[2,2,2,112,768]{4,3,2,1,0:T(8,128)(2,1)} %collective-permute-done.31.refs_2_, ...), custom_call_target="tpu_custom_call" | custom-call | flops 1000 | bytes 1000 | tf_op jit(solution)/shard_map/finish_down/pallas_call | solution.py:761
  259.7 0.9 slice_reduce_fusion
  260.6 1.6 slice_reduce_fusion.1
  262.2 7.6 %collective-permute-done.45.refs_8_ = bf16[3,96,256]{2,1,0:T(8,128)(2,1)S(1)} collective-permute-done((bf16[3,96,256]{2,1,0:T(8,128)(2,1)}, bf16[3,96,256]{2,1,0:T(8,128)(2,1)S(1)}, u32[]{:S(2)}, u32[]{:S(2)}) %collective-permute-start.45) | collective-permute-done | bytes 147488 | tf_op jit(solution)/shard_map/ppermute | solution.py:56
  270.7 2.6 finish.1
  (177 shorter events, 11.5 us)
Async XLA Ops:
  0.7 23.5 %collective-permute-start.3 = (bf16[512,768]{1,0:T(8,128)(2,1)}, bf16[512,768]{1,0:T(8,128)(2,1)S(1)}, u32[]{:S(2)}, u32[]{:S(2)}) collective-permute-start(bf16[512,768]{1,0:T(8,128)(2,1)} %refs_4_.3), channel_id=1, source_target_pairs={{0,2},{1,3},{2,0},{3,1},{4,6},{5,7},{6,4},{7,5},{8,10},{9,11},{10,... | collective-permute-start | bytes 2359304 | tf_op jit(solution)/shard_map/ppermute | solution.py:56
  4.6 8.4 %collective-permute-start = (bf16[1,96,576]{2,1,0:T(8,128)(2,1)S(1)}, bf16[1,96,576]{2,1,0:T(8,128)(2,1)S(1)}, u32[]{:S(2)}, u32[]{:S(2)}) collective-permute-start(bf16[1,96,576]{2,1,0:T(8,128)(2,1)S(1)} %get-tuple-element.256), channel_id=1, source_target_pairs={{0,16},{4,20},{8,24},{12,28},{16,0},{20,4},{24,8},{28,12},{1,17},{... | collective-permute-start | bytes 331784 | tf_op jit(solution)/shard_map/ppermute | solution.py:56
  13.0 11.1 %collective-permute-start.1 = (bf16[2,96,576]{2,1,0:T(8,128)(2,1)S(1)}, bf16[2,96,576]{2,1,0:T(8,128)(2,1)S(1)}, u32[]{:S(2)}, u32[]{:S(2)}) collective-permute-start(bf16[2,96,576]{2,1,0:T(8,128)(2,1)S(1)} %get-tuple-element.254), channel_id=1, source_target_pairs={{0,8},{4,12},{8,0},{12,4},{16,24},{20,28},{24,16},{28,20},{1,9},{5... | collective-permute-start | bytes 663560 | tf_op jit(solution)/shard_map/ppermute | solution.py:56
  13.8 9.7 %collective-permute-start.2 = (bf16[1,96,1024]{2,1,0:T(8,128)(2,1)S(1)}, bf16[1,96,1024]{2,1,0:T(8,128)(2,1)S(1)}, u32[]{:S(2)}, u32[]{:S(2)}) collective-permute-start(bf16[1,96,1024]{2,1,0:T(8,128)(2,1)S(1)} %maximum_bitcast_fusion.1), channel_id=1, source_target_pairs={{0,16},{4,20},{8,24},{12,28},{16,0},{20,4},{24,8},{28,12},{1,17},{... | collective-permute-start | bytes 589832 | tf_op jit(solution)/shard_map/ppermute | solution.py:56
  24.1 21.7 %copy-start.6 = (bf16[512,768]{1,0:T(8,128)(2,1)}, bf16[512,768]{1,0:T(8,128)(2,1)S(1)}, u32[]{:S(2)}) copy-start(bf16[512,768]{1,0:T(8,128)(2,1)S(1)} %collective-permute-done.3.refs_2_.refs_6_) | copy-start | bytes 2359300
  24.1 16.0 %collective-permute-start.7 = (bf16[512,768]{1,0:T(8,128)(2,1)S(1)}, bf16[512,768]{1,0:T(8,128)(2,1)S(1)}, u32[]{:S(2)}, u32[]{:S(2)}) collective-permute-start(bf16[512,768]{1,0:T(8,128)(2,1)S(1)} %collective-permute-done.3.refs_2_.refs_6_), channel_id=1, source_target_pairs={{0,1},{1,0},{2,3},{3,2},{4,5},{5,4},{6,7},{7,6},{8,9},{9,8},{10,11... | collective-permute-start | bytes 2359304 | tf_op jit(solution)/shard_map/ppermute | solution.py:56
  24.2 6.8 %copy-start.50 = (bf16[192]{0:T(256)(128)(2,1)S(1)}, bf16[192]{0:T(256)(128)(2,1)}, u32[]{:S(2)}) copy-start(bf16[192]{0:T(256)(128)(2,1)} %param.29) | copy-start | bytes 1156
  24.4 21.4 %copy-start.5 = (bf16[2,2,96,576]{3,2,1,0:T(8,128)(2,1)}, bf16[2,2,96,576]{3,2,1,0:T(8,128)(2,1)S(1)}, u32[]{:S(2)}) copy-start(bf16[2,2,96,576]{3,2,1,0:T(8,128)(2,1)S(1)} %copy.44) | copy-start | bytes 1327108
  24.4 15.7 %collective-permute-start.4 = (bf16[4,96,576]{2,1,0:T(8,128)(2,1)S(1)}, bf16[4,96,576]{2,1,0:T(8,128)(2,1)S(1)}, u32[]{:S(2)}, u32[]{:S(2)}) collective-permute-start(bf16[4,96,576]{2,1,0:T(8,128)(2,1)S(1)} %bitcast.41), channel_id=1, source_target_pairs={{0,4},{4,0},{8,12},{12,8},{16,20},{20,16},{24,28},{28,24},{1,5},{5... | collective-permute-start | bytes 1327112 | tf_op jit(solution)/shard_map/ppermute | solution.py:56
  26.9 13.2 %collective-permute-start.5 = (bf16[2,96,1024]{2,1,0:T(8,128)(2,1)}, bf16[2,96,1024]{2,1,0:T(8,128)(2,1)}, u32[]{:S(2)}, u32[]{:S(2)}) collective-permute-start(bf16[2,96,1024]{2,1,0:T(8,128)(2,1)} %get-tuple-element.250), channel_id=1, source_target_pairs={{0,8},{4,12},{8,0},{12,4},{16,24},{20,28},{24,16},{28,20},{1,9},{5... | collective-permute-start | bytes 1179656 | tf_op jit(solution)/shard_map/ppermute | solution.py:56
  30.4 5.8 %collective-permute-start.6 = (bf16[1,96,768]{2,1,0:T(8,128)(2,1)S(1)}, bf16[1,96,768]{2,1,0:T(8,128)(2,1)}, u32[]{:S(2)}, u32[]{:S(2)}) collective-permute-start(bf16[1,96,768]{2,1,0:T(8,128)(2,1)S(1)} %bitcast.68), channel_id=1, source_target_pairs={{0,2},{1,3},{2,0},{3,1},{4,6},{5,7},{6,4},{7,5},{8,10},{9,11},{10,... | collective-permute-start | bytes 442376 | tf_op jit(solution)/shard_map/ppermute | solution.py:56
  30.9 14.9 %collective-permute-start.8 = (bf16[512,768]{1,0:T(8,128)(2,1)S(1)}, bf16[512,768]{1,0:T(8,128)(2,1)}, u32[]{:S(2)}, u32[]{:S(2)}) collective-permute-start(bf16[512,768]{1,0:T(8,128)(2,1)S(1)} %copy-done.4), channel_id=1, source_target_pairs={{0,1},{1,0},{2,3},{3,2},{4,5},{5,4},{6,7},{7,6},{8,9},{9,8},{10,11... | collective-permute-start | bytes 2359304 | tf_op jit(solution)/shard_map/ppermute | solution.py:56
  41.9 9.2 %copy-start.14 = (bf16[2,2,96,1024]{3,2,1,0:T(8,128)(2,1)}, bf16[2,2,96,1024]{3,2,1,0:T(8,128)(2,1)S(1)}, u32[]{:S(2)}) copy-start(bf16[2,2,96,1024]{3,2,1,0:T(8,128)(2,1)S(1)} %copy.45) | copy-start | bytes 2359300
  41.9 19.2 %collective-permute-start.10 = (bf16[4,96,1024]{2,1,0:T(8,128)(2,1)S(1)}, bf16[4,96,1024]{2,1,0:T(8,128)(2,1)S(1)}, u32[]{:S(2)}, u32[]{:S(2)}) collective-permute-start(bf16[4,96,1024]{2,1,0:T(8,128)(2,1)S(1)} %bitcast.59), channel_id=1, source_target_pairs={{0,4},{4,0},{8,12},{12,8},{16,20},{20,16},{24,28},{28,24},{1,5},{5... | collective-permute-start | bytes 2359304 | tf_op jit(solution)/shard_map/ppermute | solution.py:56
  42.5 18.8 %collective-permute-start.11 = (bf16[4,96,1024]{2,1,0:T(8,128)(2,1)S(1)}, bf16[4,96,1024]{2,1,0:T(8,128)(2,1)S(1)}, u32[]{:S(2)}, u32[]{:S(2)}) collective-permute-start(bf16[4,96,1024]{2,1,0:T(8,128)(2,1)S(1)} %bitcast.60), channel_id=1, source_target_pairs={{0,2},{1,3},{2,0},{3,1},{4,6},{5,7},{6,4},{7,5},{8,10},{9,11},{10,... | collective-permute-start | bytes 2359304 | tf_op jit(solution)/shard_map/ppermute | solution.py:56
  43.0 18.3 %collective-permute-start.12 = (bf16[4,96,1024]{2,1,0:T(8,128)(2,1)S(1)}, bf16[4,96,1024]{2,1,0:T(8,128)(2,1)S(1)}, u32[]{:S(2)}, u32[]{:S(2)}) collective-permute-start(bf16[4,96,1024]{2,1,0:T(8,128)(2,1)S(1)} %bitcast.61), channel_id=1, source_target_pairs={{0,1},{1,0},{2,3},{3,2},{4,5},{5,4},{6,7},{7,6},{8,9},{9,8},{10,11... | collective-permute-start | bytes 2359304 | tf_op jit(solution)/shard_map/ppermute | solution.py:56
  44.0 16.7 %collective-permute-start.9 = (bf16[1,2,96,768]{3,2,1,0:T(8,128)(2,1)S(1)}, bf16[1,2,96,768]{3,2,1,0:T(8,128)(2,1)S(1)}, u32[]{:S(2)}, u32[]{:S(2)}) collective-permute-start(bf16[1,2,96,768]{3,2,1,0:T(8,128)(2,1)S(1)} %get-tuple-element.252), channel_id=1, source_target_pairs={{0,16},{4,20},{8,24},{12,28},{16,0},{20,4},{24,8},{28,12},{1,17},{... | collective-permute-start | bytes 884744 | tf_op jit(solution)/shard_map/ppermute | solution.py:56
  51.1 13.9 %copy-start.1 = (bf16[3,2048,128]{2,1,0:T(8,128)(2,1)}, bf16[3,2048,128]{2,1,0:T(8,128)(2,1)S(1)}, u32[]{:S(2)}) copy-start(bf16[3,2048,128]{2,1,0:T(8,128)(2,1)S(1)} %get-tuple-element.144.k_ref) | copy-start | bytes 4718596
  51.1 13.9 %copy-start.2 = (bf16[3,2048,128]{2,1,0:T(8,128)(2,1)}, bf16[3,2048,128]{2,1,0:T(8,128)(2,1)S(1)}, u32[]{:S(2)}) copy-start(bf16[3,2048,128]{2,1,0:T(8,128)(2,1)S(1)} %get-tuple-element.145.v_ref) | copy-start | bytes 4718596
  61.1 18.9 %copy-start.22 = (bf16[4,96,1024]{2,1,0:T(8,128)(2,1)}, bf16[4,96,1024]{2,1,0:T(8,128)(2,1)S(1)}, u32[]{:S(2)}) copy-start(bf16[4,96,1024]{2,1,0:T(8,128)(2,1)S(1)} %collective-permute-done.10.refs_1_) | copy-start | bytes 2359300
  61.3 15.6 %copy-start.23 = (bf16[4,96,1024]{2,1,0:T(8,128)(2,1)}, bf16[4,96,1024]{2,1,0:T(8,128)(2,1)S(1)}, u32[]{:S(2)}) copy-start(bf16[4,96,1024]{2,1,0:T(8,128)(2,1)S(1)} %collective-permute-done.11.refs_2_) | copy-start | bytes 2359300
  61.3 15.6 %copy-start.24 = (bf16[4,96,1024]{2,1,0:T(8,128)(2,1)}, bf16[4,96,1024]{2,1,0:T(8,128)(2,1)S(1)}, u32[]{:S(2)}) copy-start(bf16[4,96,1024]{2,1,0:T(8,128)(2,1)S(1)} %collective-permute-done.12.refs_8_) | copy-start | bytes 2359300
  61.3 18.6 %collective-permute-start.14 = (bf16[4,96,1024]{2,1,0:T(8,128)(2,1)S(1)}, bf16[4,96,1024]{2,1,0:T(8,128)(2,1)S(1)}, u32[]{:S(2)}, u32[]{:S(2)}) collective-permute-start(bf16[4,96,1024]{2,1,0:T(8,128)(2,1)S(1)} %collective-permute-done.10.refs_1_), channel_id=1, source_target_pairs={{0,2},{1,3},{2,0},{3,1},{4,6},{5,7},{6,4},{7,5},{8,10},{9,11},{10,... | collective-permute-start | bytes 2359304 | tf_op jit(solution)/shard_map/ppermute | solution.py:56
  62.3 17.7 %collective-permute-start.16 = (bf16[4,96,1024]{2,1,0:T(8,128)(2,1)S(1)}, bf16[4,96,1024]{2,1,0:T(8,128)(2,1)S(1)}, u32[]{:S(2)}, u32[]{:S(2)}) collective-permute-start(bf16[4,96,1024]{2,1,0:T(8,128)(2,1)S(1)} %collective-permute-done.11.refs_2_), channel_id=1, source_target_pairs={{0,1},{1,0},{2,3},{3,2},{4,5},{5,4},{6,7},{7,6},{8,9},{9,8},{10,11... | collective-permute-start | bytes 2359304 | tf_op jit(solution)/shard_map/ppermute | solution.py:56
  62.3 17.7 %copy-start.15 = (bf16[2,2,96,768]{3,2,1,0:T(8,128)(2,1)}, bf16[2,2,96,768]{3,2,1,0:T(8,128)(2,1)S(1)}, u32[]{:S(2)}) copy-start(bf16[2,2,96,768]{3,2,1,0:T(8,128)(2,1)S(1)} %maximum_bitcast_fusion.refs_4_) | copy-start | bytes 1769476
  62.3 17.4 %collective-permute-start.13 = (bf16[2,2,96,768]{3,2,1,0:T(8,128)(2,1)S(1)}, bf16[2,2,96,768]{3,2,1,0:T(8,128)(2,1)S(1)}, u32[]{:S(2)}, u32[]{:S(2)}) collective-permute-start(bf16[2,2,96,768]{3,2,1,0:T(8,128)(2,1)S(1)} %maximum_bitcast_fusion.refs_4_), channel_id=1, source_target_pairs={{0,8},{4,12},{8,0},{12,4},{16,24},{20,28},{24,16},{28,20},{1,9},{5... | collective-permute-start | bytes 1769480 | tf_op jit(solution)/shard_map/ppermute | solution.py:56
  64.4 15.5 %collective-permute-start.15 = (bf16[2,2,96,768]{3,2,1,0:T(8,128)(2,1)S(1)}, bf16[2,2,96,768]{3,2,1,0:T(8,128)(2,1)S(1)}, u32[]{:S(2)}, u32[]{:S(2)}) collective-permute-start(bf16[2,2,96,768]{3,2,1,0:T(8,128)(2,1)S(1)} %maximum_bitcast_fusion.refs_4_), channel_id=1, source_target_pairs={{0,4},{4,0},{8,12},{12,8},{16,20},{20,16},{24,28},{28,24},{1,5},{5... | collective-permute-start | bytes 1769480 | tf_op jit(solution)/shard_map/ppermute | solution.py:56
  79.7 23.7 %copy-start.9 = (bf16[3,256,128]{2,1,0:T(8,128)(2,1)}, bf16[3,256,128]{2,1,0:T(8,128)(2,1)S(1)}, u32[]{:S(2)}) copy-start(bf16[3,256,128]{2,1,0:T(8,128)(2,1)S(1)} %get-tuple-element.175.refs_16_) | copy-start | bytes 589828
  79.7 22.7 %copy-start.29 = (bf16[2,2,96,768]{3,2,1,0:T(8,128)(2,1)}, bf16[2,2,96,768]{3,2,1,0:T(8,128)(2,1)S(1)}, u32[]{:S(2)}) copy-start(bf16[2,2,96,768]{3,2,1,0:T(8,128)(2,1)S(1)} %collective-permute-done.13.refs_6_) | copy-start | bytes 1769476
  79.9 22.5 %copy-start.30 = (bf16[2,2,96,768]{3,2,1,0:T(8,128)(2,1)}, bf16[2,2,96,768]{3,2,1,0:T(8,128)(2,1)S(1)}, u32[]{:S(2)}) copy-start(bf16[2,2,96,768]{3,2,1,0:T(8,128)(2,1)S(1)} %collective-permute-done.15.refs_5_) | copy-start | bytes 1769476
  80.0 20.0 %copy-start.25 = (bf16[4,96,1024]{2,1,0:T(8,128)(2,1)}, bf16[4,96,1024]{2,1,0:T(8,128)(2,1)S(1)}, u32[]{:S(2)}) copy-start(bf16[4,96,1024]{2,1,0:T(8,128)(2,1)S(1)} %collective-permute-done.14.refs_3_) | copy-start | bytes 2359300
  80.0 20.5 %copy-start.26 = (bf16[4,96,1024]{2,1,0:T(8,128)(2,1)}, bf16[4,96,1024]{2,1,0:T(8,128)(2,1)S(1)}, u32[]{:S(2)}) copy-start(bf16[4,96,1024]{2,1,0:T(8,128)(2,1)S(1)} %collective-permute-done.16.refs_10_) | copy-start | bytes 2359300
  80.0 4.0 %collective-permute-start.18 = (bf16[4,96,1024]{2,1,0:T(8,128)(2,1)S(1)}, bf16[4,96,1024]{2,1,0:T(8,128)(2,1)S(1)}, u32[]{:S(2)}, u32[]{:S(2)}) collective-permute-start(bf16[4,96,1024]{2,1,0:T(8,128)(2,1)S(1)} %collective-permute-done.10.refs_1_), channel_id=1, source_target_pairs={{0,1},{1,0},{2,3},{3,2},{4,5},{5,4},{6,7},{7,6},{8,9},{9,8},{10,11... | collective-permute-start | bytes 2359304 | tf_op jit(solution)/shard_map/ppermute | solution.py:56
  80.1 3.1 %collective-permute-start.17 = (bf16[2,2,96,768]{3,2,1,0:T(8,128)(2,1)S(1)}, bf16[2,2,96,768]{3,2,1,0:T(8,128)(2,1)S(1)}, u32[]{:S(2)}, u32[]{:S(2)}) collective-permute-start(bf16[2,2,96,768]{3,2,1,0:T(8,128)(2,1)S(1)} %maximum_bitcast_fusion.refs_4_), channel_id=1, source_target_pairs={{0,1},{1,0},{2,3},{3,2},{4,5},{5,4},{6,7},{7,6},{8,9},{9,8},{10,11... | collective-permute-start | bytes 1769480 | tf_op jit(solution)/shard_map/ppermute | solution.py:56
  84.0 18.4 %copy-start.27 = (bf16[4,96,1024]{2,1,0:T(8,128)(2,1)}, bf16[4,96,1024]{2,1,0:T(8,128)(2,1)S(1)}, u32[]{:S(2)}) copy-start(bf16[4,96,1024]{2,1,0:T(8,128)(2,1)S(1)} %collective-permute-done.18.refs_9_) | copy-start | bytes 2359300
  84.0 15.8 %collective-permute-start.21 = (bf16[4,96,1024]{2,1,0:T(8,128)(2,1)S(1)}, bf16[4,96,1024]{2,1,0:T(8,128)(2,1)S(1)}, u32[]{:S(2)}, u32[]{:S(2)}) collective-permute-start(bf16[4,96,1024]{2,1,0:T(8,128)(2,1)S(1)} %collective-permute-done.14.refs_3_), channel_id=1, source_target_pairs={{0,1},{1,0},{2,3},{3,2},{4,5},{5,4},{6,7},{7,6},{8,9},{9,8},{10,11... | collective-permute-start | bytes 2359304 | tf_op jit(solution)/shard_map/ppermute | solution.py:56
  84.1 15.6 %collective-permute-start.19 = (bf16[2,2,96,768]{3,2,1,0:T(8,128)(2,1)S(1)}, bf16[2,2,96,768]{3,2,1,0:T(8,128)(2,1)S(1)}, u32[]{:S(2)}, u32[]{:S(2)}) collective-permute-start(bf16[2,2,96,768]{3,2,1,0:T(8,128)(2,1)S(1)} %collective-permute-done.13.refs_6_), channel_id=1, source_target_pairs={{0,4},{4,0},{8,12},{12,8},{16,20},{20,16},{24,28},{28,24},{1,5},{5... | collective-permute-start | bytes 1769480 | tf_op jit(solution)/shard_map/ppermute | solution.py:56
  85.6 14.1 %collective-permute-start.22 = (bf16[2,2,96,768]{3,2,1,0:T(8,128)(2,1)S(1)}, bf16[2,2,96,768]{3,2,1,0:T(8,128)(2,1)S(1)}, u32[]{:S(2)}, u32[]{:S(2)}) collective-permute-start(bf16[2,2,96,768]{3,2,1,0:T(8,128)(2,1)S(1)} %collective-permute-done.13.refs_6_), channel_id=1, source_target_pairs={{0,1},{1,0},{2,3},{3,2},{4,5},{5,4},{6,7},{7,6},{8,9},{9,8},{10,11... | collective-permute-start | bytes 1769480 | tf_op jit(solution)/shard_map/ppermute | solution.py:56
  85.7 14.0 %collective-permute-start.23 = (bf16[2,2,96,768]{3,2,1,0:T(8,128)(2,1)S(1)}, bf16[2,2,96,768]{3,2,1,0:T(8,128)(2,1)S(1)}, u32[]{:S(2)}, u32[]{:S(2)}) collective-permute-start(bf16[2,2,96,768]{3,2,1,0:T(8,128)(2,1)S(1)} %collective-permute-done.15.refs_5_), channel_id=1, source_target_pairs={{0,1},{1,0},{2,3},{3,2},{4,5},{5,4},{6,7},{7,6},{8,9},{9,8},{10,11... | collective-permute-start | bytes 1769480 | tf_op jit(solution)/shard_map/ppermute | solution.py:56
  86.2 11.1 %collective-permute-start.20 = (bf16[2,3,256,128]{3,2,1,0:T(8,128)(2,1)S(1)}, bf16[2,3,256,128]{3,2,1,0:T(8,128)(2,1)S(1)}, u32[]{:S(2)}, u32[]{:S(2)}) collective-permute-start(bf16[2,3,256,128]{3,2,1,0:T(8,128)(2,1)S(1)} %get-tuple-element.171), channel_id=1, source_target_pairs={{0,2},{1,3},{2,0},{3,1},{4,6},{5,7},{6,4},{7,5},{8,10},{9,11},{10,... | collective-permute-start | bytes 1179656 | tf_op jit(solution)/shard_map/ppermute | solution.py:56
  99.8 2.6 collective-permute-start.24
  99.9 2.5 collective-permute-start.25
  142.4 6.1 %collective-permute-start.27 = (bf16[2,8,96,960]{3,2,1,0:T(8,128)(2,1)}, bf16[2,8,96,960]{3,2,1,0:T(8,128)(2,1)}, u32[]{:S(2)}, u32[]{:S(2)}) collective-permute-start(bf16[2,8,96,960]{3,2,1,0:T(8,128)(2,1)} %get-tuple-element.183), channel_id=1, source_target_pairs={{0,1},{1,0},{2,3},{3,2},{4,5},{5,4},{6,7},{7,6},{8,9},{9,8},{10,11... | collective-permute-start | bytes 8847368 | tf_op jit(solution)/shard_map/ppermute | solution.py:56
  142.6 10.9 %collective-permute-start.26 = (bf16[2,8,112,768]{3,2,1,0:T(8,128)(2,1)}, bf16[2,8,112,768]{3,2,1,0:T(8,128)(2,1)}, u32[]{:S(2)}, u32[]{:S(2)}) collective-permute-start(bf16[2,8,112,768]{3,2,1,0:T(8,128)(2,1)} %get-tuple-element.181), channel_id=1, source_target_pairs={{0,1},{1,0},{2,3},{3,2},{4,5},{5,4},{6,7},{7,6},{8,9},{9,8},{10,11... | collective-permute-start | bytes 8257544 | tf_op jit(solution)/shard_map/ppermute | solution.py:56
  143.0 13.6 %collective-permute-start.28 = (bf16[3,256,128]{2,1,0:T(8,128)(2,1)}, bf16[3,256,128]{2,1,0:T(8,128)(2,1)S(1)}, u32[]{:S(2)}, u32[]{:S(2)}) collective-permute-start(bf16[3,256,128]{2,1,0:T(8,128)(2,1)} %get-tuple-element.186), channel_id=1, source_target_pairs={{0,1},{1,0},{2,3},{3,2},{4,5},{5,4},{6,7},{7,6},{8,9},{9,8},{10,11... | collective-permute-start | bytes 589832 | tf_op jit(solution)/shard_map/ppermute | solution.py:56
  143.1 13.5 %collective-permute-start.29 = (bf16[3,256,128]{2,1,0:T(8,128)(2,1)}, bf16[3,256,128]{2,1,0:T(8,128)(2,1)S(1)}, u32[]{:S(2)}, u32[]{:S(2)}) collective-permute-start(bf16[3,256,128]{2,1,0:T(8,128)(2,1)} %get-tuple-element.187), channel_id=1, source_target_pairs={{0,2},{1,3},{2,0},{3,1},{4,6},{5,7},{6,4},{7,5},{8,10},{9,11},{10,... | collective-permute-start | bytes 589832 | tf_op jit(solution)/shard_map/ppermute | solution.py:56
  144.6 12.0 %collective-permute-start.30 = (bf16[3,256,128]{2,1,0:T(8,128)(2,1)}, bf16[3,256,128]{2,1,0:T(8,128)(2,1)S(1)}, u32[]{:S(2)}, u32[]{:S(2)}) collective-permute-start(bf16[3,256,128]{2,1,0:T(8,128)(2,1)} %get-tuple-element.188), channel_id=1, source_target_pairs={{0,3},{1,2},{2,1},{3,0},{4,7},{5,6},{6,5},{7,4},{8,11},{9,10},{10,... | collective-permute-start | bytes 589832 | tf_op jit(solution)/shard_map/ppermute | solution.py:56
  151.9 37.1 %collective-permute-start.32 = (bf16[2,2,2,96,960]{4,3,2,1,0:T(8,128)(2,1)}, bf16[2,2,2,96,960]{4,3,2,1,0:T(8,128)(2,1)}, u32[]{:S(2)}, u32[]{:S(2)}) collective-permute-start(bf16[2,2,2,96,960]{4,3,2,1,0:T(8,128)(2,1)} %sum_up.1), channel_id=1, source_target_pairs={{0,4},{4,0},{8,12},{12,8},{16,20},{20,16},{24,28},{28,24},{1,5},{5... | collective-permute-start | bytes 4423688 | tf_op jit(solution)/shard_map/ppermute | solution.py:56
  156.7 32.3 %collective-permute-start.31 = (bf16[2,2,2,112,768]{4,3,2,1,0:T(8,128)(2,1)}, bf16[2,2,2,112,768]{4,3,2,1,0:T(8,128)(2,1)}, u32[]{:S(2)}, u32[]{:S(2)}) collective-permute-start(bf16[2,2,2,112,768]{4,3,2,1,0:T(8,128)(2,1)} %sum_down.1), channel_id=1, source_target_pairs={{0,2},{1,3},{2,0},{3,1},{4,6},{5,7},{6,4},{7,5},{8,10},{9,11},{10,... | collective-permute-start | bytes 4128776 | tf_op jit(solution)/shard_map/ppermute | solution.py:56
  192.5 22.7 %collective-permute-start.34 = (bf16[2,2,96,960]{3,2,1,0:T(8,128)(2,1)}, bf16[2,2,96,960]{3,2,1,0:T(8,128)(2,1)S(1)}, u32[]{:S(2)}, u32[]{:S(2)}) collective-permute-start(bf16[2,2,96,960]{3,2,1,0:T(8,128)(2,1)} %get-tuple-element.203), channel_id=1, source_target_pairs={{0,2},{1,3},{2,0},{3,1},{4,6},{5,7},{6,4},{7,5},{8,10},{9,11},{10,... | collective-permute-start | bytes 2211848 | tf_op jit(solution)/shard_map/ppermute | solution.py:56
  194.0 21.1 %collective-permute-start.33 = (bf16[2,2,112,768]{3,2,1,0:T(8,128)(2,1)}, bf16[2,2,112,768]{3,2,1,0:T(8,128)(2,1)}, u32[]{:S(2)}, u32[]{:S(2)}) collective-permute-start(bf16[2,2,112,768]{3,2,1,0:T(8,128)(2,1)} %get-tuple-element.198), channel_id=1, source_target_pairs={{0,8},{4,12},{8,0},{12,4},{16,24},{20,28},{24,16},{28,20},{1,9},{5... | collective-permute-start | bytes 2064392 | tf_op jit(solution)/shard_map/ppermute | solution.py:56
  214.6 2.1 collective-permute-start.35
  214.6 2.6 collective-permute-start.36
  221.1 28.7 %collective-permute-start.41 = (bf16[2,256,768]{2,1,0:T(8,128)(2,1)}, bf16[2,256,768]{2,1,0:T(8,128)(2,1)}, u32[]{:S(2)}, u32[]{:S(2)}) collective-permute-start(bf16[2,256,768]{2,1,0:T(8,128)(2,1)} %get-tuple-element.222), channel_id=1, source_target_pairs={{0,2},{1,3},{2,0},{3,1},{4,6},{5,7},{6,4},{7,5},{8,10},{9,11},{10,... | collective-permute-start | bytes 2359304 | tf_op jit(solution)/shard_map/ppermute | solution.py:56
  222.7 20.8 %collective-permute-start.39 = (bf16[3,2,2,96,256]{4,3,2,1,0:T(8,128)(2,1)}, bf16[3,2,2,96,256]{4,3,2,1,0:T(8,128)(2,1)S(1)}, u32[]{:S(2)}, u32[]{:S(2)}) collective-permute-start(bf16[3,2,2,96,256]{4,3,2,1,0:T(8,128)(2,1)} %get-tuple-element.218), channel_id=1, source_target_pairs={{0,4},{4,0},{8,12},{12,8},{16,20},{20,16},{24,28},{28,24},{1,5},{5... | collective-permute-start | bytes 1769480 | tf_op jit(solution)/shard_map/ppermute | solution.py:56
  223.5 18.1 %collective-permute-start.37 = (bf16[2,112,768]{2,1,0:T(8,128)(2,1)}, bf16[2,112,768]{2,1,0:T(8,128)(2,1)S(1)}, u32[]{:S(2)}, u32[]{:S(2)}) collective-permute-start(bf16[2,112,768]{2,1,0:T(8,128)(2,1)} %get-tuple-element.209), channel_id=1, source_target_pairs={{0,16},{4,20},{8,24},{12,28},{16,0},{20,4},{24,8},{28,12},{1,17},{... | collective-permute-start | bytes 1032200 | tf_op jit(solution)/shard_map/ppermute | solution.py:56
  226.0 17.5 %collective-permute-start.38 = (bf16[2,96,960]{2,1,0:T(8,128)(2,1)}, bf16[2,96,960]{2,1,0:T(8,128)(2,1)}, u32[]{:S(2)}, u32[]{:S(2)}) collective-permute-start(bf16[2,96,960]{2,1,0:T(8,128)(2,1)} %get-tuple-element.216), channel_id=1, source_target_pairs={{0,8},{4,12},{8,0},{12,4},{16,24},{20,28},{24,16},{28,20},{1,9},{5... | collective-permute-start | bytes 1105928 | tf_op jit(solution)/shard_map/ppermute | solution.py:56
  230.8 21.9 %collective-permute-start.42 = (bf16[256,768]{1,0:T(8,128)(2,1)}, bf16[256,768]{1,0:T(8,128)(2,1)}, u32[]{:S(2)}, u32[]{:S(2)}) collective-permute-start(bf16[256,768]{1,0:T(8,128)(2,1)} %get-tuple-element.212), channel_id=1, source_target_pairs={{0,1},{1,0},{2,3},{3,2},{4,5},{5,4},{6,7},{7,6},{8,9},{9,8},{10,11... | collective-permute-start | bytes 1179656 | tf_op jit(solution)/shard_map/ppermute | solution.py:56
  241.6 11.6 %collective-permute-start.43 = (bf16[256,768]{1,0:T(8,128)(2,1)}, bf16[256,768]{1,0:T(8,128)(2,1)}, u32[]{:S(2)}, u32[]{:S(2)}) collective-permute-start(bf16[256,768]{1,0:T(8,128)(2,1)} %get-tuple-element.213), channel_id=1, source_target_pairs={{0,1},{1,0},{2,3},{3,2},{4,5},{5,4},{6,7},{7,6},{8,9},{9,8},{10,11... | collective-permute-start | bytes 1179656 | tf_op jit(solution)/shard_map/ppermute | solution.py:56
  247.1 7.1 %collective-permute-start.40 = (bf16[112,768]{1,0:T(8,128)(2,1)}, bf16[112,768]{1,0:T(8,128)(2,1)S(1)}, u32[]{:S(2)}, u32[]{:S(2)}) collective-permute-start(bf16[112,768]{1,0:T(8,128)(2,1)} %get-tuple-element.220), channel_id=1, source_target_pairs={{0,4},{4,0},{8,12},{12,8},{16,20},{20,16},{24,28},{28,24},{1,5},{5... | collective-permute-start | bytes 516104 | tf_op jit(solution)/shard_map/ppermute | solution.py:56
  249.7 20.2 %collective-permute-start.44 = (bf16[96,960]{1,0:T(8,128)(2,1)}, bf16[96,960]{1,0:T(8,128)(2,1)S(1)}, u32[]{:S(2)}, u32[]{:S(2)}) collective-permute-start(bf16[96,960]{1,0:T(8,128)(2,1)} %get-tuple-element.225), channel_id=1, source_target_pairs={{0,16},{4,20},{8,24},{12,28},{16,0},{20,4},{24,8},{28,12},{1,17},{... | collective-permute-start | bytes 552968 | tf_op jit(solution)/shard_map/ppermute | solution.py:56
  249.8 20.0 %collective-permute-start.45 = (bf16[3,96,256]{2,1,0:T(8,128)(2,1)}, bf16[3,96,256]{2,1,0:T(8,128)(2,1)S(1)}, u32[]{:S(2)}, u32[]{:S(2)}) collective-permute-start(bf16[3,96,256]{2,1,0:T(8,128)(2,1)} %get-tuple-element.226), channel_id=1, source_target_pairs={{0,16},{4,20},{8,24},{12,28},{16,0},{20,4},{24,8},{28,12},{1,17},{... | collective-permute-start | bytes 442376 | tf_op jit(solution)/shard_map/ppermute | solution.py:56
  252.7 17.1 %collective-permute-start.46 = (bf16[3,96,256]{2,1,0:T(8,128)(2,1)}, bf16[3,96,256]{2,1,0:T(8,128)(2,1)S(1)}, u32[]{:S(2)}, u32[]{:S(2)}) collective-permute-start(bf16[3,96,256]{2,1,0:T(8,128)(2,1)} %get-tuple-element.227), channel_id=1, source_target_pairs={{0,8},{4,12},{8,0},{12,4},{16,24},{20,28},{24,16},{28,20},{1,9},{5... | collective-permute-start | bytes 442376 | tf_op jit(solution)/shard_map/ppermute | solution.py:56
  253.2 16.6 %collective-permute-start.47 = (bf16[3,96,256]{2,1,0:T(8,128)(2,1)}, bf16[3,96,256]{2,1,0:T(8,128)(2,1)S(1)}, u32[]{:S(2)}, u32[]{:S(2)}) collective-permute-start(bf16[3,96,256]{2,1,0:T(8,128)(2,1)} %get-tuple-element.228), channel_id=1, source_target_pairs={{0,24},{4,28},{8,16},{12,20},{16,8},{20,12},{24,0},{28,4},{1,25},{... | collective-permute-start | bytes 442376 | tf_op jit(solution)/shard_map/ppermute | solution.py:56
  (35 other events, 122.3 us)

commit v7 on v6

--- a/solution.py
+++ b/solution.py
@@ -497,7 +497,7 @@
         if second:
             copy.wait()
 
-    wide = 256
+    wide = 384
     per = hidden // wide
 
     def chunk_of(c):
@@ -669,8 +669,8 @@
             vmem((rows, LANES), F32),
             vmem((16, width), F32),
             vmem((4, EXTRA, width), BF16),
-            vmem((2, rows, 256), F32),
-            vmem((rows, 256), BF16),
+            vmem((2, rows, 384), F32),
+            vmem((rows, 384), BF16),
             pltpu.SemaphoreType.DMA((loads,)),
             pltpu.SemaphoreType.DMA((4, blocks)),
             pltpu.SemaphoreType.DMA((4, blocks)),

time: 275 us -> 274 us (level)
  no operation moved by 1% of the time
where the time goes in v7:
time: 274 us; the launch traced here: 273 us
  Pallas kernels  141 us (51%)
  waiting for transfers between devices  65.3 us (24%)
  starting transfers between devices  45.5 us (17%)
  local copies, waits for them, and re-layouts  10.6 us (4%)
  other arithmetic  7.83 us (3%)
    ppermute x48, waiting for transfers between devices, swap(): return lax.ppermute(value, axis, [(i, i ^ bits) for i in range(size)])  65.3 us
    pallas_call x2, Pallas kernels, attention_backward(): pl.pallas_call(functools.partial(backward_kernel, placed=blocks > 1, mask...  50.8 us
    ppermute x48, starting transfers between devices, swap(): return lax.ppermute(value, axis, [(i, i ^ bits) for i in range(size)])  45.5 us
    pallas_call x1, Pallas kernels, middle(): pl.pallas_call(functools.partial(middle_kernel, plan=plan, blocks=blocks)...  38.6 us
    pallas_call x7, Pallas kernels, reduce_call(): pl.pallas_call(functools.partial(reduce_kernel if keep else reduce_inside...  24 us
    pallas_call x2, Pallas kernels, attention_forward(): pl.pallas_call(functools.partial(forward_kernel, unroll=4 if first else 2...  18.1 us
    unnamed x103, local copies, waits for them, and re-layouts  7.33 us
  transfers between devices with their start and end apart: 48, of which 21 were waited for; matrix products, arithmetic and copies ran while one was open for 4% of the time, Pallas kernels for 34%

profile of v7, /device:TPU:0, one launch (start us, length us, event | category | flops | bytes accessed | tf_op | source)
XLA Modules:
  0.0 273.1 jit_solution(9701273631774470120)
XLA Ops:
  0.7 3.0 %collective-permute-start.3 = (bf16[512,768]{1,0:T(8,128)(2,1)}, bf16[512,768]{1,0:T(8,128)(2,1)S(1)}, u32[]{:S(2)}, u32[]{:S(2)}) collective-permute-start(bf16[512,768]{1,0:T(8,128)(2,1)} %refs_4_.3), channel_id=1, source_target_pairs={{0,2},{1,3},{2,0},{3,1},{4,6},{5,7},{6,4},{7,5},{8,10},{9,11},{10,... | collective-permute-start | bytes 2359304 | tf_op jit(solution)/shard_map/ppermute | solution.py:56
  3.7 0.9 fusion.5
  4.6 2.7 collective-permute-start
  7.3 0.9 copy.43
  8.1 0.8 dynamic_slice.3
  9.0 1.0 maximum_bitcast_fusion.1
  10.0 3.0 %collective-permute-done = bf16[1,96,576]{2,1,0:T(8,128)(2,1)S(1)} collective-permute-done((bf16[1,96,576]{2,1,0:T(8,128)(2,1)S(1)}, bf16[1,96,576]{2,1,0:T(8,128)(2,1)S(1)}, u32[]{:S(2)}, u32[]{:S(2)}) %collective-permute-start) | collective-permute-done | bytes 110624 | tf_op jit(solution)/shard_map/ppermute | solution.py:56
  13.0 0.7 collective-permute-start.1
  13.8 3.4 %collective-permute-start.2 = (bf16[1,96,1024]{2,1,0:T(8,128)(2,1)S(1)}, bf16[1,96,1024]{2,1,0:T(8,128)(2,1)S(1)}, u32[]{:S(2)}, u32[]{:S(2)}) collective-permute-start(bf16[1,96,1024]{2,1,0:T(8,128)(2,1)S(1)} %maximum_bitcast_fusion.1), channel_id=1, source_target_pairs={{0,16},{4,20},{8,24},{12,28},{16,0},{20,4},{24,8},{28,12},{1,17},{... | collective-permute-start | bytes 589832 | tf_op jit(solution)/shard_map/ppermute | solution.py:56
  17.1 6.3 %collective-permute-done.2 = bf16[1,96,1024]{2,1,0:T(8,128)(2,1)S(1)} collective-permute-done((bf16[1,96,1024]{2,1,0:T(8,128)(2,1)S(1)}, bf16[1,96,1024]{2,1,0:T(8,128)(2,1)S(1)}, u32[]{:S(2)}, u32[]{:S(2)}) %collective-permute-start.2) | collective-permute-done | bytes 196640 | tf_op jit(solution)/shard_map/ppermute | solution.py:56
  23.4 0.7 collective-permute-done.1
  24.4 1.6 collective-permute-start.4
  26.0 0.9 fusion.1
  26.9 3.5 %collective-permute-start.5 = (bf16[2,96,1024]{2,1,0:T(8,128)(2,1)}, bf16[2,96,1024]{2,1,0:T(8,128)(2,1)}, u32[]{:S(2)}, u32[]{:S(2)}) collective-permute-start(bf16[2,96,1024]{2,1,0:T(8,128)(2,1)} %get-tuple-element.250), channel_id=1, source_target_pairs={{0,8},{4,12},{8,0},{12,4},{16,24},{20,28},{24,16},{28,20},{1,9},{5... | collective-permute-start | bytes 1179656 | tf_op jit(solution)/shard_map/ppermute | solution.py:56
  31.7 4.4 %collective-permute-done.6 = bf16[1,96,768]{2,1,0:T(8,128)(2,1)} collective-permute-done((bf16[1,96,768]{2,1,0:T(8,128)(2,1)S(1)}, bf16[1,96,768]{2,1,0:T(8,128)(2,1)}, u32[]{:S(2)}, u32[]{:S(2)}) %collective-permute-start.6) | collective-permute-done | bytes 147488 | tf_op jit(solution)/shard_map/ppermute | solution.py:56
  36.1 4.0 %collective-permute-done.5 = bf16[2,96,1024]{2,1,0:T(8,128)(2,1)} collective-permute-done((bf16[2,96,1024]{2,1,0:T(8,128)(2,1)}, bf16[2,96,1024]{2,1,0:T(8,128)(2,1)}, u32[]{:S(2)}, u32[]{:S(2)}) %collective-permute-start.5) | collective-permute-done | bytes 393248 | tf_op jit(solution)/shard_map/ppermute | solution.py:56
  40.2 1.7 pad_maximum_fusion
  43.0 0.9 fusion.6
  44.0 1.8 collective-permute-start.9
  45.8 5.3 %project.1 = (bf16[3,2048,128]{2,1,0:T(8,128)(2,1)S(1)}, bf16[3,2048,128]{2,1,0:T(8,128)(2,1)S(1)}, bf16[3,2048,128]{2,1,0:T(8,128)(2,1)S(1)}) custom-call(bf16[512,768]{1,0:T(8,128)(2,1)S(1)} %copy-done.4, bf16[512,768]{1,0:T(8,128)(2,1)} %collective-permute-done.8.refs_1_.refs_5_, bf16[512,768]{1,0:T(8,128)(2,1)S(1)} %collective-permute-done.3.refs_2_.refs_6_, ...), custom_call_target="tpu_custom_call" | custom-call | flops 1000 | bytes 1000 | tf_op jit(solution)/shard_map/project/pallas_call | solution.py:157
  51.1 6.2 %attention_forward.2 = (bf16[3,2048,128]{2,1,0:T(8,128)(2,1)S(1)}, f32[3,2048,128]{2,1,0:T(8,128)S(1)}, bf16[3,256,128]{2,1,0:T(8,128)(2,1)S(1)}, bf16[3,256,128...) custom-call(bf16[3,2048,128]{2,1,0:T(8,128)(2,1)S(1)} %get-tuple-element.143.q_ref, ...), custom_call_target="tpu_custom_call" | custom-call | flops 1000 | bytes 1000 | tf_op jit(solution)/shard_map/attention_forward/pallas_call | solution.py:231
  57.3 3.3 %collective-permute-done.9 = bf16[1,2,96,768]{3,2,1,0:T(8,128)(2,1)S(1)} collective-permute-done((bf16[1,2,96,768]{3,2,1,0:T(8,128)(2,1)S(1)}, bf16[1,2,96,768]{3,2,1,0:T(8,128)(2,1)S(1)}, u32[]{:S(2)}, u32[]{:S(2)}) %collective-permute-start.9) | collective-permute-done | bytes 294944 | tf_op jit(solution)/shard_map/ppermute | solution.py:56
  61.3 0.9 collective-permute-start.14
  62.3 2.1 collective-permute-start.13
  65.0 11.8 %attention_forward.3 = (bf16[3,2048,128]{2,1,0:T(8,128)(2,1)S(1)}, f32[3,2048,128]{2,1,0:T(8,128)S(1)}, bf16[3,256,128]{2,1,0:T(8,128)(2,1)S(1)}, bf16[3,256,128...) custom-call(bf16[3,2048,128]{2,1,0:T(8,128)(2,1)S(1)} %get-tuple-ele, ...), custom_call_target="tpu_custom_call", output_to_operand_aliasing={{0}: (3, {}), {1}: (4, {}), {2}: (5, {}), {3}: (6, {}), {4}... | custom-call | flops 1000 | bytes 1000 | tf_op jit(solution)/shard_map/attention_forward/pallas_call | solution.py:231
  76.9 1.7 copy-done
  78.6 1.1 copy-done.3
  80.5 2.6 collective-permute-done.17.refs_12_
  83.2 0.8 copy-done.31
  84.1 1.5 collective-permute-start.19
  86.2 1.5 collective-permute-start.20
  87.6 9.6 %collective-permute-done.20.refs_18_ = bf16[2,3,256,128]{3,2,1,0:T(8,128)(2,1)S(1)} collective-permute-done((bf16[2,3,256,128]{3,2,1,0:T(8,128)(2,1)S(1)}, bf16[2,3,256,128]{3,2,1,0:T(8,128)(2,1)S(1)}, u32[]{:S(2)}, u32[]{:S(2)}) %collective-permute-start.20) | collective-permute-done | bytes 393248 | tf_op jit(solution)/shard_map/ppermute | solution.py:56
  97.3 2.5 collective-permute-done.19.refs_7_
  100.5 1.9 collective-permute-done.25.refs_17_
  102.5 0.9 copy-done.35
  103.4 38.6 %middle.1 = (bf16[512,768]{1,0:T(8,128)(2,1)}, f32[512,768]{1,0:T(8,128)}, bf16[2,8,112,768]{3,2,1,0:T(8,128)(2,1)}, bf16[2,8,112,768]{3,2,1,0:T(8,128)(2,1)}, b...) custom-call(bf16[4,96,1024]{2,1,0:T(8,128)(2,1)} %bitcast.62, ...), custom_call_target="tpu_custom_call" | custom-call | flops 1000 | bytes 1000 | tf_op jit(solution)/shard_map/middle/pallas_call | solution.py:639
  142.7 1.5 collective-permute-start.29
  144.4 3.6 %collective-permute-done.27 = bf16[2,8,96,960]{3,2,1,0:T(8,128)(2,1)} collective-permute-done((bf16[2,8,96,960]{3,2,1,0:T(8,128)(2,1)}, bf16[2,8,96,960]{3,2,1,0:T(8,128)(2,1)}, u32[]{:S(2)}, u32[]{:S(2)}) %collective-permute-start.27) | collective-permute-done | bytes 2949152 | tf_op jit(solution)/shard_map/ppermute | solution.py:56
  148.1 3.4 %sum_up.1 = bf16[2,2,2,96,960]{4,3,2,1,0:T(8,128)(2,1)} custom-call(bf16[2,2,2,2,96,960]{5,4,3,2,1,0:T(8,128)(2,1)} %bitcast.46, bf16[2,2,2,2,96,960]{5,4,3,2,1,0:T(8,128)(2,1)} %bitcast.26.refs_1_.refs_4_.refs_5_.refs_6_), custom_call_target="tpu_custom_call" | custom-call | flops 1000 | bytes 1000 | tf_op jit(solution)/shard_map/sum_up/pallas_call | solution.py:761
  151.5 1.6 collective-permute-start.32
  153.0 3.1 %sum_down.1 = bf16[2,2,2,112,768]{4,3,2,1,0:T(8,128)(2,1)} custom-call(bf16[2,2,2,2,112,768]{5,4,3,2,1,0:T(8,128)(2,1)} %bitcast.51, bf16[2,2,2,2,112,768]{5,4,3,2,1,0:T(8,128)(2,1)} %bitcast.27.refs_1_), custom_call_target="tpu_custom_call" | custom-call | flops 1000 | bytes 1000 | tf_op jit(solution)/shard_map/sum_down/pallas_call | solution.py:761
  156.3 1.6 collective-permute-start.31
  157.8 30.7 %attention_backward.2 = (bf16[2,2048,192]{2,1,0:T(8,128)(2,1)}, bf16[3,8,96,256]{3,2,1,0:T(8,128)(2,1)}) custom-call(bf16[3,2048,128]{2,1,0:T(8,128)(2,1)} %copy-done.3, bf16[3,2048,128]{2,1,0:T(8,128)(2,1)} %copy-done.1, bf16[3,2048,128]{2,1,0:T(8,128)(2,1)} %copy-done.2, f32[3,2048,128]{2,1,0:T(8,128)} %copy-done, ...), custom_call_target="tpu_custom_call" | custom-call | flops 1000 | bytes 1000 | tf_op jit(solution)/shard_map/attention_backward/pallas_call | solution.py:353
  188.6 3.4 %sum_second.1 = (bf16[2,2,112,768]{3,2,1,0:T(8,128)(2,1)}, bf16[2,2,96,960]{3,2,1,0:T(8,128)(2,1)}) custom-call(bf16[2,2,2,2,112,768]{5,4,3,2,1,0:T(8,128)(2,1)} %bitcast.52, bf16[2,2,2,2,112,768]{5,4,3,2,1,0:T(8,128)(2,1)} %bitcast.27.refs_1_, bf16[2,2,2,112,768]{4,3,2,1,0:T(8,128)(2,1)} %collective-permute-done.31.refs_2_, ...), custom_call_target="tpu_custom_call" | custom-call | flops 1000 | bytes 1000 | tf_op jit(solution)/shard_map/sum_second/pallas_call | solution.py:761
  192.0 1.6 collective-permute-start.34
  194.0 20.1 %attention_backward.3 = (bf16[1,2048,192]{2,1,0:T(8,128)(2,1)}, bf16[3,8,96,256]{3,2,1,0:T(8,128)(2,1)}, bf16[256,768]{1,0:T(8,128)(2,1)}, bf16[256,768]{1,0:T(8,128)(2,1)}, bf16[2,256,768]{2,1,0:T(8,128)(2,1)}) custom-call(bf16[3,2048,128]{2,1,0:T(8,128)(2,1)} %copy-done.3, bf16[3,2048,128]{2,1,0:T(8,128)(2,1)} %copy-done.1, ...), custom_call_target="tpu_custom_call", output_to_operand_aliasing={{1}: (15, {})} | custom-call | flops 1000 | bytes 1000 | tf_op jit(solution)/shard_map/attention_backward/pallas_call | solution.py:353
  214.7 1.5 collective-permute-done.35.refs_10_
  216.8 3.8 %sum_third.1 = (bf16[2,112,768]{2,1,0:T(8,128)(2,1)}, bf16[2,96,960]{2,1,0:T(8,128)(2,1)}, bf16[3,2,2,96,256]{4,3,2,1,0:T(8,128)(2,1)}, bf16[2,256,768]{2,1,0:T(8,128)(2,1)}) custom-call(bf16[2,2,2,2,112,768]{5,4,3,2,1,0:T(8,128)(2,1)} %bitcast.53, bf16[2,2,2,2,112,768]{5,4,3,2,1,0:T(8,128)(2,1)} %bitcast.27.refs_1_, ...), custom_call_target="tpu_custom_call" | custom-call | flops 1000 | bytes 1000 | tf_op jit(solution)/shard_map/sum_third/pallas_call | solution.py:761
  220.7 1.6 collective-permute-start.41
  222.2 0.8 collective-permute-start.39
  223.1 2.5 collective-permute-start.37
  225.6 4.8 %input_part.1 = (bf16[256,768]{1,0:T(8,128)(2,1)}, bf16[256,768]{1,0:T(8,128)(2,1)}, bf16[512,768]{1,0:T(8,128)(2,1)}) custom-call(bf16[2,2048,192]{2,1,0:T(8,128)(2,1)} %get-tuple-element.210.refs_8_.refs_0_, bf16[1,2048,192]{2,1,0:T(8,128)(2,1)} %get-tuple-element.211.refs_1_, bf16[4,96,576]{2,1,0:T(8,128)(2,1)} %bitcast.44, bf16[4,96,576]{2,1,0:T(8,128)(2,1)} %copy-done.8), custom_call_target="tpu_custom_call" | custom-call | flops 1000 | bytes 1000 | tf_op jit(solution)/shard_map/input_part/pallas_call | solution.py:397
  230.3 10.8 %collective-permute-done.37.refs_4_ = bf16[2,112,768]{2,1,0:T(8,128)(2,1)S(1)} collective-permute-done((bf16[2,112,768]{2,1,0:T(8,128)(2,1)}, bf16[2,112,768]{2,1,0:T(8,128)(2,1)S(1)}, u32[]{:S(2)}, u32[]{:S(2)}) %collective-permute-start.37) | collective-permute-done | bytes 344096 | tf_op jit(solution)/shard_map/ppermute | solution.py:56
  241.2 1.9 collective-permute-done.38.refs_9_.refs_4_
  243.1 0.8 copy-done.16
  243.9 2.8 %sum_fourth.1 = (bf16[112,768]{1,0:T(8,128)(2,1)}, bf16[96,960]{1,0:T(8,128)(2,1)}, bf16[3,96,256]{2,1,0:T(8,128)(2,1)}, bf16[3,96,256]{2,1,0:T(8,128)(2,1)}, bf16[3,96,256]{2,1,0:T(8,128)(2,1)}) custom-call(bf16[2,2,2,2,112,768]{5,4,3,2,1,0:T(8,128)(2,1)} %bitcast.54, bf16[2,2,2,2,112,768]{5,4,3,2,1,0:T(8,128)(2,1)} %bitcast.27.refs_1_, ...), custom_call_target="tpu_custom_call" | custom-call | flops 1000 | bytes 1000 | tf_op jit(solution)/shard_map/sum_fourth/pallas_call | solution.py:761
  246.7 1.3 collective-permute-start.40
  249.4 2.9 %collective-permute-start.45 = (bf16[3,96,256]{2,1,0:T(8,128)(2,1)}, bf16[3,96,256]{2,1,0:T(8,128)(2,1)S(1)}, u32[]{:S(2)}, u32[]{:S(2)}) collective-permute-start(bf16[3,96,256]{2,1,0:T(8,128)(2,1)} %get-tuple-element.226), channel_id=1, source_target_pairs={{0,16},{4,20},{8,24},{12,28},{16,0},{20,4},{24,8},{28,12},{1,17},{... | collective-permute-start | bytes 442376 | tf_op jit(solution)/shard_map/ppermute | solution.py:56
  252.8 1.1 collective-permute-start.47
  254.5 4.8 %finish_down.1 = (f32[96,768]{1,0:T(8,128)}, f32[16,768]{1,0:T(8,128)}, bf16[512,768]{1,0:T(8,128)(2,1)}) custom-call(bf16[2,2,2,2,112,768]{5,4,3,2,1,0:T(8,128)(2,1)} %bitcast.55, bf16[2,2,2,2,112,768]{5,4,3,2,1,0:T(8,128)(2,1)} %bitcast.27.refs_1_, bf16[2,2,2,112,768]{4,3,2,1,0:T(8,128)(2,1)} %collective-permute-done.31.refs_2_, ...), custom_call_target="tpu_custom_call" | custom-call | flops 1000 | bytes 1000 | tf_op jit(solution)/shard_map/finish_down/pallas_call | solution.py:761
  259.2 0.9 slice_reduce_fusion
  260.2 1.6 slice_reduce_fusion.1
  261.8 7.6 %collective-permute-done.45.refs_8_ = bf16[3,96,256]{2,1,0:T(8,128)(2,1)S(1)} collective-permute-done((bf16[3,96,256]{2,1,0:T(8,128)(2,1)}, bf16[3,96,256]{2,1,0:T(8,128)(2,1)S(1)}, u32[]{:S(2)}, u32[]{:S(2)}) %collective-permute-start.45) | collective-permute-done | bytes 147488 | tf_op jit(solution)/shard_map/ppermute | solution.py:56
  270.2 2.6 finish.1
  (177 shorter events, 11.5 us)
Async XLA Ops:
  0.7 23.5 %collective-permute-start.3 = (bf16[512,768]{1,0:T(8,128)(2,1)}, bf16[512,768]{1,0:T(8,128)(2,1)S(1)}, u32[]{:S(2)}, u32[]{:S(2)}) collective-permute-start(bf16[512,768]{1,0:T(8,128)(2,1)} %refs_4_.3), channel_id=1, source_target_pairs={{0,2},{1,3},{2,0},{3,1},{4,6},{5,7},{6,4},{7,5},{8,10},{9,11},{10,... | collective-permute-start | bytes 2359304 | tf_op jit(solution)/shard_map/ppermute | solution.py:56
  4.6 8.4 %collective-permute-start = (bf16[1,96,576]{2,1,0:T(8,128)(2,1)S(1)}, bf16[1,96,576]{2,1,0:T(8,128)(2,1)S(1)}, u32[]{:S(2)}, u32[]{:S(2)}) collective-permute-start(bf16[1,96,576]{2,1,0:T(8,128)(2,1)S(1)} %get-tuple-element.256), channel_id=1, source_target_pairs={{0,16},{4,20},{8,24},{12,28},{16,0},{20,4},{24,8},{28,12},{1,17},{... | collective-permute-start | bytes 331784 | tf_op jit(solution)/shard_map/ppermute | solution.py:56
  13.0 11.1 %collective-permute-start.1 = (bf16[2,96,576]{2,1,0:T(8,128)(2,1)S(1)}, bf16[2,96,576]{2,1,0:T(8,128)(2,1)S(1)}, u32[]{:S(2)}, u32[]{:S(2)}) collective-permute-start(bf16[2,96,576]{2,1,0:T(8,128)(2,1)S(1)} %get-tuple-element.254), channel_id=1, source_target_pairs={{0,8},{4,12},{8,0},{12,4},{16,24},{20,28},{24,16},{28,20},{1,9},{5... | collective-permute-start | bytes 663560 | tf_op jit(solution)/shard_map/ppermute | solution.py:56
  13.8 9.7 %collective-permute-start.2 = (bf16[1,96,1024]{2,1,0:T(8,128)(2,1)S(1)}, bf16[1,96,1024]{2,1,0:T(8,128)(2,1)S(1)}, u32[]{:S(2)}, u32[]{:S(2)}) collective-permute-start(bf16[1,96,1024]{2,1,0:T(8,128)(2,1)S(1)} %maximum_bitcast_fusion.1), channel_id=1, source_target_pairs={{0,16},{4,20},{8,24},{12,28},{16,0},{20,4},{24,8},{28,12},{1,17},{... | collective-permute-start | bytes 589832 | tf_op jit(solution)/shard_map/ppermute | solution.py:56
  24.1 21.7 %copy-start.6 = (bf16[512,768]{1,0:T(8,128)(2,1)}, bf16[512,768]{1,0:T(8,128)(2,1)S(1)}, u32[]{:S(2)}) copy-start(bf16[512,768]{1,0:T(8,128)(2,1)S(1)} %collective-permute-done.3.refs_2_.refs_6_) | copy-start | bytes 2359300
  24.1 16.0 %collective-permute-start.7 = (bf16[512,768]{1,0:T(8,128)(2,1)S(1)}, bf16[512,768]{1,0:T(8,128)(2,1)S(1)}, u32[]{:S(2)}, u32[]{:S(2)}) collective-permute-start(bf16[512,768]{1,0:T(8,128)(2,1)S(1)} %collective-permute-done.3.refs_2_.refs_6_), channel_id=1, source_target_pairs={{0,1},{1,0},{2,3},{3,2},{4,5},{5,4},{6,7},{7,6},{8,9},{9,8},{10,11... | collective-permute-start | bytes 2359304 | tf_op jit(solution)/shard_map/ppermute | solution.py:56
  24.2 6.8 %copy-start.50 = (bf16[192]{0:T(256)(128)(2,1)S(1)}, bf16[192]{0:T(256)(128)(2,1)}, u32[]{:S(2)}) copy-start(bf16[192]{0:T(256)(128)(2,1)} %param.29) | copy-start | bytes 1156
  24.4 21.4 %copy-start.5 = (bf16[2,2,96,576]{3,2,1,0:T(8,128)(2,1)}, bf16[2,2,96,576]{3,2,1,0:T(8,128)(2,1)S(1)}, u32[]{:S(2)}) copy-start(bf16[2,2,96,576]{3,2,1,0:T(8,128)(2,1)S(1)} %copy.44) | copy-start | bytes 1327108
  24.4 15.7 %collective-permute-start.4 = (bf16[4,96,576]{2,1,0:T(8,128)(2,1)S(1)}, bf16[4,96,576]{2,1,0:T(8,128)(2,1)S(1)}, u32[]{:S(2)}, u32[]{:S(2)}) collective-permute-start(bf16[4,96,576]{2,1,0:T(8,128)(2,1)S(1)} %bitcast.41), channel_id=1, source_target_pairs={{0,4},{4,0},{8,12},{12,8},{16,20},{20,16},{24,28},{28,24},{1,5},{5... | collective-permute-start | bytes 1327112 | tf_op jit(solution)/shard_map/ppermute | solution.py:56
  26.9 13.2 %collective-permute-start.5 = (bf16[2,96,1024]{2,1,0:T(8,128)(2,1)}, bf16[2,96,1024]{2,1,0:T(8,128)(2,1)}, u32[]{:S(2)}, u32[]{:S(2)}) collective-permute-start(bf16[2,96,1024]{2,1,0:T(8,128)(2,1)} %get-tuple-element.250), channel_id=1, source_target_pairs={{0,8},{4,12},{8,0},{12,4},{16,24},{20,28},{24,16},{28,20},{1,9},{5... | collective-permute-start | bytes 1179656 | tf_op jit(solution)/shard_map/ppermute | solution.py:56
  30.4 5.8 %collective-permute-start.6 = (bf16[1,96,768]{2,1,0:T(8,128)(2,1)S(1)}, bf16[1,96,768]{2,1,0:T(8,128)(2,1)}, u32[]{:S(2)}, u32[]{:S(2)}) collective-permute-start(bf16[1,96,768]{2,1,0:T(8,128)(2,1)S(1)} %bitcast.68), channel_id=1, source_target_pairs={{0,2},{1,3},{2,0},{3,1},{4,6},{5,7},{6,4},{7,5},{8,10},{9,11},{10,... | collective-permute-start | bytes 442376 | tf_op jit(solution)/shard_map/ppermute | solution.py:56
  30.9 14.9 %collective-permute-start.8 = (bf16[512,768]{1,0:T(8,128)(2,1)S(1)}, bf16[512,768]{1,0:T(8,128)(2,1)}, u32[]{:S(2)}, u32[]{:S(2)}) collective-permute-start(bf16[512,768]{1,0:T(8,128)(2,1)S(1)} %copy-done.4), channel_id=1, source_target_pairs={{0,1},{1,0},{2,3},{3,2},{4,5},{5,4},{6,7},{7,6},{8,9},{9,8},{10,11... | collective-permute-start | bytes 2359304 | tf_op jit(solution)/shard_map/ppermute | solution.py:56
  41.9 9.2 %copy-start.14 = (bf16[2,2,96,1024]{3,2,1,0:T(8,128)(2,1)}, bf16[2,2,96,1024]{3,2,1,0:T(8,128)(2,1)S(1)}, u32[]{:S(2)}) copy-start(bf16[2,2,96,1024]{3,2,1,0:T(8,128)(2,1)S(1)} %copy.45) | copy-start | bytes 2359300
  41.9 19.2 %collective-permute-start.10 = (bf16[4,96,1024]{2,1,0:T(8,128)(2,1)S(1)}, bf16[4,96,1024]{2,1,0:T(8,128)(2,1)S(1)}, u32[]{:S(2)}, u32[]{:S(2)}) collective-permute-start(bf16[4,96,1024]{2,1,0:T(8,128)(2,1)S(1)} %bitcast.59), channel_id=1, source_target_pairs={{0,4},{4,0},{8,12},{12,8},{16,20},{20,16},{24,28},{28,24},{1,5},{5... | collective-permute-start | bytes 2359304 | tf_op jit(solution)/shard_map/ppermute | solution.py:56
  42.5 18.8 %collective-permute-start.11 = (bf16[4,96,1024]{2,1,0:T(8,128)(2,1)S(1)}, bf16[4,96,1024]{2,1,0:T(8,128)(2,1)S(1)}, u32[]{:S(2)}, u32[]{:S(2)}) collective-permute-start(bf16[4,96,1024]{2,1,0:T(8,128)(2,1)S(1)} %bitcast.60), channel_id=1, source_target_pairs={{0,2},{1,3},{2,0},{3,1},{4,6},{5,7},{6,4},{7,5},{8,10},{9,11},{10,... | collective-permute-start | bytes 2359304 | tf_op jit(solution)/shard_map/ppermute | solution.py:56
  43.0 18.3 %collective-permute-start.12 = (bf16[4,96,1024]{2,1,0:T(8,128)(2,1)S(1)}, bf16[4,96,1024]{2,1,0:T(8,128)(2,1)S(1)}, u32[]{:S(2)}, u32[]{:S(2)}) collective-permute-start(bf16[4,96,1024]{2,1,0:T(8,128)(2,1)S(1)} %bitcast.61), channel_id=1, source_target_pairs={{0,1},{1,0},{2,3},{3,2},{4,5},{5,4},{6,7},{7,6},{8,9},{9,8},{10,11... | collective-permute-start | bytes 2359304 | tf_op jit(solution)/shard_map/ppermute | solution.py:56
  44.0 16.7 %collective-permute-start.9 = (bf16[1,2,96,768]{3,2,1,0:T(8,128)(2,1)S(1)}, bf16[1,2,96,768]{3,2,1,0:T(8,128)(2,1)S(1)}, u32[]{:S(2)}, u32[]{:S(2)}) collective-permute-start(bf16[1,2,96,768]{3,2,1,0:T(8,128)(2,1)S(1)} %get-tuple-element.252), channel_id=1, source_target_pairs={{0,16},{4,20},{8,24},{12,28},{16,0},{20,4},{24,8},{28,12},{1,17},{... | collective-permute-start | bytes 884744 | tf_op jit(solution)/shard_map/ppermute | solution.py:56
  51.1 13.9 %copy-start.1 = (bf16[3,2048,128]{2,1,0:T(8,128)(2,1)}, bf16[3,2048,128]{2,1,0:T(8,128)(2,1)S(1)}, u32[]{:S(2)}) copy-start(bf16[3,2048,128]{2,1,0:T(8,128)(2,1)S(1)} %get-tuple-element.144.k_ref) | copy-start | bytes 4718596
  51.1 13.9 %copy-start.2 = (bf16[3,2048,128]{2,1,0:T(8,128)(2,1)}, bf16[3,2048,128]{2,1,0:T(8,128)(2,1)S(1)}, u32[]{:S(2)}) copy-start(bf16[3,2048,128]{2,1,0:T(8,128)(2,1)S(1)} %get-tuple-element.145.v_ref) | copy-start | bytes 4718596
  61.1 18.9 %copy-start.22 = (bf16[4,96,1024]{2,1,0:T(8,128)(2,1)}, bf16[4,96,1024]{2,1,0:T(8,128)(2,1)S(1)}, u32[]{:S(2)}) copy-start(bf16[4,96,1024]{2,1,0:T(8,128)(2,1)S(1)} %collective-permute-done.10.refs_1_) | copy-start | bytes 2359300
  61.3 15.6 %copy-start.23 = (bf16[4,96,1024]{2,1,0:T(8,128)(2,1)}, bf16[4,96,1024]{2,1,0:T(8,128)(2,1)S(1)}, u32[]{:S(2)}) copy-start(bf16[4,96,1024]{2,1,0:T(8,128)(2,1)S(1)} %collective-permute-done.11.refs_2_) | copy-start | bytes 2359300
  61.3 15.6 %copy-start.24 = (bf16[4,96,1024]{2,1,0:T(8,128)(2,1)}, bf16[4,96,1024]{2,1,0:T(8,128)(2,1)S(1)}, u32[]{:S(2)}) copy-start(bf16[4,96,1024]{2,1,0:T(8,128)(2,1)S(1)} %collective-permute-done.12.refs_8_) | copy-start | bytes 2359300
  61.3 18.6 %collective-permute-start.14 = (bf16[4,96,1024]{2,1,0:T(8,128)(2,1)S(1)}, bf16[4,96,1024]{2,1,0:T(8,128)(2,1)S(1)}, u32[]{:S(2)}, u32[]{:S(2)}) collective-permute-start(bf16[4,96,1024]{2,1,0:T(8,128)(2,1)S(1)} %collective-permute-done.10.refs_1_), channel_id=1, source_target_pairs={{0,2},{1,3},{2,0},{3,1},{4,6},{5,7},{6,4},{7,5},{8,10},{9,11},{10,... | collective-permute-start | bytes 2359304 | tf_op jit(solution)/shard_map/ppermute | solution.py:56
  62.3 17.7 %collective-permute-start.16 = (bf16[4,96,1024]{2,1,0:T(8,128)(2,1)S(1)}, bf16[4,96,1024]{2,1,0:T(8,128)(2,1)S(1)}, u32[]{:S(2)}, u32[]{:S(2)}) collective-permute-start(bf16[4,96,1024]{2,1,0:T(8,128)(2,1)S(1)} %collective-permute-done.11.refs_2_), channel_id=1, source_target_pairs={{0,1},{1,0},{2,3},{3,2},{4,5},{5,4},{6,7},{7,6},{8,9},{9,8},{10,11... | collective-permute-start | bytes 2359304 | tf_op jit(solution)/shard_map/ppermute | solution.py:56
  62.3 17.7 %copy-start.15 = (bf16[2,2,96,768]{3,2,1,0:T(8,128)(2,1)}, bf16[2,2,96,768]{3,2,1,0:T(8,128)(2,1)S(1)}, u32[]{:S(2)}) copy-start(bf16[2,2,96,768]{3,2,1,0:T(8,128)(2,1)S(1)} %maximum_bitcast_fusion.refs_4_) | copy-start | bytes 1769476
  62.3 17.4 %collective-permute-start.13 = (bf16[2,2,96,768]{3,2,1,0:T(8,128)(2,1)S(1)}, bf16[2,2,96,768]{3,2,1,0:T(8,128)(2,1)S(1)}, u32[]{:S(2)}, u32[]{:S(2)}) collective-permute-start(bf16[2,2,96,768]{3,2,1,0:T(8,128)(2,1)S(1)} %maximum_bitcast_fusion.refs_4_), channel_id=1, source_target_pairs={{0,8},{4,12},{8,0},{12,4},{16,24},{20,28},{24,16},{28,20},{1,9},{5... | collective-permute-start | bytes 1769480 | tf_op jit(solution)/shard_map/ppermute | solution.py:56
  64.4 15.5 %collective-permute-start.15 = (bf16[2,2,96,768]{3,2,1,0:T(8,128)(2,1)S(1)}, bf16[2,2,96,768]{3,2,1,0:T(8,128)(2,1)S(1)}, u32[]{:S(2)}, u32[]{:S(2)}) collective-permute-start(bf16[2,2,96,768]{3,2,1,0:T(8,128)(2,1)S(1)} %maximum_bitcast_fusion.refs_4_), channel_id=1, source_target_pairs={{0,4},{4,0},{8,12},{12,8},{16,20},{20,16},{24,28},{28,24},{1,5},{5... | collective-permute-start | bytes 1769480 | tf_op jit(solution)/shard_map/ppermute | solution.py:56
  79.7 23.7 %copy-start.9 = (bf16[3,256,128]{2,1,0:T(8,128)(2,1)}, bf16[3,256,128]{2,1,0:T(8,128)(2,1)S(1)}, u32[]{:S(2)}) copy-start(bf16[3,256,128]{2,1,0:T(8,128)(2,1)S(1)} %get-tuple-element.175.refs_16_) | copy-start | bytes 589828
  79.7 22.7 %copy-start.29 = (bf16[2,2,96,768]{3,2,1,0:T(8,128)(2,1)}, bf16[2,2,96,768]{3,2,1,0:T(8,128)(2,1)S(1)}, u32[]{:S(2)}) copy-start(bf16[2,2,96,768]{3,2,1,0:T(8,128)(2,1)S(1)} %collective-permute-done.13.refs_6_) | copy-start | bytes 1769476
  79.9 22.5 %copy-start.30 = (bf16[2,2,96,768]{3,2,1,0:T(8,128)(2,1)}, bf16[2,2,96,768]{3,2,1,0:T(8,128)(2,1)S(1)}, u32[]{:S(2)}) copy-start(bf16[2,2,96,768]{3,2,1,0:T(8,128)(2,1)S(1)} %collective-permute-done.15.refs_5_) | copy-start | bytes 1769476
  80.0 20.0 %copy-start.25 = (bf16[4,96,1024]{2,1,0:T(8,128)(2,1)}, bf16[4,96,1024]{2,1,0:T(8,128)(2,1)S(1)}, u32[]{:S(2)}) copy-start(bf16[4,96,1024]{2,1,0:T(8,128)(2,1)S(1)} %collective-permute-done.14.refs_3_) | copy-start | bytes 2359300
  80.0 20.5 %copy-start.26 = (bf16[4,96,1024]{2,1,0:T(8,128)(2,1)}, bf16[4,96,1024]{2,1,0:T(8,128)(2,1)S(1)}, u32[]{:S(2)}) copy-start(bf16[4,96,1024]{2,1,0:T(8,128)(2,1)S(1)} %collective-permute-done.16.refs_10_) | copy-start | bytes 2359300
  80.0 4.0 %collective-permute-start.18 = (bf16[4,96,1024]{2,1,0:T(8,128)(2,1)S(1)}, bf16[4,96,1024]{2,1,0:T(8,128)(2,1)S(1)}, u32[]{:S(2)}, u32[]{:S(2)}) collective-permute-start(bf16[4,96,1024]{2,1,0:T(8,128)(2,1)S(1)} %collective-permute-done.10.refs_1_), channel_id=1, source_target_pairs={{0,1},{1,0},{2,3},{3,2},{4,5},{5,4},{6,7},{7,6},{8,9},{9,8},{10,11... | collective-permute-start | bytes 2359304 | tf_op jit(solution)/shard_map/ppermute | solution.py:56
  80.1 3.1 %collective-permute-start.17 = (bf16[2,2,96,768]{3,2,1,0:T(8,128)(2,1)S(1)}, bf16[2,2,96,768]{3,2,1,0:T(8,128)(2,1)S(1)}, u32[]{:S(2)}, u32[]{:S(2)}) collective-permute-start(bf16[2,2,96,768]{3,2,1,0:T(8,128)(2,1)S(1)} %maximum_bitcast_fusion.refs_4_), channel_id=1, source_target_pairs={{0,1},{1,0},{2,3},{3,2},{4,5},{5,4},{6,7},{7,6},{8,9},{9,8},{10,11... | collective-permute-start | bytes 1769480 | tf_op jit(solution)/shard_map/ppermute | solution.py:56
  84.0 18.4 %copy-start.27 = (bf16[4,96,1024]{2,1,0:T(8,128)(2,1)}, bf16[4,96,1024]{2,1,0:T(8,128)(2,1)S(1)}, u32[]{:S(2)}) copy-start(bf16[4,96,1024]{2,1,0:T(8,128)(2,1)S(1)} %collective-permute-done.18.refs_9_) | copy-start | bytes 2359300
  84.0 15.8 %collective-permute-start.21 = (bf16[4,96,1024]{2,1,0:T(8,128)(2,1)S(1)}, bf16[4,96,1024]{2,1,0:T(8,128)(2,1)S(1)}, u32[]{:S(2)}, u32[]{:S(2)}) collective-permute-start(bf16[4,96,1024]{2,1,0:T(8,128)(2,1)S(1)} %collective-permute-done.14.refs_3_), channel_id=1, source_target_pairs={{0,1},{1,0},{2,3},{3,2},{4,5},{5,4},{6,7},{7,6},{8,9},{9,8},{10,11... | collective-permute-start | bytes 2359304 | tf_op jit(solution)/shard_map/ppermute | solution.py:56
  84.1 15.6 %collective-permute-start.19 = (bf16[2,2,96,768]{3,2,1,0:T(8,128)(2,1)S(1)}, bf16[2,2,96,768]{3,2,1,0:T(8,128)(2,1)S(1)}, u32[]{:S(2)}, u32[]{:S(2)}) collective-permute-start(bf16[2,2,96,768]{3,2,1,0:T(8,128)(2,1)S(1)} %collective-permute-done.13.refs_6_), channel_id=1, source_target_pairs={{0,4},{4,0},{8,12},{12,8},{16,20},{20,16},{24,28},{28,24},{1,5},{5... | collective-permute-start | bytes 1769480 | tf_op jit(solution)/shard_map/ppermute | solution.py:56
  85.6 14.1 %collective-permute-start.22 = (bf16[2,2,96,768]{3,2,1,0:T(8,128)(2,1)S(1)}, bf16[2,2,96,768]{3,2,1,0:T(8,128)(2,1)S(1)}, u32[]{:S(2)}, u32[]{:S(2)}) collective-permute-start(bf16[2,2,96,768]{3,2,1,0:T(8,128)(2,1)S(1)} %collective-permute-done.13.refs_6_), channel_id=1, source_target_pairs={{0,1},{1,0},{2,3},{3,2},{4,5},{5,4},{6,7},{7,6},{8,9},{9,8},{10,11... | collective-permute-start | bytes 1769480 | tf_op jit(solution)/shard_map/ppermute | solution.py:56
  85.7 14.0 %collective-permute-start.23 = (bf16[2,2,96,768]{3,2,1,0:T(8,128)(2,1)S(1)}, bf16[2,2,96,768]{3,2,1,0:T(8,128)(2,1)S(1)}, u32[]{:S(2)}, u32[]{:S(2)}) collective-permute-start(bf16[2,2,96,768]{3,2,1,0:T(8,128)(2,1)S(1)} %collective-permute-done.15.refs_5_), channel_id=1, source_target_pairs={{0,1},{1,0},{2,3},{3,2},{4,5},{5,4},{6,7},{7,6},{8,9},{9,8},{10,11... | collective-permute-start | bytes 1769480 | tf_op jit(solution)/shard_map/ppermute | solution.py:56
  86.2 11.1 %collective-permute-start.20 = (bf16[2,3,256,128]{3,2,1,0:T(8,128)(2,1)S(1)}, bf16[2,3,256,128]{3,2,1,0:T(8,128)(2,1)S(1)}, u32[]{:S(2)}, u32[]{:S(2)}) collective-permute-start(bf16[2,3,256,128]{3,2,1,0:T(8,128)(2,1)S(1)} %get-tuple-element.171), channel_id=1, source_target_pairs={{0,2},{1,3},{2,0},{3,1},{4,6},{5,7},{6,4},{7,5},{8,10},{9,11},{10,... | collective-permute-start | bytes 1179656 | tf_op jit(solution)/shard_map/ppermute | solution.py:56
  99.8 2.6 collective-permute-start.24
  99.9 2.5 collective-permute-start.25
  142.0 6.1 %collective-permute-start.27 = (bf16[2,8,96,960]{3,2,1,0:T(8,128)(2,1)}, bf16[2,8,96,960]{3,2,1,0:T(8,128)(2,1)}, u32[]{:S(2)}, u32[]{:S(2)}) collective-permute-start(bf16[2,8,96,960]{3,2,1,0:T(8,128)(2,1)} %get-tuple-element.183), channel_id=1, source_target_pairs={{0,1},{1,0},{2,3},{3,2},{4,5},{5,4},{6,7},{7,6},{8,9},{9,8},{10,11... | collective-permute-start | bytes 8847368 | tf_op jit(solution)/shard_map/ppermute | solution.py:56
  142.2 10.9 %collective-permute-start.26 = (bf16[2,8,112,768]{3,2,1,0:T(8,128)(2,1)}, bf16[2,8,112,768]{3,2,1,0:T(8,128)(2,1)}, u32[]{:S(2)}, u32[]{:S(2)}) collective-permute-start(bf16[2,8,112,768]{3,2,1,0:T(8,128)(2,1)} %get-tuple-element.181), channel_id=1, source_target_pairs={{0,1},{1,0},{2,3},{3,2},{4,5},{5,4},{6,7},{7,6},{8,9},{9,8},{10,11... | collective-permute-start | bytes 8257544 | tf_op jit(solution)/shard_map/ppermute | solution.py:56
  142.6 13.6 %collective-permute-start.28 = (bf16[3,256,128]{2,1,0:T(8,128)(2,1)}, bf16[3,256,128]{2,1,0:T(8,128)(2,1)S(1)}, u32[]{:S(2)}, u32[]{:S(2)}) collective-permute-start(bf16[3,256,128]{2,1,0:T(8,128)(2,1)} %get-tuple-element.186), channel_id=1, source_target_pairs={{0,1},{1,0},{2,3},{3,2},{4,5},{5,4},{6,7},{7,6},{8,9},{9,8},{10,11... | collective-permute-start | bytes 589832 | tf_op jit(solution)/shard_map/ppermute | solution.py:56
  142.7 13.5 %collective-permute-start.29 = (bf16[3,256,128]{2,1,0:T(8,128)(2,1)}, bf16[3,256,128]{2,1,0:T(8,128)(2,1)S(1)}, u32[]{:S(2)}, u32[]{:S(2)}) collective-permute-start(bf16[3,256,128]{2,1,0:T(8,128)(2,1)} %get-tuple-element.187), channel_id=1, source_target_pairs={{0,2},{1,3},{2,0},{3,1},{4,6},{5,7},{6,4},{7,5},{8,10},{9,11},{10,... | collective-permute-start | bytes 589832 | tf_op jit(solution)/shard_map/ppermute | solution.py:56
  144.2 12.0 %collective-permute-start.30 = (bf16[3,256,128]{2,1,0:T(8,128)(2,1)}, bf16[3,256,128]{2,1,0:T(8,128)(2,1)S(1)}, u32[]{:S(2)}, u32[]{:S(2)}) collective-permute-start(bf16[3,256,128]{2,1,0:T(8,128)(2,1)} %get-tuple-element.188), channel_id=1, source_target_pairs={{0,3},{1,2},{2,1},{3,0},{4,7},{5,6},{6,5},{7,4},{8,11},{9,10},{10,... | collective-permute-start | bytes 589832 | tf_op jit(solution)/shard_map/ppermute | solution.py:56
  151.5 37.1 %collective-permute-start.32 = (bf16[2,2,2,96,960]{4,3,2,1,0:T(8,128)(2,1)}, bf16[2,2,2,96,960]{4,3,2,1,0:T(8,128)(2,1)}, u32[]{:S(2)}, u32[]{:S(2)}) collective-permute-start(bf16[2,2,2,96,960]{4,3,2,1,0:T(8,128)(2,1)} %sum_up.1), channel_id=1, source_target_pairs={{0,4},{4,0},{8,12},{12,8},{16,20},{20,16},{24,28},{28,24},{1,5},{5... | collective-permute-start | bytes 4423688 | tf_op jit(solution)/shard_map/ppermute | solution.py:56
  156.3 32.3 %collective-permute-start.31 = (bf16[2,2,2,112,768]{4,3,2,1,0:T(8,128)(2,1)}, bf16[2,2,2,112,768]{4,3,2,1,0:T(8,128)(2,1)}, u32[]{:S(2)}, u32[]{:S(2)}) collective-permute-start(bf16[2,2,2,112,768]{4,3,2,1,0:T(8,128)(2,1)} %sum_down.1), channel_id=1, source_target_pairs={{0,2},{1,3},{2,0},{3,1},{4,6},{5,7},{6,4},{7,5},{8,10},{9,11},{10,... | collective-permute-start | bytes 4128776 | tf_op jit(solution)/shard_map/ppermute | solution.py:56
  192.0 22.7 %collective-permute-start.34 = (bf16[2,2,96,960]{3,2,1,0:T(8,128)(2,1)}, bf16[2,2,96,960]{3,2,1,0:T(8,128)(2,1)S(1)}, u32[]{:S(2)}, u32[]{:S(2)}) collective-permute-start(bf16[2,2,96,960]{3,2,1,0:T(8,128)(2,1)} %get-tuple-element.203), channel_id=1, source_target_pairs={{0,2},{1,3},{2,0},{3,1},{4,6},{5,7},{6,4},{7,5},{8,10},{9,11},{10,... | collective-permute-start | bytes 2211848 | tf_op jit(solution)/shard_map/ppermute | solution.py:56
  193.6 21.1 %collective-permute-start.33 = (bf16[2,2,112,768]{3,2,1,0:T(8,128)(2,1)}, bf16[2,2,112,768]{3,2,1,0:T(8,128)(2,1)}, u32[]{:S(2)}, u32[]{:S(2)}) collective-permute-start(bf16[2,2,112,768]{3,2,1,0:T(8,128)(2,1)} %get-tuple-element.198), channel_id=1, source_target_pairs={{0,8},{4,12},{8,0},{12,4},{16,24},{20,28},{24,16},{28,20},{1,9},{5... | collective-permute-start | bytes 2064392 | tf_op jit(solution)/shard_map/ppermute | solution.py:56
  214.2 2.1 collective-permute-start.35
  214.2 2.6 collective-permute-start.36
  220.7 28.7 %collective-permute-start.41 = (bf16[2,256,768]{2,1,0:T(8,128)(2,1)}, bf16[2,256,768]{2,1,0:T(8,128)(2,1)}, u32[]{:S(2)}, u32[]{:S(2)}) collective-permute-start(bf16[2,256,768]{2,1,0:T(8,128)(2,1)} %get-tuple-element.222), channel_id=1, source_target_pairs={{0,2},{1,3},{2,0},{3,1},{4,6},{5,7},{6,4},{7,5},{8,10},{9,11},{10,... | collective-permute-start | bytes 2359304 | tf_op jit(solution)/shard_map/ppermute | solution.py:56
  222.2 20.8 %collective-permute-start.39 = (bf16[3,2,2,96,256]{4,3,2,1,0:T(8,128)(2,1)}, bf16[3,2,2,96,256]{4,3,2,1,0:T(8,128)(2,1)S(1)}, u32[]{:S(2)}, u32[]{:S(2)}) collective-permute-start(bf16[3,2,2,96,256]{4,3,2,1,0:T(8,128)(2,1)} %get-tuple-element.218), channel_id=1, source_target_pairs={{0,4},{4,0},{8,12},{12,8},{16,20},{20,16},{24,28},{28,24},{1,5},{5... | collective-permute-start | bytes 1769480 | tf_op jit(solution)/shard_map/ppermute | solution.py:56
  223.1 18.1 %collective-permute-start.37 = (bf16[2,112,768]{2,1,0:T(8,128)(2,1)}, bf16[2,112,768]{2,1,0:T(8,128)(2,1)S(1)}, u32[]{:S(2)}, u32[]{:S(2)}) collective-permute-start(bf16[2,112,768]{2,1,0:T(8,128)(2,1)} %get-tuple-element.209), channel_id=1, source_target_pairs={{0,16},{4,20},{8,24},{12,28},{16,0},{20,4},{24,8},{28,12},{1,17},{... | collective-permute-start | bytes 1032200 | tf_op jit(solution)/shard_map/ppermute | solution.py:56
  225.6 17.5 %collective-permute-start.38 = (bf16[2,96,960]{2,1,0:T(8,128)(2,1)}, bf16[2,96,960]{2,1,0:T(8,128)(2,1)}, u32[]{:S(2)}, u32[]{:S(2)}) collective-permute-start(bf16[2,96,960]{2,1,0:T(8,128)(2,1)} %get-tuple-element.216), channel_id=1, source_target_pairs={{0,8},{4,12},{8,0},{12,4},{16,24},{20,28},{24,16},{28,20},{1,9},{5... | collective-permute-start | bytes 1105928 | tf_op jit(solution)/shard_map/ppermute | solution.py:56
  230.3 21.9 %collective-permute-start.42 = (bf16[256,768]{1,0:T(8,128)(2,1)}, bf16[256,768]{1,0:T(8,128)(2,1)}, u32[]{:S(2)}, u32[]{:S(2)}) collective-permute-start(bf16[256,768]{1,0:T(8,128)(2,1)} %get-tuple-element.212), channel_id=1, source_target_pairs={{0,1},{1,0},{2,3},{3,2},{4,5},{5,4},{6,7},{7,6},{8,9},{9,8},{10,11... | collective-permute-start | bytes 1179656 | tf_op jit(solution)/shard_map/ppermute | solution.py:56
  241.2 11.6 %collective-permute-start.43 = (bf16[256,768]{1,0:T(8,128)(2,1)}, bf16[256,768]{1,0:T(8,128)(2,1)}, u32[]{:S(2)}, u32[]{:S(2)}) collective-permute-start(bf16[256,768]{1,0:T(8,128)(2,1)} %get-tuple-element.213), channel_id=1, source_target_pairs={{0,1},{1,0},{2,3},{3,2},{4,5},{5,4},{6,7},{7,6},{8,9},{9,8},{10,11... | collective-permute-start | bytes 1179656 | tf_op jit(solution)/shard_map/ppermute | solution.py:56
  246.7 7.1 %collective-permute-start.40 = (bf16[112,768]{1,0:T(8,128)(2,1)}, bf16[112,768]{1,0:T(8,128)(2,1)S(1)}, u32[]{:S(2)}, u32[]{:S(2)}) collective-permute-start(bf16[112,768]{1,0:T(8,128)(2,1)} %get-tuple-element.220), channel_id=1, source_target_pairs={{0,4},{4,0},{8,12},{12,8},{16,20},{20,16},{24,28},{28,24},{1,5},{5... | collective-permute-start | bytes 516104 | tf_op jit(solution)/shard_map/ppermute | solution.py:56
  249.3 20.2 %collective-permute-start.44 = (bf16[96,960]{1,0:T(8,128)(2,1)}, bf16[96,960]{1,0:T(8,128)(2,1)S(1)}, u32[]{:S(2)}, u32[]{:S(2)}) collective-permute-start(bf16[96,960]{1,0:T(8,128)(2,1)} %get-tuple-element.225), channel_id=1, source_target_pairs={{0,16},{4,20},{8,24},{12,28},{16,0},{20,4},{24,8},{28,12},{1,17},{... | collective-permute-start | bytes 552968 | tf_op jit(solution)/shard_map/ppermute | solution.py:56
  249.4 20.0 %collective-permute-start.45 = (bf16[3,96,256]{2,1,0:T(8,128)(2,1)}, bf16[3,96,256]{2,1,0:T(8,128)(2,1)S(1)}, u32[]{:S(2)}, u32[]{:S(2)}) collective-permute-start(bf16[3,96,256]{2,1,0:T(8,128)(2,1)} %get-tuple-element.226), channel_id=1, source_target_pairs={{0,16},{4,20},{8,24},{12,28},{16,0},{20,4},{24,8},{28,12},{1,17},{... | collective-permute-start | bytes 442376 | tf_op jit(solution)/shard_map/ppermute | solution.py:56
  252.3 17.1 %collective-permute-start.46 = (bf16[3,96,256]{2,1,0:T(8,128)(2,1)}, bf16[3,96,256]{2,1,0:T(8,128)(2,1)S(1)}, u32[]{:S(2)}, u32[]{:S(2)}) collective-permute-start(bf16[3,96,256]{2,1,0:T(8,128)(2,1)} %get-tuple-element.227), channel_id=1, source_target_pairs={{0,8},{4,12},{8,0},{12,4},{16,24},{20,28},{24,16},{28,20},{1,9},{5... | collective-permute-start | bytes 442376 | tf_op jit(solution)/shard_map/ppermute | solution.py:56
  252.8 16.6 %collective-permute-start.47 = (bf16[3,96,256]{2,1,0:T(8,128)(2,1)}, bf16[3,96,256]{2,1,0:T(8,128)(2,1)S(1)}, u32[]{:S(2)}, u32[]{:S(2)}) collective-permute-start(bf16[3,96,256]{2,1,0:T(8,128)(2,1)} %get-tuple-element.228), channel_id=1, source_target_pairs={{0,24},{4,28},{8,16},{12,20},{16,8},{20,12},{24,0},{28,4},{1,25},{... | collective-permute-start | bytes 442376 | tf_op jit(solution)/shard_map/ppermute | solution.py:56
  (35 other events, 122.4 us)
